TPU v7x, 32 devices: a whole 2x2x4 slice. The times are simulated.
32 devices in a mesh: groups: 2 (over x), tiles: 16 (over z, y, core).
Axes of the slice: x: 2, y: 2, z: 4, core: 2. Of those that a mesh axis runs over, the one named last changes fastest.
Arguments:
- features: bfloat16 [128, 8, 16, 256], P(('groups', 'tiles')), parts along dimension 0, may hold values from -6 to 6
- weight_one: bfloat16 [6912, 256], P('tiles'), may hold values from -0.078125 to 0.078125
- weight_two: bfloat16 [6912, 256], P('tiles'), may hold values from -0.078125 to 0.078125
- cotangent: bfloat16 [128, 8, 16, 256], P(('groups', 'tiles')), parts along dimension 0, may hold values from -6 to 6
- block_mask: int32 [32, 2, 4], P('groups'), parts along dimension 0, may hold values 0 or 1
Outputs:
- features_out: bfloat16 [128, 8, 16, 256], P(('groups', 'tiles')), parts along dimension 0
- grad_w1: float32 [13824, 256], P(('groups', 'tiles')), parts along dimension 0
- grad_w2: float32 [13824, 256], P(('groups', 'tiles')), parts along dimension 0
There are 2 independent parts, one for each index of `groups`. A program takes and returns all parts, laid end to end along the dimension named above; an argument that names none is the same for every part. Nothing has to cross between parts.
All inputs are finite; a program needn't handle non-finite values.
Results may differ from a plain program's by a relative error of at most 0.0049.
Values may be sent and summed in bfloat16 or wider, within the bound.
No kernel may reach another device: no remote copies, remote signals or barrier semaphores. Data moves between devices by JAX's collectives and lax.ppermute only.
A program may use at most 128 MiB of HBM per device.

v0:
```python
import functools
import math

import jax
import jax.numpy as jnp
from jax import lax
from jax.experimental import pallas as pl
from jax.experimental.pallas import tpu as pltpu
from jax.sharding import PartitionSpec as P

B = 4
RING = (0, 2, 4, 6, 7, 5, 3, 1)
BF = jnp.bfloat16
F32 = jnp.float32


def with_halo(block, axis, width):
    count = lax.axis_size(axis)
    forward = [(i, i + 1) for i in range(count - 1)]
    backward = [(target, source) for source, target in forward]
    low = lax.ppermute(block[-width:], axis, forward)
    high = lax.ppermute(block[:width], axis, backward)
    return low, high


def tap_columns(padded, flipped):
    extent = [padded.shape[d] - 2 for d in range(3)]
    taps = []
    for a in range(3):
        for b in range(3):
            for c in range(3):
                x, y, z = (2 - a, 2 - b, 2 - c) if flipped else (a, b, c)
                taps.append(padded[x : x + extent[0], y : y + extent[1], z : z + extent[2]])
    stacked = jnp.stack(taps, axis=3)
    return stacked.reshape(extent[0] * extent[1] * extent[2], 27 * padded.shape[3])


def expand_mask(cells, edge):
    planes, rows_y, rows_z = cells.shape
    values = jnp.broadcast_to(
        cells.astype(F32)[:, None, :, None, :, None], (planes, edge, rows_y, edge, rows_z, edge)
    )
    return values.reshape(planes * edge, rows_y * edge, rows_z * edge, 1)


def silu_slope(values):
    logistic = jax.nn.sigmoid(values)
    return logistic * (1.0 + values * (1.0 - logistic))


def near_cells_of(block_mask):
    padded_cells = jnp.pad(block_mask, ((1, 1), (0, 0), (0, 0)))
    return lax.dynamic_slice_in_dim(padded_cells, lax.axis_index("tiles"), 3, 0)


def on_any(features, weight_one, weight_two, cotangent, block_mask):
    depth, width_y, width_z, channels = features.shape
    loss_scale = 1.0 / math.sqrt(lax.axis_size("tiles") * depth * width_y * width_z)
    own_mask = expand_mask(near_cells_of(block_mask), B)[depth : 2 * depth]
    own_flat = own_mask.reshape(-1, 1)

    def cube(field):
        low, high = with_halo(field, "tiles", 1)
        field = jnp.concatenate([low, field, high], axis=0)
        return jnp.pad(field, ((0, 0), (1, 1), (1, 1), (0, 0)))

    def grad_piece(columns_in, rows_in):
        product = lax.dot_general(
            columns_in, rows_in, (((0,), (0,)), ((), ())), preferred_element_type=F32
        )
        return lax.psum_scatter(product * loss_scale, "tiles", scatter_dimension=0, tiled=True)

    full_one = lax.all_gather(weight_one, "tiles", axis=0, tiled=True)
    full_two = lax.all_gather(weight_two, "tiles", axis=0, tiled=True)
    weight_back = jnp.swapaxes(full_two.reshape(27, channels, channels), 1, 2).reshape(
        27 * channels, channels
    )
    inputs = (features * own_mask).astype(BF)
    feature_cols = tap_columns(cube(inputs), False)
    hidden_pre = jnp.dot(feature_cols, full_one, preferred_element_type=F32)
    active = (jax.nn.silu(hidden_pre) * own_flat).astype(BF).reshape(features.shape)
    active_cols = tap_columns(cube(active), False)
    second = jnp.dot(active_cols, full_two, preferred_element_type=F32)
    features_out = (second * own_flat).astype(BF).reshape(features.shape)
    cot = (cotangent * own_mask).astype(BF)
    grad_two = grad_piece(active_cols, cot.reshape(-1, channels))
    upstream = jnp.dot(tap_columns(cube(cot), True), weight_back, preferred_element_type=F32)
    hidden_grad = (upstream * silu_slope(hidden_pre) * own_flat).astype(BF)
    grad_one = grad_piece(feature_cols, hidden_grad)
    return (features_out, grad_one, grad_two)


def chip_at(place):
    return jnp.where(place < 4, 2 * place, 15 - 2 * place)


def place_of(tile):
    chip = tile // 2
    return jnp.where(chip % 2 == 0, chip // 2, 7 - chip // 2)


def shard_rows(tile, core, hop, flip, rows):
    step = jnp.where(core == 0, -hop, hop)
    chip = chip_at((place_of(tile) + step + 8) % 8)
    return pl.multiple_of((2 * chip + (1 - core if flip else core)) * rows, 16)


def store_shifted(out_ref, x0, rows, ny, nz, channels):
    planes = rows.shape[0] // (ny * nz)
    wide = rows.astype(F32)
    z = lax.broadcasted_iota(jnp.int32, wide.shape, 0) % nz
    before = jnp.where(z == 0, 0.0, pltpu.roll(wide, 1, 0)).astype(BF)
    after = jnp.where(z == nz - 1, 0.0, pltpu.roll(wide, wide.shape[0] - 1, 0)).astype(BF)
    for rho, value in enumerate((before, rows.astype(BF), after)):
        out_ref[x0 : x0 + planes, 1 : ny + 1, :, rho * channels : (rho + 1) * channels] = (
            value.reshape(planes, ny, nz, channels)
        )


def clear_edges(out_ref, ny):
    edge = jnp.zeros((out_ref.shape[0], 1) + tuple(out_ref.shape[2:]), BF)
    out_ref[:, 0:1] = edge
    out_ref[:, ny + 1 : ny + 2] = edge


def prep_kernel(tile_ref, cells_ref, low, f_own, c_own, high, sx_ref, sc_ref, int_ref, mask_ref):
    depth, ny, nz, channels = f_own.shape
    area = ny * nz
    tile = tile_ref[0]
    last = cells_ref.shape[0] - 1
    row = lax.broadcasted_iota(jnp.int32, (area, channels), 0)
    block_y, block_z = row // (B * nz), (row % nz) // B
    m = []
    for i in range(3):
        at = tile + i - 1
        inside = jnp.logical_and(at >= 0, at <= last)
        at = jnp.clip(at, 0, last)
        value = jnp.zeros((area, channels), F32)
        for y in range(ny // B):
            for z in range(nz // B):
                cell = jnp.where(inside, cells_ref[at, y * (nz // B) + z], 0).astype(F32)
                here = jnp.logical_and(block_y == y, block_z == z)
                value = jnp.where(here, cell, value)
        value = value.astype(BF)
        mask_ref[i] = value
        m.append(value.reshape(1, area, channels))

    def rows(value, side):
        planes = value.shape[0]
        value = value.reshape(planes, area, channels) * m[side]
        return value.reshape(planes * area, channels)

    clear_edges(sx_ref, ny)
    clear_edges(sc_ref, ny)
    fs = [rows(low[0:2], 0), rows(f_own[...], 1), rows(high[0:2], 2)]
    for x0, value in zip((0, 2, 2 + depth), fs):
        store_shifted(sx_ref, x0, value, ny, nz, channels)
    int_ref[:, 0:area] = fs[0][area:].T
    int_ref[:, area : area + depth * area] = fs[1].T
    int_ref[:, area + depth * area :] = fs[2][:area].T
    for x0, value, side in ((0, low[2:3], 0), (1, c_own[...], 1), (1 + depth, high[2:3], 2)):
        store_shifted(sc_ref, x0, rows(value, side), ny, nz, channels)


def fill_weight(tile_ref, pieces, w_ref):
    tile = tile_ref[0]
    core = tile % 2
    rows = w_ref.shape[0] // 16
    for k, piece in enumerate(pieces):
        hop, holder = (k, core) if k < 5 else (k - 4, 1 - core)
        for half in range(piece.shape[0] // rows):
            start = shard_rows(tile, holder, hop, half == 1, rows)
            w_ref[pl.ds(start, rows)] = piece[half * rows : (half + 1) * rows]


def split_shards(tile_ref, g_ref, keep_ref, send_ref):
    tile = tile_ref[0]
    core = tile % 2
    rows = g_ref.shape[0] // 16
    for out_ref, holder in ((send_ref, 1 - core), (keep_ref, core)):
        at = 0
        for hop in (4, 3, 2, 1, 0):
            for flip in (False,) if hop in (0, 4) else (False, True):
                start = shard_rows(tile, holder, -hop, flip, rows)
                out_ref[at : at + rows] = g_ref[pl.ds(start, rows)]
                at += rows


def window(ref, x, y, planes, ny, lo=0, hi=None):
    value = ref[x : x + planes, y : y + ny, :, lo:hi]
    return value.reshape(-1, value.shape[-1])


def conv(s_ref, w_ref, x0, planes, ny, channels):
    acc = None
    for p in range(3):
        for q in range(3):
            t = 9 * p + 3 * q
            part = jnp.dot(
                window(s_ref, x0 + p, q, planes, ny),
                w_ref[t * channels : (t + 3) * channels],
                preferred_element_type=F32,
            )
            acc = part if acc is None else acc + part
    return acc


def store_taps(g_ref, p, q, part, channels):
    for rho in range(3):
        t = 9 * p + 3 * q + 2 - rho
        g_ref[t * channels : (t + 1) * channels] = part[:, rho * channels : (rho + 1) * channels]


def masked(value, mask_ref, side):
    area, channels = mask_ref.shape[1:]
    own = mask_ref[side].reshape(1, area, channels).astype(F32)
    return (value.reshape(-1, area, channels) * own).reshape(-1, channels)


def first_kernel(n, tile_ref, sx_ref, sc_ref, mask_ref, *rest):
    pieces, (pre_ref, act_ref, keep_ref, send_ref, w_ref, g_ref) = rest[:n], rest[n:]
    area, channels = mask_ref.shape[1:]
    ny = sx_ref.shape[1] - 2
    depth = pre_ref.shape[0] // area
    fill_weight(tile_ref, pieces, w_ref)
    pre = conv(sx_ref, w_ref, 1, depth, ny, channels)
    pre_ref[...] = pre
    act = masked(pre * jax.nn.sigmoid(pre), mask_ref, 1).astype(BF)
    act_ref[...] = act
    act_t = act.T
    for p in range(3):
        for q in range(3):
            part = jnp.dot(
                act_t, window(sc_ref, 2 - p, 2 - q, depth, ny), preferred_element_type=F32
            )
            store_taps(g_ref, p, q, part.astype(BF), channels)
    split_shards(tile_ref, g_ref, keep_ref, send_ref)


def second_kernel(n, tile_ref, sc_ref, int_ref, pre_ref, mask_ref, *rest):
    pieces, (keep_ref, send_ref, w_ref, sd_ref, g_ref) = rest[:n], rest[n:]
    area, channels = mask_ref.shape[1:]
    ny, nz = sc_ref.shape[1] - 2, sc_ref.shape[2]
    depth = pre_ref.shape[0] // area
    fill_weight(tile_ref, pieces, w_ref)
    acc = None
    for p in range(3):
        for q in range(3):
            for r in range(3):
                t = 9 * p + 3 * q + r
                lo = (2 - r) * channels
                part = lax.dot_general(
                    window(sc_ref, 2 - p, 2 - q, depth, ny, lo, lo + channels),
                    w_ref[t * channels : (t + 1) * channels],
                    (((1,), (1,)), ((), ())),
                    preferred_element_type=F32,
                )
                acc = part if acc is None else acc + part
    delta = masked(acc * silu_slope(pre_ref[...]), mask_ref, 1).astype(BF)
    clear_edges(sd_ref, ny)
    store_shifted(sd_ref, 0, delta, ny, nz, channels)
    for q in range(3):
        right = window(sd_ref, 0, 2 - q, depth, ny)
        for p in range(3):
            part = jnp.dot(
                int_ref[:, p * area : (p + depth) * area], right, preferred_element_type=F32
            )
            store_taps(g_ref, p, q, part.astype(BF), channels)
    split_shards(tile_ref, g_ref, keep_ref, send_ref)


def third_kernel(n, tile_ref, sx_ref, act_ref, mask_ref, *rest):
    out_ref, w_ref, v_ref, sa_ref = rest[2 * n :]
    area, channels = mask_ref.shape[1:]
    ny, nz = sx_ref.shape[1] - 2, sx_ref.shape[2]
    depth = act_ref.shape[0] // area
    fill_weight(tile_ref, rest[:n], w_ref)
    fill_weight(tile_ref, rest[n : 2 * n], v_ref)
    clear_edges(sa_ref, ny)
    store_shifted(sa_ref, 1, act_ref[...], ny, nz, channels)
    for x0, side in ((0, 0), (1 + depth, 2)):
        pre = conv(sx_ref, w_ref, x0, 1, ny, channels)
        act = masked(pre * jax.nn.sigmoid(pre), mask_ref, side).astype(BF)
        store_shifted(sa_ref, x0, act, ny, nz, channels)
    second = conv(sa_ref, v_ref, 0, depth, ny, channels)
    out_ref[...] = masked(second, mask_ref, 1).astype(BF).reshape(out_ref.shape)


VMEM_LIMIT = 32 * 1024 * 1024


def on_ring(features, weight_one, weight_two, cotangent, block_mask):
    depth, ny, nz, channels = features.shape
    area = ny * nz
    rows = weight_one.shape[0]
    chips = len(RING)
    tiles = 2 * chips
    loss_scale = 1.0 / math.sqrt(tiles * depth * area)
    tile = lax.axis_index("tiles").astype(jnp.int32)[None]

    def permute(pairs):
        return functools.partial(lax.ppermute, axis_name="tiles", perm=pairs)

    onward = permute(
        [(2 * RING[i], 2 * RING[(i + 1) % chips]) for i in range(chips)]
        + [(2 * RING[i] + 1, 2 * RING[i - 1] + 1) for i in range(chips)]
    )
    sibling = permute([(i, i ^ 1) for i in range(tiles)])
    up = permute([(i, (i + 1) % tiles) for i in range(tiles)])
    down = permute([(i, (i - 1) % tiles) for i in range(tiles)])

    def gathered(weight, other):
        pair = jnp.concatenate([weight, other])
        p1 = onward(pair)
        p2 = onward(p1)
        p3 = onward(p2)
        p4 = onward(p3[:rows])
        return [pair, p1, p2, p3, p4] + [sibling(p) for p in (p1, p2, p3, p4)]

    other_one, other_two = sibling(weight_one), sibling(weight_two)
    features_late, cot_late, _ = lax.optimization_barrier((features, cotangent, other_one))
    low = up(jnp.concatenate([features_late[-2:], cot_late[-1:]]))
    high = down(jnp.concatenate([features_late[:2], cot_late[:1]]))
    ones, twos = gathered(weight_one, other_one), gathered(weight_two, other_two)
    n = len(ones)

    smem = pl.BlockSpec(memory_space=pltpu.SMEM)
    vmem = pl.BlockSpec(memory_space=pltpu.VMEM)
    params = pltpu.CompilerParams(vmem_limit_bytes=VMEM_LIMIT)
    shape = jax.ShapeDtypeStruct
    flops = 2 * depth * area * 27 * channels * channels

    def cost(convs):
        return pl.CostEstimate(
            flops=convs * flops, transcendentals=0, bytes_accessed=8 << 20
        )

    sx, sc, in_t, near = pl.pallas_call(
        prep_kernel,
        name="prep",
        out_shape=(
            shape((depth + 4, ny + 2, nz, 3 * channels), BF),
            shape((depth + 2, ny + 2, nz, 3 * channels), BF),
            shape((channels, (depth + 2) * area), BF),
            shape((3, area, channels), BF),
        ),
        in_specs=[smem, smem] + [vmem] * 4,
        out_specs=(vmem,) * 4,
        compiler_params=params,
    )(tile, block_mask.reshape(tiles, -1), low, features, cotangent, high)

    shards = (shape((chips * rows, channels), BF),) * 2
    weights = pltpu.VMEM((27 * channels, channels), BF)
    pre, act, keep_two, send_two = pl.pallas_call(
        functools.partial(first_kernel, n),
        name="first",
        out_shape=(shape((depth * area, channels), F32), shape((depth * area, channels), BF))
        + shards,
        in_specs=[smem] + [vmem] * (3 + n),
        out_specs=(vmem,) * 4,
        scratch_shapes=[weights, weights],
        compiler_params=params,
        cost_estimate=cost(2),
    )(tile, sx, sc, near, *ones)
    got_two = sibling(send_two)

    keep_one, send_one = pl.pallas_call(
        functools.partial(second_kernel, n),
        name="second",
        out_shape=shards,
        in_specs=[smem] + [vmem] * (4 + n),
        out_specs=(vmem,) * 2,
        scratch_shapes=[
            weights,
            pltpu.VMEM((depth, ny + 2, nz, 3 * channels), BF),
            weights,
        ],
        compiler_params=params,
        cost_estimate=cost(2),
    )(tile, sc, in_t, pre, near, *twos)
    got_one = sibling(send_one)

    act_late, _ = lax.optimization_barrier((act, got_two))
    features_out = pl.pallas_call(
        functools.partial(third_kernel, n),
        name="third",
        out_shape=shape(features.shape, BF),
        in_specs=[smem] + [vmem] * (3 + 2 * n),
        out_specs=vmem,
        scratch_shapes=[
            weights,
            weights,
            pltpu.VMEM((depth + 2, ny + 2, nz, 3 * channels), BF),
        ],
        compiler_params=params,
        cost_estimate=cost(2),
    )(tile, sx, act_late, near, *ones, *twos)

    def scattered(keep, got):
        def both(lo, hi):
            return keep[lo:hi].astype(F32) + got[lo:hi].astype(F32)

        moving = onward(both(0, rows).astype(BF)).astype(F32)
        moving = jnp.concatenate([moving, jnp.zeros_like(moving)])
        for k in range(3):
            lo = (1 + 2 * k) * rows
            moving = onward((both(lo, lo + 2 * rows) + moving).astype(BF)).astype(F32)
        across = sibling(moving[rows:].astype(BF)).astype(F32)
        return (both(7 * rows, 8 * rows) + moving[:rows] + across) * loss_scale

    return (features_out, scattered(keep_one, got_one), scattered(keep_two, got_two))


def solution(mesh):
    placed = (
        P(("groups", "tiles"), None, None, None),
        P("tiles", None),
        P("tiles", None),
        P(("groups", "tiles"), None, None, None),
        P("groups", None, None),
    )
    on_device = on_ring if mesh.shape["tiles"] == 2 * len(RING) else on_any
    return jax.shard_map(
        on_device,
        mesh=mesh,
        in_specs=placed,
        out_specs=(
            P(("groups", "tiles"), None, None, None),
            P(("groups", "tiles"), None),
            P(("groups", "tiles"), None),
        ),
        check_vma=False,
    )
```

profile of v0, /device:TPU:0, one launch (start us, length us, event | category | flops | bytes accessed | tf_op | source)
XLA Modules:
  0.0 118.5 jit_solution(13792805656382886337)
XLA Ops:
  0.7 0.5 collective-permute-start
  1.2 0.9 constant_dynamic-update-slice_fusion.1
  2.2 1.0 constant_dynamic-update-slice_fusion.3
  3.2 3.1 %collective-permute-start.3 = (bf16[864,256]{1,0:T(8,128)(2,1)S(1)}, bf16[864,256]{1,0:T(8,128)(2,1)S(1)}, u32[]{:S(2)}, u32[]{:S(2)}) collective-permute-start(bf16[864,256]{1,0:T(8,128)(2,1)S(1)} %constant_dynamic-update-slice_fusion.rest_0_), channel_id=1, source_target_pairs={{0,4},{4,8},{8,12},{12,14},{14,10},{10,6},{6,2},{2,0},{1,3},{5,1},... | collective-permute-start | bytes 1327112 | tf_op jit(solution)/shard_map/ppermute | solution.py:314
  6.3 1.6 %collective-permute-start.13 = (bf16[864,256]{1,0:T(8,128)(2,1)S(1)}, bf16[864,256]{1,0:T(8,128)(2,1)}, u32[]{:S(2)}, u32[]{:S(2)}) collective-permute-start(bf16[864,256]{1,0:T(8,128)(2,1)S(1)} %constant_dynamic-update-slice_fusion.2.rest_9_.rest_0_), channel_id=1, source_target_pairs={{0,4},{4,8},{8,12},{12,14},{14,10},{10,6},{6,2},{2,0},{1,3},{5,1},... | collective-permute-start | bytes 1327112 | tf_op jit(solution)/shard_map/ppermute | solution.py:314
  7.9 4.6 %collective-permute-done.3.rest_1_ = bf16[864,256]{1,0:T(8,128)(2,1)S(1)} collective-permute-done((bf16[864,256]{1,0:T(8,128)(2,1)S(1)}, bf16[864,256]{1,0:T(8,128)(2,1)S(1)}, u32[]{:S(2)}, u32[]{:S(2)}) %collective-permute-start.3) | collective-permute-done | bytes 442400 | tf_op jit(solution)/shard_map/ppermute | solution.py:314
  12.5 2.1 %collective-permute-start.4 = (bf16[864,256]{1,0:T(8,128)(2,1)S(1)}, bf16[864,256]{1,0:T(8,128)(2,1)S(1)}, u32[]{:S(2)}, u32[]{:S(2)}) collective-permute-start(bf16[864,256]{1,0:T(8,128)(2,1)S(1)} %collective-permute-done.3.rest_1_), channel_id=1, source_target_pairs={{0,4},{4,8},{8,12},{12,14},{14,10},{10,6},{6,2},{2,0},{1,3},{5,1},... | collective-permute-start | bytes 1327112 | tf_op jit(solution)/shard_map/ppermute | solution.py:315
  14.6 2.8 %collective-permute-done.13.rest_10_.rest_1_ = bf16[864,256]{1,0:T(8,128)(2,1)} collective-permute-done((bf16[864,256]{1,0:T(8,128)(2,1)S(1)}, bf16[864,256]{1,0:T(8,128)(2,1)}, u32[]{:S(2)}, u32[]{:S(2)}) %collective-permute-start.13) | collective-permute-done | bytes 442400 | tf_op jit(solution)/shard_map/ppermute | solution.py:314
  17.3 2.1 %collective-permute-start.14 = (bf16[864,256]{1,0:T(8,128)(2,1)}, bf16[864,256]{1,0:T(8,128)(2,1)}, u32[]{:S(2)}, u32[]{:S(2)}) collective-permute-start(bf16[864,256]{1,0:T(8,128)(2,1)} %collective-permute-done.13.rest_10_.rest_1_), channel_id=1, source_target_pairs={{0,4},{4,8},{8,12},{12,14},{14,10},{10,6},{6,2},{2,0},{1,3},{5,1},... | collective-permute-start | bytes 1327112 | tf_op jit(solution)/shard_map/ppermute | solution.py:315
  19.4 2.5 %collective-permute-done.4.rest_2_ = bf16[864,256]{1,0:T(8,128)(2,1)S(1)} collective-permute-done((bf16[864,256]{1,0:T(8,128)(2,1)S(1)}, bf16[864,256]{1,0:T(8,128)(2,1)S(1)}, u32[]{:S(2)}, u32[]{:S(2)}) %collective-permute-start.4) | collective-permute-done | bytes 442400 | tf_op jit(solution)/shard_map/ppermute | solution.py:315
  22.0 2.1 %collective-permute-start.5 = (bf16[864,256]{1,0:T(8,128)(2,1)S(1)}, bf16[864,256]{1,0:T(8,128)(2,1)S(1)}, u32[]{:S(2)}, u32[]{:S(2)}) collective-permute-start(bf16[864,256]{1,0:T(8,128)(2,1)S(1)} %collective-permute-done.4.rest_2_), channel_id=1, source_target_pairs={{0,4},{4,8},{8,12},{12,14},{14,10},{10,6},{6,2},{2,0},{1,3},{5,1},... | collective-permute-start | bytes 1327112 | tf_op jit(solution)/shard_map/ppermute | solution.py:316
  24.0 2.8 %collective-permute-done.14.rest_11_.rest_2_ = bf16[864,256]{1,0:T(8,128)(2,1)} collective-permute-done((bf16[864,256]{1,0:T(8,128)(2,1)}, bf16[864,256]{1,0:T(8,128)(2,1)}, u32[]{:S(2)}, u32[]{:S(2)}) %collective-permute-start.14) | collective-permute-done | bytes 442400 | tf_op jit(solution)/shard_map/ppermute | solution.py:315
  26.8 2.1 %collective-permute-start.15 = (bf16[864,256]{1,0:T(8,128)(2,1)}, bf16[864,256]{1,0:T(8,128)(2,1)S(1)}, u32[]{:S(2)}, u32[]{:S(2)}) collective-permute-start(bf16[864,256]{1,0:T(8,128)(2,1)} %collective-permute-done.14.rest_11_.rest_2_), channel_id=1, source_target_pairs={{0,4},{4,8},{8,12},{12,14},{14,10},{10,6},{6,2},{2,0},{1,3},{5,1},... | collective-permute-start | bytes 1327112 | tf_op jit(solution)/shard_map/ppermute | solution.py:316
  29.1 0.5 collective-permute-start.8
  29.6 1.8 %collective-permute-done.5.rest_3_ = bf16[864,256]{1,0:T(8,128)(2,1)S(1)} collective-permute-done((bf16[864,256]{1,0:T(8,128)(2,1)S(1)}, bf16[864,256]{1,0:T(8,128)(2,1)S(1)}, u32[]{:S(2)}, u32[]{:S(2)}) %collective-permute-start.5) | collective-permute-done | bytes 442400 | tf_op jit(solution)/shard_map/ppermute | solution.py:316
  31.4 3.9 %collective-permute-start.2 = (bf16[3,8,16,256]{3,2,1,0:T(8,128)(2,1)S(1)}, bf16[3,8,16,256]{3,2,1,0:T(8,128)(2,1)S(1)}, u32[]{:S(2)}, u32[]{:S(2)}) collective-permute-start(bf16[3,8,16,256]{3,2,1,0:T(8,128)(2,1)S(1)} %pad_maximum_fusion.1), channel_id=1, source_target_pairs={{0,15},{1,0},{2,1},{3,2},{4,3},{5,4},{6,5},{7,6},{8,7},{9,8},{10,9... | collective-permute-start | bytes 589832 | tf_op jit(solution)/shard_map/ppermute | solution.py:323
  35.4 3.6 %collective-permute-done.1.low = bf16[3,8,16,256]{3,2,1,0:T(8,128)(2,1)S(1)} collective-permute-done((bf16[3,8,16,256]{3,2,1,0:T(8,128)(2,1)S(1)}, bf16[3,8,16,256]{3,2,1,0:T(8,128)(2,1)S(1)}, u32[]{:S(2)}, u32[]{:S(2)}) %collective-permute-start.1) | collective-permute-done | bytes 196640 | tf_op jit(solution)/shard_map/ppermute | solution.py:322
  39.0 0.2 collective-permute-start.9
  39.2 1.4 %collective-permute-start.6 = (bf16[432,256]{1,0:T(8,128)(2,1)S(1)}, bf16[432,256]{1,0:T(8,128)(2,1)S(1)}, u32[]{:S(2)}, u32[]{:S(2)}) collective-permute-start(bf16[432,256]{1,0:T(8,128)(2,1)S(1)} %slice.130), channel_id=1, source_target_pairs={{0,4},{4,8},{8,12},{12,14},{14,10},{10,6},{6,2},{2,0},{1,3},{5,1},... | collective-permute-start | bytes 663560 | tf_op jit(solution)/shard_map/ppermute | solution.py:317
  40.6 1.6 %collective-permute-start.16 = (bf16[432,256]{1,0:T(8,128)(2,1)S(1)}, bf16[432,256]{1,0:T(8,128)(2,1)S(1)}, u32[]{:S(2)}, u32[]{:S(2)}) collective-permute-start(bf16[432,256]{1,0:T(8,128)(2,1)S(1)} %slice.131), channel_id=1, source_target_pairs={{0,4},{4,8},{8,12},{12,14},{14,10},{10,6},{6,2},{2,0},{1,3},{5,1},... | collective-permute-start | bytes 663560 | tf_op jit(solution)/shard_map/ppermute | solution.py:317
  42.2 3.2 %collective-permute-done.6.rest_4_ = bf16[432,256]{1,0:T(8,128)(2,1)S(1)} collective-permute-done((bf16[432,256]{1,0:T(8,128)(2,1)S(1)}, bf16[432,256]{1,0:T(8,128)(2,1)S(1)}, u32[]{:S(2)}, u32[]{:S(2)}) %collective-permute-start.6) | collective-permute-done | bytes 221216 | tf_op jit(solution)/shard_map/ppermute | solution.py:317
  45.5 0.8 copy-done.5
  46.2 0.5 collective-permute-start.17
  46.7 0.8 copy-done.8
  47.5 0.3 collective-permute-done.16.rest_13_.rest_4_
  47.8 0.7 copy-done.11
  48.5 0.2 collective-permute-start.19
  48.8 1.4 %prep.1 = (bf16[8,10,16,768]{3,2,1,0:T(8,128)(2,1)S(1)}, bf16[6,10,16,768]{3,2,1,0:T(8,128)(2,1)S(1)}, bf16[256,768]{1,0:T(8,128)(2,1)S(1)}, bf16[3,128,256]{2,1,0:T(8,128)(2,1)S(1)}) custom-call(s32[1]{0:T(128)} %bitcast.tile_ref, s32[16,8]{1,0:T(8,128)S(1)} %copy.8.cells_ref, bf16[3,8,16,256]{3,2,1,0:T(8,128)(2,1)S(1)} %collective-permute-done.1.low, ...), custom_call_target="tpu_custom_call" | custom-call | tf_op jit(solution)/shard_map/prep/pallas_call | solution.py:338
  50.2 0.4 collective-permute-start.20
  50.6 1.0 copy-done.3
  51.6 1.0 copy-done.6
  52.6 1.0 copy-done.9
  53.6 9.2 %first.1 = (f32[512,256]{1,0:T(8,128)S(1)}, bf16[512,256]{1,0:T(8,128)(2,1)S(1)}, bf16[3456,256]{1,0:T(8,128)(2,1)S(1)}, bf16[3456,256]{1,0:T(8,128)(2,1)S(1)}) custom-call(s32[1]{0:T(128)} %bitcast.tile_ref, bf16[8,10,16,768]{3,2,1,0:T(8,128)(2,1)S(1)} %get-tuple-element.18.sx_ref, bf16[6,10,16,768]{3,2,1,0:T(8,128)(2,1)S(1)} %get-tuple-element.19.sc_ref, ...), custom_call_target="tpu_custom_call" | custom-call | flops 3623878656 | bytes 8388608 | tf_op jit(solution)/shard_map/first/pallas_call | solution.py:354
  62.8 9.7 %second.1 = (bf16[3456,256]{1,0:T(8,128)(2,1)S(1)}, bf16[3456,256]{1,0:T(8,128)(2,1)S(1)}) custom-call(s32[1]{0:T(128)} %bitcast.tile_ref, bf16[6,10,16,768]{3,2,1,0:T(8,128)(2,1)S(1)} %get-tuple-element.19.sc_ref, bf16[256,768]{1,0:T(8,128)(2,1)S(1)} %get-tuple-element.24.int_ref, f32[512,256]{1,0:T(8,128)S(1)} %get-tuple-element.25.pre_ref, ...), custom_call_target="tpu_custom_call" | custom-call | flops 3623878656 | bytes 8388608 | tf_op jit(solution)/shard_map/second/pallas_call | solution.py:367
  72.5 0.3 collective-permute-start.21
  72.8 0.3 collective-permute-start.11
  73.1 3.2 %collective-permute-done.21 = bf16[3456,256]{1,0:T(8,128)(2,1)S(1)} collective-permute-done((bf16[3456,256]{1,0:T(8,128)(2,1)S(1)}, bf16[3456,256]{1,0:T(8,128)(2,1)S(1)}, u32[]{:S(2)}, u32[]{:S(2)}) %collective-permute-start.21) | collective-permute-done | bytes 1769504 | tf_op jit(solution)/shard_map/ppermute | solution.py:381
  76.3 1.1 collective-permute-start.22
  77.4 1.4 %collective-permute-done.11 = bf16[3456,256]{1,0:T(8,128)(2,1)S(1)} collective-permute-done((bf16[3456,256]{1,0:T(8,128)(2,1)S(1)}, bf16[3456,256]{1,0:T(8,128)(2,1)S(1)}, u32[]{:S(2)}, u32[]{:S(2)}) %collective-permute-start.11) | collective-permute-done | bytes 1769504 | tf_op jit(solution)/shard_map/ppermute | solution.py:365
  78.8 1.1 collective-permute-start.27
  79.9 2.4 %collective-permute-done.22 = bf16[432,256]{1,0:T(8,128)(2,1)S(1)} collective-permute-done((bf16[432,256]{1,0:T(8,128)(2,1)S(1)}, bf16[432,256]{1,0:T(8,128)(2,1)S(1)}, u32[]{:S(2)}, u32[]{:S(2)}) %collective-permute-start.22) | collective-permute-done | bytes 221216 | tf_op jit(solution)/shard_map/ppermute | solution.py:403
  82.3 0.2 add_convert_fusion.5
  82.5 1.1 collective-permute-start.23
  83.6 1.3 %collective-permute-done.27 = bf16[432,256]{1,0:T(8,128)(2,1)S(1)} collective-permute-done((bf16[432,256]{1,0:T(8,128)(2,1)S(1)}, bf16[432,256]{1,0:T(8,128)(2,1)S(1)}, u32[]{:S(2)}, u32[]{:S(2)}) %collective-permute-start.27) | collective-permute-done | bytes 221216 | tf_op jit(solution)/shard_map/ppermute | solution.py:403
  84.8 0.1 add_convert_fusion.2
  85.0 1.1 collective-permute-start.28
  86.0 4.8 %collective-permute-done.23 = bf16[864,256]{1,0:T(8,128)(2,1)S(1)} collective-permute-done((bf16[864,256]{1,0:T(8,128)(2,1)S(1)}, bf16[864,256]{1,0:T(8,128)(2,1)S(1)}, u32[]{:S(2)}, u32[]{:S(2)}) %collective-permute-start.23) | collective-permute-done | bytes 442400 | tf_op jit(solution)/shard_map/ppermute | solution.py:407
  90.8 0.2 add_convert_fusion.4
  91.0 1.3 %collective-permute-start.24 = (bf16[864,256]{1,0:T(8,128)(2,1)S(1)}, bf16[864,256]{1,0:T(8,128)(2,1)S(1)}, u32[]{:S(2)}, u32[]{:S(2)}) collective-permute-start(bf16[864,256]{1,0:T(8,128)(2,1)S(1)} %add_convert_fusion.4), channel_id=1, source_target_pairs={{0,4},{4,8},{8,12},{12,14},{14,10},{10,6},{6,2},{2,0},{1,3},{5,1},... | collective-permute-start | bytes 1327112 | tf_op jit(solution)/shard_map/ppermute | solution.py:407
  92.3 3.3 %collective-permute-done.28 = bf16[864,256]{1,0:T(8,128)(2,1)S(1)} collective-permute-done((bf16[864,256]{1,0:T(8,128)(2,1)S(1)}, bf16[864,256]{1,0:T(8,128)(2,1)S(1)}, u32[]{:S(2)}, u32[]{:S(2)}) %collective-permute-start.28) | collective-permute-done | bytes 442400 | tf_op jit(solution)/shard_map/ppermute | solution.py:407
  95.6 0.2 add_convert_fusion.1
  95.8 1.1 collective-permute-start.29
  96.8 3.5 %collective-permute-done.24 = bf16[864,256]{1,0:T(8,128)(2,1)S(1)} collective-permute-done((bf16[864,256]{1,0:T(8,128)(2,1)S(1)}, bf16[864,256]{1,0:T(8,128)(2,1)S(1)}, u32[]{:S(2)}, u32[]{:S(2)}) %collective-permute-start.24) | collective-permute-done | bytes 442400 | tf_op jit(solution)/shard_map/ppermute | solution.py:407
  100.3 0.2 add_convert_fusion.3
  100.5 1.1 collective-permute-start.25
  101.6 3.5 %collective-permute-done.29 = bf16[864,256]{1,0:T(8,128)(2,1)S(1)} collective-permute-done((bf16[864,256]{1,0:T(8,128)(2,1)S(1)}, bf16[864,256]{1,0:T(8,128)(2,1)S(1)}, u32[]{:S(2)}, u32[]{:S(2)}) %collective-permute-start.29) | collective-permute-done | bytes 442400 | tf_op jit(solution)/shard_map/ppermute | solution.py:407
  105.0 0.2 add_convert_fusion
  105.2 1.1 collective-permute-start.30
  106.3 3.5 %collective-permute-done.25 = bf16[864,256]{1,0:T(8,128)(2,1)S(1)} collective-permute-done((bf16[864,256]{1,0:T(8,128)(2,1)S(1)}, bf16[864,256]{1,0:T(8,128)(2,1)S(1)}, u32[]{:S(2)}, u32[]{:S(2)}) %collective-permute-start.25) | collective-permute-done | bytes 442400 | tf_op jit(solution)/shard_map/ppermute | solution.py:407
  109.9 6.0 %third.1 = bf16[4,8,16,256]{3,2,1,0:T(8,128)(2,1)} custom-call(s32[1]{0:T(128)} %bitcast.tile_ref, bf16[8,10,16,768]{3,2,1,0:T(8,128)(2,1)S(1)} %get-tuple-element.18.sx_ref, bf16[512,256]{1,0:T(8,128)(2,1)S(1)} %get-tuple-element.23.act_ref, bf16[3,128,256]{2,1,0:T(8,128)(2,1)S(1)} %get-tuple-element.20.mask_ref, ...), custom_call_target="tpu_custom_call" | custom-call | flops 3623878656 | bytes 8388608 | tf_op jit(solution)/shard_map/third/pallas_call | solution.py:384
  116.0 0.5 collective-permute-start.31
  116.5 0.9 add_multiply_fusion.1
  117.4 0.2 collective-permute-done.31
  117.6 0.9 add_multiply_fusion
  (55 shorter events, 0.7 us)
Async XLA Ops:
  0.6 18.8 %copy-start = (bf16[4,8,16,256]{3,2,1,0:T(8,128)(2,1)S(1)}, bf16[4,8,16,256]{3,2,1,0:T(8,128)(2,1)}, u32[]{:S(2)}) copy-start(bf16[4,8,16,256]{3,2,1,0:T(8,128)(2,1)} %f_own.1) | copy-start | bytes 786436
  0.6 28.3 %copy-start.1 = (bf16[4,8,16,256]{3,2,1,0:T(8,128)(2,1)S(1)}, bf16[4,8,16,256]{3,2,1,0:T(8,128)(2,1)}, u32[]{:S(2)}) copy-start(bf16[4,8,16,256]{3,2,1,0:T(8,128)(2,1)} %c_own.1) | copy-start | bytes 786436
  0.7 2.5 %collective-permute-start = (bf16[432,256]{1,0:T(8,128)(2,1)}, bf16[432,256]{1,0:T(8,128)(2,1)S(1)}, u32[]{:S(2)}, u32[]{:S(2)}) collective-permute-start(bf16[432,256]{1,0:T(8,128)(2,1)} %param.6), channel_id=1, source_target_pairs={{0,1},{1,0},{2,3},{3,2},{4,5},{5,4},{6,7},{7,6},{8,9},{9,8},{10,11... | collective-permute-start | bytes 663560 | tf_op jit(solution)/shard_map/ppermute | solution.py:320
  1.2 5.1 %collective-permute-start.12 = (bf16[432,256]{1,0:T(8,128)(2,1)}, bf16[432,256]{1,0:T(8,128)(2,1)S(1)}, u32[]{:S(2)}, u32[]{:S(2)}) collective-permute-start(bf16[432,256]{1,0:T(8,128)(2,1)} %param.7), channel_id=1, source_target_pairs={{0,1},{1,0},{2,3},{3,2},{4,5},{5,4},{6,7},{7,6},{8,9},{9,8},{10,11... | collective-permute-start | bytes 663560 | tf_op jit(solution)/shard_map/ppermute | solution.py:320
  3.2 45.6 %copy-start.13 = (s32[16,2,4]{0,2,1:T(4,128)S(1)}, s32[16,2,4]{0,2,1:T(4,128)}, u32[]{:S(2)}) copy-start(s32[16,2,4]{0,2,1:T(4,128)} %param.9) | copy-start | bytes 1540
  3.2 9.3 %collective-permute-start.3 = (bf16[864,256]{1,0:T(8,128)(2,1)S(1)}, bf16[864,256]{1,0:T(8,128)(2,1)S(1)}, u32[]{:S(2)}, u32[]{:S(2)}) collective-permute-start(bf16[864,256]{1,0:T(8,128)(2,1)S(1)} %constant_dynamic-update-slice_fusion.rest_0_), channel_id=1, source_target_pairs={{0,4},{4,8},{8,12},{12,14},{14,10},{10,6},{6,2},{2,0},{1,3},{5,1},... | collective-permute-start | bytes 1327112 | tf_op jit(solution)/shard_map/ppermute | solution.py:314
  6.3 11.0 %collective-permute-start.13 = (bf16[864,256]{1,0:T(8,128)(2,1)S(1)}, bf16[864,256]{1,0:T(8,128)(2,1)}, u32[]{:S(2)}, u32[]{:S(2)}) collective-permute-start(bf16[864,256]{1,0:T(8,128)(2,1)S(1)} %constant_dynamic-update-slice_fusion.2.rest_9_.rest_0_), channel_id=1, source_target_pairs={{0,4},{4,8},{8,12},{12,14},{14,10},{10,6},{6,2},{2,0},{1,3},{5,1},... | collective-permute-start | bytes 1327112 | tf_op jit(solution)/shard_map/ppermute | solution.py:314
  12.5 9.5 %collective-permute-start.4 = (bf16[864,256]{1,0:T(8,128)(2,1)S(1)}, bf16[864,256]{1,0:T(8,128)(2,1)S(1)}, u32[]{:S(2)}, u32[]{:S(2)}) collective-permute-start(bf16[864,256]{1,0:T(8,128)(2,1)S(1)} %collective-permute-done.3.rest_1_), channel_id=1, source_target_pairs={{0,4},{4,8},{8,12},{12,14},{14,10},{10,6},{6,2},{2,0},{1,3},{5,1},... | collective-permute-start | bytes 1327112 | tf_op jit(solution)/shard_map/ppermute | solution.py:315
  17.3 9.5 %collective-permute-start.14 = (bf16[864,256]{1,0:T(8,128)(2,1)}, bf16[864,256]{1,0:T(8,128)(2,1)}, u32[]{:S(2)}, u32[]{:S(2)}) collective-permute-start(bf16[864,256]{1,0:T(8,128)(2,1)} %collective-permute-done.13.rest_10_.rest_1_), channel_id=1, source_target_pairs={{0,4},{4,8},{8,12},{12,14},{14,10},{10,6},{6,2},{2,0},{1,3},{5,1},... | collective-permute-start | bytes 1327112 | tf_op jit(solution)/shard_map/ppermute | solution.py:315
  22.0 25.5 %copy-start.2 = (bf16[864,256]{1,0:T(8,128)(2,1)}, bf16[864,256]{1,0:T(8,128)(2,1)S(1)}, u32[]{:S(2)}) copy-start(bf16[864,256]{1,0:T(8,128)(2,1)S(1)} %collective-permute-done.4.rest_2_) | copy-start | bytes 1327108
  22.0 9.5 %collective-permute-start.5 = (bf16[864,256]{1,0:T(8,128)(2,1)S(1)}, bf16[864,256]{1,0:T(8,128)(2,1)S(1)}, u32[]{:S(2)}, u32[]{:S(2)}) collective-permute-start(bf16[864,256]{1,0:T(8,128)(2,1)S(1)} %collective-permute-done.4.rest_2_), channel_id=1, source_target_pairs={{0,4},{4,8},{8,12},{12,14},{14,10},{10,6},{6,2},{2,0},{1,3},{5,1},... | collective-permute-start | bytes 1327112 | tf_op jit(solution)/shard_map/ppermute | solution.py:316
  26.8 12.4 %collective-permute-start.15 = (bf16[864,256]{1,0:T(8,128)(2,1)}, bf16[864,256]{1,0:T(8,128)(2,1)S(1)}, u32[]{:S(2)}, u32[]{:S(2)}) collective-permute-start(bf16[864,256]{1,0:T(8,128)(2,1)} %collective-permute-done.14.rest_11_.rest_2_), channel_id=1, source_target_pairs={{0,4},{4,8},{8,12},{12,14},{14,10},{10,6},{6,2},{2,0},{1,3},{5,1},... | collective-permute-start | bytes 1327112 | tf_op jit(solution)/shard_map/ppermute | solution.py:316
  28.9 10.0 %collective-permute-start.1 = (bf16[3,8,16,256]{3,2,1,0:T(8,128)(2,1)S(1)}, bf16[3,8,16,256]{3,2,1,0:T(8,128)(2,1)S(1)}, u32[]{:S(2)}, u32[]{:S(2)}) collective-permute-start(bf16[3,8,16,256]{3,2,1,0:T(8,128)(2,1)S(1)} %pad_maximum_fusion), channel_id=1, source_target_pairs={{0,1},{1,2},{2,3},{3,4},{4,5},{5,6},{6,7},{7,8},{8,9},{9,10},{10,1... | collective-permute-start | bytes 589832 | tf_op jit(solution)/shard_map/ppermute | solution.py:322
  29.0 16.5 %collective-permute-start.7 = (bf16[864,256]{1,0:T(8,128)(2,1)S(1)}, bf16[864,256]{1,0:T(8,128)(2,1)S(1)}, u32[]{:S(2)}, u32[]{:S(2)}) collective-permute-start(bf16[864,256]{1,0:T(8,128)(2,1)S(1)} %collective-permute-done.3.rest_1_), channel_id=1, source_target_pairs={{0,1},{1,0},{2,3},{3,2},{4,5},{5,4},{6,7},{7,6},{8,9},{9,8},{10,11... | collective-permute-start | bytes 1327112 | tf_op jit(solution)/shard_map/ppermute | solution.py:318
  29.1 17.6 %collective-permute-start.8 = (bf16[864,256]{1,0:T(8,128)(2,1)S(1)}, bf16[864,256]{1,0:T(8,128)(2,1)S(1)}, u32[]{:S(2)}, u32[]{:S(2)}) collective-permute-start(bf16[864,256]{1,0:T(8,128)(2,1)S(1)} %collective-permute-done.4.rest_2_), channel_id=1, source_target_pairs={{0,1},{1,0},{2,3},{3,2},{4,5},{5,4},{6,7},{7,6},{8,9},{9,8},{10,11... | collective-permute-start | bytes 1327112 | tf_op jit(solution)/shard_map/ppermute | solution.py:318
  31.4 9.1 %collective-permute-start.2 = (bf16[3,8,16,256]{3,2,1,0:T(8,128)(2,1)S(1)}, bf16[3,8,16,256]{3,2,1,0:T(8,128)(2,1)S(1)}, u32[]{:S(2)}, u32[]{:S(2)}) collective-permute-start(bf16[3,8,16,256]{3,2,1,0:T(8,128)(2,1)S(1)} %pad_maximum_fusion.1), channel_id=1, source_target_pairs={{0,15},{1,0},{2,1},{3,2},{4,3},{5,4},{6,5},{7,6},{8,7},{9,8},{10,9... | collective-permute-start | bytes 589832 | tf_op jit(solution)/shard_map/ppermute | solution.py:323
  39.0 11.2 %collective-permute-start.9 = (bf16[864,256]{1,0:T(8,128)(2,1)S(1)}, bf16[864,256]{1,0:T(8,128)(2,1)}, u32[]{:S(2)}, u32[]{:S(2)}) collective-permute-start(bf16[864,256]{1,0:T(8,128)(2,1)S(1)} %collective-permute-done.5.rest_3_), channel_id=1, source_target_pairs={{0,1},{1,0},{2,3},{3,2},{4,5},{5,4},{6,7},{7,6},{8,9},{9,8},{10,11... | collective-permute-start | bytes 1327112 | tf_op jit(solution)/shard_map/ppermute | solution.py:318
  39.2 6.3 %collective-permute-start.6 = (bf16[432,256]{1,0:T(8,128)(2,1)S(1)}, bf16[432,256]{1,0:T(8,128)(2,1)S(1)}, u32[]{:S(2)}, u32[]{:S(2)}) collective-permute-start(bf16[432,256]{1,0:T(8,128)(2,1)S(1)} %slice.130), channel_id=1, source_target_pairs={{0,4},{4,8},{8,12},{12,14},{14,10},{10,6},{6,2},{2,0},{1,3},{5,1},... | collective-permute-start | bytes 663560 | tf_op jit(solution)/shard_map/ppermute | solution.py:317
  40.6 7.2 %collective-permute-start.16 = (bf16[432,256]{1,0:T(8,128)(2,1)S(1)}, bf16[432,256]{1,0:T(8,128)(2,1)S(1)}, u32[]{:S(2)}, u32[]{:S(2)}) collective-permute-start(bf16[432,256]{1,0:T(8,128)(2,1)S(1)} %slice.131), channel_id=1, source_target_pairs={{0,4},{4,8},{8,12},{12,14},{14,10},{10,6},{6,2},{2,0},{1,3},{5,1},... | collective-permute-start | bytes 663560 | tf_op jit(solution)/shard_map/ppermute | solution.py:317
  45.4 5.1 %collective-permute-start.10 = (bf16[432,256]{1,0:T(8,128)(2,1)S(1)}, bf16[432,256]{1,0:T(8,128)(2,1)}, u32[]{:S(2)}, u32[]{:S(2)}) collective-permute-start(bf16[432,256]{1,0:T(8,128)(2,1)S(1)} %collective-permute-done.6.rest_4_), channel_id=1, source_target_pairs={{0,1},{1,0},{2,3},{3,2},{4,5},{5,4},{6,7},{7,6},{8,9},{9,8},{10,11... | collective-permute-start | bytes 663560 | tf_op jit(solution)/shard_map/ppermute | solution.py:318
  45.5 0.8 copy-start.5
  46.2 16.5 %collective-permute-start.17 = (bf16[864,256]{1,0:T(8,128)(2,1)}, bf16[864,256]{1,0:T(8,128)(2,1)}, u32[]{:S(2)}, u32[]{:S(2)}) collective-permute-start(bf16[864,256]{1,0:T(8,128)(2,1)} %collective-permute-done.13.rest_10_.rest_1_), channel_id=1, source_target_pairs={{0,1},{1,0},{2,3},{3,2},{4,5},{5,4},{6,7},{7,6},{8,9},{9,8},{10,11... | collective-permute-start | bytes 1327112 | tf_op jit(solution)/shard_map/ppermute | solution.py:318
  46.7 0.8 copy-start.8
  47.5 15.3 %collective-permute-start.18 = (bf16[864,256]{1,0:T(8,128)(2,1)}, bf16[864,256]{1,0:T(8,128)(2,1)}, u32[]{:S(2)}, u32[]{:S(2)}) collective-permute-start(bf16[864,256]{1,0:T(8,128)(2,1)} %collective-permute-done.14.rest_11_.rest_2_), channel_id=1, source_target_pairs={{0,1},{1,0},{2,3},{3,2},{4,5},{5,4},{6,7},{7,6},{8,9},{9,8},{10,11... | collective-permute-start | bytes 1327112 | tf_op jit(solution)/shard_map/ppermute | solution.py:318
  47.8 0.7 copy-start.11
  48.5 14.3 %collective-permute-start.19 = (bf16[864,256]{1,0:T(8,128)(2,1)S(1)}, bf16[864,256]{1,0:T(8,128)(2,1)}, u32[]{:S(2)}, u32[]{:S(2)}) collective-permute-start(bf16[864,256]{1,0:T(8,128)(2,1)S(1)} %collective-permute-done.15.rest_12_.rest_3_), channel_id=1, source_target_pairs={{0,1},{1,0},{2,3},{3,2},{4,5},{5,4},{6,7},{7,6},{8,9},{9,8},{10,11... | collective-permute-start | bytes 1327112 | tf_op jit(solution)/shard_map/ppermute | solution.py:318
  50.2 12.6 %collective-permute-start.20 = (bf16[432,256]{1,0:T(8,128)(2,1)}, bf16[432,256]{1,0:T(8,128)(2,1)S(1)}, u32[]{:S(2)}, u32[]{:S(2)}) collective-permute-start(bf16[432,256]{1,0:T(8,128)(2,1)} %copy-done.11), channel_id=1, source_target_pairs={{0,1},{1,0},{2,3},{3,2},{4,5},{5,4},{6,7},{7,6},{8,9},{9,8},{10,11... | collective-permute-start | bytes 663560 | tf_op jit(solution)/shard_map/ppermute | solution.py:318
  50.6 1.0 copy-start.3
  51.6 1.0 copy-start.6
  52.6 1.0 copy-start.9
  53.6 9.2 %copy-start.12 = (bf16[432,256]{1,0:T(8,128)(2,1)S(1)}, bf16[432,256]{1,0:T(8,128)(2,1)}, u32[]{:S(2)}) copy-start(bf16[432,256]{1,0:T(8,128)(2,1)} %copy-done.11) | copy-start | bytes 663556
  72.5 3.8 %collective-permute-start.21 = (bf16[3456,256]{1,0:T(8,128)(2,1)S(1)}, bf16[3456,256]{1,0:T(8,128)(2,1)S(1)}, u32[]{:S(2)}, u32[]{:S(2)}) collective-permute-start(bf16[3456,256]{1,0:T(8,128)(2,1)S(1)} %get-tuple-element.27), channel_id=1, source_target_pairs={{0,1},{1,0},{2,3},{3,2},{4,5},{5,4},{6,7},{7,6},{8,9},{9,8},{10,11... | collective-permute-start | bytes 5308424 | tf_op jit(solution)/shard_map/ppermute | solution.py:381
  72.8 6.0 %collective-permute-start.11 = (bf16[3456,256]{1,0:T(8,128)(2,1)S(1)}, bf16[3456,256]{1,0:T(8,128)(2,1)S(1)}, u32[]{:S(2)}, u32[]{:S(2)}) collective-permute-start(bf16[3456,256]{1,0:T(8,128)(2,1)S(1)} %get-tuple-element.22), channel_id=1, source_target_pairs={{0,1},{1,0},{2,3},{3,2},{4,5},{5,4},{6,7},{7,6},{8,9},{9,8},{10,11... | collective-permute-start | bytes 5308424 | tf_op jit(solution)/shard_map/ppermute | solution.py:365
  76.3 6.0 %collective-permute-start.22 = (bf16[432,256]{1,0:T(8,128)(2,1)S(1)}, bf16[432,256]{1,0:T(8,128)(2,1)S(1)}, u32[]{:S(2)}, u32[]{:S(2)}) collective-permute-start(bf16[432,256]{1,0:T(8,128)(2,1)S(1)} %add_convert_fusion.7), channel_id=1, source_target_pairs={{0,4},{4,8},{8,12},{12,14},{14,10},{10,6},{6,2},{2,0},{1,3},{5,1},... | collective-permute-start | bytes 663560 | tf_op jit(solution)/shard_map/ppermute | solution.py:403
  78.8 6.0 %collective-permute-start.27 = (bf16[432,256]{1,0:T(8,128)(2,1)S(1)}, bf16[432,256]{1,0:T(8,128)(2,1)S(1)}, u32[]{:S(2)}, u32[]{:S(2)}) collective-permute-start(bf16[432,256]{1,0:T(8,128)(2,1)S(1)} %add_convert_fusion.6), channel_id=1, source_target_pairs={{0,4},{4,8},{8,12},{12,14},{14,10},{10,6},{6,2},{2,0},{1,3},{5,1},... | collective-permute-start | bytes 663560 | tf_op jit(solution)/shard_map/ppermute | solution.py:403
  82.5 8.4 %collective-permute-start.23 = (bf16[864,256]{1,0:T(8,128)(2,1)S(1)}, bf16[864,256]{1,0:T(8,128)(2,1)S(1)}, u32[]{:S(2)}, u32[]{:S(2)}) collective-permute-start(bf16[864,256]{1,0:T(8,128)(2,1)S(1)} %add_convert_fusion.5), channel_id=1, source_target_pairs={{0,4},{4,8},{8,12},{12,14},{14,10},{10,6},{6,2},{2,0},{1,3},{5,1},... | collective-permute-start | bytes 1327112 | tf_op jit(solution)/shard_map/ppermute | solution.py:407
  85.0 10.6 %collective-permute-start.28 = (bf16[864,256]{1,0:T(8,128)(2,1)S(1)}, bf16[864,256]{1,0:T(8,128)(2,1)S(1)}, u32[]{:S(2)}, u32[]{:S(2)}) collective-permute-start(bf16[864,256]{1,0:T(8,128)(2,1)S(1)} %add_convert_fusion.2), channel_id=1, source_target_pairs={{0,4},{4,8},{8,12},{12,14},{14,10},{10,6},{6,2},{2,0},{1,3},{5,1},... | collective-permute-start | bytes 1327112 | tf_op jit(solution)/shard_map/ppermute | solution.py:407
  91.0 9.3 %collective-permute-start.24 = (bf16[864,256]{1,0:T(8,128)(2,1)S(1)}, bf16[864,256]{1,0:T(8,128)(2,1)S(1)}, u32[]{:S(2)}, u32[]{:S(2)}) collective-permute-start(bf16[864,256]{1,0:T(8,128)(2,1)S(1)} %add_convert_fusion.4), channel_id=1, source_target_pairs={{0,4},{4,8},{8,12},{12,14},{14,10},{10,6},{6,2},{2,0},{1,3},{5,1},... | collective-permute-start | bytes 1327112 | tf_op jit(solution)/shard_map/ppermute | solution.py:407
  95.7 14.2 %copy-start.4 = (bf16[864,256]{1,0:T(8,128)(2,1)S(1)}, bf16[864,256]{1,0:T(8,128)(2,1)}, u32[]{:S(2)}) copy-start(bf16[864,256]{1,0:T(8,128)(2,1)} %copy-done.2) | copy-start | bytes 1327108
  95.7 14.2 %copy-start.7 = (bf16[864,256]{1,0:T(8,128)(2,1)S(1)}, bf16[864,256]{1,0:T(8,128)(2,1)}, u32[]{:S(2)}) copy-start(bf16[864,256]{1,0:T(8,128)(2,1)} %copy-done.5) | copy-start | bytes 1327108
  95.8 14.2 %copy-start.10 = (bf16[864,256]{1,0:T(8,128)(2,1)S(1)}, bf16[864,256]{1,0:T(8,128)(2,1)}, u32[]{:S(2)}) copy-start(bf16[864,256]{1,0:T(8,128)(2,1)} %copy-done.8) | copy-start | bytes 1327108
  95.8 9.3 %collective-permute-start.29 = (bf16[864,256]{1,0:T(8,128)(2,1)S(1)}, bf16[864,256]{1,0:T(8,128)(2,1)S(1)}, u32[]{:S(2)}, u32[]{:S(2)}) collective-permute-start(bf16[864,256]{1,0:T(8,128)(2,1)S(1)} %add_convert_fusion.1), channel_id=1, source_target_pairs={{0,4},{4,8},{8,12},{12,14},{14,10},{10,6},{6,2},{2,0},{1,3},{5,1},... | collective-permute-start | bytes 1327112 | tf_op jit(solution)/shard_map/ppermute | solution.py:407
  100.5 9.3 %collective-permute-start.25 = (bf16[864,256]{1,0:T(8,128)(2,1)S(1)}, bf16[864,256]{1,0:T(8,128)(2,1)S(1)}, u32[]{:S(2)}, u32[]{:S(2)}) collective-permute-start(bf16[864,256]{1,0:T(8,128)(2,1)S(1)} %add_convert_fusion.3), channel_id=1, source_target_pairs={{0,4},{4,8},{8,12},{12,14},{14,10},{10,6},{6,2},{2,0},{1,3},{5,1},... | collective-permute-start | bytes 1327112 | tf_op jit(solution)/shard_map/ppermute | solution.py:407
  105.2 10.7 %collective-permute-start.30 = (bf16[864,256]{1,0:T(8,128)(2,1)S(1)}, bf16[864,256]{1,0:T(8,128)(2,1)S(1)}, u32[]{:S(2)}, u32[]{:S(2)}) collective-permute-start(bf16[864,256]{1,0:T(8,128)(2,1)S(1)} %add_convert_fusion), channel_id=1, source_target_pairs={{0,4},{4,8},{8,12},{12,14},{14,10},{10,6},{6,2},{2,0},{1,3},{5,1},... | collective-permute-start | bytes 1327112 | tf_op jit(solution)/shard_map/ppermute | solution.py:407
  109.8 6.7 %collective-permute-start.26 = (bf16[432,256]{1,0:T(8,128)(2,1)S(1)}, bf16[432,256]{1,0:T(8,128)(2,1)S(1)}, u32[]{:S(2)}, u32[]{:S(2)}) collective-permute-start(bf16[432,256]{1,0:T(8,128)(2,1)S(1)} %slice.138), channel_id=1, source_target_pairs={{0,1},{1,0},{2,3},{3,2},{4,5},{5,4},{6,7},{7,6},{8,9},{9,8},{10,11... | collective-permute-start | bytes 663560 | tf_op jit(solution)/shard_map/ppermute | solution.py:408
  116.0 1.6 %collective-permute-start.31 = (bf16[432,256]{1,0:T(8,128)(2,1)S(1)}, bf16[432,256]{1,0:T(8,128)(2,1)S(1)}, u32[]{:S(2)}, u32[]{:S(2)}) collective-permute-start(bf16[432,256]{1,0:T(8,128)(2,1)S(1)} %slice.145), channel_id=1, source_target_pairs={{0,1},{1,0},{2,3},{3,2},{4,5},{5,4},{6,7},{7,6},{8,9},{9,8},{10,11... | collective-permute-start | bytes 663560 | tf_op jit(solution)/shard_map/ppermute | solution.py:408
where the time goes:
time: 119 us; the launch traced here: 118 us
  waiting for transfers between devices  48.6 us (41%)
  starting transfers between devices  32.4 us (27%)
  Pallas kernels  26.2 us (22%)
  local copies, waits for them, and re-layouts  7.39 us (6%)
  other arithmetic  2.91 us (2%)
    ppermute x6, waiting for transfers between devices, scattered(): moving = onward((both(lo, lo + 2 * rows) + moving).astype(BF)).astype(F32)  18.5 us
    pallas_call x1, Pallas kernels, on_ring(): pl.pallas_call(functools.partial(second_kernel, n), name='second', out_sh...  9.66 us
    pallas_call x1, Pallas kernels, on_ring(): pl.pallas_call(functools.partial(first_kernel, n), name='first', out_shap...  9.15 us
    ppermute x2, waiting for transfers between devices, gathered(): p1 = onward(pair)  7.34 us
    unnamed x30, local copies, waits for them, and re-layouts  7.2 us
    ppermute x6, starting transfers between devices, scattered(): moving = onward((both(lo, lo + 2 * rows) + moving).astype(BF)).astype(F32)  6.7 us
    pallas_call x1, Pallas kernels, on_ring(): pl.pallas_call(functools.partial(third_kernel, n), name='third', out_shap...  6.03 us
    ppermute x2, waiting for transfers between devices, gathered(): p2 = onward(p1)  5.3 us
  transfers between devices with their start and end apart: 32, of which 18 were waited for; matrix products, arithmetic and copies ran while one was open for 3% of the time, Pallas kernels for 14%

commit v1 on v0

--- a/solution.py
+++ b/solution.py
@@ -237,8 +237,8 @@
     split_shards(tile_ref, g_ref, keep_ref, send_ref)
 
 
-def second_kernel(n, tile_ref, sc_ref, int_ref, pre_ref, mask_ref, *rest):
-    pieces, (keep_ref, send_ref, w_ref, sd_ref, g_ref) = rest[:n], rest[n:]
+def back_kernel(n, tile_ref, sc_ref, pre_ref, mask_ref, *rest):
+    pieces, (sd_ref, w_ref) = rest[:n], rest[n:]
     area, channels = mask_ref.shape[1:]
     ny, nz = sc_ref.shape[1] - 2, sc_ref.shape[2]
     depth = pre_ref.shape[0] // area
@@ -259,6 +259,11 @@
     delta = masked(acc * silu_slope(pre_ref[...]), mask_ref, 1).astype(BF)
     clear_edges(sd_ref, ny)
     store_shifted(sd_ref, 0, delta, ny, nz, channels)
+
+
+def grad_kernel(tile_ref, sd_ref, int_ref, keep_ref, send_ref, g_ref):
+    depth, ny, nz, channels = sd_ref.shape
+    ny, area, channels = ny - 2, (ny - 2) * nz, channels // 3
     for q in range(3):
         right = window(sd_ref, 0, 2 - q, depth, ny)
         for p in range(3):
@@ -286,7 +291,7 @@
     out_ref[...] = masked(second, mask_ref, 1).astype(BF).reshape(out_ref.shape)
 
 
-VMEM_LIMIT = 32 * 1024 * 1024
+VMEM_LIMIT = 24 * 1024 * 1024
 
 
 def on_ring(features, weight_one, weight_two, cotangent, block_mask):
@@ -309,20 +314,8 @@
     up = permute([(i, (i + 1) % tiles) for i in range(tiles)])
     down = permute([(i, (i - 1) % tiles) for i in range(tiles)])
 
-    def gathered(weight, other):
-        pair = jnp.concatenate([weight, other])
-        p1 = onward(pair)
-        p2 = onward(p1)
-        p3 = onward(p2)
-        p4 = onward(p3[:rows])
-        return [pair, p1, p2, p3, p4] + [sibling(p) for p in (p1, p2, p3, p4)]
-
-    other_one, other_two = sibling(weight_one), sibling(weight_two)
-    features_late, cot_late, _ = lax.optimization_barrier((features, cotangent, other_one))
-    low = up(jnp.concatenate([features_late[-2:], cot_late[-1:]]))
-    high = down(jnp.concatenate([features_late[:2], cot_late[:1]]))
-    ones, twos = gathered(weight_one, other_one), gathered(weight_two, other_two)
-    n = len(ones)
+    def after(value, *others):
+        return lax.optimization_barrier((value,) + others)[0]
 
     smem = pl.BlockSpec(memory_space=pltpu.SMEM)
     vmem = pl.BlockSpec(memory_space=pltpu.VMEM)
@@ -335,7 +328,15 @@
             flops=convs * flops, transcendentals=0, bytes_accessed=8 << 20
         )
 
-    sx, sc, in_t, near = pl.pallas_call(
+    pair_one = jnp.concatenate([weight_one, sibling(weight_one)])
+    pair_two = jnp.concatenate([after(weight_two, pair_one), sibling(weight_two)])
+    pairs = [pair_one, pair_two]
+    rings = [[pair, onward(pair)] for pair in pairs]
+    features_late, cot_late, _ = lax.optimization_barrier((features, cotangent, pairs[1]))
+    low = up(jnp.concatenate([features_late[-2:], cot_late[-1:]]))
+    high = down(jnp.concatenate([features_late[:2], cot_late[:1]]))
+
+    prep = pl.pallas_call(
         prep_kernel,
         name="prep",
         out_shape=(
@@ -347,7 +348,30 @@
         in_specs=[smem, smem] + [vmem] * 4,
         out_specs=(vmem,) * 4,
         compiler_params=params,
-    )(tile, block_mask.reshape(tiles, -1), low, features, cotangent, high)
+    )
+    crossed = [[], []]
+    sx, sc, in_t, near = None, None, None, None
+    for hop in (1, 2, 3):
+        for k in range(2):
+            here = rings[k][hop]
+            if k == 0 and hop > 1:
+                here = after(here, rings[1][hop - 1])
+            if hop == 1:
+                if k == 0:
+                    here = after(here, low, high)
+                    sx, sc, in_t, near = prep(
+                        tile, block_mask.reshape(tiles, -1), low, features, cotangent, high
+                    )
+            elif hop == 2:
+                here = after(here, crossed[k][0], sx) if k == 0 else after(here, crossed[k][0])
+            else:
+                here = after(here, crossed[k][1])
+            rings[k].append(onward(here[:rows] if hop == 3 else here))
+            crossed[k].append(sibling(rings[k][hop]))
+    for k in range(2):
+        crossed[k].append(sibling(rings[k][4]))
+    ones, twos = (rings[k] + crossed[k] for k in range(2))
+    n = len(ones)
 
     shards = (shape((chips * rows, channels), BF),) * 2
     weights = pltpu.VMEM((27 * channels, channels), BF)
@@ -361,26 +385,9 @@
         scratch_shapes=[weights, weights],
         compiler_params=params,
         cost_estimate=cost(2),
-    )(tile, sx, sc, near, *ones)
+    )(tile, after(sx, rings[1][3]), sc, near, *ones)
     got_two = sibling(send_two)
 
-    keep_one, send_one = pl.pallas_call(
-        functools.partial(second_kernel, n),
-        name="second",
-        out_shape=shards,
-        in_specs=[smem] + [vmem] * (4 + n),
-        out_specs=(vmem,) * 2,
-        scratch_shapes=[
-            weights,
-            pltpu.VMEM((depth, ny + 2, nz, 3 * channels), BF),
-            weights,
-        ],
-        compiler_params=params,
-        cost_estimate=cost(2),
-    )(tile, sc, in_t, pre, near, *twos)
-    got_one = sibling(send_one)
-
-    act_late, _ = lax.optimization_barrier((act, got_two))
     features_out = pl.pallas_call(
         functools.partial(third_kernel, n),
         name="third",
@@ -393,22 +400,60 @@
             pltpu.VMEM((depth + 2, ny + 2, nz, 3 * channels), BF),
         ],
         compiler_params=params,
-        cost_estimate=cost(2),
-    )(tile, sx, act_late, near, *ones, *twos)
-
-    def scattered(keep, got):
-        def both(lo, hi):
-            return keep[lo:hi].astype(F32) + got[lo:hi].astype(F32)
-
-        moving = onward(both(0, rows).astype(BF)).astype(F32)
-        moving = jnp.concatenate([moving, jnp.zeros_like(moving)])
-        for k in range(3):
-            lo = (1 + 2 * k) * rows
-            moving = onward((both(lo, lo + 2 * rows) + moving).astype(BF)).astype(F32)
-        across = sibling(moving[rows:].astype(BF)).astype(F32)
-        return (both(7 * rows, 8 * rows) + moving[:rows] + across) * loss_scale
-
-    return (features_out, scattered(keep_one, got_one), scattered(keep_two, got_two))
+        cost_estimate=cost(1),
+    )(tile, sx, act, near, *ones, *twos)
+
+    def both(keep, got, lo, hi):
+        return keep[lo * rows : hi * rows].astype(F32) + got[lo * rows : hi * rows].astype(F32)
+
+    def step(keep, got, moving, k):
+        if k == 0:
+            return both(keep, got, 0, 1).astype(BF)
+        if k == 1:
+            moving = jnp.concatenate([moving, jnp.zeros_like(moving)])
+        return (both(keep, got, 2 * k - 1, 2 * k + 1) + moving.astype(F32)).astype(BF)
+
+    def finish(keep, got, moving):
+        across = sibling(moving[rows:])
+        total = both(keep, got, 7, 8) + moving[:rows].astype(F32) + across.astype(F32)
+        return total * loss_scale
+
+    message = step(keep_two, got_two, None, 0)
+    two = onward(message)
+
+    delta = pl.pallas_call(
+        functools.partial(back_kernel, n),
+        name="back",
+        out_shape=shape((depth, ny + 2, nz, 3 * channels), BF),
+        in_specs=[smem] + [vmem] * (3 + n),
+        out_specs=vmem,
+        scratch_shapes=[weights],
+        compiler_params=params,
+        cost_estimate=cost(1),
+    )(tile, after(sc, message, features_out), pre, near, *twos)
+    message = step(keep_two, got_two, after(two, delta), 1)
+    two = onward(message)
+
+    keep_one, send_one = pl.pallas_call(
+        grad_kernel,
+        name="grad",
+        out_shape=shards,
+        in_specs=[smem] + [vmem] * 2,
+        out_specs=(vmem,) * 2,
+        scratch_shapes=[weights],
+        compiler_params=params,
+        cost_estimate=cost(1),
+    )(tile, after(delta, message), in_t)
+    got_one = sibling(after(send_one, two))
+
+    two = onward(step(keep_two, got_two, two, 2))
+    one = onward(step(keep_one, got_one, None, 0))
+    one = onward(step(keep_one, got_one, one, 1))
+    two = onward(step(keep_two, got_two, two, 3))
+    one = onward(step(keep_one, got_one, one, 2))
+    grad_two = finish(keep_two, got_two, two)
+    one = onward(step(keep_one, got_one, one, 3))
+    return (features_out, finish(keep_one, got_one, one), grad_two)
 
 
 def solution(mesh):

time: 119 us -> 119 us (level)
  waiting for transfers between devices: 48.6 us -> 69.6 us
  starting transfers between devices: 32.4 us -> 22.9 us
  Pallas kernels: 26.2 us -> 18.4 us
  local copies, waits for them, and re-layouts: 7.39 us -> 3.71 us
    ppermute x29, waiting for transfers between devices: 43.6 us -> 64.2 us  [the longest x6 23.2 us: on_ring(): rings[k].append(onward(here[:rows] if hop == 3 else here))]
    ppermute x29, starting transfers between devices: 28.2 us -> 18.2 us  [the longest x6 3.83 us: on_ring(): rings[k].append(onward(here[:rows] if hop == 3 else here))]
    pallas_call x2 -> x3, Pallas kernels: 11 us -> 6.05 us  [the longest x1 2.41 us: on_ring(): pl.pallas_call(functools.partial(back_kernel, n), name='back', out_shape=...]
    unnamed x30 -> x12, local copies, waits for them, and re-layouts: 7.2 us -> 3.52 us
    ppermute x1, waiting for transfers between devices: 3.6 us -> 5.45 us  [on_ring(): low = up(jnp.concatenate([features_late[-2:], cot_late[-1:]]))]
    pallas_call x1, Pallas kernels: 6.03 us -> 4.25 us  [on_ring(): pl.pallas_call(functools.partial(third_kernel, n), name='third', out_shap...]
    ppermute x1, waiting for transfers between devices: 1.38 us -> 0.01 us  [on_ring(): got_two = sibling(send_two)]
  transfers between devices with their start and end apart: 32 -> 32, of which waited for: 18 -> 19; matrix products, arithmetic and copies ran while one was open for 3% -> 3% of each run, Pallas kernels for 14% -> 9%
where the time goes in v1:
time: 119 us
  waiting for transfers between devices  69.6 us (58%)
  starting transfers between devices  22.9 us (19%)
  Pallas kernels  18.4 us (15%)
  local copies, waits for them, and re-layouts  3.71 us (3%)
  other arithmetic  3 us (3%)
    ppermute x6, waiting for transfers between devices, on_ring(): rings[k].append(onward(here[:rows] if hop == 3 else here))  23.2 us
    pallas_call x1, Pallas kernels, on_ring(): pl.pallas_call(functools.partial(first_kernel, n), name='first', out_shap...  8.09 us
    ppermute x1, waiting for transfers between devices, on_ring(): low = up(jnp.concatenate([features_late[-2:], cot_late[-1:]]))  5.45 us
    ppermute x2, waiting for transfers between devices, on_ring(): two = onward(message)  5.14 us
    ppermute x1, waiting for transfers between devices, on_ring(): one = onward(step(keep_one, got_one, one, 1))  5.11 us
    ppermute x1, waiting for transfers between devices, on_ring(): one = onward(step(keep_one, got_one, None, 0))  5.03 us
    ppermute x1, waiting for transfers between devices, on_ring(): one = onward(step(keep_one, got_one, one, 3))  4.64 us
    ppermute x1, starting transfers between devices, on_ring(): high = down(jnp.concatenate([features_late[:2], cot_late[:1]]))  4.48 us
  transfers between devices with their start and end apart: 32, of which 19 were waited for; matrix products, arithmetic and copies ran while one was open for 3% of the time, Pallas kernels for 9%

profile of v1, /device:TPU:0, one launch (start us, length us, event | category | flops | bytes accessed | tf_op | source)
XLA Modules:
  0.0 118.5 jit_solution(12773287920298267370)
XLA Ops:
  0.7 0.5 collective-permute-start
  1.2 0.1 collective-permute-start.1
  1.3 0.9 constant_dynamic-update-slice_fusion.1
  2.2 0.3 collective-permute-done
  2.5 3.0 %collective-permute-start.8 = (bf16[864,256]{1,0:T(8,128)(2,1)S(1)}, bf16[864,256]{1,0:T(8,128)(2,1)S(1)}, u32[]{:S(2)}, u32[]{:S(2)}) collective-permute-start(bf16[864,256]{1,0:T(8,128)(2,1)S(1)} %constant_dynamic-update-slice_fusion.rest_0_), channel_id=1, source_target_pairs={{0,4},{4,8},{8,12},{12,14},{14,10},{10,6},{6,2},{2,0},{1,3},{5,1},... | collective-permute-start | bytes 1327112 | tf_op jit(solution)/shard_map/ppermute | solution.py:334
  5.5 0.9 constant_dynamic-update-slice_fusion.3
  6.6 0.1 collective-permute-start.2
  6.7 4.5 %collective-permute-start.3 = (bf16[3,8,16,256]{3,2,1,0:T(8,128)(2,1)S(1)}, bf16[3,8,16,256]{3,2,1,0:T(8,128)(2,1)S(1)}, u32[]{:S(2)}, u32[]{:S(2)}) collective-permute-start(bf16[3,8,16,256]{3,2,1,0:T(8,128)(2,1)S(1)} %pad_maximum_fusion.1), channel_id=1, source_target_pairs={{0,15},{1,0},{2,1},{3,2},{4,3},{5,4},{6,5},{7,6},{8,7},{9,8},{10,9... | collective-permute-start | bytes 589832 | tf_op jit(solution)/shard_map/ppermute | solution.py:337
  11.2 5.4 %collective-permute-done.2.low = bf16[3,8,16,256]{3,2,1,0:T(8,128)(2,1)S(1)} collective-permute-done((bf16[3,8,16,256]{3,2,1,0:T(8,128)(2,1)S(1)}, bf16[3,8,16,256]{3,2,1,0:T(8,128)(2,1)S(1)}, u32[]{:S(2)}, u32[]{:S(2)}) %collective-permute-start.2) | collective-permute-done | bytes 196640 | tf_op jit(solution)/shard_map/ppermute | solution.py:336
  16.6 0.7 copy-done.2
  17.3 1.1 collective-permute-start.10
  18.4 0.1 copy.8.cells_ref
  18.5 0.9 copy-done.3
  19.4 1.4 %prep.1 = (bf16[8,10,16,768]{3,2,1,0:T(8,128)(2,1)S(1)}, bf16[6,10,16,768]{3,2,1,0:T(8,128)(2,1)S(1)}, bf16[256,768]{1,0:T(8,128)(2,1)S(1)}, bf16[3,128,256]{2,1,0:T(8,128)(2,1)S(1)}) custom-call(s32[1]{0:T(128)} %bitcast.tile_ref, s32[16,8]{1,0:T(8,128)S(1)} %copy.8.cells_ref, bf16[3,8,16,256]{3,2,1,0:T(8,128)(2,1)S(1)} %collective-permute-done.2.low, ...), custom_call_target="tpu_custom_call" | custom-call | tf_op jit(solution)/shard_map/prep/pallas_call | solution.py:362
  20.8 0.1 collective-permute-start.6
  20.9 0.7 collective-permute-start.5
  21.6 4.0 %collective-permute-done.9.rest_2_ = bf16[864,256]{1,0:T(8,128)(2,1)S(1)} collective-permute-done((bf16[864,256]{1,0:T(8,128)(2,1)S(1)}, bf16[864,256]{1,0:T(8,128)(2,1)S(1)}, u32[]{:S(2)}, u32[]{:S(2)}) %collective-permute-start.9) | collective-permute-done | bytes 442400 | tf_op jit(solution)/shard_map/ppermute | solution.py:369
  25.6 0.8 collective-permute-start.11
  26.4 0.1 collective-permute-start.12
  26.5 3.9 %collective-permute-done.5.rest_11_.rest_2_ = bf16[864,256]{1,0:T(8,128)(2,1)S(1)} collective-permute-done((bf16[864,256]{1,0:T(8,128)(2,1)S(1)}, bf16[864,256]{1,0:T(8,128)(2,1)S(1)}, u32[]{:S(2)}, u32[]{:S(2)}) %collective-permute-start.5) | collective-permute-done | bytes 442400 | tf_op jit(solution)/shard_map/ppermute | solution.py:369
  30.3 0.8 collective-permute-start.7
  31.1 4.0 %collective-permute-done.11.rest_3_ = bf16[864,256]{1,0:T(8,128)(2,1)S(1)} collective-permute-done((bf16[864,256]{1,0:T(8,128)(2,1)S(1)}, bf16[864,256]{1,0:T(8,128)(2,1)S(1)}, u32[]{:S(2)}, u32[]{:S(2)}) %collective-permute-start.11) | collective-permute-done | bytes 442400 | tf_op jit(solution)/shard_map/ppermute | solution.py:369
  35.1 0.8 collective-permute-start.13
  35.9 0.1 collective-permute-start.14
  36.0 6.2 %collective-permute-done.13.rest_4_ = bf16[432,256]{1,0:T(8,128)(2,1)S(1)} collective-permute-done((bf16[432,256]{1,0:T(8,128)(2,1)S(1)}, bf16[432,256]{1,0:T(8,128)(2,1)S(1)}, u32[]{:S(2)}, u32[]{:S(2)}) %collective-permute-start.13) | collective-permute-done | bytes 221216 | tf_op jit(solution)/shard_map/ppermute | solution.py:369
  42.2 1.5 %collective-permute-done.15.rest_8_ = bf16[432,256]{1,0:T(8,128)(2,1)S(1)} collective-permute-done((bf16[432,256]{1,0:T(8,128)(2,1)S(1)}, bf16[432,256]{1,0:T(8,128)(2,1)S(1)}, u32[]{:S(2)}, u32[]{:S(2)}) %collective-permute-start.15) | collective-permute-done | bytes 221216 | tf_op jit(solution)/shard_map/ppermute | solution.py:372
  43.7 8.1 %first.1 = (f32[512,256]{1,0:T(8,128)S(1)}, bf16[512,256]{1,0:T(8,128)(2,1)S(1)}, bf16[3456,256]{1,0:T(8,128)(2,1)S(1)}, bf16[3456,256]{1,0:T(8,128)(2,1)S(1)}) custom-call(s32[1]{0:T(128)} %bitcast.tile_ref, bf16[8,10,16,768]{3,2,1,0:T(8,128)(2,1)S(1)} %get-tuple-element.33.sx_ref, bf16[6,10,16,768]{3,2,1,0:T(8,128)(2,1)S(1)} %get-tuple-element.45.sc_ref, ...), custom_call_target="tpu_custom_call" | custom-call | flops 3623878656 | bytes 8388608 | tf_op jit(solution)/shard_map/first/pallas_call | solution.py:378
  51.8 0.2 collective-permute-start.20
  52.0 0.4 collective-permute-start.16
  52.4 3.8 %collective-permute-done.16.rest_15_.rest_6_ = bf16[864,256]{1,0:T(8,128)(2,1)S(1)} collective-permute-done((bf16[864,256]{1,0:T(8,128)(2,1)S(1)}, bf16[864,256]{1,0:T(8,128)(2,1)S(1)}, u32[]{:S(2)}, u32[]{:S(2)}) %collective-permute-start.16) | collective-permute-done | bytes 442400 | tf_op jit(solution)/shard_map/ppermute | solution.py:370
  56.2 0.8 collective-permute-start.17
  57.0 5.2 %collective-permute-done.17.rest_13_.rest_4_ = bf16[432,256]{1,0:T(8,128)(2,1)S(1)} collective-permute-done((bf16[432,256]{1,0:T(8,128)(2,1)S(1)}, bf16[432,256]{1,0:T(8,128)(2,1)S(1)}, u32[]{:S(2)}, u32[]{:S(2)}) %collective-permute-start.17) | collective-permute-done | bytes 221216 | tf_op jit(solution)/shard_map/ppermute | solution.py:369
  62.2 1.0 collective-permute-start.21
  63.2 0.4 collective-permute-done.19.rest_17_.rest_8_
  63.6 4.3 %third.1 = bf16[4,8,16,256]{3,2,1,0:T(8,128)(2,1)} custom-call(s32[1]{0:T(128)} %bitcast.tile_ref, bf16[8,10,16,768]{3,2,1,0:T(8,128)(2,1)S(1)} %get-tuple-element.33.sx_ref, bf16[512,256]{1,0:T(8,128)(2,1)S(1)} %get-tuple-element.41.act_ref, bf16[3,128,256]{2,1,0:T(8,128)(2,1)S(1)} %get-tuple-element.35.mask_ref, ...), custom_call_target="tpu_custom_call" | custom-call | flops 1811939328 | bytes 8388608 | tf_op jit(solution)/shard_map/third/pallas_call | solution.py:391
  67.9 2.4 %back.1.sd_ref = bf16[4,10,16,768]{3,2,1,0:T(8,128)(2,1)S(1)} custom-call(s32[1]{0:T(128)} %bitcast.tile_ref, bf16[6,10,16,768]{3,2,1,0:T(8,128)(2,1)S(1)} %get-tuple-element.45.sc_ref, f32[512,256]{1,0:T(8,128)S(1)} %get-tuple-element.46.pre_ref, bf16[3,128,256]{2,1,0:T(8,128)(2,1)S(1)} %get-tuple-element.35.mask_ref, ...), custom_call_target="tpu_custom_call" | custom-call | flops 1811939328 | bytes 8388608 | tf_op jit(solution)/shard_map/back/pallas_call | solution.py:424
  70.3 0.2 add_convert_fusion.5
  70.5 1.0 collective-permute-start.22
  71.5 2.3 %grad.1 = (bf16[3456,256]{1,0:T(8,128)(2,1)S(1)}, bf16[3456,256]{1,0:T(8,128)(2,1)S(1)}) custom-call(s32[1]{0:T(128)} %bitcast.tile_ref, bf16[4,10,16,768]{3,2,1,0:T(8,128)(2,1)S(1)} %back.1.sd_ref, bf16[256,768]{1,0:T(8,128)(2,1)S(1)} %get-tuple-element.49.int_ref), custom_call_target="tpu_custom_call" | custom-call | flops 1811939328 | bytes 8388608 | tf_op jit(solution)/shard_map/grad/pallas_call | solution.py:437
  73.7 5.1 %collective-permute-done.22 = bf16[864,256]{1,0:T(8,128)(2,1)S(1)} collective-permute-done((bf16[864,256]{1,0:T(8,128)(2,1)S(1)}, bf16[864,256]{1,0:T(8,128)(2,1)S(1)}, u32[]{:S(2)}, u32[]{:S(2)}) %collective-permute-start.22) | collective-permute-done | bytes 442400 | tf_op jit(solution)/shard_map/ppermute | solution.py:435
  78.9 3.7 %collective-permute-done.23 = bf16[3456,256]{1,0:T(8,128)(2,1)S(1)} collective-permute-done((bf16[3456,256]{1,0:T(8,128)(2,1)S(1)}, bf16[3456,256]{1,0:T(8,128)(2,1)S(1)}, u32[]{:S(2)}, u32[]{:S(2)}) %collective-permute-start.23) | collective-permute-done | bytes 1769504 | tf_op jit(solution)/shard_map/ppermute | solution.py:447
  82.6 0.1 add_convert_fusion.6
  82.6 1.0 collective-permute-start.24
  83.6 5.0 %collective-permute-done.24 = bf16[432,256]{1,0:T(8,128)(2,1)S(1)} collective-permute-done((bf16[432,256]{1,0:T(8,128)(2,1)S(1)}, bf16[432,256]{1,0:T(8,128)(2,1)S(1)}, u32[]{:S(2)}, u32[]{:S(2)}) %collective-permute-start.24) | collective-permute-done | bytes 221216 | tf_op jit(solution)/shard_map/ppermute | solution.py:450
  88.6 0.2 add_convert_fusion.4
  88.8 1.0 collective-permute-start.25
  89.7 0.2 add_convert_fusion.1
  89.9 2.1 %collective-permute-start.29 = (bf16[864,256]{1,0:T(8,128)(2,1)S(1)}, bf16[864,256]{1,0:T(8,128)(2,1)S(1)}, u32[]{:S(2)}, u32[]{:S(2)}) collective-permute-start(bf16[864,256]{1,0:T(8,128)(2,1)S(1)} %add_convert_fusion.1), channel_id=1, source_target_pairs={{0,4},{4,8},{8,12},{12,14},{14,10},{10,6},{6,2},{2,0},{1,3},{5,1},... | collective-permute-start | bytes 1327112 | tf_op jit(solution)/shard_map/ppermute | solution.py:449
  92.0 5.1 %collective-permute-done.25 = bf16[864,256]{1,0:T(8,128)(2,1)S(1)} collective-permute-done((bf16[864,256]{1,0:T(8,128)(2,1)S(1)}, bf16[864,256]{1,0:T(8,128)(2,1)S(1)}, u32[]{:S(2)}, u32[]{:S(2)}) %collective-permute-start.25) | collective-permute-done | bytes 442400 | tf_op jit(solution)/shard_map/ppermute | solution.py:451
  97.1 0.2 add_convert_fusion.3
  97.3 1.0 collective-permute-start.26
  98.3 3.6 %collective-permute-done.29 = bf16[864,256]{1,0:T(8,128)(2,1)S(1)} collective-permute-done((bf16[864,256]{1,0:T(8,128)(2,1)S(1)}, bf16[864,256]{1,0:T(8,128)(2,1)S(1)}, u32[]{:S(2)}, u32[]{:S(2)}) %collective-permute-start.29) | collective-permute-done | bytes 442400 | tf_op jit(solution)/shard_map/ppermute | solution.py:449
  101.9 0.2 add_convert_fusion
  102.1 1.0 collective-permute-start.30
  103.0 3.6 %collective-permute-done.26 = bf16[864,256]{1,0:T(8,128)(2,1)S(1)} collective-permute-done((bf16[864,256]{1,0:T(8,128)(2,1)S(1)}, bf16[864,256]{1,0:T(8,128)(2,1)S(1)}, u32[]{:S(2)}, u32[]{:S(2)}) %collective-permute-start.26) | collective-permute-done | bytes 442400 | tf_op jit(solution)/shard_map/ppermute | solution.py:453
  106.6 0.2 add_convert_fusion.2
  106.8 1.0 collective-permute-start.27
  107.7 3.6 %collective-permute-done.30 = bf16[864,256]{1,0:T(8,128)(2,1)S(1)} collective-permute-done((bf16[864,256]{1,0:T(8,128)(2,1)S(1)}, bf16[864,256]{1,0:T(8,128)(2,1)S(1)}, u32[]{:S(2)}, u32[]{:S(2)}) %collective-permute-start.30) | collective-permute-done | bytes 442400 | tf_op jit(solution)/shard_map/ppermute | solution.py:452
  111.4 0.1 collective-permute-start.31
  111.5 4.6 %collective-permute-done.27 = bf16[864,256]{1,0:T(8,128)(2,1)S(1)} collective-permute-done((bf16[864,256]{1,0:T(8,128)(2,1)S(1)}, bf16[864,256]{1,0:T(8,128)(2,1)S(1)}, u32[]{:S(2)}, u32[]{:S(2)}) %collective-permute-start.27) | collective-permute-done | bytes 442400 | tf_op jit(solution)/shard_map/ppermute | solution.py:455
  116.1 0.1 collective-permute-start.28
  116.2 0.9 add_multiply_fusion
  117.1 0.6 collective-permute-done.28
  117.7 0.9 add_multiply_fusion.1
  (38 shorter events, 0.3 us)
Async XLA Ops:
  0.6 5.9 %copy-start.1 = (bf16[4,8,16,256]{3,2,1,0:T(8,128)(2,1)S(1)}, bf16[4,8,16,256]{3,2,1,0:T(8,128)(2,1)}, u32[]{:S(2)}) copy-start(bf16[4,8,16,256]{3,2,1,0:T(8,128)(2,1)} %c_own.1) | copy-start | bytes 786436
  0.6 5.9 %copy-start = (bf16[4,8,16,256]{3,2,1,0:T(8,128)(2,1)S(1)}, bf16[4,8,16,256]{3,2,1,0:T(8,128)(2,1)}, u32[]{:S(2)}) copy-start(bf16[4,8,16,256]{3,2,1,0:T(8,128)(2,1)} %f_own.1) | copy-start | bytes 786436
  0.7 17.8 %copy-start.4 = (s32[16,2,4]{0,2,1:T(4,128)S(1)}, s32[16,2,4]{0,2,1:T(4,128)}, u32[]{:S(2)}) copy-start(s32[16,2,4]{0,2,1:T(4,128)} %param.9) | copy-start | bytes 1540
  0.7 1.8 %collective-permute-start = (bf16[432,256]{1,0:T(8,128)(2,1)}, bf16[432,256]{1,0:T(8,128)(2,1)S(1)}, u32[]{:S(2)}, u32[]{:S(2)}) collective-permute-start(bf16[432,256]{1,0:T(8,128)(2,1)} %param.6), channel_id=1, source_target_pairs={{0,1},{1,0},{2,3},{3,2},{4,5},{5,4},{6,7},{7,6},{8,9},{9,8},{10,11... | collective-permute-start | bytes 663560 | tf_op jit(solution)/shard_map/ppermute | solution.py:331
  1.2 5.3 %collective-permute-start.1 = (bf16[432,256]{1,0:T(8,128)(2,1)}, bf16[432,256]{1,0:T(8,128)(2,1)S(1)}, u32[]{:S(2)}, u32[]{:S(2)}) collective-permute-start(bf16[432,256]{1,0:T(8,128)(2,1)} %param.7), channel_id=1, source_target_pairs={{0,1},{1,0},{2,3},{3,2},{4,5},{5,4},{6,7},{7,6},{8,9},{9,8},{10,11... | collective-permute-start | bytes 663560 | tf_op jit(solution)/shard_map/ppermute | solution.py:332
  2.5 14.8 %collective-permute-start.8 = (bf16[864,256]{1,0:T(8,128)(2,1)S(1)}, bf16[864,256]{1,0:T(8,128)(2,1)S(1)}, u32[]{:S(2)}, u32[]{:S(2)}) collective-permute-start(bf16[864,256]{1,0:T(8,128)(2,1)S(1)} %constant_dynamic-update-slice_fusion.rest_0_), channel_id=1, source_target_pairs={{0,4},{4,8},{8,12},{12,14},{14,10},{10,6},{6,2},{2,0},{1,3},{5,1},... | collective-permute-start | bytes 1327112 | tf_op jit(solution)/shard_map/ppermute | solution.py:334
  6.6 10.0 %collective-permute-start.2 = (bf16[3,8,16,256]{3,2,1,0:T(8,128)(2,1)S(1)}, bf16[3,8,16,256]{3,2,1,0:T(8,128)(2,1)S(1)}, u32[]{:S(2)}, u32[]{:S(2)}) collective-permute-start(bf16[3,8,16,256]{3,2,1,0:T(8,128)(2,1)S(1)} %pad_maximum_fusion), channel_id=1, source_target_pairs={{0,1},{1,2},{2,3},{3,4},{4,5},{5,6},{6,7},{7,8},{8,9},{9,10},{10,1... | collective-permute-start | bytes 589832 | tf_op jit(solution)/shard_map/ppermute | solution.py:336
  6.7 9.9 %collective-permute-start.3 = (bf16[3,8,16,256]{3,2,1,0:T(8,128)(2,1)S(1)}, bf16[3,8,16,256]{3,2,1,0:T(8,128)(2,1)S(1)}, u32[]{:S(2)}, u32[]{:S(2)}) collective-permute-start(bf16[3,8,16,256]{3,2,1,0:T(8,128)(2,1)S(1)} %pad_maximum_fusion.1), channel_id=1, source_target_pairs={{0,15},{1,0},{2,1},{3,2},{4,3},{5,4},{6,5},{7,6},{8,7},{9,8},{10,9... | collective-permute-start | bytes 589832 | tf_op jit(solution)/shard_map/ppermute | solution.py:337
  11.2 9.7 %collective-permute-start.4 = (bf16[864,256]{1,0:T(8,128)(2,1)S(1)}, bf16[864,256]{1,0:T(8,128)(2,1)S(1)}, u32[]{:S(2)}, u32[]{:S(2)}) collective-permute-start(bf16[864,256]{1,0:T(8,128)(2,1)S(1)} %constant_dynamic-update-slice_fusion.2.rest_9_.rest_0_), channel_id=1, source_target_pairs={{0,4},{4,8},{8,12},{12,14},{14,10},{10,6},{6,2},{2,0},{1,3},{5,1},... | collective-permute-start | bytes 1327112 | tf_op jit(solution)/shard_map/ppermute | solution.py:334
  16.6 0.7 copy-start.2
  17.3 8.3 %collective-permute-start.9 = (bf16[864,256]{1,0:T(8,128)(2,1)S(1)}, bf16[864,256]{1,0:T(8,128)(2,1)S(1)}, u32[]{:S(2)}, u32[]{:S(2)}) collective-permute-start(bf16[864,256]{1,0:T(8,128)(2,1)S(1)} %collective-permute-done.8.rest_1_), channel_id=1, source_target_pairs={{0,4},{4,8},{8,12},{12,14},{14,10},{10,6},{6,2},{2,0},{1,3},{5,1},... | collective-permute-start | bytes 1327112 | tf_op jit(solution)/shard_map/ppermute | solution.py:369
  17.3 8.3 %collective-permute-start.10 = (bf16[864,256]{1,0:T(8,128)(2,1)S(1)}, bf16[864,256]{1,0:T(8,128)(2,1)S(1)}, u32[]{:S(2)}, u32[]{:S(2)}) collective-permute-start(bf16[864,256]{1,0:T(8,128)(2,1)S(1)} %collective-permute-done.8.rest_1_), channel_id=1, source_target_pairs={{0,1},{1,0},{2,3},{3,2},{4,5},{5,4},{6,7},{7,6},{8,9},{9,8},{10,11... | collective-permute-start | bytes 1327112 | tf_op jit(solution)/shard_map/ppermute | solution.py:370
  18.5 0.9 copy-start.3
  20.8 5.6 %collective-permute-start.6 = (bf16[864,256]{1,0:T(8,128)(2,1)S(1)}, bf16[864,256]{1,0:T(8,128)(2,1)S(1)}, u32[]{:S(2)}, u32[]{:S(2)}) collective-permute-start(bf16[864,256]{1,0:T(8,128)(2,1)S(1)} %collective-permute-done.4.rest_10_.rest_1_), channel_id=1, source_target_pairs={{0,1},{1,0},{2,3},{3,2},{4,5},{5,4},{6,7},{7,6},{8,9},{9,8},{10,11... | collective-permute-start | bytes 1327112 | tf_op jit(solution)/shard_map/ppermute | solution.py:370
  20.9 9.4 %collective-permute-start.5 = (bf16[864,256]{1,0:T(8,128)(2,1)S(1)}, bf16[864,256]{1,0:T(8,128)(2,1)S(1)}, u32[]{:S(2)}, u32[]{:S(2)}) collective-permute-start(bf16[864,256]{1,0:T(8,128)(2,1)S(1)} %collective-permute-done.4.rest_10_.rest_1_), channel_id=1, source_target_pairs={{0,4},{4,8},{8,12},{12,14},{14,10},{10,6},{6,2},{2,0},{1,3},{5,1},... | collective-permute-start | bytes 1327112 | tf_op jit(solution)/shard_map/ppermute | solution.py:369
  25.6 9.5 %collective-permute-start.11 = (bf16[864,256]{1,0:T(8,128)(2,1)S(1)}, bf16[864,256]{1,0:T(8,128)(2,1)S(1)}, u32[]{:S(2)}, u32[]{:S(2)}) collective-permute-start(bf16[864,256]{1,0:T(8,128)(2,1)S(1)} %collective-permute-done.9.rest_2_), channel_id=1, source_target_pairs={{0,4},{4,8},{8,12},{12,14},{14,10},{10,6},{6,2},{2,0},{1,3},{5,1},... | collective-permute-start | bytes 1327112 | tf_op jit(solution)/shard_map/ppermute | solution.py:369
  26.4 8.7 %collective-permute-start.12 = (bf16[864,256]{1,0:T(8,128)(2,1)S(1)}, bf16[864,256]{1,0:T(8,128)(2,1)S(1)}, u32[]{:S(2)}, u32[]{:S(2)}) collective-permute-start(bf16[864,256]{1,0:T(8,128)(2,1)S(1)} %collective-permute-done.9.rest_2_), channel_id=1, source_target_pairs={{0,1},{1,0},{2,3},{3,2},{4,5},{5,4},{6,7},{7,6},{8,9},{9,8},{10,11... | collective-permute-start | bytes 1327112 | tf_op jit(solution)/shard_map/ppermute | solution.py:370
  30.3 11.9 %collective-permute-start.7 = (bf16[864,256]{1,0:T(8,128)(2,1)S(1)}, bf16[864,256]{1,0:T(8,128)(2,1)S(1)}, u32[]{:S(2)}, u32[]{:S(2)}) collective-permute-start(bf16[864,256]{1,0:T(8,128)(2,1)S(1)} %collective-permute-done.5.rest_11_.rest_2_), channel_id=1, source_target_pairs={{0,4},{4,8},{8,12},{12,14},{14,10},{10,6},{6,2},{2,0},{1,3},{5,1},... | collective-permute-start | bytes 1327112 | tf_op jit(solution)/shard_map/ppermute | solution.py:369
  35.1 7.1 %collective-permute-start.13 = (bf16[432,256]{1,0:T(8,128)(2,1)S(1)}, bf16[432,256]{1,0:T(8,128)(2,1)S(1)}, u32[]{:S(2)}, u32[]{:S(2)}) collective-permute-start(bf16[432,256]{1,0:T(8,128)(2,1)S(1)} %slice.94), channel_id=1, source_target_pairs={{0,4},{4,8},{8,12},{12,14},{14,10},{10,6},{6,2},{2,0},{1,3},{5,1},... | collective-permute-start | bytes 663560 | tf_op jit(solution)/shard_map/ppermute | solution.py:369
  35.9 7.8 %collective-permute-start.14 = (bf16[864,256]{1,0:T(8,128)(2,1)S(1)}, bf16[864,256]{1,0:T(8,128)(2,1)S(1)}, u32[]{:S(2)}, u32[]{:S(2)}) collective-permute-start(bf16[864,256]{1,0:T(8,128)(2,1)S(1)} %collective-permute-done.11.rest_3_), channel_id=1, source_target_pairs={{0,1},{1,0},{2,3},{3,2},{4,5},{5,4},{6,7},{7,6},{8,9},{9,8},{10,11... | collective-permute-start | bytes 1327112 | tf_op jit(solution)/shard_map/ppermute | solution.py:370
  42.2 1.5 %collective-permute-start.15 = (bf16[432,256]{1,0:T(8,128)(2,1)S(1)}, bf16[432,256]{1,0:T(8,128)(2,1)S(1)}, u32[]{:S(2)}, u32[]{:S(2)}) collective-permute-start(bf16[432,256]{1,0:T(8,128)(2,1)S(1)} %collective-permute-done.13.rest_4_), channel_id=1, source_target_pairs={{0,1},{1,0},{2,3},{3,2},{4,5},{5,4},{6,7},{7,6},{8,9},{9,8},{10,11... | collective-permute-start | bytes 663560 | tf_op jit(solution)/shard_map/ppermute | solution.py:372
  51.8 10.4 %collective-permute-start.20 = (bf16[3456,256]{1,0:T(8,128)(2,1)S(1)}, bf16[3456,256]{1,0:T(8,128)(2,1)S(1)}, u32[]{:S(2)}, u32[]{:S(2)}) collective-permute-start(bf16[3456,256]{1,0:T(8,128)(2,1)S(1)} %get-tuple-element.44), channel_id=1, source_target_pairs={{0,1},{1,0},{2,3},{3,2},{4,5},{5,4},{6,7},{7,6},{8,9},{9,8},{10,11... | collective-permute-start | bytes 5308424 | tf_op jit(solution)/shard_map/ppermute | solution.py:389
  52.0 4.2 %collective-permute-start.16 = (bf16[864,256]{1,0:T(8,128)(2,1)S(1)}, bf16[864,256]{1,0:T(8,128)(2,1)S(1)}, u32[]{:S(2)}, u32[]{:S(2)}) collective-permute-start(bf16[864,256]{1,0:T(8,128)(2,1)S(1)} %collective-permute-done.5.rest_11_.rest_2_), channel_id=1, source_target_pairs={{0,1},{1,0},{2,3},{3,2},{4,5},{5,4},{6,7},{7,6},{8,9},{9,8},{10,11... | collective-permute-start | bytes 1327112 | tf_op jit(solution)/shard_map/ppermute | solution.py:370
  56.2 6.0 %collective-permute-start.17 = (bf16[432,256]{1,0:T(8,128)(2,1)S(1)}, bf16[432,256]{1,0:T(8,128)(2,1)S(1)}, u32[]{:S(2)}, u32[]{:S(2)}) collective-permute-start(bf16[432,256]{1,0:T(8,128)(2,1)S(1)} %slice.95), channel_id=1, source_target_pairs={{0,4},{4,8},{8,12},{12,14},{14,10},{10,6},{6,2},{2,0},{1,3},{5,1},... | collective-permute-start | bytes 663560 | tf_op jit(solution)/shard_map/ppermute | solution.py:369
  57.0 6.2 %collective-permute-start.18 = (bf16[864,256]{1,0:T(8,128)(2,1)S(1)}, bf16[864,256]{1,0:T(8,128)(2,1)S(1)}, u32[]{:S(2)}, u32[]{:S(2)}) collective-permute-start(bf16[864,256]{1,0:T(8,128)(2,1)S(1)} %collective-permute-done.7.rest_12_.rest_3_), channel_id=1, source_target_pairs={{0,1},{1,0},{2,3},{3,2},{4,5},{5,4},{6,7},{7,6},{8,9},{9,8},{10,11... | collective-permute-start | bytes 1327112 | tf_op jit(solution)/shard_map/ppermute | solution.py:370
  62.2 1.5 %collective-permute-start.19 = (bf16[432,256]{1,0:T(8,128)(2,1)S(1)}, bf16[432,256]{1,0:T(8,128)(2,1)S(1)}, u32[]{:S(2)}, u32[]{:S(2)}) collective-permute-start(bf16[432,256]{1,0:T(8,128)(2,1)S(1)} %collective-permute-done.17.rest_13_.rest_4_), channel_id=1, source_target_pairs={{0,1},{1,0},{2,3},{3,2},{4,5},{5,4},{6,7},{7,6},{8,9},{9,8},{10,11... | collective-permute-start | bytes 663560 | tf_op jit(solution)/shard_map/ppermute | solution.py:372
  62.2 8.1 %collective-permute-start.21 = (bf16[432,256]{1,0:T(8,128)(2,1)S(1)}, bf16[432,256]{1,0:T(8,128)(2,1)S(1)}, u32[]{:S(2)}, u32[]{:S(2)}) collective-permute-start(bf16[432,256]{1,0:T(8,128)(2,1)S(1)} %add_convert_fusion.7), channel_id=1, source_target_pairs={{0,4},{4,8},{8,12},{12,14},{14,10},{10,6},{6,2},{2,0},{1,3},{5,1},... | collective-permute-start | bytes 663560 | tf_op jit(solution)/shard_map/ppermute | solution.py:422
  70.5 8.4 %collective-permute-start.22 = (bf16[864,256]{1,0:T(8,128)(2,1)S(1)}, bf16[864,256]{1,0:T(8,128)(2,1)S(1)}, u32[]{:S(2)}, u32[]{:S(2)}) collective-permute-start(bf16[864,256]{1,0:T(8,128)(2,1)S(1)} %add_convert_fusion.5), channel_id=1, source_target_pairs={{0,4},{4,8},{8,12},{12,14},{14,10},{10,6},{6,2},{2,0},{1,3},{5,1},... | collective-permute-start | bytes 1327112 | tf_op jit(solution)/shard_map/ppermute | solution.py:435
  78.9 3.7 %collective-permute-start.23 = (bf16[3456,256]{1,0:T(8,128)(2,1)S(1)}, bf16[3456,256]{1,0:T(8,128)(2,1)S(1)}, u32[]{:S(2)}, u32[]{:S(2)}) collective-permute-start(bf16[3456,256]{1,0:T(8,128)(2,1)S(1)} %get-tuple-element.52), channel_id=1, source_target_pairs={{0,1},{1,0},{2,3},{3,2},{4,5},{5,4},{6,7},{7,6},{8,9},{9,8},{10,11... | collective-permute-start | bytes 5308424 | tf_op jit(solution)/shard_map/ppermute | solution.py:447
  82.6 6.0 %collective-permute-start.24 = (bf16[432,256]{1,0:T(8,128)(2,1)S(1)}, bf16[432,256]{1,0:T(8,128)(2,1)S(1)}, u32[]{:S(2)}, u32[]{:S(2)}) collective-permute-start(bf16[432,256]{1,0:T(8,128)(2,1)S(1)} %add_convert_fusion.6), channel_id=1, source_target_pairs={{0,4},{4,8},{8,12},{12,14},{14,10},{10,6},{6,2},{2,0},{1,3},{5,1},... | collective-permute-start | bytes 663560 | tf_op jit(solution)/shard_map/ppermute | solution.py:450
  88.8 8.4 %collective-permute-start.25 = (bf16[864,256]{1,0:T(8,128)(2,1)S(1)}, bf16[864,256]{1,0:T(8,128)(2,1)S(1)}, u32[]{:S(2)}, u32[]{:S(2)}) collective-permute-start(bf16[864,256]{1,0:T(8,128)(2,1)S(1)} %add_convert_fusion.4), channel_id=1, source_target_pairs={{0,4},{4,8},{8,12},{12,14},{14,10},{10,6},{6,2},{2,0},{1,3},{5,1},... | collective-permute-start | bytes 1327112 | tf_op jit(solution)/shard_map/ppermute | solution.py:451
  89.9 12.0 %collective-permute-start.29 = (bf16[864,256]{1,0:T(8,128)(2,1)S(1)}, bf16[864,256]{1,0:T(8,128)(2,1)S(1)}, u32[]{:S(2)}, u32[]{:S(2)}) collective-permute-start(bf16[864,256]{1,0:T(8,128)(2,1)S(1)} %add_convert_fusion.1), channel_id=1, source_target_pairs={{0,4},{4,8},{8,12},{12,14},{14,10},{10,6},{6,2},{2,0},{1,3},{5,1},... | collective-permute-start | bytes 1327112 | tf_op jit(solution)/shard_map/ppermute | solution.py:449
  97.3 9.3 %collective-permute-start.26 = (bf16[864,256]{1,0:T(8,128)(2,1)S(1)}, bf16[864,256]{1,0:T(8,128)(2,1)S(1)}, u32[]{:S(2)}, u32[]{:S(2)}) collective-permute-start(bf16[864,256]{1,0:T(8,128)(2,1)S(1)} %add_convert_fusion.3), channel_id=1, source_target_pairs={{0,4},{4,8},{8,12},{12,14},{14,10},{10,6},{6,2},{2,0},{1,3},{5,1},... | collective-permute-start | bytes 1327112 | tf_op jit(solution)/shard_map/ppermute | solution.py:453
  102.1 9.3 %collective-permute-start.30 = (bf16[864,256]{1,0:T(8,128)(2,1)S(1)}, bf16[864,256]{1,0:T(8,128)(2,1)S(1)}, u32[]{:S(2)}, u32[]{:S(2)}) collective-permute-start(bf16[864,256]{1,0:T(8,128)(2,1)S(1)} %add_convert_fusion), channel_id=1, source_target_pairs={{0,4},{4,8},{8,12},{12,14},{14,10},{10,6},{6,2},{2,0},{1,3},{5,1},... | collective-permute-start | bytes 1327112 | tf_op jit(solution)/shard_map/ppermute | solution.py:452
  106.8 9.3 %collective-permute-start.27 = (bf16[864,256]{1,0:T(8,128)(2,1)S(1)}, bf16[864,256]{1,0:T(8,128)(2,1)S(1)}, u32[]{:S(2)}, u32[]{:S(2)}) collective-permute-start(bf16[864,256]{1,0:T(8,128)(2,1)S(1)} %add_convert_fusion.2), channel_id=1, source_target_pairs={{0,4},{4,8},{8,12},{12,14},{14,10},{10,6},{6,2},{2,0},{1,3},{5,1},... | collective-permute-start | bytes 1327112 | tf_op jit(solution)/shard_map/ppermute | solution.py:455
  111.4 4.8 %collective-permute-start.31 = (bf16[432,256]{1,0:T(8,128)(2,1)S(1)}, bf16[432,256]{1,0:T(8,128)(2,1)S(1)}, u32[]{:S(2)}, u32[]{:S(2)}) collective-permute-start(bf16[432,256]{1,0:T(8,128)(2,1)S(1)} %slice.133), channel_id=1, source_target_pairs={{0,1},{1,0},{2,3},{3,2},{4,5},{5,4},{6,7},{7,6},{8,9},{9,8},{10,11... | collective-permute-start | bytes 663560 | tf_op jit(solution)/shard_map/ppermute | solution.py:417
  116.1 1.5 %collective-permute-start.28 = (bf16[432,256]{1,0:T(8,128)(2,1)S(1)}, bf16[432,256]{1,0:T(8,128)(2,1)S(1)}, u32[]{:S(2)}, u32[]{:S(2)}) collective-permute-start(bf16[432,256]{1,0:T(8,128)(2,1)S(1)} %slice.128), channel_id=1, source_target_pairs={{0,1},{1,0},{2,3},{3,2},{4,5},{5,4},{6,7},{7,6},{8,9},{9,8},{10,11... | collective-permute-start | bytes 663560 | tf_op jit(solution)/shard_map/ppermute | solution.py:417

commit v2 on v1

--- a/solution.py
+++ b/solution.py
@@ -123,11 +123,11 @@
     out_ref[:, ny + 1 : ny + 2] = edge
 
 
-def prep_kernel(tile_ref, cells_ref, low, f_own, c_own, high, sx_ref, sc_ref, int_ref, mask_ref):
+def prep_kernel(cells_ref, low, f_own, c_own, high, sx_ref, sc_ref, int_ref, mask_ref):
     depth, ny, nz, channels = f_own.shape
     area = ny * nz
-    tile = tile_ref[0]
-    last = cells_ref.shape[0] - 1
+    tile = lax.axis_index("tiles")
+    last = cells_ref.shape[2] - 1
     row = lax.broadcasted_iota(jnp.int32, (area, channels), 0)
     block_y, block_z = row // (B * nz), (row % nz) // B
     m = []
@@ -138,7 +138,7 @@
         value = jnp.zeros((area, channels), F32)
         for y in range(ny // B):
             for z in range(nz // B):
-                cell = jnp.where(inside, cells_ref[at, y * (nz // B) + z], 0).astype(F32)
+                cell = jnp.where(inside, cells_ref[y, z, at], 0).astype(F32)
                 here = jnp.logical_and(block_y == y, block_z == z)
                 value = jnp.where(here, cell, value)
         value = value.astype(BF)
@@ -162,8 +162,8 @@
         store_shifted(sc_ref, x0, rows(value, side), ny, nz, channels)
 
 
-def fill_weight(tile_ref, pieces, w_ref):
-    tile = tile_ref[0]
+def fill_weight(pieces, w_ref):
+    tile = lax.axis_index("tiles")
     core = tile % 2
     rows = w_ref.shape[0] // 16
     for k, piece in enumerate(pieces):
@@ -173,8 +173,8 @@
             w_ref[pl.ds(start, rows)] = piece[half * rows : (half + 1) * rows]
 
 
-def split_shards(tile_ref, g_ref, keep_ref, send_ref):
-    tile = tile_ref[0]
+def split_shards(g_ref, keep_ref, send_ref):
+    tile = lax.axis_index("tiles")
     core = tile % 2
     rows = g_ref.shape[0] // 16
     for out_ref, holder in ((send_ref, 1 - core), (keep_ref, core)):
@@ -217,12 +217,12 @@
     return (value.reshape(-1, area, channels) * own).reshape(-1, channels)
 
 
-def first_kernel(n, tile_ref, sx_ref, sc_ref, mask_ref, *rest):
+def first_kernel(n, sx_ref, sc_ref, mask_ref, *rest):
     pieces, (pre_ref, act_ref, keep_ref, send_ref, w_ref, g_ref) = rest[:n], rest[n:]
     area, channels = mask_ref.shape[1:]
     ny = sx_ref.shape[1] - 2
     depth = pre_ref.shape[0] // area
-    fill_weight(tile_ref, pieces, w_ref)
+    fill_weight(pieces, w_ref)
     pre = conv(sx_ref, w_ref, 1, depth, ny, channels)
     pre_ref[...] = pre
     act = masked(pre * jax.nn.sigmoid(pre), mask_ref, 1).astype(BF)
@@ -234,15 +234,15 @@
                 act_t, window(sc_ref, 2 - p, 2 - q, depth, ny), preferred_element_type=F32
             )
             store_taps(g_ref, p, q, part.astype(BF), channels)
-    split_shards(tile_ref, g_ref, keep_ref, send_ref)
-
-
-def back_kernel(n, tile_ref, sc_ref, pre_ref, mask_ref, *rest):
+    split_shards(g_ref, keep_ref, send_ref)
+
+
+def back_kernel(n, sc_ref, pre_ref, mask_ref, *rest):
     pieces, (sd_ref, w_ref) = rest[:n], rest[n:]
     area, channels = mask_ref.shape[1:]
     ny, nz = sc_ref.shape[1] - 2, sc_ref.shape[2]
     depth = pre_ref.shape[0] // area
-    fill_weight(tile_ref, pieces, w_ref)
+    fill_weight(pieces, w_ref)
     acc = None
     for p in range(3):
         for q in range(3):
@@ -261,7 +261,7 @@
     store_shifted(sd_ref, 0, delta, ny, nz, channels)
 
 
-def grad_kernel(tile_ref, sd_ref, int_ref, keep_ref, send_ref, g_ref):
+def grad_kernel(sd_ref, int_ref, keep_ref, send_ref, g_ref):
     depth, ny, nz, channels = sd_ref.shape
     ny, area, channels = ny - 2, (ny - 2) * nz, channels // 3
     for q in range(3):
@@ -271,16 +271,16 @@
                 int_ref[:, p * area : (p + depth) * area], right, preferred_element_type=F32
             )
             store_taps(g_ref, p, q, part.astype(BF), channels)
-    split_shards(tile_ref, g_ref, keep_ref, send_ref)
-
-
-def third_kernel(n, tile_ref, sx_ref, act_ref, mask_ref, *rest):
+    split_shards(g_ref, keep_ref, send_ref)
+
+
+def third_kernel(n, sx_ref, act_ref, mask_ref, *rest):
     out_ref, w_ref, v_ref, sa_ref = rest[2 * n :]
     area, channels = mask_ref.shape[1:]
     ny, nz = sx_ref.shape[1] - 2, sx_ref.shape[2]
     depth = act_ref.shape[0] // area
-    fill_weight(tile_ref, rest[:n], w_ref)
-    fill_weight(tile_ref, rest[n : 2 * n], v_ref)
+    fill_weight(rest[:n], w_ref)
+    fill_weight(rest[n : 2 * n], v_ref)
     clear_edges(sa_ref, ny)
     store_shifted(sa_ref, 1, act_ref[...], ny, nz, channels)
     for x0, side in ((0, 0), (1 + depth, 2)):
@@ -291,9 +291,6 @@
     out_ref[...] = masked(second, mask_ref, 1).astype(BF).reshape(out_ref.shape)
 
 
-VMEM_LIMIT = 24 * 1024 * 1024
-
-
 def on_ring(features, weight_one, weight_two, cotangent, block_mask):
     depth, ny, nz, channels = features.shape
     area = ny * nz
@@ -301,7 +298,6 @@
     chips = len(RING)
     tiles = 2 * chips
     loss_scale = 1.0 / math.sqrt(tiles * depth * area)
-    tile = lax.axis_index("tiles").astype(jnp.int32)[None]
 
     def permute(pairs):
         return functools.partial(lax.ppermute, axis_name="tiles", perm=pairs)
@@ -319,7 +315,10 @@
 
     smem = pl.BlockSpec(memory_space=pltpu.SMEM)
     vmem = pl.BlockSpec(memory_space=pltpu.VMEM)
-    params = pltpu.CompilerParams(vmem_limit_bytes=VMEM_LIMIT)
+
+    def params(mib):
+        return pltpu.CompilerParams(vmem_limit_bytes=mib << 20)
+
     shape = jax.ShapeDtypeStruct
     flops = 2 * depth * area * 27 * channels * channels
 
@@ -345,28 +344,28 @@
             shape((channels, (depth + 2) * area), BF),
             shape((3, area, channels), BF),
         ),
-        in_specs=[smem, smem] + [vmem] * 4,
+        in_specs=[smem] + [vmem] * 4,
         out_specs=(vmem,) * 4,
-        compiler_params=params,
+        compiler_params=params(8),
     )
     crossed = [[], []]
-    sx, sc, in_t, near = None, None, None, None
     for hop in (1, 2, 3):
         for k in range(2):
             here = rings[k][hop]
+            if hop == 3:
+                here = here[:rows]
             if k == 0 and hop > 1:
                 here = after(here, rings[1][hop - 1])
-            if hop == 1:
-                if k == 0:
-                    here = after(here, low, high)
-                    sx, sc, in_t, near = prep(
-                        tile, block_mask.reshape(tiles, -1), low, features, cotangent, high
-                    )
-            elif hop == 2:
-                here = after(here, crossed[k][0], sx) if k == 0 else after(here, crossed[k][0])
-            else:
-                here = after(here, crossed[k][1])
-            rings[k].append(onward(here[:rows] if hop == 3 else here))
+            if k == 0 and hop == 2:
+                here = after(here, low, high)
+                sx, sc, in_t, near = prep(
+                    jnp.transpose(block_mask, (1, 2, 0)), low, features, cotangent, high
+                )
+            if k == 0 and hop == 3:
+                here = after(here, sx)
+            if hop > 1:
+                here = after(here, crossed[k][hop - 2])
+            rings[k].append(onward(here))
             crossed[k].append(sibling(rings[k][hop]))
     for k in range(2):
         crossed[k].append(sibling(rings[k][4]))
@@ -380,79 +379,75 @@
         name="first",
         out_shape=(shape((depth * area, channels), F32), shape((depth * area, channels), BF))
         + shards,
-        in_specs=[smem] + [vmem] * (3 + n),
+        in_specs=[vmem] * (3 + n),
         out_specs=(vmem,) * 4,
         scratch_shapes=[weights, weights],
-        compiler_params=params,
+        compiler_params=params(12),
         cost_estimate=cost(2),
-    )(tile, after(sx, rings[1][3]), sc, near, *ones)
+    )(after(sx, rings[1][4]), sc, near, *ones)
     got_two = sibling(send_two)
 
+    def both(keep, got, lo, hi):
+        return keep[lo * rows : hi * rows].astype(F32) + got[lo * rows : hi * rows].astype(F32)
+
+    def step(keep, got, moving, k):
+        if k == 0:
+            return both(keep, got, 0, 1).astype(BF)
+        if k == 1:
+            moving = jnp.concatenate([moving, jnp.zeros_like(moving)])
+        return (both(keep, got, 2 * k - 1, 2 * k + 1) + moving.astype(F32)).astype(BF)
+
+    def finish(keep, got, moving):
+        across = sibling(moving[rows:])
+        total = both(keep, got, 7, 8) + moving[:rows].astype(F32) + across.astype(F32)
+        return total * loss_scale
+
+    delta = pl.pallas_call(
+        functools.partial(back_kernel, n),
+        name="back",
+        out_shape=shape((depth, ny + 2, nz, 3 * channels), BF),
+        in_specs=[vmem] * (3 + n),
+        out_specs=vmem,
+        scratch_shapes=[weights],
+        compiler_params=params(8),
+        cost_estimate=cost(1),
+    )(sc, pre, near, *twos)
+    keep_one, send_one = pl.pallas_call(
+        grad_kernel,
+        name="grad",
+        out_shape=shards,
+        in_specs=[vmem] * 2,
+        out_specs=(vmem,) * 2,
+        scratch_shapes=[weights],
+        compiler_params=params(8),
+        cost_estimate=cost(1),
+    )(delta, in_t)
+    got_two_late = after(got_two, keep_one)
+    two = onward(step(keep_two, got_two_late, None, 0))
+    got_one = sibling(send_one)
+    one = onward(step(keep_one, got_one, None, 0))
     features_out = pl.pallas_call(
         functools.partial(third_kernel, n),
         name="third",
         out_shape=shape(features.shape, BF),
-        in_specs=[smem] + [vmem] * (3 + 2 * n),
+        in_specs=[vmem] * (3 + 2 * n),
         out_specs=vmem,
         scratch_shapes=[
             weights,
             weights,
             pltpu.VMEM((depth + 2, ny + 2, nz, 3 * channels), BF),
         ],
-        compiler_params=params,
+        compiler_params=params(14),
         cost_estimate=cost(1),
-    )(tile, sx, act, near, *ones, *twos)
-
-    def both(keep, got, lo, hi):
-        return keep[lo * rows : hi * rows].astype(F32) + got[lo * rows : hi * rows].astype(F32)
-
-    def step(keep, got, moving, k):
-        if k == 0:
-            return both(keep, got, 0, 1).astype(BF)
-        if k == 1:
-            moving = jnp.concatenate([moving, jnp.zeros_like(moving)])
-        return (both(keep, got, 2 * k - 1, 2 * k + 1) + moving.astype(F32)).astype(BF)
-
-    def finish(keep, got, moving):
-        across = sibling(moving[rows:])
-        total = both(keep, got, 7, 8) + moving[:rows].astype(F32) + across.astype(F32)
-        return total * loss_scale
-
-    message = step(keep_two, got_two, None, 0)
-    two = onward(message)
-
-    delta = pl.pallas_call(
-        functools.partial(back_kernel, n),
-        name="back",
-        out_shape=shape((depth, ny + 2, nz, 3 * channels), BF),
-        in_specs=[smem] + [vmem] * (3 + n),
-        out_specs=vmem,
-        scratch_shapes=[weights],
-        compiler_params=params,
-        cost_estimate=cost(1),
-    )(tile, after(sc, message, features_out), pre, near, *twos)
-    message = step(keep_two, got_two, after(two, delta), 1)
-    two = onward(message)
-
-    keep_one, send_one = pl.pallas_call(
-        grad_kernel,
-        name="grad",
-        out_shape=shards,
-        in_specs=[smem] + [vmem] * 2,
-        out_specs=(vmem,) * 2,
-        scratch_shapes=[weights],
-        compiler_params=params,
-        cost_estimate=cost(1),
-    )(tile, after(delta, message), in_t)
-    got_one = sibling(after(send_one, two))
-
-    two = onward(step(keep_two, got_two, two, 2))
-    one = onward(step(keep_one, got_one, None, 0))
+    )(sx, after(act, two), near, *ones, *twos)
+
+    two = onward(step(keep_two, got_two, two, 1))
     one = onward(step(keep_one, got_one, one, 1))
+    two = onward(step(keep_two, got_two, after(two, features_out), 2))
+    one = onward(step(keep_one, got_one, one, 2))
     two = onward(step(keep_two, got_two, two, 3))
-    one = onward(step(keep_one, got_one, one, 2))
+    one = onward(step(keep_one, got_one, one, 3))
     grad_two = finish(keep_two, got_two, two)
-    one = onward(step(keep_one, got_one, one, 3))
     return (features_out, finish(keep_one, got_one, one), grad_two)
 
 

time: 119 us -> 102 us (0.86)
  waiting for transfers between devices: 69.6 us -> 54.2 us
  local copies, waits for them, and re-layouts: 3.71 us -> 2.03 us
    ppermute x10, waiting for transfers between devices: 35.6 us -> 26.1 us  [the longest x6 17 us: on_ring(): rings[k].append(onward(here))]
    ppermute x2, waiting for transfers between devices: 0.01 us -> 5.94 us  [on_ring(): rings = [[pair, onward(pair)] for pair in pairs]]
    ppermute x1, waiting for transfers between devices: 5.45 us -> 0.01 us  [on_ring(): low = up(jnp.concatenate([features_late[-2:], cot_late[-1:]]))]
    ppermute x6, waiting for transfers between devices: 3.83 us -> 0.02 us  [on_ring(): crossed[k].append(sibling(rings[k][hop]))]
    ppermute x1, waiting for transfers between devices: 0.01 us -> 3.19 us  [on_ring(): high = down(jnp.concatenate([features_late[:2], cot_late[:1]]))]
    ppermute x1, waiting for transfers between devices: 5.03 us -> 2.63 us  [on_ring(): one = onward(step(keep_one, got_one, None, 0))]
    ppermute x1, starting transfers between devices: 4.48 us -> 2.4 us  [on_ring(): high = down(jnp.concatenate([features_late[:2], cot_late[:1]]))]
    ppermute x1, waiting for transfers between devices: 5.11 us -> 3.09 us  [on_ring(): one = onward(step(keep_one, got_one, one, 1))]
  transfers between devices with their start and end apart: 32 -> 32, of which waited for: 19 -> 19; matrix products, arithmetic and copies ran while one was open for 3% -> 4% of each run, Pallas kernels for 9% -> 18%
where the time goes in v2:
time: 102 us
  waiting for transfers between devices  54.2 us (53%)
  starting transfers between devices  23.4 us (23%)
  Pallas kernels  18.3 us (18%)
  other arithmetic  2.98 us (3%)
  local copies, waits for them, and re-layouts  2.03 us (2%)
    ppermute x6, waiting for transfers between devices, on_ring(): rings[k].append(onward(here))  17 us
    pallas_call x1, Pallas kernels, on_ring(): pl.pallas_call(functools.partial(first_kernel, n), name='first', out_shap...  8.07 us
    ppermute x6, starting transfers between devices, on_ring(): rings[k].append(onward(here))  6.02 us
    ppermute x2, waiting for transfers between devices, on_ring(): rings = [[pair, onward(pair)] for pair in pairs]  5.94 us
    ppermute x1, waiting for transfers between devices, on_ring(): one = onward(step(keep_one, got_one, one, 3))  4.64 us
    ppermute x2, starting transfers between devices, on_ring(): rings = [[pair, onward(pair)] for pair in pairs]  4.63 us
    pallas_call x1, Pallas kernels, on_ring(): pl.pallas_call(functools.partial(third_kernel, n), name='third', out_shap...  4.21 us
    ppermute x1, waiting for transfers between devices, on_ring(): two = onward(step(keep_two, got_two, after(two, features_out), 2))  3.89 us
  transfers between devices with their start and end apart: 32, of which 19 were waited for; matrix products, arithmetic and copies ran while one was open for 4% of the time, Pallas kernels for 18%

profile of v2, /device:TPU:0, one launch (start us, length us, event | category | flops | bytes accessed | tf_op | source)
XLA Modules:
  0.0 101.7 jit_solution(9357361724746090647)
XLA Ops:
  0.7 0.5 collective-permute-start
  1.2 0.1 collective-permute-start.1
  1.3 0.9 constant_dynamic-update-slice_fusion.1
  2.2 0.3 collective-permute-done
  2.5 3.0 %collective-permute-start.10 = (bf16[864,256]{1,0:T(8,128)(2,1)S(1)}, bf16[864,256]{1,0:T(8,128)(2,1)S(1)}, u32[]{:S(2)}, u32[]{:S(2)}) collective-permute-start(bf16[864,256]{1,0:T(8,128)(2,1)S(1)} %constant_dynamic-update-slice_fusion.rest_0_), channel_id=1, source_target_pairs={{0,4},{4,8},{8,12},{12,14},{14,10},{10,6},{6,2},{2,0},{1,3},{5,1},... | collective-permute-start | bytes 1327112 | tf_op jit(solution)/shard_map/ppermute | solution.py:333
  5.5 0.9 constant_dynamic-update-slice_fusion.3
  6.5 0.0 collective-permute-done.1
  6.5 1.6 %collective-permute-start.4 = (bf16[864,256]{1,0:T(8,128)(2,1)S(1)}, bf16[864,256]{1,0:T(8,128)(2,1)S(1)}, u32[]{:S(2)}, u32[]{:S(2)}) collective-permute-start(bf16[864,256]{1,0:T(8,128)(2,1)S(1)} %constant_dynamic-update-slice_fusion.2.rest_0_.rest_9_), channel_id=1, source_target_pairs={{0,4},{4,8},{8,12},{12,14},{14,10},{10,6},{6,2},{2,0},{1,3},{5,1},... | collective-permute-start | bytes 1327112 | tf_op jit(solution)/shard_map/ppermute | solution.py:333
  8.2 3.6 %collective-permute-done.10.rest_1_ = bf16[864,256]{1,0:T(8,128)(2,1)S(1)} collective-permute-done((bf16[864,256]{1,0:T(8,128)(2,1)S(1)}, bf16[864,256]{1,0:T(8,128)(2,1)S(1)}, u32[]{:S(2)}, u32[]{:S(2)}) %collective-permute-start.10) | collective-permute-done | bytes 442400 | tf_op jit(solution)/shard_map/ppermute | solution.py:333
  11.7 2.1 %collective-permute-start.11 = (bf16[864,256]{1,0:T(8,128)(2,1)S(1)}, bf16[864,256]{1,0:T(8,128)(2,1)S(1)}, u32[]{:S(2)}, u32[]{:S(2)}) collective-permute-start(bf16[864,256]{1,0:T(8,128)(2,1)S(1)} %collective-permute-done.10.rest_1_), channel_id=1, source_target_pairs={{0,4},{4,8},{8,12},{12,14},{14,10},{10,6},{6,2},{2,0},{1,3},{5,1},... | collective-permute-start | bytes 1327112 | tf_op jit(solution)/shard_map/ppermute | solution.py:368
  13.9 0.3 collective-permute-start.2
  14.1 2.4 %collective-permute-done.4.rest_1_.rest_10_ = bf16[864,256]{1,0:T(8,128)(2,1)S(1)} collective-permute-done((bf16[864,256]{1,0:T(8,128)(2,1)S(1)}, bf16[864,256]{1,0:T(8,128)(2,1)S(1)}, u32[]{:S(2)}, u32[]{:S(2)}) %collective-permute-start.4) | collective-permute-done | bytes 442400 | tf_op jit(solution)/shard_map/ppermute | solution.py:333
  16.5 2.1 %collective-permute-start.5 = (bf16[864,256]{1,0:T(8,128)(2,1)S(1)}, bf16[864,256]{1,0:T(8,128)(2,1)S(1)}, u32[]{:S(2)}, u32[]{:S(2)}) collective-permute-start(bf16[864,256]{1,0:T(8,128)(2,1)S(1)} %collective-permute-done.4.rest_1_.rest_10_), channel_id=1, source_target_pairs={{0,4},{4,8},{8,12},{12,14},{14,10},{10,6},{6,2},{2,0},{1,3},{5,1},... | collective-permute-start | bytes 1327112 | tf_op jit(solution)/shard_map/ppermute | solution.py:368
  18.6 4.2 %collective-permute-done.11.rest_2_ = bf16[864,256]{1,0:T(8,128)(2,1)S(1)} collective-permute-done((bf16[864,256]{1,0:T(8,128)(2,1)S(1)}, bf16[864,256]{1,0:T(8,128)(2,1)S(1)}, u32[]{:S(2)}, u32[]{:S(2)}) %collective-permute-start.11) | collective-permute-done | bytes 442400 | tf_op jit(solution)/shard_map/ppermute | solution.py:368
  22.8 2.4 %collective-permute-start.3 = (bf16[3,8,16,256]{3,2,1,0:T(8,128)(2,1)S(1)}, bf16[3,8,16,256]{3,2,1,0:T(8,128)(2,1)S(1)}, u32[]{:S(2)}, u32[]{:S(2)}) collective-permute-start(bf16[3,8,16,256]{3,2,1,0:T(8,128)(2,1)S(1)} %pad_maximum_fusion.1), channel_id=1, source_target_pairs={{0,15},{1,0},{2,1},{3,2},{4,3},{5,4},{6,5},{7,6},{8,7},{9,8},{10,9... | collective-permute-start | bytes 589832 | tf_op jit(solution)/shard_map/ppermute | solution.py:336
  25.2 3.2 %collective-permute-done.3.high = bf16[3,8,16,256]{3,2,1,0:T(8,128)(2,1)S(1)} collective-permute-done((bf16[3,8,16,256]{3,2,1,0:T(8,128)(2,1)S(1)}, bf16[3,8,16,256]{3,2,1,0:T(8,128)(2,1)S(1)}, u32[]{:S(2)}, u32[]{:S(2)}) %collective-permute-start.3) | collective-permute-done | bytes 196640 | tf_op jit(solution)/shard_map/ppermute | solution.py:336
  28.4 1.6 %collective-permute-start.14 = (bf16[864,256]{1,0:T(8,128)(2,1)S(1)}, bf16[864,256]{1,0:T(8,128)(2,1)S(1)}, u32[]{:S(2)}, u32[]{:S(2)}) collective-permute-start(bf16[864,256]{1,0:T(8,128)(2,1)S(1)} %collective-permute-done.11.rest_2_), channel_id=1, source_target_pairs={{0,1},{1,0},{2,3},{3,2},{4,5},{5,4},{6,7},{7,6},{8,9},{9,8},{10,11... | collective-permute-start | bytes 1327112 | tf_op jit(solution)/shard_map/ppermute | solution.py:369
  30.0 1.7 %collective-permute-start.7 = (bf16[864,256]{1,0:T(8,128)(2,1)S(1)}, bf16[864,256]{1,0:T(8,128)(2,1)S(1)}, u32[]{:S(2)}, u32[]{:S(2)}) collective-permute-start(bf16[864,256]{1,0:T(8,128)(2,1)S(1)} %collective-permute-done.5.rest_2_.rest_11_), channel_id=1, source_target_pairs={{0,4},{4,8},{8,12},{12,14},{14,10},{10,6},{6,2},{2,0},{1,3},{5,1},... | collective-permute-start | bytes 1327112 | tf_op jit(solution)/shard_map/ppermute | solution.py:368
  31.8 1.3 %prep.1 = (bf16[8,10,16,768]{3,2,1,0:T(8,128)(2,1)S(1)}, bf16[6,10,16,768]{3,2,1,0:T(8,128)(2,1)S(1)}, bf16[256,768]{1,0:T(8,128)(2,1)S(1)}, bf16[3,128,256]{2,1,0:T(8,128)(2,1)S(1)}) custom-call(s32[2,4,16]{2,1,0:T(4,128)S(1)} %bitcast.1, bf16[3,8,16,256]{3,2,1,0:T(8,128)(2,1)S(1)} %collective-permute-done.2.low, bf16[4,8,16,256]{3,2,1,0:T(8,128)(2,1)S(1)} %copy-done, ...), custom_call_target="tpu_custom_call" | custom-call | tf_op jit(solution)/shard_map/prep/pallas_call | solution.py:361
  33.1 3.6 %collective-permute-done.13.rest_3_ = bf16[864,256]{1,0:T(8,128)(2,1)S(1)} collective-permute-done((bf16[864,256]{1,0:T(8,128)(2,1)S(1)}, bf16[864,256]{1,0:T(8,128)(2,1)S(1)}, u32[]{:S(2)}, u32[]{:S(2)}) %collective-permute-start.13) | collective-permute-done | bytes 442400 | tf_op jit(solution)/shard_map/ppermute | solution.py:368
  36.7 0.1 collective-permute-start.15
  36.8 0.9 collective-permute-start.16
  37.6 3.8 %collective-permute-done.7.rest_3_.rest_12_ = bf16[864,256]{1,0:T(8,128)(2,1)S(1)} collective-permute-done((bf16[864,256]{1,0:T(8,128)(2,1)S(1)}, bf16[864,256]{1,0:T(8,128)(2,1)S(1)}, u32[]{:S(2)}, u32[]{:S(2)}) %collective-permute-start.7) | collective-permute-done | bytes 442400 | tf_op jit(solution)/shard_map/ppermute | solution.py:368
  41.4 0.1 collective-permute-start.9
  41.5 2.3 %collective-permute-done.15.rest_4_ = bf16[432,256]{1,0:T(8,128)(2,1)S(1)} collective-permute-done((bf16[432,256]{1,0:T(8,128)(2,1)S(1)}, bf16[432,256]{1,0:T(8,128)(2,1)S(1)}, u32[]{:S(2)}, u32[]{:S(2)}) %collective-permute-start.15) | collective-permute-done | bytes 221216 | tf_op jit(solution)/shard_map/ppermute | solution.py:368
  43.8 0.5 collective-permute-start.17
  44.3 0.0 collective-permute-start.19
  44.3 3.1 %collective-permute-done.9.rest_4_.rest_13_ = bf16[432,256]{1,0:T(8,128)(2,1)S(1)} collective-permute-done((bf16[432,256]{1,0:T(8,128)(2,1)S(1)}, bf16[432,256]{1,0:T(8,128)(2,1)S(1)}, u32[]{:S(2)}, u32[]{:S(2)}) %collective-permute-start.9) | collective-permute-done | bytes 221216 | tf_op jit(solution)/shard_map/ppermute | solution.py:368
  47.4 8.1 %first.1 = (f32[512,256]{1,0:T(8,128)S(1)}, bf16[512,256]{1,0:T(8,128)(2,1)S(1)}, bf16[3456,256]{1,0:T(8,128)(2,1)S(1)}, bf16[3456,256]{1,0:T(8,128)(2,1)S(1)}) custom-call(bf16[8,10,16,768]{3,2,1,0:T(8,128)(2,1)S(1)} %get-tuple-element.34.sx_ref, bf16[6,10,16,768]{3,2,1,0:T(8,128)(2,1)S(1)} %get-tuple-element.35.sc_ref, ...), custom_call_target="tpu_custom_call" | custom-call | flops 3623878656 | bytes 8388608 | tf_op jit(solution)/shard_map/first/pallas_call | solution.py:377
  55.5 0.6 collective-permute-start.18
  56.1 2.4 %back.1.sd_ref = bf16[4,10,16,768]{3,2,1,0:T(8,128)(2,1)S(1)} custom-call(bf16[6,10,16,768]{3,2,1,0:T(8,128)(2,1)S(1)} %get-tuple-element.35.sc_ref, f32[512,256]{1,0:T(8,128)S(1)} %get-tuple-element.46.pre_ref, bf16[3,128,256]{2,1,0:T(8,128)(2,1)S(1)} %get-tuple-element.36.mask_ref, ...), custom_call_target="tpu_custom_call" | custom-call | flops 1811939328 | bytes 8388608 | tf_op jit(solution)/shard_map/back/pallas_call | solution.py:405
  58.5 2.2 %grad.1 = (bf16[3456,256]{1,0:T(8,128)(2,1)S(1)}, bf16[3456,256]{1,0:T(8,128)(2,1)S(1)}) custom-call(bf16[4,10,16,768]{3,2,1,0:T(8,128)(2,1)S(1)} %back.1.sd_ref, bf16[256,768]{1,0:T(8,128)(2,1)S(1)} %get-tuple-element.47.int_ref), custom_call_target="tpu_custom_call" | custom-call | flops 1811939328 | bytes 8388608 | tf_op jit(solution)/shard_map/grad/pallas_call | solution.py:415
  60.7 0.1 collective-permute-start.22
  60.8 0.1 add_convert_fusion.7
  60.9 0.7 collective-permute-start.21
  61.6 2.9 %collective-permute-done.22 = bf16[3456,256]{1,0:T(8,128)(2,1)S(1)} collective-permute-done((bf16[3456,256]{1,0:T(8,128)(2,1)S(1)}, bf16[3456,256]{1,0:T(8,128)(2,1)S(1)}, u32[]{:S(2)}, u32[]{:S(2)}) %collective-permute-start.22) | collective-permute-done | bytes 1769504 | tf_op jit(solution)/shard_map/ppermute | solution.py:427
  64.5 0.1 add_convert_fusion.6
  64.6 0.3 collective-permute-start.23
  64.9 2.0 %collective-permute-done.21 = bf16[432,256]{1,0:T(8,128)(2,1)S(1)} collective-permute-done((bf16[432,256]{1,0:T(8,128)(2,1)S(1)}, bf16[432,256]{1,0:T(8,128)(2,1)S(1)}, u32[]{:S(2)}, u32[]{:S(2)}) %collective-permute-start.21) | collective-permute-done | bytes 221216 | tf_op jit(solution)/shard_map/ppermute | solution.py:426
  66.9 0.2 add_convert_fusion.2
  67.1 0.9 collective-permute-start.28
  67.9 2.6 %collective-permute-done.23 = bf16[432,256]{1,0:T(8,128)(2,1)S(1)} collective-permute-done((bf16[432,256]{1,0:T(8,128)(2,1)S(1)}, bf16[432,256]{1,0:T(8,128)(2,1)S(1)}, u32[]{:S(2)}, u32[]{:S(2)}) %collective-permute-start.23) | collective-permute-done | bytes 221216 | tf_op jit(solution)/shard_map/ppermute | solution.py:428
  70.5 0.2 add_convert_fusion.5
  70.7 0.3 collective-permute-start.24
  71.0 4.2 %third.1 = bf16[4,8,16,256]{3,2,1,0:T(8,128)(2,1)} custom-call(bf16[8,10,16,768]{3,2,1,0:T(8,128)(2,1)S(1)} %get-tuple-element.34.sx_ref, bf16[512,256]{1,0:T(8,128)(2,1)S(1)} %get-tuple-element.50.act_ref, bf16[3,128,256]{2,1,0:T(8,128)(2,1)S(1)} %get-tuple-element.36.mask_ref, bf16[864,256]{1,0:T(8,128)(2,1)S(1)} %constant_dynamic-update-slice_fusion.rest_0_, ...), custom_call_target="tpu_custom_call" | custom-call | flops 1811939328 | bytes 8388608 | tf_op jit(solution)/shard_map/third/pallas_call | solution.py:429
  75.3 0.3 collective-permute-done.28
  75.6 0.2 add_convert_fusion.1
  75.8 1.5 %collective-permute-start.29 = (bf16[864,256]{1,0:T(8,128)(2,1)S(1)}, bf16[864,256]{1,0:T(8,128)(2,1)S(1)}, u32[]{:S(2)}, u32[]{:S(2)}) collective-permute-start(bf16[864,256]{1,0:T(8,128)(2,1)S(1)} %add_convert_fusion.1), channel_id=1, source_target_pairs={{0,4},{4,8},{8,12},{12,14},{14,10},{10,6},{6,2},{2,0},{1,3},{5,1},... | collective-permute-start | bytes 1327112 | tf_op jit(solution)/shard_map/ppermute | solution.py:446
  77.2 3.1 %collective-permute-done.24 = bf16[864,256]{1,0:T(8,128)(2,1)S(1)} collective-permute-done((bf16[864,256]{1,0:T(8,128)(2,1)S(1)}, bf16[864,256]{1,0:T(8,128)(2,1)S(1)}, u32[]{:S(2)}, u32[]{:S(2)}) %collective-permute-start.24) | collective-permute-done | bytes 442400 | tf_op jit(solution)/shard_map/ppermute | solution.py:445
  80.3 0.2 add_convert_fusion.4
  80.5 0.7 collective-permute-start.25
  81.2 3.9 %collective-permute-done.29 = bf16[864,256]{1,0:T(8,128)(2,1)S(1)} collective-permute-done((bf16[864,256]{1,0:T(8,128)(2,1)S(1)}, bf16[864,256]{1,0:T(8,128)(2,1)S(1)}, u32[]{:S(2)}, u32[]{:S(2)}) %collective-permute-start.29) | collective-permute-done | bytes 442400 | tf_op jit(solution)/shard_map/ppermute | solution.py:446
  85.1 0.2 add_convert_fusion
  85.3 0.7 collective-permute-start.30
  85.9 3.9 %collective-permute-done.25 = bf16[864,256]{1,0:T(8,128)(2,1)S(1)} collective-permute-done((bf16[864,256]{1,0:T(8,128)(2,1)S(1)}, bf16[864,256]{1,0:T(8,128)(2,1)S(1)}, u32[]{:S(2)}, u32[]{:S(2)}) %collective-permute-start.25) | collective-permute-done | bytes 442400 | tf_op jit(solution)/shard_map/ppermute | solution.py:447
  89.8 0.2 add_convert_fusion.3
  90.0 0.7 collective-permute-start.26
  90.7 3.9 %collective-permute-done.30 = bf16[864,256]{1,0:T(8,128)(2,1)S(1)} collective-permute-done((bf16[864,256]{1,0:T(8,128)(2,1)S(1)}, bf16[864,256]{1,0:T(8,128)(2,1)S(1)}, u32[]{:S(2)}, u32[]{:S(2)}) %collective-permute-start.30) | collective-permute-done | bytes 442400 | tf_op jit(solution)/shard_map/ppermute | solution.py:448
  94.6 0.1 collective-permute-start.31
  94.7 4.6 %collective-permute-done.26 = bf16[864,256]{1,0:T(8,128)(2,1)S(1)} collective-permute-done((bf16[864,256]{1,0:T(8,128)(2,1)S(1)}, bf16[864,256]{1,0:T(8,128)(2,1)S(1)}, u32[]{:S(2)}, u32[]{:S(2)}) %collective-permute-start.26) | collective-permute-done | bytes 442400 | tf_op jit(solution)/shard_map/ppermute | solution.py:449
  99.3 0.1 collective-permute-start.27
  99.4 0.9 add_multiply_fusion
  100.3 0.6 collective-permute-done.27
  100.9 0.9 add_multiply_fusion.1
  (33 shorter events, 0.2 us)
Async XLA Ops:
  0.6 13.2 %copy-start.1 = (bf16[4,8,16,256]{3,2,1,0:T(8,128)(2,1)S(1)}, bf16[4,8,16,256]{3,2,1,0:T(8,128)(2,1)}, u32[]{:S(2)}) copy-start(bf16[4,8,16,256]{3,2,1,0:T(8,128)(2,1)} %c_own.1) | copy-start | bytes 786436
  0.6 7.5 %copy-start = (bf16[4,8,16,256]{3,2,1,0:T(8,128)(2,1)S(1)}, bf16[4,8,16,256]{3,2,1,0:T(8,128)(2,1)}, u32[]{:S(2)}) copy-start(bf16[4,8,16,256]{3,2,1,0:T(8,128)(2,1)} %f_own.1) | copy-start | bytes 786436
  0.7 31.1 %copy-start.2 = (s32[16,2,4]{0,2,1:T(4,128)S(1)}, s32[16,2,4]{0,2,1:T(4,128)}, u32[]{:S(2)}) copy-start(s32[16,2,4]{0,2,1:T(4,128)} %param.9) | copy-start | bytes 1540
  0.7 1.8 %collective-permute-start = (bf16[432,256]{1,0:T(8,128)(2,1)}, bf16[432,256]{1,0:T(8,128)(2,1)S(1)}, u32[]{:S(2)}, u32[]{:S(2)}) collective-permute-start(bf16[432,256]{1,0:T(8,128)(2,1)} %param.6), channel_id=1, source_target_pairs={{0,1},{1,0},{2,3},{3,2},{4,5},{5,4},{6,7},{7,6},{8,9},{9,8},{10,11... | collective-permute-start | bytes 663560 | tf_op jit(solution)/shard_map/ppermute | solution.py:330
  1.2 5.3 %collective-permute-start.1 = (bf16[432,256]{1,0:T(8,128)(2,1)}, bf16[432,256]{1,0:T(8,128)(2,1)S(1)}, u32[]{:S(2)}, u32[]{:S(2)}) collective-permute-start(bf16[432,256]{1,0:T(8,128)(2,1)} %param.7), channel_id=1, source_target_pairs={{0,1},{1,0},{2,3},{3,2},{4,5},{5,4},{6,7},{7,6},{8,9},{9,8},{10,11... | collective-permute-start | bytes 663560 | tf_op jit(solution)/shard_map/ppermute | solution.py:331
  2.5 9.2 %collective-permute-start.10 = (bf16[864,256]{1,0:T(8,128)(2,1)S(1)}, bf16[864,256]{1,0:T(8,128)(2,1)S(1)}, u32[]{:S(2)}, u32[]{:S(2)}) collective-permute-start(bf16[864,256]{1,0:T(8,128)(2,1)S(1)} %constant_dynamic-update-slice_fusion.rest_0_), channel_id=1, source_target_pairs={{0,4},{4,8},{8,12},{12,14},{14,10},{10,6},{6,2},{2,0},{1,3},{5,1},... | collective-permute-start | bytes 1327112 | tf_op jit(solution)/shard_map/ppermute | solution.py:333
  6.5 10.0 %collective-permute-start.4 = (bf16[864,256]{1,0:T(8,128)(2,1)S(1)}, bf16[864,256]{1,0:T(8,128)(2,1)S(1)}, u32[]{:S(2)}, u32[]{:S(2)}) collective-permute-start(bf16[864,256]{1,0:T(8,128)(2,1)S(1)} %constant_dynamic-update-slice_fusion.2.rest_0_.rest_9_), channel_id=1, source_target_pairs={{0,4},{4,8},{8,12},{12,14},{14,10},{10,6},{6,2},{2,0},{1,3},{5,1},... | collective-permute-start | bytes 1327112 | tf_op jit(solution)/shard_map/ppermute | solution.py:333
  11.7 16.6 %collective-permute-start.12 = (bf16[864,256]{1,0:T(8,128)(2,1)S(1)}, bf16[864,256]{1,0:T(8,128)(2,1)S(1)}, u32[]{:S(2)}, u32[]{:S(2)}) collective-permute-start(bf16[864,256]{1,0:T(8,128)(2,1)S(1)} %collective-permute-done.10.rest_1_), channel_id=1, source_target_pairs={{0,1},{1,0},{2,3},{3,2},{4,5},{5,4},{6,7},{7,6},{8,9},{9,8},{10,11... | collective-permute-start | bytes 1327112 | tf_op jit(solution)/shard_map/ppermute | solution.py:369
  11.7 11.0 %collective-permute-start.11 = (bf16[864,256]{1,0:T(8,128)(2,1)S(1)}, bf16[864,256]{1,0:T(8,128)(2,1)S(1)}, u32[]{:S(2)}, u32[]{:S(2)}) collective-permute-start(bf16[864,256]{1,0:T(8,128)(2,1)S(1)} %collective-permute-done.10.rest_1_), channel_id=1, source_target_pairs={{0,4},{4,8},{8,12},{12,14},{14,10},{10,6},{6,2},{2,0},{1,3},{5,1},... | collective-permute-start | bytes 1327112 | tf_op jit(solution)/shard_map/ppermute | solution.py:368
  13.9 11.3 %collective-permute-start.2 = (bf16[3,8,16,256]{3,2,1,0:T(8,128)(2,1)S(1)}, bf16[3,8,16,256]{3,2,1,0:T(8,128)(2,1)S(1)}, u32[]{:S(2)}, u32[]{:S(2)}) collective-permute-start(bf16[3,8,16,256]{3,2,1,0:T(8,128)(2,1)S(1)} %pad_maximum_fusion), channel_id=1, source_target_pairs={{0,1},{1,2},{2,3},{3,4},{4,5},{5,6},{6,7},{7,8},{8,9},{9,10},{10,1... | collective-permute-start | bytes 589832 | tf_op jit(solution)/shard_map/ppermute | solution.py:335
  16.5 13.5 %collective-permute-start.6 = (bf16[864,256]{1,0:T(8,128)(2,1)S(1)}, bf16[864,256]{1,0:T(8,128)(2,1)S(1)}, u32[]{:S(2)}, u32[]{:S(2)}) collective-permute-start(bf16[864,256]{1,0:T(8,128)(2,1)S(1)} %collective-permute-done.4.rest_1_.rest_10_), channel_id=1, source_target_pairs={{0,1},{1,0},{2,3},{3,2},{4,5},{5,4},{6,7},{7,6},{8,9},{9,8},{10,11... | collective-permute-start | bytes 1327112 | tf_op jit(solution)/shard_map/ppermute | solution.py:369
  16.5 13.5 %collective-permute-start.5 = (bf16[864,256]{1,0:T(8,128)(2,1)S(1)}, bf16[864,256]{1,0:T(8,128)(2,1)S(1)}, u32[]{:S(2)}, u32[]{:S(2)}) collective-permute-start(bf16[864,256]{1,0:T(8,128)(2,1)S(1)} %collective-permute-done.4.rest_1_.rest_10_), channel_id=1, source_target_pairs={{0,4},{4,8},{8,12},{12,14},{14,10},{10,6},{6,2},{2,0},{1,3},{5,1},... | collective-permute-start | bytes 1327112 | tf_op jit(solution)/shard_map/ppermute | solution.py:368
  22.8 5.6 %collective-permute-start.3 = (bf16[3,8,16,256]{3,2,1,0:T(8,128)(2,1)S(1)}, bf16[3,8,16,256]{3,2,1,0:T(8,128)(2,1)S(1)}, u32[]{:S(2)}, u32[]{:S(2)}) collective-permute-start(bf16[3,8,16,256]{3,2,1,0:T(8,128)(2,1)S(1)} %pad_maximum_fusion.1), channel_id=1, source_target_pairs={{0,15},{1,0},{2,1},{3,2},{4,3},{5,4},{6,5},{7,6},{8,7},{9,8},{10,9... | collective-permute-start | bytes 589832 | tf_op jit(solution)/shard_map/ppermute | solution.py:336
  28.4 8.3 %collective-permute-start.13 = (bf16[864,256]{1,0:T(8,128)(2,1)S(1)}, bf16[864,256]{1,0:T(8,128)(2,1)S(1)}, u32[]{:S(2)}, u32[]{:S(2)}) collective-permute-start(bf16[864,256]{1,0:T(8,128)(2,1)S(1)} %collective-permute-done.11.rest_2_), channel_id=1, source_target_pairs={{0,4},{4,8},{8,12},{12,14},{14,10},{10,6},{6,2},{2,0},{1,3},{5,1},... | collective-permute-start | bytes 1327112 | tf_op jit(solution)/shard_map/ppermute | solution.py:368
  28.4 8.3 %collective-permute-start.14 = (bf16[864,256]{1,0:T(8,128)(2,1)S(1)}, bf16[864,256]{1,0:T(8,128)(2,1)S(1)}, u32[]{:S(2)}, u32[]{:S(2)}) collective-permute-start(bf16[864,256]{1,0:T(8,128)(2,1)S(1)} %collective-permute-done.11.rest_2_), channel_id=1, source_target_pairs={{0,1},{1,0},{2,3},{3,2},{4,5},{5,4},{6,7},{7,6},{8,9},{9,8},{10,11... | collective-permute-start | bytes 1327112 | tf_op jit(solution)/shard_map/ppermute | solution.py:369
  30.0 11.4 %collective-permute-start.7 = (bf16[864,256]{1,0:T(8,128)(2,1)S(1)}, bf16[864,256]{1,0:T(8,128)(2,1)S(1)}, u32[]{:S(2)}, u32[]{:S(2)}) collective-permute-start(bf16[864,256]{1,0:T(8,128)(2,1)S(1)} %collective-permute-done.5.rest_2_.rest_11_), channel_id=1, source_target_pairs={{0,4},{4,8},{8,12},{12,14},{14,10},{10,6},{6,2},{2,0},{1,3},{5,1},... | collective-permute-start | bytes 1327112 | tf_op jit(solution)/shard_map/ppermute | solution.py:368
  31.7 9.7 %collective-permute-start.8 = (bf16[864,256]{1,0:T(8,128)(2,1)S(1)}, bf16[864,256]{1,0:T(8,128)(2,1)S(1)}, u32[]{:S(2)}, u32[]{:S(2)}) collective-permute-start(bf16[864,256]{1,0:T(8,128)(2,1)S(1)} %collective-permute-done.5.rest_2_.rest_11_), channel_id=1, source_target_pairs={{0,1},{1,0},{2,3},{3,2},{4,5},{5,4},{6,7},{7,6},{8,9},{9,8},{10,11... | collective-permute-start | bytes 1327112 | tf_op jit(solution)/shard_map/ppermute | solution.py:369
  36.7 7.1 %collective-permute-start.15 = (bf16[432,256]{1,0:T(8,128)(2,1)S(1)}, bf16[432,256]{1,0:T(8,128)(2,1)S(1)}, u32[]{:S(2)}, u32[]{:S(2)}) collective-permute-start(bf16[432,256]{1,0:T(8,128)(2,1)S(1)} %slice.121), channel_id=1, source_target_pairs={{0,4},{4,8},{8,12},{12,14},{14,10},{10,6},{6,2},{2,0},{1,3},{5,1},... | collective-permute-start | bytes 663560 | tf_op jit(solution)/shard_map/ppermute | solution.py:368
  36.8 10.7 %collective-permute-start.16 = (bf16[864,256]{1,0:T(8,128)(2,1)S(1)}, bf16[864,256]{1,0:T(8,128)(2,1)S(1)}, u32[]{:S(2)}, u32[]{:S(2)}) collective-permute-start(bf16[864,256]{1,0:T(8,128)(2,1)S(1)} %collective-permute-done.13.rest_3_), channel_id=1, source_target_pairs={{0,1},{1,0},{2,3},{3,2},{4,5},{5,4},{6,7},{7,6},{8,9},{9,8},{10,11... | collective-permute-start | bytes 1327112 | tf_op jit(solution)/shard_map/ppermute | solution.py:369
  41.4 6.0 %collective-permute-start.9 = (bf16[432,256]{1,0:T(8,128)(2,1)S(1)}, bf16[432,256]{1,0:T(8,128)(2,1)S(1)}, u32[]{:S(2)}, u32[]{:S(2)}) collective-permute-start(bf16[432,256]{1,0:T(8,128)(2,1)S(1)} %slice.120), channel_id=1, source_target_pairs={{0,4},{4,8},{8,12},{12,14},{14,10},{10,6},{6,2},{2,0},{1,3},{5,1},... | collective-permute-start | bytes 663560 | tf_op jit(solution)/shard_map/ppermute | solution.py:368
  43.8 3.7 %collective-permute-start.17 = (bf16[432,256]{1,0:T(8,128)(2,1)S(1)}, bf16[432,256]{1,0:T(8,128)(2,1)S(1)}, u32[]{:S(2)}, u32[]{:S(2)}) collective-permute-start(bf16[432,256]{1,0:T(8,128)(2,1)S(1)} %collective-permute-done.15.rest_4_), channel_id=1, source_target_pairs={{0,1},{1,0},{2,3},{3,2},{4,5},{5,4},{6,7},{7,6},{8,9},{9,8},{10,11... | collective-permute-start | bytes 663560 | tf_op jit(solution)/shard_map/ppermute | solution.py:371
  44.3 11.8 %collective-permute-start.19 = (bf16[864,256]{1,0:T(8,128)(2,1)S(1)}, bf16[864,256]{1,0:T(8,128)(2,1)S(1)}, u32[]{:S(2)}, u32[]{:S(2)}) collective-permute-start(bf16[864,256]{1,0:T(8,128)(2,1)S(1)} %collective-permute-done.7.rest_3_.rest_12_), channel_id=1, source_target_pairs={{0,1},{1,0},{2,3},{3,2},{4,5},{5,4},{6,7},{7,6},{8,9},{9,8},{10,11... | collective-permute-start | bytes 1327112 | tf_op jit(solution)/shard_map/ppermute | solution.py:369
  47.4 8.7 %collective-permute-start.20 = (bf16[432,256]{1,0:T(8,128)(2,1)S(1)}, bf16[432,256]{1,0:T(8,128)(2,1)S(1)}, u32[]{:S(2)}, u32[]{:S(2)}) collective-permute-start(bf16[432,256]{1,0:T(8,128)(2,1)S(1)} %collective-permute-done.9.rest_4_.rest_13_), channel_id=1, source_target_pairs={{0,1},{1,0},{2,3},{3,2},{4,5},{5,4},{6,7},{7,6},{8,9},{9,8},{10,11... | collective-permute-start | bytes 663560 | tf_op jit(solution)/shard_map/ppermute | solution.py:371
  55.5 5.3 %collective-permute-start.18 = (bf16[3456,256]{1,0:T(8,128)(2,1)S(1)}, bf16[3456,256]{1,0:T(8,128)(2,1)S(1)}, u32[]{:S(2)}, u32[]{:S(2)}) collective-permute-start(bf16[3456,256]{1,0:T(8,128)(2,1)S(1)} %get-tuple-element.45), channel_id=1, source_target_pairs={{0,1},{1,0},{2,3},{3,2},{4,5},{5,4},{6,7},{7,6},{8,9},{9,8},{10,11... | collective-permute-start | bytes 5308424 | tf_op jit(solution)/shard_map/ppermute | solution.py:388
  60.7 3.8 %collective-permute-start.22 = (bf16[3456,256]{1,0:T(8,128)(2,1)S(1)}, bf16[3456,256]{1,0:T(8,128)(2,1)S(1)}, u32[]{:S(2)}, u32[]{:S(2)}) collective-permute-start(bf16[3456,256]{1,0:T(8,128)(2,1)S(1)} %get-tuple-element.51), channel_id=1, source_target_pairs={{0,1},{1,0},{2,3},{3,2},{4,5},{5,4},{6,7},{7,6},{8,9},{9,8},{10,11... | collective-permute-start | bytes 5308424 | tf_op jit(solution)/shard_map/ppermute | solution.py:427
  60.9 6.0 %collective-permute-start.21 = (bf16[432,256]{1,0:T(8,128)(2,1)S(1)}, bf16[432,256]{1,0:T(8,128)(2,1)S(1)}, u32[]{:S(2)}, u32[]{:S(2)}) collective-permute-start(bf16[432,256]{1,0:T(8,128)(2,1)S(1)} %add_convert_fusion.7), channel_id=1, source_target_pairs={{0,4},{4,8},{8,12},{12,14},{14,10},{10,6},{6,2},{2,0},{1,3},{5,1},... | collective-permute-start | bytes 663560 | tf_op jit(solution)/shard_map/ppermute | solution.py:426
  64.6 6.0 %collective-permute-start.23 = (bf16[432,256]{1,0:T(8,128)(2,1)S(1)}, bf16[432,256]{1,0:T(8,128)(2,1)S(1)}, u32[]{:S(2)}, u32[]{:S(2)}) collective-permute-start(bf16[432,256]{1,0:T(8,128)(2,1)S(1)} %add_convert_fusion.6), channel_id=1, source_target_pairs={{0,4},{4,8},{8,12},{12,14},{14,10},{10,6},{6,2},{2,0},{1,3},{5,1},... | collective-permute-start | bytes 663560 | tf_op jit(solution)/shard_map/ppermute | solution.py:428
  67.1 8.5 %collective-permute-start.28 = (bf16[864,256]{1,0:T(8,128)(2,1)S(1)}, bf16[864,256]{1,0:T(8,128)(2,1)S(1)}, u32[]{:S(2)}, u32[]{:S(2)}) collective-permute-start(bf16[864,256]{1,0:T(8,128)(2,1)S(1)} %add_convert_fusion.2), channel_id=1, source_target_pairs={{0,4},{4,8},{8,12},{12,14},{14,10},{10,6},{6,2},{2,0},{1,3},{5,1},... | collective-permute-start | bytes 1327112 | tf_op jit(solution)/shard_map/ppermute | solution.py:444
  70.7 9.6 %collective-permute-start.24 = (bf16[864,256]{1,0:T(8,128)(2,1)S(1)}, bf16[864,256]{1,0:T(8,128)(2,1)S(1)}, u32[]{:S(2)}, u32[]{:S(2)}) collective-permute-start(bf16[864,256]{1,0:T(8,128)(2,1)S(1)} %add_convert_fusion.5), channel_id=1, source_target_pairs={{0,4},{4,8},{8,12},{12,14},{14,10},{10,6},{6,2},{2,0},{1,3},{5,1},... | collective-permute-start | bytes 1327112 | tf_op jit(solution)/shard_map/ppermute | solution.py:445
  75.8 9.3 %collective-permute-start.29 = (bf16[864,256]{1,0:T(8,128)(2,1)S(1)}, bf16[864,256]{1,0:T(8,128)(2,1)S(1)}, u32[]{:S(2)}, u32[]{:S(2)}) collective-permute-start(bf16[864,256]{1,0:T(8,128)(2,1)S(1)} %add_convert_fusion.1), channel_id=1, source_target_pairs={{0,4},{4,8},{8,12},{12,14},{14,10},{10,6},{6,2},{2,0},{1,3},{5,1},... | collective-permute-start | bytes 1327112 | tf_op jit(solution)/shard_map/ppermute | solution.py:446
  80.5 9.3 %collective-permute-start.25 = (bf16[864,256]{1,0:T(8,128)(2,1)S(1)}, bf16[864,256]{1,0:T(8,128)(2,1)S(1)}, u32[]{:S(2)}, u32[]{:S(2)}) collective-permute-start(bf16[864,256]{1,0:T(8,128)(2,1)S(1)} %add_convert_fusion.4), channel_id=1, source_target_pairs={{0,4},{4,8},{8,12},{12,14},{14,10},{10,6},{6,2},{2,0},{1,3},{5,1},... | collective-permute-start | bytes 1327112 | tf_op jit(solution)/shard_map/ppermute | solution.py:447
  85.3 9.3 %collective-permute-start.30 = (bf16[864,256]{1,0:T(8,128)(2,1)S(1)}, bf16[864,256]{1,0:T(8,128)(2,1)S(1)}, u32[]{:S(2)}, u32[]{:S(2)}) collective-permute-start(bf16[864,256]{1,0:T(8,128)(2,1)S(1)} %add_convert_fusion), channel_id=1, source_target_pairs={{0,4},{4,8},{8,12},{12,14},{14,10},{10,6},{6,2},{2,0},{1,3},{5,1},... | collective-permute-start | bytes 1327112 | tf_op jit(solution)/shard_map/ppermute | solution.py:448
  90.0 9.3 %collective-permute-start.26 = (bf16[864,256]{1,0:T(8,128)(2,1)S(1)}, bf16[864,256]{1,0:T(8,128)(2,1)S(1)}, u32[]{:S(2)}, u32[]{:S(2)}) collective-permute-start(bf16[864,256]{1,0:T(8,128)(2,1)S(1)} %add_convert_fusion.3), channel_id=1, source_target_pairs={{0,4},{4,8},{8,12},{12,14},{14,10},{10,6},{6,2},{2,0},{1,3},{5,1},... | collective-permute-start | bytes 1327112 | tf_op jit(solution)/shard_map/ppermute | solution.py:449
  94.6 4.8 %collective-permute-start.31 = (bf16[432,256]{1,0:T(8,128)(2,1)S(1)}, bf16[432,256]{1,0:T(8,128)(2,1)S(1)}, u32[]{:S(2)}, u32[]{:S(2)}) collective-permute-start(bf16[432,256]{1,0:T(8,128)(2,1)S(1)} %slice.134), channel_id=1, source_target_pairs={{0,1},{1,0},{2,3},{3,2},{4,5},{5,4},{6,7},{7,6},{8,9},{9,8},{10,11... | collective-permute-start | bytes 663560 | tf_op jit(solution)/shard_map/ppermute | solution.py:401
  99.3 1.5 %collective-permute-start.27 = (bf16[432,256]{1,0:T(8,128)(2,1)S(1)}, bf16[432,256]{1,0:T(8,128)(2,1)S(1)}, u32[]{:S(2)}, u32[]{:S(2)}) collective-permute-start(bf16[432,256]{1,0:T(8,128)(2,1)S(1)} %slice.128), channel_id=1, source_target_pairs={{0,1},{1,0},{2,3},{3,2},{4,5},{5,4},{6,7},{7,6},{8,9},{9,8},{10,11... | collective-permute-start | bytes 663560 | tf_op jit(solution)/shard_map/ppermute | solution.py:401

commit v3 on v2

--- a/solution.py
+++ b/solution.py
@@ -162,14 +162,29 @@
         store_shifted(sc_ref, x0, rows(value, side), ny, nz, channels)
 
 
+PIECES = (
+    (0, False, False),
+    (0, False, True),
+    (1, False, False),
+    (1, False, True),
+    (2, False, False),
+    (3, False, False),
+    (4, False, False),
+    (1, True, False),
+    (2, True, False),
+    (3, True, False),
+    (4, True, False),
+)
+
+
 def fill_weight(pieces, w_ref):
     tile = lax.axis_index("tiles")
     core = tile % 2
     rows = w_ref.shape[0] // 16
-    for k, piece in enumerate(pieces):
-        hop, holder = (k, core) if k < 5 else (k - 4, 1 - core)
+    for piece, (hop, crossed, flip) in zip(pieces, PIECES):
+        holder = 1 - core if crossed else core
         for half in range(piece.shape[0] // rows):
-            start = shard_rows(tile, holder, hop, half == 1, rows)
+            start = shard_rows(tile, holder, hop, flip or half == 1, rows)
             w_ref[pl.ds(start, rows)] = piece[half * rows : (half + 1) * rows]
 
 
@@ -217,8 +232,8 @@
     return (value.reshape(-1, area, channels) * own).reshape(-1, channels)
 
 
-def first_kernel(n, sx_ref, sc_ref, mask_ref, *rest):
-    pieces, (pre_ref, act_ref, keep_ref, send_ref, w_ref, g_ref) = rest[:n], rest[n:]
+def first_kernel(n, sx_ref, mask_ref, *rest):
+    pieces, (pre_ref, act_ref, act_t_ref, w_ref) = rest[:n], rest[n:]
     area, channels = mask_ref.shape[1:]
     ny = sx_ref.shape[1] - 2
     depth = pre_ref.shape[0] // area
@@ -227,11 +242,18 @@
     pre_ref[...] = pre
     act = masked(pre * jax.nn.sigmoid(pre), mask_ref, 1).astype(BF)
     act_ref[...] = act
-    act_t = act.T
+    act_t_ref[...] = act.T
+
+
+def grad_two_kernel(sc_ref, act_t_ref, keep_ref, send_ref, g_ref):
+    depth, ny, nz, channels = sc_ref.shape
+    depth, ny, channels = depth - 2, ny - 2, channels // 3
     for p in range(3):
         for q in range(3):
             part = jnp.dot(
-                act_t, window(sc_ref, 2 - p, 2 - q, depth, ny), preferred_element_type=F32
+                act_t_ref[...],
+                window(sc_ref, 2 - p, 2 - q, depth, ny),
+                preferred_element_type=F32,
             )
             store_taps(g_ref, p, q, part.astype(BF), channels)
     split_shards(g_ref, keep_ref, send_ref)
@@ -261,7 +283,7 @@
     store_shifted(sd_ref, 0, delta, ny, nz, channels)
 
 
-def grad_kernel(sd_ref, int_ref, keep_ref, send_ref, g_ref):
+def grad_one_kernel(sd_ref, int_ref, keep_ref, send_ref, g_ref):
     depth, ny, nz, channels = sd_ref.shape
     ny, area, channels = ny - 2, (ny - 2) * nz, channels // 3
     for q in range(3):
@@ -298,14 +320,25 @@
     chips = len(RING)
     tiles = 2 * chips
     loss_scale = 1.0 / math.sqrt(tiles * depth * area)
+    shape = jax.ShapeDtypeStruct
+    scratch = pltpu.VMEM
+    shards = (shape((chips * rows, channels), BF),) * 2
+    weights = scratch((27 * channels, channels), BF)
+    flops = 2 * depth * area * 27 * channels * channels
 
     def permute(pairs):
         return functools.partial(lax.ppermute, axis_name="tiles", perm=pairs)
 
-    onward = permute(
-        [(2 * RING[i], 2 * RING[(i + 1) % chips]) for i in range(chips)]
-        + [(2 * RING[i] + 1, 2 * RING[i - 1] + 1) for i in range(chips)]
-    )
+    def along_ring(core_from, core_to):
+        return permute(
+            [(2 * RING[i] + core_from, 2 * RING[(i + 1) % chips] + core_to) for i in range(chips)]
+            + [
+                (2 * RING[i] + 1 - core_from, 2 * RING[i - 1] + 1 - core_to)
+                for i in range(chips)
+            ]
+        )
+
+    onward, gather_across, scatter_across = along_ring(0, 0), along_ring(1, 0), along_ring(0, 1)
     sibling = permute([(i, i ^ 1) for i in range(tiles)])
     up = permute([(i, (i + 1) % tiles) for i in range(tiles)])
     down = permute([(i, (i - 1) % tiles) for i in range(tiles)])
@@ -313,79 +346,86 @@
     def after(value, *others):
         return lax.optimization_barrier((value,) + others)[0]
 
-    smem = pl.BlockSpec(memory_space=pltpu.SMEM)
-    vmem = pl.BlockSpec(memory_space=pltpu.VMEM)
-
-    def params(mib):
-        return pltpu.CompilerParams(vmem_limit_bytes=mib << 20)
-
-    shape = jax.ShapeDtypeStruct
-    flops = 2 * depth * area * 27 * channels * channels
-
-    def cost(convs):
-        return pl.CostEstimate(
-            flops=convs * flops, transcendentals=0, bytes_accessed=8 << 20
-        )
-
-    pair_one = jnp.concatenate([weight_one, sibling(weight_one)])
-    pair_two = jnp.concatenate([after(weight_two, pair_one), sibling(weight_two)])
-    pairs = [pair_one, pair_two]
-    rings = [[pair, onward(pair)] for pair in pairs]
-    features_late, cot_late, _ = lax.optimization_barrier((features, cotangent, pairs[1]))
+    def kernel(body, name, mib, convs, outs, scratches, *operands, smem=0):
+        return pl.pallas_call(
+            body,
+            name=name,
+            out_shape=outs,
+            in_specs=[pl.BlockSpec(memory_space=pltpu.SMEM)] * smem
+            + [pl.BlockSpec(memory_space=pltpu.VMEM)] * (len(operands) - smem),
+            out_specs=jax.tree.map(lambda _: pl.BlockSpec(memory_space=pltpu.VMEM), outs),
+            scratch_shapes=scratches,
+            compiler_params=pltpu.CompilerParams(vmem_limit_bytes=mib << 20),
+            cost_estimate=pl.CostEstimate(
+                flops=4 * convs * flops, transcendentals=0, bytes_accessed=4 << 20
+            ),
+        )(*operands)
+
+    a1 = [onward(weight_one), gather_across(weight_one)]
+    weight_late = after(weight_two, weight_one)
+    b1 = [onward(weight_late), gather_across(weight_late)]
+    features_late, cot_late, _ = lax.optimization_barrier((features, cotangent, a1[0]))
     low = up(jnp.concatenate([features_late[-2:], cot_late[-1:]]))
     high = down(jnp.concatenate([features_late[:2], cot_late[:1]]))
 
-    prep = pl.pallas_call(
+    a1_pair = jnp.concatenate(a1)
+    a2 = onward(a1_pair)
+    qa1 = sibling(a1_pair)
+    b1_pair = jnp.concatenate(b1)
+    b2 = onward(after(b1_pair, low, high))
+    a3 = onward(after(a2, qa1, b1_pair))
+    qa2 = sibling(a2)
+    other_one = sibling(weight_one)
+    sx, sc, in_t, near = kernel(
         prep_kernel,
-        name="prep",
-        out_shape=(
+        "prep",
+        8,
+        0,
+        (
             shape((depth + 4, ny + 2, nz, 3 * channels), BF),
             shape((depth + 2, ny + 2, nz, 3 * channels), BF),
             shape((channels, (depth + 2) * area), BF),
             shape((3, area, channels), BF),
         ),
-        in_specs=[smem] + [vmem] * 4,
-        out_specs=(vmem,) * 4,
-        compiler_params=params(8),
-    )
-    crossed = [[], []]
-    for hop in (1, 2, 3):
-        for k in range(2):
-            here = rings[k][hop]
-            if hop == 3:
-                here = here[:rows]
-            if k == 0 and hop > 1:
-                here = after(here, rings[1][hop - 1])
-            if k == 0 and hop == 2:
-                here = after(here, low, high)
-                sx, sc, in_t, near = prep(
-                    jnp.transpose(block_mask, (1, 2, 0)), low, features, cotangent, high
-                )
-            if k == 0 and hop == 3:
-                here = after(here, sx)
-            if hop > 1:
-                here = after(here, crossed[k][hop - 2])
-            rings[k].append(onward(here))
-            crossed[k].append(sibling(rings[k][hop]))
-    for k in range(2):
-        crossed[k].append(sibling(rings[k][4]))
-    ones, twos = (rings[k] + crossed[k] for k in range(2))
+        [],
+        jnp.transpose(block_mask, (1, 2, 0)),
+        low,
+        features,
+        cotangent,
+        high,
+        smem=1,
+    )
+    a4 = onward(after(a3[:rows], qa2, other_one, sx))
+    qa3, qa4 = sibling(a3), sibling(a4)
+    ones = [weight_one, other_one, *a1, a2, a3, a4, qa1, qa2, qa3, qa4]
     n = len(ones)
 
-    shards = (shape((chips * rows, channels), BF),) * 2
-    weights = pltpu.VMEM((27 * channels, channels), BF)
-    pre, act, keep_two, send_two = pl.pallas_call(
+    qb1 = sibling(b1_pair)
+    b3 = onward(after(b2, qb1))
+    qb2 = sibling(b2)
+    other_two = sibling(weight_two)
+    pre, act, act_t = kernel(
         functools.partial(first_kernel, n),
-        name="first",
-        out_shape=(shape((depth * area, channels), F32), shape((depth * area, channels), BF))
-        + shards,
-        in_specs=[vmem] * (3 + n),
-        out_specs=(vmem,) * 4,
-        scratch_shapes=[weights, weights],
-        compiler_params=params(12),
-        cost_estimate=cost(2),
-    )(after(sx, rings[1][4]), sc, near, *ones)
-    got_two = sibling(send_two)
+        "first",
+        8,
+        1,
+        (
+            shape((depth * area, channels), F32),
+            shape((depth * area, channels), BF),
+            shape((channels, depth * area), BF),
+        ),
+        [weights],
+        after(sx, b2),
+        near,
+        *ones,
+    )
+    b4 = onward(after(b3[:rows], qb2, other_two))
+    qb3, qb4 = sibling(b3), sibling(b4)
+    twos = [weight_two, other_two, *b1, b2, b3, b4, qb1, qb2, qb3, qb4]
+    keep_two, send_two = kernel(
+        grad_two_kernel, "grad_two", 8, 1, shards, [weights], sc, after(act_t, b3)
+    )
+    got_two = sibling(after(send_two, b4))
 
     def both(keep, got, lo, hi):
         return keep[lo * rows : hi * rows].astype(F32) + got[lo * rows : hi * rows].astype(F32)
@@ -397,58 +437,48 @@
             moving = jnp.concatenate([moving, jnp.zeros_like(moving)])
         return (both(keep, got, 2 * k - 1, 2 * k + 1) + moving.astype(F32)).astype(BF)
 
-    def finish(keep, got, moving):
-        across = sibling(moving[rows:])
-        total = both(keep, got, 7, 8) + moving[:rows].astype(F32) + across.astype(F32)
-        return total * loss_scale
-
-    delta = pl.pallas_call(
+    def finish(keep, got, message):
+        total = both(keep, got, 7, 8) + onward(message[:rows]).astype(F32)
+        return (total + scatter_across(message[rows:]).astype(F32)) * loss_scale
+
+    two = onward(step(keep_two, got_two, None, 0))
+    delta = kernel(
         functools.partial(back_kernel, n),
-        name="back",
-        out_shape=shape((depth, ny + 2, nz, 3 * channels), BF),
-        in_specs=[vmem] * (3 + n),
-        out_specs=vmem,
-        scratch_shapes=[weights],
-        compiler_params=params(8),
-        cost_estimate=cost(1),
-    )(sc, pre, near, *twos)
-    keep_one, send_one = pl.pallas_call(
-        grad_kernel,
-        name="grad",
-        out_shape=shards,
-        in_specs=[vmem] * 2,
-        out_specs=(vmem,) * 2,
-        scratch_shapes=[weights],
-        compiler_params=params(8),
-        cost_estimate=cost(1),
-    )(delta, in_t)
-    got_two_late = after(got_two, keep_one)
-    two = onward(step(keep_two, got_two_late, None, 0))
-    got_one = sibling(send_one)
+        "back",
+        8,
+        1,
+        shape((depth, ny + 2, nz, 3 * channels), BF),
+        [weights],
+        sc,
+        pre,
+        near,
+        *twos,
+    )
+    keep_one, send_one = kernel(
+        grad_one_kernel, "grad_one", 8, 1, shards, [weights], delta, in_t
+    )
+    got_one = sibling(after(send_one, two))
+    act_late = after(act, two)
+    two = onward(step(keep_two, got_two, two, 1))
     one = onward(step(keep_one, got_one, None, 0))
-    features_out = pl.pallas_call(
+    features_out = kernel(
         functools.partial(third_kernel, n),
-        name="third",
-        out_shape=shape(features.shape, BF),
-        in_specs=[vmem] * (3 + 2 * n),
-        out_specs=vmem,
-        scratch_shapes=[
-            weights,
-            weights,
-            pltpu.VMEM((depth + 2, ny + 2, nz, 3 * channels), BF),
-        ],
-        compiler_params=params(14),
-        cost_estimate=cost(1),
-    )(sx, after(act, two), near, *ones, *twos)
-
-    two = onward(step(keep_two, got_two, two, 1))
-    one = onward(step(keep_one, got_one, one, 1))
-    two = onward(step(keep_two, got_two, after(two, features_out), 2))
+        "third",
+        14,
+        1,
+        shape(features.shape, BF),
+        [weights, weights, scratch((depth + 2, ny + 2, nz, 3 * channels), BF)],
+        sx,
+        act_late,
+        near,
+        *ones,
+        *twos,
+    )
+    one = onward(after(step(keep_one, got_one, one, 1), features_out, two))
+    two = onward(step(keep_two, got_two, two, 2))
+    grad_two = finish(keep_two, got_two, step(keep_two, got_two, two, 3))
     one = onward(step(keep_one, got_one, one, 2))
-    two = onward(step(keep_two, got_two, two, 3))
-    one = onward(step(keep_one, got_one, one, 3))
-    grad_two = finish(keep_two, got_two, two)
-    return (features_out, finish(keep_one, got_one, one), grad_two)
+    return (features_out, finish(keep_one, got_one, step(keep_one, got_one, one, 3)), grad_two)
 
 
 def solution(mesh):

time: 102 us -> 103 us (level)
  waiting for transfers between devices: 54.2 us -> 61.9 us
  starting transfers between devices: 23.4 us -> 19.8 us
  Pallas kernels: 18.3 us -> 14.8 us
    ppermute x27 -> x29, waiting for transfers between devices: 44.2 us -> 50.7 us  [the longest x1 7.4 us: on_ring(): one = onward(after(step(keep_one, got_one, one, 1), features_out, two))]
    ppermute x27 -> x29, starting transfers between devices: 18.9 us -> 13.4 us  [the longest x2 3.75 us: on_ring(): a1 = [onward(weight_one), gather_across(weight_one)]]
    ppermute x1, waiting for transfers between devices: 0.01 us -> 5.05 us  [on_ring(): low = up(jnp.concatenate([features_late[-2:], cot_late[-1:]]))]
    pallas_call x5 -> x6, Pallas kernels: 18.3 us -> 14.8 us  [kernel(): pl.pallas_call(body, name=name, out_shape=outs, in_specs=[pl.BlockSpec(me...]
    ppermute x1, waiting for transfers between devices: 3.19 us -> 0.01 us  [on_ring(): high = down(jnp.concatenate([features_late[:2], cot_late[:1]]))]
    ppermute x1, starting transfers between devices: 2.4 us -> 4.48 us  [on_ring(): high = down(jnp.concatenate([features_late[:2], cot_late[:1]]))]
    slice x2, local copies, waits for them, and re-layouts: 0.03 us -> 1.91 us  [on_ring(): high = down(jnp.concatenate([features_late[:2], cot_late[:1]]))]
    unnamed x8 -> x12, local copies, waits for them, and re-layouts: 1.91 us -> 0.06 us
  transfers between devices with their start and end apart: 32 -> 34, of which waited for: 19 -> 18; matrix products, arithmetic and copies ran while one was open for 4% -> 4% of each run, Pallas kernels for 18% -> 14%
where the time goes in v3:
time: 103 us; the launch traced here: 102 us
  waiting for transfers between devices  61.9 us (60%)
  starting transfers between devices  19.8 us (19%)
  Pallas kernels  14.8 us (14%)
  other arithmetic  2.91 us (3%)
  local copies, waits for them, and re-layouts  2.09 us (2%)
    pallas_call x6, Pallas kernels, kernel(): pl.pallas_call(body, name=name, out_shape=outs, in_specs=[pl.BlockSpec(me...  14.8 us
    ppermute x1, waiting for transfers between devices, on_ring(): one = onward(after(step(keep_one, got_one, one, 1), features_out, two))  7.4 us
    ppermute x1, waiting for transfers between devices, on_ring(): a4 = onward(after(a3[:rows], qa2, other_one, sx))  6.42 us
    ppermute x1, waiting for transfers between devices, on_ring(): b2 = onward(after(b1_pair, low, high))  6.21 us
    ppermute x1, waiting for transfers between devices, on_ring(): low = up(jnp.concatenate([features_late[-2:], cot_late[-1:]]))  5.05 us
    ppermute x1, waiting for transfers between devices, on_ring(): a3 = onward(after(a2, qa1, b1_pair))  4.73 us
    ppermute x1, starting transfers between devices, on_ring(): high = down(jnp.concatenate([features_late[:2], cot_late[:1]]))  4.48 us
    ppermute x2, waiting for transfers between devices, finish(): total = both(keep, got, 7, 8) + onward(message[:rows]).astype(F32)  4.4 us
  transfers between devices with their start and end apart: 34, of which 18 were waited for; matrix products, arithmetic and copies ran while one was open for 4% of the time, Pallas kernels for 14%

profile of v3, /device:TPU:0, one launch (start us, length us, event | category | flops | bytes accessed | tf_op | source)
XLA Modules:
  0.0 102.5 jit_solution(7100876300016078924)
XLA Ops:
  0.7 0.0 copy-start
  0.7 3.1 %collective-permute-start = (bf16[432,256]{1,0:T(8,128)(2,1)}, bf16[432,256]{1,0:T(8,128)(2,1)S(1)}, u32[]{:S(2)}, u32[]{:S(2)}) collective-permute-start(bf16[432,256]{1,0:T(8,128)(2,1)} %rest_0_.4), channel_id=1, source_target_pairs={{0,4},{4,8},{8,12},{12,14},{14,10},{10,6},{6,2},{2,0},{1,3},{5,1},... | collective-permute-start | bytes 663560 | tf_op jit(solution)/shard_map/ppermute | solution.py:364
  3.8 0.7 collective-permute-start.7
  4.4 1.1 %collective-permute-start.4 = (bf16[432,256]{1,0:T(8,128)(2,1)}, bf16[432,256]{1,0:T(8,128)(2,1)S(1)}, u32[]{:S(2)}, u32[]{:S(2)}) collective-permute-start(bf16[432,256]{1,0:T(8,128)(2,1)} %rest_0_.5), channel_id=1, source_target_pairs={{1,4},{5,8},{9,12},{13,14},{15,10},{11,6},{7,2},{3,0},{0,3},{4,1},... | collective-permute-start | bytes 663560 | tf_op jit(solution)/shard_map/ppermute | solution.py:366
  5.5 1.6 %collective-permute-start.3 = (bf16[432,256]{1,0:T(8,128)(2,1)}, bf16[432,256]{1,0:T(8,128)(2,1)S(1)}, u32[]{:S(2)}, u32[]{:S(2)}) collective-permute-start(bf16[432,256]{1,0:T(8,128)(2,1)} %rest_0_.5), channel_id=1, source_target_pairs={{0,4},{4,8},{8,12},{12,14},{14,10},{10,6},{6,2},{2,0},{1,3},{5,1},... | collective-permute-start | bytes 663560 | tf_op jit(solution)/shard_map/ppermute | solution.py:366
  7.1 1.8 %collective-permute-done.rest_2_ = bf16[432,256]{1,0:T(8,128)(2,1)S(1)} collective-permute-done((bf16[432,256]{1,0:T(8,128)(2,1)}, bf16[432,256]{1,0:T(8,128)(2,1)S(1)}, u32[]{:S(2)}, u32[]{:S(2)}) %collective-permute-start) | collective-permute-done | bytes 221216 | tf_op jit(solution)/shard_map/ppermute | solution.py:364
  8.9 2.1 %collective-permute-done.7.rest_3_ = bf16[432,256]{1,0:T(8,128)(2,1)S(1)} collective-permute-done((bf16[432,256]{1,0:T(8,128)(2,1)}, bf16[432,256]{1,0:T(8,128)(2,1)S(1)}, u32[]{:S(2)}, u32[]{:S(2)}) %collective-permute-start.7) | collective-permute-done | bytes 221216 | tf_op jit(solution)/shard_map/ppermute | solution.py:364
  11.1 0.1 collective-permute-start.9
  11.1 2.3 %collective-permute-start.8 = (bf16[864,256]{1,0:T(8,128)(2,1)S(1)}, bf16[864,256]{1,0:T(8,128)(2,1)S(1)}, u32[]{:S(2)}, u32[]{:S(2)}) collective-permute-start(bf16[864,256]{1,0:T(8,128)(2,1)S(1)} %constant_dynamic-update-slice_fusion.2), channel_id=1, source_target_pairs={{0,4},{4,8},{8,12},{12,14},{14,10},{10,6},{6,2},{2,0},{1,3},{5,1},... | collective-permute-start | bytes 1327112 | tf_op jit(solution)/shard_map/ppermute | solution.py:372
  13.4 0.9 fusion.3
  14.3 1.0 %fusion.2 = (bf16[2,8,16,256]{3,2,1,0:T(8,128)(2,1)S(1)}, bf16[2,8,16,256]{3,2,1,0:T(8,128)(2,1)S(1)}) fusion(bf16[4,8,16,256]{3,2,1,0:T(8,128)(2,1)} %f_own.1), kind=kLoop, calls=%fused_computation.18 | loop fusion | bytes 524288 | tf_op jit(solution)/shard_map/slice | solution.py:369
  15.4 0.1 collective-permute-start.1
  15.5 4.5 %collective-permute-start.2 = (bf16[3,8,16,256]{3,2,1,0:T(8,128)(2,1)S(1)}, bf16[3,8,16,256]{3,2,1,0:T(8,128)(2,1)S(1)}, u32[]{:S(2)}, u32[]{:S(2)}) collective-permute-start(bf16[3,8,16,256]{3,2,1,0:T(8,128)(2,1)S(1)} %pad_maximum_fusion.1), channel_id=1, source_target_pairs={{0,15},{1,0},{2,1},{3,2},{4,3},{5,4},{6,5},{7,6},{8,7},{9,8},{10,9... | collective-permute-start | bytes 589832 | tf_op jit(solution)/shard_map/ppermute | solution.py:369
  20.0 0.1 collective-permute-start.15
  20.1 5.0 %collective-permute-done.1.low = bf16[3,8,16,256]{3,2,1,0:T(8,128)(2,1)S(1)} collective-permute-done((bf16[3,8,16,256]{3,2,1,0:T(8,128)(2,1)S(1)}, bf16[3,8,16,256]{3,2,1,0:T(8,128)(2,1)S(1)}, u32[]{:S(2)}, u32[]{:S(2)}) %collective-permute-start.1) | collective-permute-done | bytes 196640 | tf_op jit(solution)/shard_map/ppermute | solution.py:368
  25.2 0.2 collective-permute-start.10
  25.4 0.2 collective-permute-start.11
  25.6 0.3 collective-permute-start.6
  25.9 1.3 %prep.1 = (bf16[8,10,16,768]{3,2,1,0:T(8,128)(2,1)S(1)}, bf16[6,10,16,768]{3,2,1,0:T(8,128)(2,1)S(1)}, bf16[256,768]{1,0:T(8,128)(2,1)S(1)}, bf16[3,128,256]{2,1,0:T(8,128)(2,1)S(1)}) custom-call(s32[2,4,16]{2,1,0:T(4,128)S(1)} %bitcast.1, bf16[3,8,16,256]{3,2,1,0:T(8,128)(2,1)S(1)} %collective-permute-done.1.low, bf16[4,8,16,256]{3,2,1,0:T(8,128)(2,1)S(1)} %copy-done, ...), custom_call_target="tpu_custom_call" | custom-call | bytes 4194304 | tf_op jit(solution)/shard_map/prep/pallas_call | solution.py:350
  27.2 6.2 %collective-permute-done.5.rest_15_.rest_4_ = bf16[864,256]{1,0:T(8,128)(2,1)S(1)} collective-permute-done((bf16[864,256]{1,0:T(8,128)(2,1)S(1)}, bf16[864,256]{1,0:T(8,128)(2,1)S(1)}, u32[]{:S(2)}, u32[]{:S(2)}) %collective-permute-start.5) | collective-permute-done | bytes 442400 | tf_op jit(solution)/shard_map/ppermute | solution.py:375
  33.4 4.7 %collective-permute-done.10.rest_5_ = bf16[864,256]{1,0:T(8,128)(2,1)S(1)} collective-permute-done((bf16[864,256]{1,0:T(8,128)(2,1)S(1)}, bf16[864,256]{1,0:T(8,128)(2,1)S(1)}, u32[]{:S(2)}, u32[]{:S(2)}) %collective-permute-start.10) | collective-permute-done | bytes 442400 | tf_op jit(solution)/shard_map/ppermute | solution.py:376
  38.2 0.1 collective-permute-start.12
  38.3 0.1 collective-permute-start.13
  38.4 0.5 collective-permute-start.18
  38.9 6.4 %collective-permute-done.12.rest_6_ = bf16[432,256]{1,0:T(8,128)(2,1)S(1)} collective-permute-done((bf16[432,256]{1,0:T(8,128)(2,1)S(1)}, bf16[432,256]{1,0:T(8,128)(2,1)S(1)}, u32[]{:S(2)}, u32[]{:S(2)}) %collective-permute-start.12) | collective-permute-done | bytes 221216 | tf_op jit(solution)/shard_map/ppermute | solution.py:398
  45.3 0.1 collective-permute-start.19
  45.4 1.4 %collective-permute-done.14.rest_10_ = bf16[432,256]{1,0:T(8,128)(2,1)S(1)} collective-permute-done((bf16[432,256]{1,0:T(8,128)(2,1)S(1)}, bf16[432,256]{1,0:T(8,128)(2,1)S(1)}, u32[]{:S(2)}, u32[]{:S(2)}) %collective-permute-start.14) | collective-permute-done | bytes 221216 | tf_op jit(solution)/shard_map/ppermute | solution.py:399
  46.8 2.3 %first.1 = (f32[512,256]{1,0:T(8,128)S(1)}, bf16[512,256]{1,0:T(8,128)(2,1)S(1)}, bf16[256,512]{1,0:T(8,128)(2,1)S(1)}) custom-call(bf16[8,10,16,768]{3,2,1,0:T(8,128)(2,1)S(1)} %get-tuple-element.33.sx_ref, bf16[3,128,256]{2,1,0:T(8,128)(2,1)S(1)} %get-tuple-element.34.mask_ref, bf16[432,256]{1,0:T(8,128)(2,1)S(1)} %copy-done.3, ...), custom_call_target="tpu_custom_call" | custom-call | flops 7247757312 | bytes 4194304 | tf_op jit(solution)/shard_map/first/pallas_call | solution.py:350
  49.1 2.2 %grad_two.1 = (bf16[3456,256]{1,0:T(8,128)(2,1)S(1)}, bf16[3456,256]{1,0:T(8,128)(2,1)S(1)}) custom-call(bf16[6,10,16,768]{3,2,1,0:T(8,128)(2,1)S(1)} %get-tuple-element.38.sc_ref, bf16[256,512]{1,0:T(8,128)(2,1)S(1)} %get-tuple-element.41.act_t_ref), custom_call_target="tpu_custom_call" | custom-call | flops 7247757312 | bytes 4194304 | tf_op jit(solution)/shard_map/grad_two/pallas_call | solution.py:350
  51.4 0.2 collective-permute-start.20
  51.6 0.4 collective-permute-start.22
  51.9 0.1 collective-permute-start.23
  52.1 4.0 %collective-permute-done.23.rest_21_.rest_10_ = bf16[432,256]{1,0:T(8,128)(2,1)S(1)} collective-permute-done((bf16[432,256]{1,0:T(8,128)(2,1)S(1)}, bf16[432,256]{1,0:T(8,128)(2,1)S(1)}, u32[]{:S(2)}, u32[]{:S(2)}) %collective-permute-start.23) | collective-permute-done | bytes 221216 | tf_op jit(solution)/shard_map/ppermute | solution.py:423
  56.1 2.4 %back.1.sd_ref = bf16[4,10,16,768]{3,2,1,0:T(8,128)(2,1)S(1)} custom-call(bf16[6,10,16,768]{3,2,1,0:T(8,128)(2,1)S(1)} %get-tuple-element.38.sc_ref, f32[512,256]{1,0:T(8,128)S(1)} %get-tuple-element.47.pre_ref, bf16[3,128,256]{2,1,0:T(8,128)(2,1)S(1)} %get-tuple-element.34.mask_ref, bf16[432,256]{1,0:T(8,128)(2,1)S(1)} %copy-done.4, ...), custom_call_target="tpu_custom_call" | custom-call | flops 7247757312 | bytes 4194304 | tf_op jit(solution)/shard_map/back/pallas_call | solution.py:350
  58.5 0.1 add_convert_fusion.7
  58.6 0.6 collective-permute-start.21
  59.1 2.2 %grad_one.1 = (bf16[3456,256]{1,0:T(8,128)(2,1)S(1)}, bf16[3456,256]{1,0:T(8,128)(2,1)S(1)}) custom-call(bf16[4,10,16,768]{3,2,1,0:T(8,128)(2,1)S(1)} %back.1.sd_ref, bf16[256,768]{1,0:T(8,128)(2,1)S(1)} %get-tuple-element.48.int_ref), custom_call_target="tpu_custom_call" | custom-call | flops 7247757312 | bytes 4194304 | tf_op jit(solution)/shard_map/grad_one/pallas_call | solution.py:350
  61.4 3.2 %collective-permute-done.21 = bf16[432,256]{1,0:T(8,128)(2,1)S(1)} collective-permute-done((bf16[432,256]{1,0:T(8,128)(2,1)S(1)}, bf16[432,256]{1,0:T(8,128)(2,1)S(1)}, u32[]{:S(2)}, u32[]{:S(2)}) %collective-permute-start.21) | collective-permute-done | bytes 221216 | tf_op jit(solution)/shard_map/ppermute | solution.py:444
  64.6 0.2 add_convert_fusion.4
  64.7 0.6 collective-permute-start.26
  65.3 3.0 %collective-permute-done.24 = bf16[3456,256]{1,0:T(8,128)(2,1)S(1)} collective-permute-done((bf16[3456,256]{1,0:T(8,128)(2,1)S(1)}, bf16[3456,256]{1,0:T(8,128)(2,1)S(1)}, u32[]{:S(2)}, u32[]{:S(2)}) %collective-permute-start.24) | collective-permute-done | bytes 1769504 | tf_op jit(solution)/shard_map/ppermute | solution.py:460
  68.2 0.1 add_convert_fusion.6
  68.3 0.7 collective-permute-start.25
  69.0 4.3 %third.1 = bf16[4,8,16,256]{3,2,1,0:T(8,128)(2,1)} custom-call(bf16[8,10,16,768]{3,2,1,0:T(8,128)(2,1)S(1)} %get-tuple-element.33.sx_ref, bf16[512,256]{1,0:T(8,128)(2,1)S(1)} %get-tuple-element.46.act_ref, bf16[3,128,256]{2,1,0:T(8,128)(2,1)S(1)} %get-tuple-element.34.mask_ref, bf16[432,256]{1,0:T(8,128)(2,1)S(1)} %copy-done.3, ...), custom_call_target="tpu_custom_call" | custom-call | flops 7247757312 | bytes 4194304 | tf_op jit(solution)/shard_map/third/pallas_call | solution.py:350
  73.3 2.1 %collective-permute-done.25 = bf16[432,256]{1,0:T(8,128)(2,1)S(1)} collective-permute-done((bf16[432,256]{1,0:T(8,128)(2,1)S(1)}, bf16[432,256]{1,0:T(8,128)(2,1)S(1)}, u32[]{:S(2)}, u32[]{:S(2)}) %collective-permute-start.25) | collective-permute-done | bytes 221216 | tf_op jit(solution)/shard_map/ppermute | solution.py:463
  75.4 0.1 add_convert_fusion.5
  75.6 0.6 collective-permute-start.27
  76.2 0.2 add_convert_fusion.1
  76.3 0.2 collective-permute-start.31
  76.6 7.4 %collective-permute-done.27 = bf16[864,256]{1,0:T(8,128)(2,1)S(1)} collective-permute-done((bf16[864,256]{1,0:T(8,128)(2,1)S(1)}, bf16[864,256]{1,0:T(8,128)(2,1)S(1)}, u32[]{:S(2)}, u32[]{:S(2)}) %collective-permute-start.27) | collective-permute-done | bytes 442400 | tf_op jit(solution)/shard_map/ppermute | solution.py:477
  84.0 0.2 add_convert_fusion.3
  84.1 0.6 collective-permute-start.28
  84.7 4.0 %collective-permute-done.31 = bf16[864,256]{1,0:T(8,128)(2,1)S(1)} collective-permute-done((bf16[864,256]{1,0:T(8,128)(2,1)S(1)}, bf16[864,256]{1,0:T(8,128)(2,1)S(1)}, u32[]{:S(2)}, u32[]{:S(2)}) %collective-permute-start.31) | collective-permute-done | bytes 442400 | tf_op jit(solution)/shard_map/ppermute | solution.py:478
  88.7 0.2 add_convert_fusion
  88.9 0.6 collective-permute-start.32
  89.5 4.0 %collective-permute-done.28 = bf16[864,256]{1,0:T(8,128)(2,1)S(1)} collective-permute-done((bf16[864,256]{1,0:T(8,128)(2,1)S(1)}, bf16[864,256]{1,0:T(8,128)(2,1)S(1)}, u32[]{:S(2)}, u32[]{:S(2)}) %collective-permute-start.28) | collective-permute-done | bytes 442400 | tf_op jit(solution)/shard_map/ppermute | solution.py:480
  93.4 0.2 add_convert_fusion.2
  93.6 0.6 collective-permute-start.29
  94.2 1.6 %collective-permute-done.32 = bf16[432,256]{1,0:T(8,128)(2,1)S(1)} collective-permute-done((bf16[432,256]{1,0:T(8,128)(2,1)S(1)}, bf16[432,256]{1,0:T(8,128)(2,1)S(1)}, u32[]{:S(2)}, u32[]{:S(2)}) %collective-permute-start.32) | collective-permute-done | bytes 221216 | tf_op jit(solution)/shard_map/ppermute | solution.py:441
  95.8 1.1 %collective-permute-done.33 = bf16[432,256]{1,0:T(8,128)(2,1)S(1)} collective-permute-done((bf16[432,256]{1,0:T(8,128)(2,1)S(1)}, bf16[432,256]{1,0:T(8,128)(2,1)S(1)}, u32[]{:S(2)}, u32[]{:S(2)}) %collective-permute-start.33) | collective-permute-done | bytes 221216 | tf_op jit(solution)/shard_map/ppermute | solution.py:442
  96.9 0.9 add_multiply_fusion
  97.7 2.8 %collective-permute-done.29 = bf16[432,256]{1,0:T(8,128)(2,1)S(1)} collective-permute-done((bf16[432,256]{1,0:T(8,128)(2,1)S(1)}, bf16[432,256]{1,0:T(8,128)(2,1)S(1)}, u32[]{:S(2)}, u32[]{:S(2)}) %collective-permute-start.29) | collective-permute-done | bytes 221216 | tf_op jit(solution)/shard_map/ppermute | solution.py:441
  100.5 1.1 %collective-permute-done.30 = bf16[432,256]{1,0:T(8,128)(2,1)S(1)} collective-permute-done((bf16[432,256]{1,0:T(8,128)(2,1)S(1)}, bf16[432,256]{1,0:T(8,128)(2,1)S(1)}, u32[]{:S(2)}, u32[]{:S(2)}) %collective-permute-start.30) | collective-permute-done | bytes 221216 | tf_op jit(solution)/shard_map/ppermute | solution.py:442
  101.6 0.9 add_multiply_fusion.1
  (42 shorter events, 0.3 us)
Async XLA Ops:
  0.6 25.0 %copy-start.3 = (bf16[432,256]{1,0:T(8,128)(2,1)S(1)}, bf16[432,256]{1,0:T(8,128)(2,1)}, u32[]{:S(2)}) copy-start(bf16[432,256]{1,0:T(8,128)(2,1)} %rest_0_.4) | copy-start | bytes 663556
  0.6 25.2 %copy-start.1 = (bf16[4,8,16,256]{3,2,1,0:T(8,128)(2,1)S(1)}, bf16[4,8,16,256]{3,2,1,0:T(8,128)(2,1)}, u32[]{:S(2)}) copy-start(bf16[4,8,16,256]{3,2,1,0:T(8,128)(2,1)} %c_own.1) | copy-start | bytes 786436
  0.7 25.2 %copy-start = (bf16[4,8,16,256]{3,2,1,0:T(8,128)(2,1)S(1)}, bf16[4,8,16,256]{3,2,1,0:T(8,128)(2,1)}, u32[]{:S(2)}) copy-start(bf16[4,8,16,256]{3,2,1,0:T(8,128)(2,1)} %f_own.1) | copy-start | bytes 786436
  0.7 25.2 %copy-start.2 = (s32[16,2,4]{0,2,1:T(4,128)S(1)}, s32[16,2,4]{0,2,1:T(4,128)}, u32[]{:S(2)}) copy-start(s32[16,2,4]{0,2,1:T(4,128)} %param.9) | copy-start | bytes 1540
  0.7 8.2 %collective-permute-start = (bf16[432,256]{1,0:T(8,128)(2,1)}, bf16[432,256]{1,0:T(8,128)(2,1)S(1)}, u32[]{:S(2)}, u32[]{:S(2)}) collective-permute-start(bf16[432,256]{1,0:T(8,128)(2,1)} %rest_0_.4), channel_id=1, source_target_pairs={{0,4},{4,8},{8,12},{12,14},{14,10},{10,6},{6,2},{2,0},{1,3},{5,1},... | collective-permute-start | bytes 663560 | tf_op jit(solution)/shard_map/ppermute | solution.py:364
  3.8 7.3 %collective-permute-start.7 = (bf16[432,256]{1,0:T(8,128)(2,1)}, bf16[432,256]{1,0:T(8,128)(2,1)S(1)}, u32[]{:S(2)}, u32[]{:S(2)}) collective-permute-start(bf16[432,256]{1,0:T(8,128)(2,1)} %rest_0_.4), channel_id=1, source_target_pairs={{1,4},{5,8},{9,12},{13,14},{15,10},{11,6},{7,2},{3,0},{0,3},{4,1},... | collective-permute-start | bytes 663560 | tf_op jit(solution)/shard_map/ppermute | solution.py:364
  4.4 15.5 %collective-permute-start.4 = (bf16[432,256]{1,0:T(8,128)(2,1)}, bf16[432,256]{1,0:T(8,128)(2,1)S(1)}, u32[]{:S(2)}, u32[]{:S(2)}) collective-permute-start(bf16[432,256]{1,0:T(8,128)(2,1)} %rest_0_.5), channel_id=1, source_target_pairs={{1,4},{5,8},{9,12},{13,14},{15,10},{11,6},{7,2},{3,0},{0,3},{4,1},... | collective-permute-start | bytes 663560 | tf_op jit(solution)/shard_map/ppermute | solution.py:366
  5.5 10.0 %collective-permute-start.3 = (bf16[432,256]{1,0:T(8,128)(2,1)}, bf16[432,256]{1,0:T(8,128)(2,1)S(1)}, u32[]{:S(2)}, u32[]{:S(2)}) collective-permute-start(bf16[432,256]{1,0:T(8,128)(2,1)} %rest_0_.5), channel_id=1, source_target_pairs={{0,4},{4,8},{8,12},{12,14},{14,10},{10,6},{6,2},{2,0},{1,3},{5,1},... | collective-permute-start | bytes 663560 | tf_op jit(solution)/shard_map/ppermute | solution.py:366
  11.1 14.1 %collective-permute-start.9 = (bf16[864,256]{1,0:T(8,128)(2,1)S(1)}, bf16[864,256]{1,0:T(8,128)(2,1)S(1)}, u32[]{:S(2)}, u32[]{:S(2)}) collective-permute-start(bf16[864,256]{1,0:T(8,128)(2,1)S(1)} %constant_dynamic-update-slice_fusion.2), channel_id=1, source_target_pairs={{0,1},{1,0},{2,3},{3,2},{4,5},{5,4},{6,7},{7,6},{8,9},{9,8},{10,11... | collective-permute-start | bytes 1327112 | tf_op jit(solution)/shard_map/ppermute | solution.py:373
  11.1 14.0 %collective-permute-start.8 = (bf16[864,256]{1,0:T(8,128)(2,1)S(1)}, bf16[864,256]{1,0:T(8,128)(2,1)S(1)}, u32[]{:S(2)}, u32[]{:S(2)}) collective-permute-start(bf16[864,256]{1,0:T(8,128)(2,1)S(1)} %constant_dynamic-update-slice_fusion.2), channel_id=1, source_target_pairs={{0,4},{4,8},{8,12},{12,14},{14,10},{10,6},{6,2},{2,0},{1,3},{5,1},... | collective-permute-start | bytes 1327112 | tf_op jit(solution)/shard_map/ppermute | solution.py:372
  14.3 24.1 %copy-start.4 = (bf16[432,256]{1,0:T(8,128)(2,1)S(1)}, bf16[432,256]{1,0:T(8,128)(2,1)}, u32[]{:S(2)}) copy-start(bf16[432,256]{1,0:T(8,128)(2,1)} %rest_0_.5) | copy-start | bytes 663556
  15.4 9.8 %collective-permute-start.1 = (bf16[3,8,16,256]{3,2,1,0:T(8,128)(2,1)S(1)}, bf16[3,8,16,256]{3,2,1,0:T(8,128)(2,1)S(1)}, u32[]{:S(2)}, u32[]{:S(2)}) collective-permute-start(bf16[3,8,16,256]{3,2,1,0:T(8,128)(2,1)S(1)} %pad_maximum_fusion), channel_id=1, source_target_pairs={{0,1},{1,2},{2,3},{3,4},{4,5},{5,6},{6,7},{7,8},{8,9},{9,10},{10,1... | collective-permute-start | bytes 589832 | tf_op jit(solution)/shard_map/ppermute | solution.py:368
  15.5 9.7 %collective-permute-start.2 = (bf16[3,8,16,256]{3,2,1,0:T(8,128)(2,1)S(1)}, bf16[3,8,16,256]{3,2,1,0:T(8,128)(2,1)S(1)}, u32[]{:S(2)}, u32[]{:S(2)}) collective-permute-start(bf16[3,8,16,256]{3,2,1,0:T(8,128)(2,1)S(1)} %pad_maximum_fusion.1), channel_id=1, source_target_pairs={{0,15},{1,0},{2,1},{3,2},{4,3},{5,4},{6,5},{7,6},{8,7},{9,8},{10,9... | collective-permute-start | bytes 589832 | tf_op jit(solution)/shard_map/ppermute | solution.py:369
  20.0 7.2 %collective-permute-start.15 = (bf16[864,256]{1,0:T(8,128)(2,1)S(1)}, bf16[864,256]{1,0:T(8,128)(2,1)S(1)}, u32[]{:S(2)}, u32[]{:S(2)}) collective-permute-start(bf16[864,256]{1,0:T(8,128)(2,1)S(1)} %constant_dynamic-update-slice_fusion), channel_id=1, source_target_pairs={{0,1},{1,0},{2,3},{3,2},{4,5},{5,4},{6,7},{7,6},{8,9},{9,8},{10,11... | collective-permute-start | bytes 1327112 | tf_op jit(solution)/shard_map/ppermute | solution.py:403
  25.1 8.3 %collective-permute-start.5 = (bf16[864,256]{1,0:T(8,128)(2,1)S(1)}, bf16[864,256]{1,0:T(8,128)(2,1)S(1)}, u32[]{:S(2)}, u32[]{:S(2)}) collective-permute-start(bf16[864,256]{1,0:T(8,128)(2,1)S(1)} %constant_dynamic-update-slice_fusion), channel_id=1, source_target_pairs={{0,4},{4,8},{8,12},{12,14},{14,10},{10,6},{6,2},{2,0},{1,3},{5,1},... | collective-permute-start | bytes 1327112 | tf_op jit(solution)/shard_map/ppermute | solution.py:375
  25.2 13.0 %collective-permute-start.10 = (bf16[864,256]{1,0:T(8,128)(2,1)S(1)}, bf16[864,256]{1,0:T(8,128)(2,1)S(1)}, u32[]{:S(2)}, u32[]{:S(2)}) collective-permute-start(bf16[864,256]{1,0:T(8,128)(2,1)S(1)} %collective-permute-done.8.rest_4_), channel_id=1, source_target_pairs={{0,4},{4,8},{8,12},{12,14},{14,10},{10,6},{6,2},{2,0},{1,3},{5,1},... | collective-permute-start | bytes 1327112 | tf_op jit(solution)/shard_map/ppermute | solution.py:376
  25.4 12.8 %collective-permute-start.11 = (bf16[864,256]{1,0:T(8,128)(2,1)S(1)}, bf16[864,256]{1,0:T(8,128)(2,1)S(1)}, u32[]{:S(2)}, u32[]{:S(2)}) collective-permute-start(bf16[864,256]{1,0:T(8,128)(2,1)S(1)} %collective-permute-done.8.rest_4_), channel_id=1, source_target_pairs={{0,1},{1,0},{2,3},{3,2},{4,5},{5,4},{6,7},{7,6},{8,9},{9,8},{10,11... | collective-permute-start | bytes 1327112 | tf_op jit(solution)/shard_map/ppermute | solution.py:377
  25.6 12.6 %collective-permute-start.6 = (bf16[432,256]{1,0:T(8,128)(2,1)S(1)}, bf16[432,256]{1,0:T(8,128)(2,1)S(1)}, u32[]{:S(2)}, u32[]{:S(2)}) collective-permute-start(bf16[432,256]{1,0:T(8,128)(2,1)S(1)} %copy-done.3), channel_id=1, source_target_pairs={{0,1},{1,0},{2,3},{3,2},{4,5},{5,4},{6,7},{7,6},{8,9},{9,8},{10,11... | collective-permute-start | bytes 663560 | tf_op jit(solution)/shard_map/ppermute | solution.py:378
  33.4 11.9 %collective-permute-start.16 = (bf16[864,256]{1,0:T(8,128)(2,1)S(1)}, bf16[864,256]{1,0:T(8,128)(2,1)S(1)}, u32[]{:S(2)}, u32[]{:S(2)}) collective-permute-start(bf16[864,256]{1,0:T(8,128)(2,1)S(1)} %collective-permute-done.5.rest_15_.rest_4_), channel_id=1, source_target_pairs={{0,4},{4,8},{8,12},{12,14},{14,10},{10,6},{6,2},{2,0},{1,3},{5,1},... | collective-permute-start | bytes 1327112 | tf_op jit(solution)/shard_map/ppermute | solution.py:404
  33.4 11.9 %collective-permute-start.17 = (bf16[864,256]{1,0:T(8,128)(2,1)S(1)}, bf16[864,256]{1,0:T(8,128)(2,1)S(1)}, u32[]{:S(2)}, u32[]{:S(2)}) collective-permute-start(bf16[864,256]{1,0:T(8,128)(2,1)S(1)} %collective-permute-done.5.rest_15_.rest_4_), channel_id=1, source_target_pairs={{0,1},{1,0},{2,3},{3,2},{4,5},{5,4},{6,7},{7,6},{8,9},{9,8},{10,11... | collective-permute-start | bytes 1327112 | tf_op jit(solution)/shard_map/ppermute | solution.py:405
  38.2 7.1 %collective-permute-start.12 = (bf16[432,256]{1,0:T(8,128)(2,1)S(1)}, bf16[432,256]{1,0:T(8,128)(2,1)S(1)}, u32[]{:S(2)}, u32[]{:S(2)}) collective-permute-start(bf16[432,256]{1,0:T(8,128)(2,1)S(1)} %slice.120), channel_id=1, source_target_pairs={{0,4},{4,8},{8,12},{12,14},{14,10},{10,6},{6,2},{2,0},{1,3},{5,1},... | collective-permute-start | bytes 663560 | tf_op jit(solution)/shard_map/ppermute | solution.py:398
  38.3 7.1 %collective-permute-start.13 = (bf16[864,256]{1,0:T(8,128)(2,1)S(1)}, bf16[864,256]{1,0:T(8,128)(2,1)S(1)}, u32[]{:S(2)}, u32[]{:S(2)}) collective-permute-start(bf16[864,256]{1,0:T(8,128)(2,1)S(1)} %collective-permute-done.10.rest_5_), channel_id=1, source_target_pairs={{0,1},{1,0},{2,3},{3,2},{4,5},{5,4},{6,7},{7,6},{8,9},{9,8},{10,11... | collective-permute-start | bytes 1327112 | tf_op jit(solution)/shard_map/ppermute | solution.py:399
  38.4 6.9 %collective-permute-start.18 = (bf16[432,256]{1,0:T(8,128)(2,1)S(1)}, bf16[432,256]{1,0:T(8,128)(2,1)S(1)}, u32[]{:S(2)}, u32[]{:S(2)}) collective-permute-start(bf16[432,256]{1,0:T(8,128)(2,1)S(1)} %copy-done.4), channel_id=1, source_target_pairs={{0,1},{1,0},{2,3},{3,2},{4,5},{5,4},{6,7},{7,6},{8,9},{9,8},{10,11... | collective-permute-start | bytes 663560 | tf_op jit(solution)/shard_map/ppermute | solution.py:406
  45.3 1.5 %collective-permute-start.14 = (bf16[432,256]{1,0:T(8,128)(2,1)S(1)}, bf16[432,256]{1,0:T(8,128)(2,1)S(1)}, u32[]{:S(2)}, u32[]{:S(2)}) collective-permute-start(bf16[432,256]{1,0:T(8,128)(2,1)S(1)} %collective-permute-done.12.rest_6_), channel_id=1, source_target_pairs={{0,1},{1,0},{2,3},{3,2},{4,5},{5,4},{6,7},{7,6},{8,9},{9,8},{10,11... | collective-permute-start | bytes 663560 | tf_op jit(solution)/shard_map/ppermute | solution.py:399
  45.3 6.0 %collective-permute-start.19 = (bf16[432,256]{1,0:T(8,128)(2,1)S(1)}, bf16[432,256]{1,0:T(8,128)(2,1)S(1)}, u32[]{:S(2)}, u32[]{:S(2)}) collective-permute-start(bf16[432,256]{1,0:T(8,128)(2,1)S(1)} %slice.121), channel_id=1, source_target_pairs={{0,4},{4,8},{8,12},{12,14},{14,10},{10,6},{6,2},{2,0},{1,3},{5,1},... | collective-permute-start | bytes 663560 | tf_op jit(solution)/shard_map/ppermute | solution.py:422
  51.4 7.1 %collective-permute-start.20 = (bf16[3456,256]{1,0:T(8,128)(2,1)S(1)}, bf16[3456,256]{1,0:T(8,128)(2,1)S(1)}, u32[]{:S(2)}, u32[]{:S(2)}) collective-permute-start(bf16[3456,256]{1,0:T(8,128)(2,1)S(1)} %get-tuple-element.45), channel_id=1, source_target_pairs={{0,1},{1,0},{2,3},{3,2},{4,5},{5,4},{6,7},{7,6},{8,9},{9,8},{10,11... | collective-permute-start | bytes 5308424 | tf_op jit(solution)/shard_map/ppermute | solution.py:428
  51.6 4.5 %collective-permute-start.22 = (bf16[864,256]{1,0:T(8,128)(2,1)S(1)}, bf16[864,256]{1,0:T(8,128)(2,1)S(1)}, u32[]{:S(2)}, u32[]{:S(2)}) collective-permute-start(bf16[864,256]{1,0:T(8,128)(2,1)S(1)} %collective-permute-done.16.rest_16_.rest_5_), channel_id=1, source_target_pairs={{0,1},{1,0},{2,3},{3,2},{4,5},{5,4},{6,7},{7,6},{8,9},{9,8},{10,11... | collective-permute-start | bytes 1327112 | tf_op jit(solution)/shard_map/ppermute | solution.py:423
  51.9 4.1 %collective-permute-start.23 = (bf16[432,256]{1,0:T(8,128)(2,1)S(1)}, bf16[432,256]{1,0:T(8,128)(2,1)S(1)}, u32[]{:S(2)}, u32[]{:S(2)}) collective-permute-start(bf16[432,256]{1,0:T(8,128)(2,1)S(1)} %collective-permute-done.19.rest_17_.rest_6_), channel_id=1, source_target_pairs={{0,1},{1,0},{2,3},{3,2},{4,5},{5,4},{6,7},{7,6},{8,9},{9,8},{10,11... | collective-permute-start | bytes 663560 | tf_op jit(solution)/shard_map/ppermute | solution.py:423
  58.6 6.0 %collective-permute-start.21 = (bf16[432,256]{1,0:T(8,128)(2,1)S(1)}, bf16[432,256]{1,0:T(8,128)(2,1)S(1)}, u32[]{:S(2)}, u32[]{:S(2)}) collective-permute-start(bf16[432,256]{1,0:T(8,128)(2,1)S(1)} %add_convert_fusion.7), channel_id=1, source_target_pairs={{0,4},{4,8},{8,12},{12,14},{14,10},{10,6},{6,2},{2,0},{1,3},{5,1},... | collective-permute-start | bytes 663560 | tf_op jit(solution)/shard_map/ppermute | solution.py:444
  64.5 3.7 %collective-permute-start.24 = (bf16[3456,256]{1,0:T(8,128)(2,1)S(1)}, bf16[3456,256]{1,0:T(8,128)(2,1)S(1)}, u32[]{:S(2)}, u32[]{:S(2)}) collective-permute-start(bf16[3456,256]{1,0:T(8,128)(2,1)S(1)} %get-tuple-element.51), channel_id=1, source_target_pairs={{0,1},{1,0},{2,3},{3,2},{4,5},{5,4},{6,7},{7,6},{8,9},{9,8},{10,11... | collective-permute-start | bytes 5308424 | tf_op jit(solution)/shard_map/ppermute | solution.py:460
  64.7 10.9 %collective-permute-start.26 = (bf16[864,256]{1,0:T(8,128)(2,1)S(1)}, bf16[864,256]{1,0:T(8,128)(2,1)S(1)}, u32[]{:S(2)}, u32[]{:S(2)}) collective-permute-start(bf16[864,256]{1,0:T(8,128)(2,1)S(1)} %add_convert_fusion.4), channel_id=1, source_target_pairs={{0,4},{4,8},{8,12},{12,14},{14,10},{10,6},{6,2},{2,0},{1,3},{5,1},... | collective-permute-start | bytes 1327112 | tf_op jit(solution)/shard_map/ppermute | solution.py:462
  68.3 7.1 %collective-permute-start.25 = (bf16[432,256]{1,0:T(8,128)(2,1)S(1)}, bf16[432,256]{1,0:T(8,128)(2,1)S(1)}, u32[]{:S(2)}, u32[]{:S(2)}) collective-permute-start(bf16[432,256]{1,0:T(8,128)(2,1)S(1)} %add_convert_fusion.6), channel_id=1, source_target_pairs={{0,4},{4,8},{8,12},{12,14},{14,10},{10,6},{6,2},{2,0},{1,3},{5,1},... | collective-permute-start | bytes 663560 | tf_op jit(solution)/shard_map/ppermute | solution.py:463
  75.6 8.4 %collective-permute-start.27 = (bf16[864,256]{1,0:T(8,128)(2,1)S(1)}, bf16[864,256]{1,0:T(8,128)(2,1)S(1)}, u32[]{:S(2)}, u32[]{:S(2)}) collective-permute-start(bf16[864,256]{1,0:T(8,128)(2,1)S(1)} %add_convert_fusion.5), channel_id=1, source_target_pairs={{0,4},{4,8},{8,12},{12,14},{14,10},{10,6},{6,2},{2,0},{1,3},{5,1},... | collective-permute-start | bytes 1327112 | tf_op jit(solution)/shard_map/ppermute | solution.py:477
  76.3 12.3 %collective-permute-start.31 = (bf16[864,256]{1,0:T(8,128)(2,1)S(1)}, bf16[864,256]{1,0:T(8,128)(2,1)S(1)}, u32[]{:S(2)}, u32[]{:S(2)}) collective-permute-start(bf16[864,256]{1,0:T(8,128)(2,1)S(1)} %add_convert_fusion.1), channel_id=1, source_target_pairs={{0,4},{4,8},{8,12},{12,14},{14,10},{10,6},{6,2},{2,0},{1,3},{5,1},... | collective-permute-start | bytes 1327112 | tf_op jit(solution)/shard_map/ppermute | solution.py:478
  84.1 9.3 %collective-permute-start.28 = (bf16[864,256]{1,0:T(8,128)(2,1)S(1)}, bf16[864,256]{1,0:T(8,128)(2,1)S(1)}, u32[]{:S(2)}, u32[]{:S(2)}) collective-permute-start(bf16[864,256]{1,0:T(8,128)(2,1)S(1)} %add_convert_fusion.3), channel_id=1, source_target_pairs={{0,4},{4,8},{8,12},{12,14},{14,10},{10,6},{6,2},{2,0},{1,3},{5,1},... | collective-permute-start | bytes 1327112 | tf_op jit(solution)/shard_map/ppermute | solution.py:480
  88.9 6.9 %collective-permute-start.32 = (bf16[432,256]{1,0:T(8,128)(2,1)S(1)}, bf16[432,256]{1,0:T(8,128)(2,1)S(1)}, u32[]{:S(2)}, u32[]{:S(2)}) collective-permute-start(bf16[432,256]{1,0:T(8,128)(2,1)S(1)} %get-tuple-element.53), channel_id=1, source_target_pairs={{0,4},{4,8},{8,12},{12,14},{14,10},{10,6},{6,2},{2,0},{1,3},{5,1},... | collective-permute-start | bytes 663560 | tf_op jit(solution)/shard_map/ppermute | solution.py:441
  89.5 7.4 %collective-permute-start.33 = (bf16[432,256]{1,0:T(8,128)(2,1)S(1)}, bf16[432,256]{1,0:T(8,128)(2,1)S(1)}, u32[]{:S(2)}, u32[]{:S(2)}) collective-permute-start(bf16[432,256]{1,0:T(8,128)(2,1)S(1)} %get-tuple-element.54), channel_id=1, source_target_pairs={{0,5},{4,9},{8,13},{12,15},{14,11},{10,7},{6,3},{2,1},{1,2},{5,0},... | collective-permute-start | bytes 663560 | tf_op jit(solution)/shard_map/ppermute | solution.py:442
  93.6 6.9 %collective-permute-start.29 = (bf16[432,256]{1,0:T(8,128)(2,1)S(1)}, bf16[432,256]{1,0:T(8,128)(2,1)S(1)}, u32[]{:S(2)}, u32[]{:S(2)}) collective-permute-start(bf16[432,256]{1,0:T(8,128)(2,1)S(1)} %get-tuple-element.55), channel_id=1, source_target_pairs={{0,4},{4,8},{8,12},{12,14},{14,10},{10,6},{6,2},{2,0},{1,3},{5,1},... | collective-permute-start | bytes 663560 | tf_op jit(solution)/shard_map/ppermute | solution.py:441
  94.2 7.4 %collective-permute-start.30 = (bf16[432,256]{1,0:T(8,128)(2,1)S(1)}, bf16[432,256]{1,0:T(8,128)(2,1)S(1)}, u32[]{:S(2)}, u32[]{:S(2)}) collective-permute-start(bf16[432,256]{1,0:T(8,128)(2,1)S(1)} %get-tuple-element.56), channel_id=1, source_target_pairs={{0,5},{4,9},{8,13},{12,15},{14,11},{10,7},{6,3},{2,1},{1,2},{5,0},... | collective-permute-start | bytes 663560 | tf_op jit(solution)/shard_map/ppermute | solution.py:442

commit v4 on v3

--- a/solution.py
+++ b/solution.py
@@ -357,22 +357,21 @@
             scratch_shapes=scratches,
             compiler_params=pltpu.CompilerParams(vmem_limit_bytes=mib << 20),
             cost_estimate=pl.CostEstimate(
-                flops=4 * convs * flops, transcendentals=0, bytes_accessed=4 << 20
+                flops=convs * flops, transcendentals=0, bytes_accessed=4 << 20
             ),
         )(*operands)
 
     a1 = [onward(weight_one), gather_across(weight_one)]
-    weight_late = after(weight_two, weight_one)
+    weight_late = after(weight_two, a1[0])
     b1 = [onward(weight_late), gather_across(weight_late)]
-    features_late, cot_late, _ = lax.optimization_barrier((features, cotangent, a1[0]))
-    low = up(jnp.concatenate([features_late[-2:], cot_late[-1:]]))
-    high = down(jnp.concatenate([features_late[:2], cot_late[:1]]))
-
-    a1_pair = jnp.concatenate(a1)
+    low = up(jnp.concatenate([features[-2:], cotangent[-1:]]))
+    high = down(jnp.concatenate([features[:2], cotangent[:1]]))
+
+    a1_pair = after(jnp.concatenate(a1), low, high)
     a2 = onward(a1_pair)
     qa1 = sibling(a1_pair)
     b1_pair = jnp.concatenate(b1)
-    b2 = onward(after(b1_pair, low, high))
+    b2 = onward(b1_pair)
     a3 = onward(after(a2, qa1, b1_pair))
     qa2 = sibling(a2)
     other_one = sibling(weight_one)
@@ -419,7 +418,7 @@
         near,
         *ones,
     )
-    b4 = onward(after(b3[:rows], qb2, other_two))
+    b4 = onward(after(b3[:rows], qb2, other_two, act_t))
     qb3, qb4 = sibling(b3), sibling(b4)
     twos = [weight_two, other_two, *b1, b2, b3, b4, qb1, qb2, qb3, qb4]
     keep_two, send_two = kernel(
@@ -465,7 +464,7 @@
         functools.partial(third_kernel, n),
         "third",
         14,
-        1,
+        4,
         shape(features.shape, BF),
         [weights, weights, scratch((depth + 2, ny + 2, nz, 3 * channels), BF)],
         sx,

time: 103 us -> 104 us (level)
  starting transfers between devices: 19.8 us -> 41.2 us
  waiting for transfers between devices: 61.9 us -> 42.3 us
    ppermute x2, waiting for transfers between devices: 0.01 us -> 7.49 us  [on_ring(): b1 = [onward(weight_late), gather_across(weight_late)]]
    ppermute x2, waiting for transfers between devices: 3.99 us -> 0.01 us  [on_ring(): qb3, qb4 = (sibling(b3), sibling(b4))]
    ppermute x2, waiting for transfers between devices: 3.94 us -> 0.01 us  [on_ring(): a1 = [onward(weight_one), gather_across(weight_one)]]
    ppermute x4, starting transfers between devices: 4.59 us -> 8.47 us  [the longest x1 4.44 us: on_ring(): high = down(jnp.concatenate([features[:2], cotangent[:1]]))]
    ppermute x4, waiting for transfers between devices: 11.3 us -> 7.44 us  [the longest x1 3.58 us: on_ring(): low = up(jnp.concatenate([features[-2:], cotangent[-1:]]))]
    ppermute x2, starting transfers between devices: 1.12 us -> 4.9 us  [finish(): total = both(keep, got, 7, 8) + onward(message[:rows]).astype(F32)]
    ppermute x1, waiting for transfers between devices: 3.18 us -> 0.01 us  [on_ring(): two = onward(step(keep_two, got_two, None, 0))]
    ppermute x1, waiting for transfers between devices: 0.01 us -> 3.18 us  [on_ring(): got_two = sibling(after(send_two, b4))]
  transfers between devices with their start and end apart: 34 -> 34, of which waited for: 18 -> 17; matrix products, arithmetic and copies ran while one was open for 4% -> 4% of each run, Pallas kernels for 14% -> 14%
where the time goes in v4:
time: 104 us
  waiting for transfers between devices  42.3 us (41%)
  starting transfers between devices  41.2 us (40%)
  Pallas kernels  14.8 us (14%)
  other arithmetic  3 us (3%)
  local copies, waits for them, and re-layouts  2.02 us (2%)
    pallas_call x6, Pallas kernels, kernel(): pl.pallas_call(body, name=name, out_shape=outs, in_specs=[pl.BlockSpec(me...  14.8 us
    ppermute x2, waiting for transfers between devices, on_ring(): b1 = [onward(weight_late), gather_across(weight_late)]  7.49 us
    ppermute x2, starting transfers between devices, finish(): total = both(keep, got, 7, 8) + onward(message[:rows]).astype(F32)  4.9 us
    ppermute x1, waiting for transfers between devices, on_ring(): a4 = onward(after(a3[:rows], qa2, other_one, sx))  4.57 us
    ppermute x1, waiting for transfers between devices, on_ring(): one = onward(after(step(keep_one, got_one, one, 1), features_out, two))  4.49 us
    ppermute x1, starting transfers between devices, on_ring(): high = down(jnp.concatenate([features[:2], cotangent[:1]]))  4.44 us
    ppermute x2, waiting for transfers between devices, finish(): return (total + scatter_across(message[rows:]).astype(F32)) * loss_scale  4.27 us
    ppermute x1, waiting for transfers between devices, on_ring(): low = up(jnp.concatenate([features[-2:], cotangent[-1:]]))  3.58 us
  transfers between devices with their start and end apart: 34, of which 17 were waited for; matrix products, arithmetic and copies ran while one was open for 4% of the time, Pallas kernels for 14%

profile of v4, /device:TPU:0, one launch (start us, length us, event | category | flops | bytes accessed | tf_op | source)
XLA Modules:
  0.0 104.1 jit_solution(3580900010790145194)
XLA Ops:
  0.7 0.0 copy-start
  0.7 0.0 copy-start.2
  0.7 2.5 %collective-permute-start.7 = (bf16[432,256]{1,0:T(8,128)(2,1)}, bf16[432,256]{1,0:T(8,128)(2,1)S(1)}, u32[]{:S(2)}, u32[]{:S(2)}) collective-permute-start(bf16[432,256]{1,0:T(8,128)(2,1)} %rest_0_.4), channel_id=1, source_target_pairs={{1,4},{5,8},{9,12},{13,14},{15,10},{11,6},{7,2},{3,0},{0,3},{4,1},... | collective-permute-start | bytes 663560 | tf_op jit(solution)/shard_map/ppermute | solution.py:364
  3.2 0.7 collective-permute-start.2
  3.8 0.9 fusion.3
  4.7 1.0 fusion.2
  5.7 0.1 collective-permute-start
  5.9 4.4 %collective-permute-start.1 = (bf16[3,8,16,256]{3,2,1,0:T(8,128)(2,1)S(1)}, bf16[3,8,16,256]{3,2,1,0:T(8,128)(2,1)S(1)}, u32[]{:S(2)}, u32[]{:S(2)}) collective-permute-start(bf16[3,8,16,256]{3,2,1,0:T(8,128)(2,1)S(1)} %pad_maximum_fusion.2), channel_id=1, source_target_pairs={{0,15},{1,0},{2,1},{3,2},{4,3},{5,4},{6,5},{7,6},{8,7},{9,8},{10,9... | collective-permute-start | bytes 589832 | tf_op jit(solution)/shard_map/ppermute | solution.py:368
  10.3 1.4 %collective-permute-start.3 = (bf16[432,256]{1,0:T(8,128)(2,1)}, bf16[432,256]{1,0:T(8,128)(2,1)S(1)}, u32[]{:S(2)}, u32[]{:S(2)}) collective-permute-start(bf16[432,256]{1,0:T(8,128)(2,1)} %rest_0_.5), channel_id=1, source_target_pairs={{0,4},{4,8},{8,12},{12,14},{14,10},{10,6},{6,2},{2,0},{1,3},{5,1},... | collective-permute-start | bytes 663560 | tf_op jit(solution)/shard_map/ppermute | solution.py:366
  11.8 3.6 %collective-permute-done.low = bf16[3,8,16,256]{3,2,1,0:T(8,128)(2,1)S(1)} collective-permute-done((bf16[3,8,16,256]{3,2,1,0:T(8,128)(2,1)S(1)}, bf16[3,8,16,256]{3,2,1,0:T(8,128)(2,1)S(1)}, u32[]{:S(2)}, u32[]{:S(2)}) %collective-permute-start) | collective-permute-done | bytes 196640 | tf_op jit(solution)/shard_map/ppermute | solution.py:367
  15.3 1.1 %collective-permute-start.8 = (bf16[864,256]{1,0:T(8,128)(2,1)S(1)}, bf16[864,256]{1,0:T(8,128)(2,1)S(1)}, u32[]{:S(2)}, u32[]{:S(2)}) collective-permute-start(bf16[864,256]{1,0:T(8,128)(2,1)S(1)} %pad_maximum_fusion), channel_id=1, source_target_pairs={{0,4},{4,8},{8,12},{12,14},{14,10},{10,6},{6,2},{2,0},{1,3},{5,1},... | collective-permute-start | bytes 1327112 | tf_op jit(solution)/shard_map/ppermute | solution.py:371
  16.4 0.1 collective-permute-start.4
  16.6 0.7 collective-permute-done.3.rest_13_.rest_2_
  17.3 6.7 %collective-permute-done.4.rest_14_.rest_3_ = bf16[432,256]{1,0:T(8,128)(2,1)S(1)} collective-permute-done((bf16[432,256]{1,0:T(8,128)(2,1)S(1)}, bf16[432,256]{1,0:T(8,128)(2,1)S(1)}, u32[]{:S(2)}, u32[]{:S(2)}) %collective-permute-start.4) | collective-permute-done | bytes 221216 | tf_op jit(solution)/shard_map/ppermute | solution.py:366
  24.1 0.4 collective-permute-start.15
  24.5 1.9 %collective-permute-start.5 = (bf16[864,256]{1,0:T(8,128)(2,1)S(1)}, bf16[864,256]{1,0:T(8,128)(2,1)S(1)}, u32[]{:S(2)}, u32[]{:S(2)}) collective-permute-start(bf16[864,256]{1,0:T(8,128)(2,1)S(1)} %constant_dynamic-update-slice_fusion), channel_id=1, source_target_pairs={{0,4},{4,8},{8,12},{12,14},{14,10},{10,6},{6,2},{2,0},{1,3},{5,1},... | collective-permute-start | bytes 1327112 | tf_op jit(solution)/shard_map/ppermute | solution.py:374
  26.4 2.4 %collective-permute-start.10 = (bf16[864,256]{1,0:T(8,128)(2,1)S(1)}, bf16[864,256]{1,0:T(8,128)(2,1)S(1)}, u32[]{:S(2)}, u32[]{:S(2)}) collective-permute-start(bf16[864,256]{1,0:T(8,128)(2,1)S(1)} %collective-permute-done.8.rest_4_), channel_id=1, source_target_pairs={{0,4},{4,8},{8,12},{12,14},{14,10},{10,6},{6,2},{2,0},{1,3},{5,1},... | collective-permute-start | bytes 1327112 | tf_op jit(solution)/shard_map/ppermute | solution.py:375
  28.8 0.5 collective-permute-start.6
  29.3 1.3 %prep.1 = (bf16[8,10,16,768]{3,2,1,0:T(8,128)(2,1)S(1)}, bf16[6,10,16,768]{3,2,1,0:T(8,128)(2,1)S(1)}, bf16[256,768]{1,0:T(8,128)(2,1)S(1)}, bf16[3,128,256]{2,1,0:T(8,128)(2,1)S(1)}) custom-call(s32[2,4,16]{2,1,0:T(4,128)S(1)} %bitcast.1, bf16[3,8,16,256]{3,2,1,0:T(8,128)(2,1)S(1)} %collective-permute-done.low, bf16[4,8,16,256]{3,2,1,0:T(8,128)(2,1)S(1)} %copy-done, ...), custom_call_target="tpu_custom_call" | custom-call | bytes 4194304 | tf_op jit(solution)/shard_map/prep/pallas_call | solution.py:350
  30.7 2.1 %collective-permute-done.5.rest_15_.rest_4_ = bf16[864,256]{1,0:T(8,128)(2,1)S(1)} collective-permute-done((bf16[864,256]{1,0:T(8,128)(2,1)S(1)}, bf16[864,256]{1,0:T(8,128)(2,1)S(1)}, u32[]{:S(2)}, u32[]{:S(2)}) %collective-permute-start.5) | collective-permute-done | bytes 442400 | tf_op jit(solution)/shard_map/ppermute | solution.py:374
  32.8 1.9 %collective-permute-start.16 = (bf16[864,256]{1,0:T(8,128)(2,1)S(1)}, bf16[864,256]{1,0:T(8,128)(2,1)S(1)}, u32[]{:S(2)}, u32[]{:S(2)}) collective-permute-start(bf16[864,256]{1,0:T(8,128)(2,1)S(1)} %collective-permute-done.5.rest_15_.rest_4_), channel_id=1, source_target_pairs={{0,4},{4,8},{8,12},{12,14},{14,10},{10,6},{6,2},{2,0},{1,3},{5,1},... | collective-permute-start | bytes 1327112 | tf_op jit(solution)/shard_map/ppermute | solution.py:403
  34.7 2.8 %collective-permute-done.10.rest_5_ = bf16[864,256]{1,0:T(8,128)(2,1)S(1)} collective-permute-done((bf16[864,256]{1,0:T(8,128)(2,1)S(1)}, bf16[864,256]{1,0:T(8,128)(2,1)S(1)}, u32[]{:S(2)}, u32[]{:S(2)}) %collective-permute-start.10) | collective-permute-done | bytes 442400 | tf_op jit(solution)/shard_map/ppermute | solution.py:375
  37.6 2.0 %collective-permute-start.12 = (bf16[432,256]{1,0:T(8,128)(2,1)S(1)}, bf16[432,256]{1,0:T(8,128)(2,1)S(1)}, u32[]{:S(2)}, u32[]{:S(2)}) collective-permute-start(bf16[432,256]{1,0:T(8,128)(2,1)S(1)} %slice.120), channel_id=1, source_target_pairs={{0,4},{4,8},{8,12},{12,14},{14,10},{10,6},{6,2},{2,0},{1,3},{5,1},... | collective-permute-start | bytes 663560 | tf_op jit(solution)/shard_map/ppermute | solution.py:397
  39.5 0.5 collective-permute-start.17
  40.1 4.6 %collective-permute-done.12.rest_6_ = bf16[432,256]{1,0:T(8,128)(2,1)S(1)} collective-permute-done((bf16[432,256]{1,0:T(8,128)(2,1)S(1)}, bf16[432,256]{1,0:T(8,128)(2,1)S(1)}, u32[]{:S(2)}, u32[]{:S(2)}) %collective-permute-start.12) | collective-permute-done | bytes 221216 | tf_op jit(solution)/shard_map/ppermute | solution.py:397
  44.6 0.5 collective-permute-start.18
  45.2 0.9 collective-permute-done.14.rest_10_
  46.1 2.3 %first.1 = (f32[512,256]{1,0:T(8,128)S(1)}, bf16[512,256]{1,0:T(8,128)(2,1)S(1)}, bf16[256,512]{1,0:T(8,128)(2,1)S(1)}) custom-call(bf16[8,10,16,768]{3,2,1,0:T(8,128)(2,1)S(1)} %get-tuple-element.28.sx_ref, bf16[3,128,256]{2,1,0:T(8,128)(2,1)S(1)} %get-tuple-element.29.mask_ref, bf16[432,256]{1,0:T(8,128)(2,1)S(1)} %copy-done.4, ...), custom_call_target="tpu_custom_call" | custom-call | flops 1811939328 | bytes 4194304 | tf_op jit(solution)/shard_map/first/pallas_call | solution.py:350
  48.5 2.0 %collective-permute-start.19 = (bf16[432,256]{1,0:T(8,128)(2,1)S(1)}, bf16[432,256]{1,0:T(8,128)(2,1)S(1)}, u32[]{:S(2)}, u32[]{:S(2)}) collective-permute-start(bf16[432,256]{1,0:T(8,128)(2,1)S(1)} %slice.121), channel_id=1, source_target_pairs={{0,4},{4,8},{8,12},{12,14},{14,10},{10,6},{6,2},{2,0},{1,3},{5,1},... | collective-permute-start | bytes 663560 | tf_op jit(solution)/shard_map/ppermute | solution.py:421
  50.4 2.2 %grad_two.1 = (bf16[3456,256]{1,0:T(8,128)(2,1)S(1)}, bf16[3456,256]{1,0:T(8,128)(2,1)S(1)}) custom-call(bf16[6,10,16,768]{3,2,1,0:T(8,128)(2,1)S(1)} %get-tuple-element.34.sc_ref, bf16[256,512]{1,0:T(8,128)(2,1)S(1)} %get-tuple-element.37.act_t_ref), custom_call_target="tpu_custom_call" | custom-call | flops 1811939328 | bytes 4194304 | tf_op jit(solution)/shard_map/grad_two/pallas_call | solution.py:350
  52.7 1.8 %collective-permute-done.19.rest_17_.rest_6_ = bf16[432,256]{1,0:T(8,128)(2,1)S(1)} collective-permute-done((bf16[432,256]{1,0:T(8,128)(2,1)S(1)}, bf16[432,256]{1,0:T(8,128)(2,1)S(1)}, u32[]{:S(2)}, u32[]{:S(2)}) %collective-permute-start.19) | collective-permute-done | bytes 221216 | tf_op jit(solution)/shard_map/ppermute | solution.py:421
  54.4 0.5 collective-permute-start.22
  55.0 0.0 collective-permute-start.23
  55.0 3.2 %collective-permute-done.20 = bf16[3456,256]{1,0:T(8,128)(2,1)S(1)} collective-permute-done((bf16[3456,256]{1,0:T(8,128)(2,1)S(1)}, bf16[3456,256]{1,0:T(8,128)(2,1)S(1)}, u32[]{:S(2)}, u32[]{:S(2)}) %collective-permute-start.20) | collective-permute-done | bytes 1769504 | tf_op jit(solution)/shard_map/ppermute | solution.py:427
  58.1 0.1 add_convert_fusion.7
  58.2 2.0 %collective-permute-start.21 = (bf16[432,256]{1,0:T(8,128)(2,1)S(1)}, bf16[432,256]{1,0:T(8,128)(2,1)S(1)}, u32[]{:S(2)}, u32[]{:S(2)}) collective-permute-start(bf16[432,256]{1,0:T(8,128)(2,1)S(1)} %add_convert_fusion.7), channel_id=1, source_target_pairs={{0,4},{4,8},{8,12},{12,14},{14,10},{10,6},{6,2},{2,0},{1,3},{5,1},... | collective-permute-start | bytes 663560 | tf_op jit(solution)/shard_map/ppermute | solution.py:443
  60.2 2.4 %back.1.sd_ref = bf16[4,10,16,768]{3,2,1,0:T(8,128)(2,1)S(1)} custom-call(bf16[6,10,16,768]{3,2,1,0:T(8,128)(2,1)S(1)} %get-tuple-element.34.sc_ref, f32[512,256]{1,0:T(8,128)S(1)} %get-tuple-element.43.pre_ref, bf16[3,128,256]{2,1,0:T(8,128)(2,1)S(1)} %get-tuple-element.29.mask_ref, bf16[432,256]{1,0:T(8,128)(2,1)S(1)} %copy-done.2, ...), custom_call_target="tpu_custom_call" | custom-call | flops 1811939328 | bytes 4194304 | tf_op jit(solution)/shard_map/back/pallas_call | solution.py:350
  62.6 2.2 %grad_one.1 = (bf16[3456,256]{1,0:T(8,128)(2,1)S(1)}, bf16[3456,256]{1,0:T(8,128)(2,1)S(1)}) custom-call(bf16[4,10,16,768]{3,2,1,0:T(8,128)(2,1)S(1)} %back.1.sd_ref, bf16[256,768]{1,0:T(8,128)(2,1)S(1)} %get-tuple-element.44.int_ref), custom_call_target="tpu_custom_call" | custom-call | flops 1811939328 | bytes 4194304 | tf_op jit(solution)/shard_map/grad_one/pallas_call | solution.py:350
  64.9 0.1 collective-permute-start.24
  65.0 0.2 add_convert_fusion.4
  65.1 2.5 %collective-permute-start.26 = (bf16[864,256]{1,0:T(8,128)(2,1)S(1)}, bf16[864,256]{1,0:T(8,128)(2,1)S(1)}, u32[]{:S(2)}, u32[]{:S(2)}) collective-permute-start(bf16[864,256]{1,0:T(8,128)(2,1)S(1)} %add_convert_fusion.4), channel_id=1, source_target_pairs={{0,4},{4,8},{8,12},{12,14},{14,10},{10,6},{6,2},{2,0},{1,3},{5,1},... | collective-permute-start | bytes 1327112 | tf_op jit(solution)/shard_map/ppermute | solution.py:461
  67.6 1.1 %collective-permute-done.24 = bf16[3456,256]{1,0:T(8,128)(2,1)S(1)} collective-permute-done((bf16[3456,256]{1,0:T(8,128)(2,1)S(1)}, bf16[3456,256]{1,0:T(8,128)(2,1)S(1)}, u32[]{:S(2)}, u32[]{:S(2)}) %collective-permute-start.24) | collective-permute-done | bytes 1769504 | tf_op jit(solution)/shard_map/ppermute | solution.py:459
  68.6 0.1 add_convert_fusion.6
  68.7 2.6 %collective-permute-start.25 = (bf16[432,256]{1,0:T(8,128)(2,1)S(1)}, bf16[432,256]{1,0:T(8,128)(2,1)S(1)}, u32[]{:S(2)}, u32[]{:S(2)}) collective-permute-start(bf16[432,256]{1,0:T(8,128)(2,1)S(1)} %add_convert_fusion.6), channel_id=1, source_target_pairs={{0,4},{4,8},{8,12},{12,14},{14,10},{10,6},{6,2},{2,0},{1,3},{5,1},... | collective-permute-start | bytes 663560 | tf_op jit(solution)/shard_map/ppermute | solution.py:462
  71.3 4.3 %third.1 = bf16[4,8,16,256]{3,2,1,0:T(8,128)(2,1)} custom-call(bf16[8,10,16,768]{3,2,1,0:T(8,128)(2,1)S(1)} %get-tuple-element.28.sx_ref, bf16[512,256]{1,0:T(8,128)(2,1)S(1)} %get-tuple-element.42.act_ref, bf16[3,128,256]{2,1,0:T(8,128)(2,1)S(1)} %get-tuple-element.29.mask_ref, bf16[432,256]{1,0:T(8,128)(2,1)S(1)} %copy-done.4, ...), custom_call_target="tpu_custom_call" | custom-call | flops 7247757312 | bytes 4194304 | tf_op jit(solution)/shard_map/third/pallas_call | solution.py:350
  75.6 0.3 collective-permute-done.25
  75.8 0.2 add_convert_fusion.5
  76.0 2.5 %collective-permute-start.27 = (bf16[864,256]{1,0:T(8,128)(2,1)S(1)}, bf16[864,256]{1,0:T(8,128)(2,1)S(1)}, u32[]{:S(2)}, u32[]{:S(2)}) collective-permute-start(bf16[864,256]{1,0:T(8,128)(2,1)S(1)} %add_convert_fusion.5), channel_id=1, source_target_pairs={{0,4},{4,8},{8,12},{12,14},{14,10},{10,6},{6,2},{2,0},{1,3},{5,1},... | collective-permute-start | bytes 1327112 | tf_op jit(solution)/shard_map/ppermute | solution.py:476
  78.5 0.2 add_convert_fusion.1
  78.7 1.2 %collective-permute-start.31 = (bf16[864,256]{1,0:T(8,128)(2,1)S(1)}, bf16[864,256]{1,0:T(8,128)(2,1)S(1)}, u32[]{:S(2)}, u32[]{:S(2)}) collective-permute-start(bf16[864,256]{1,0:T(8,128)(2,1)S(1)} %add_convert_fusion.1), channel_id=1, source_target_pairs={{0,4},{4,8},{8,12},{12,14},{14,10},{10,6},{6,2},{2,0},{1,3},{5,1},... | collective-permute-start | bytes 1327112 | tf_op jit(solution)/shard_map/ppermute | solution.py:477
  79.9 4.5 %collective-permute-done.27 = bf16[864,256]{1,0:T(8,128)(2,1)S(1)} collective-permute-done((bf16[864,256]{1,0:T(8,128)(2,1)S(1)}, bf16[864,256]{1,0:T(8,128)(2,1)S(1)}, u32[]{:S(2)}, u32[]{:S(2)}) %collective-permute-start.27) | collective-permute-done | bytes 442400 | tf_op jit(solution)/shard_map/ppermute | solution.py:476
  84.4 0.2 add_convert_fusion.3
  84.6 2.5 %collective-permute-start.28 = (bf16[864,256]{1,0:T(8,128)(2,1)S(1)}, bf16[864,256]{1,0:T(8,128)(2,1)S(1)}, u32[]{:S(2)}, u32[]{:S(2)}) collective-permute-start(bf16[864,256]{1,0:T(8,128)(2,1)S(1)} %add_convert_fusion.3), channel_id=1, source_target_pairs={{0,4},{4,8},{8,12},{12,14},{14,10},{10,6},{6,2},{2,0},{1,3},{5,1},... | collective-permute-start | bytes 1327112 | tf_op jit(solution)/shard_map/ppermute | solution.py:479
  87.0 2.1 %collective-permute-done.31 = bf16[864,256]{1,0:T(8,128)(2,1)S(1)} collective-permute-done((bf16[864,256]{1,0:T(8,128)(2,1)S(1)}, bf16[864,256]{1,0:T(8,128)(2,1)S(1)}, u32[]{:S(2)}, u32[]{:S(2)}) %collective-permute-start.31) | collective-permute-done | bytes 442400 | tf_op jit(solution)/shard_map/ppermute | solution.py:477
  89.1 0.2 add_convert_fusion
  89.3 2.5 %collective-permute-start.32 = (bf16[432,256]{1,0:T(8,128)(2,1)S(1)}, bf16[432,256]{1,0:T(8,128)(2,1)S(1)}, u32[]{:S(2)}, u32[]{:S(2)}) collective-permute-start(bf16[432,256]{1,0:T(8,128)(2,1)S(1)} %get-tuple-element.49), channel_id=1, source_target_pairs={{0,4},{4,8},{8,12},{12,14},{14,10},{10,6},{6,2},{2,0},{1,3},{5,1},... | collective-permute-start | bytes 663560 | tf_op jit(solution)/shard_map/ppermute | solution.py:440
  91.8 2.1 %collective-permute-done.28 = bf16[864,256]{1,0:T(8,128)(2,1)S(1)} collective-permute-done((bf16[864,256]{1,0:T(8,128)(2,1)S(1)}, bf16[864,256]{1,0:T(8,128)(2,1)S(1)}, u32[]{:S(2)}, u32[]{:S(2)}) %collective-permute-start.28) | collective-permute-done | bytes 442400 | tf_op jit(solution)/shard_map/ppermute | solution.py:479
  93.9 0.2 add_convert_fusion.2
  94.1 2.5 %collective-permute-start.29 = (bf16[432,256]{1,0:T(8,128)(2,1)S(1)}, bf16[432,256]{1,0:T(8,128)(2,1)S(1)}, u32[]{:S(2)}, u32[]{:S(2)}) collective-permute-start(bf16[432,256]{1,0:T(8,128)(2,1)S(1)} %get-tuple-element.51), channel_id=1, source_target_pairs={{0,4},{4,8},{8,12},{12,14},{14,10},{10,6},{6,2},{2,0},{1,3},{5,1},... | collective-permute-start | bytes 663560 | tf_op jit(solution)/shard_map/ppermute | solution.py:440
  96.5 2.0 %collective-permute-done.33 = bf16[432,256]{1,0:T(8,128)(2,1)S(1)} collective-permute-done((bf16[432,256]{1,0:T(8,128)(2,1)S(1)}, bf16[432,256]{1,0:T(8,128)(2,1)S(1)}, u32[]{:S(2)}, u32[]{:S(2)}) %collective-permute-start.33) | collective-permute-done | bytes 221216 | tf_op jit(solution)/shard_map/ppermute | solution.py:441
  98.5 0.9 add_multiply_fusion
  99.4 1.6 %collective-permute-done.29 = bf16[432,256]{1,0:T(8,128)(2,1)S(1)} collective-permute-done((bf16[432,256]{1,0:T(8,128)(2,1)S(1)}, bf16[432,256]{1,0:T(8,128)(2,1)S(1)}, u32[]{:S(2)}, u32[]{:S(2)}) %collective-permute-start.29) | collective-permute-done | bytes 221216 | tf_op jit(solution)/shard_map/ppermute | solution.py:440
  101.0 2.3 %collective-permute-done.30 = bf16[432,256]{1,0:T(8,128)(2,1)S(1)} collective-permute-done((bf16[432,256]{1,0:T(8,128)(2,1)S(1)}, bf16[432,256]{1,0:T(8,128)(2,1)S(1)}, u32[]{:S(2)}, u32[]{:S(2)}) %collective-permute-start.30) | collective-permute-done | bytes 221216 | tf_op jit(solution)/shard_map/ppermute | solution.py:441
  103.3 0.9 add_multiply_fusion.1
  (41 shorter events, 0.3 us)
Async XLA Ops:
  0.6 28.2 %copy-start.4 = (bf16[432,256]{1,0:T(8,128)(2,1)S(1)}, bf16[432,256]{1,0:T(8,128)(2,1)}, u32[]{:S(2)}) copy-start(bf16[432,256]{1,0:T(8,128)(2,1)} %rest_0_.4) | copy-start | bytes 663556
  0.6 28.7 %copy-start.1 = (bf16[4,8,16,256]{3,2,1,0:T(8,128)(2,1)S(1)}, bf16[4,8,16,256]{3,2,1,0:T(8,128)(2,1)}, u32[]{:S(2)}) copy-start(bf16[4,8,16,256]{3,2,1,0:T(8,128)(2,1)} %c_own.1) | copy-start | bytes 786436
  0.7 28.7 %copy-start = (bf16[4,8,16,256]{3,2,1,0:T(8,128)(2,1)S(1)}, bf16[4,8,16,256]{3,2,1,0:T(8,128)(2,1)}, u32[]{:S(2)}) copy-start(bf16[4,8,16,256]{3,2,1,0:T(8,128)(2,1)} %f_own.1) | copy-start | bytes 786436
  0.7 15.7 %copy-start.2 = (bf16[432,256]{1,0:T(8,128)(2,1)S(1)}, bf16[432,256]{1,0:T(8,128)(2,1)}, u32[]{:S(2)}) copy-start(bf16[432,256]{1,0:T(8,128)(2,1)} %rest_0_.5) | copy-start | bytes 663556
  0.7 28.7 %copy-start.3 = (s32[16,2,4]{0,2,1:T(4,128)S(1)}, s32[16,2,4]{0,2,1:T(4,128)}, u32[]{:S(2)}) copy-start(s32[16,2,4]{0,2,1:T(4,128)} %param.9) | copy-start | bytes 1540
  0.7 11.0 %collective-permute-start.7 = (bf16[432,256]{1,0:T(8,128)(2,1)}, bf16[432,256]{1,0:T(8,128)(2,1)S(1)}, u32[]{:S(2)}, u32[]{:S(2)}) collective-permute-start(bf16[432,256]{1,0:T(8,128)(2,1)} %rest_0_.4), channel_id=1, source_target_pairs={{1,4},{5,8},{9,12},{13,14},{15,10},{11,6},{7,2},{3,0},{0,3},{4,1},... | collective-permute-start | bytes 663560 | tf_op jit(solution)/shard_map/ppermute | solution.py:364
  3.2 7.2 %collective-permute-start.2 = (bf16[432,256]{1,0:T(8,128)(2,1)}, bf16[432,256]{1,0:T(8,128)(2,1)S(1)}, u32[]{:S(2)}, u32[]{:S(2)}) collective-permute-start(bf16[432,256]{1,0:T(8,128)(2,1)} %rest_0_.4), channel_id=1, source_target_pairs={{0,4},{4,8},{8,12},{12,14},{14,10},{10,6},{6,2},{2,0},{1,3},{5,1},... | collective-permute-start | bytes 663560 | tf_op jit(solution)/shard_map/ppermute | solution.py:364
  5.7 9.6 %collective-permute-start = (bf16[3,8,16,256]{3,2,1,0:T(8,128)(2,1)S(1)}, bf16[3,8,16,256]{3,2,1,0:T(8,128)(2,1)S(1)}, u32[]{:S(2)}, u32[]{:S(2)}) collective-permute-start(bf16[3,8,16,256]{3,2,1,0:T(8,128)(2,1)S(1)} %pad_maximum_fusion.1), channel_id=1, source_target_pairs={{0,1},{1,2},{2,3},{3,4},{4,5},{5,6},{6,7},{7,8},{8,9},{9,10},{10,1... | collective-permute-start | bytes 589832 | tf_op jit(solution)/shard_map/ppermute | solution.py:367
  5.9 9.5 %collective-permute-start.1 = (bf16[3,8,16,256]{3,2,1,0:T(8,128)(2,1)S(1)}, bf16[3,8,16,256]{3,2,1,0:T(8,128)(2,1)S(1)}, u32[]{:S(2)}, u32[]{:S(2)}) collective-permute-start(bf16[3,8,16,256]{3,2,1,0:T(8,128)(2,1)S(1)} %pad_maximum_fusion.2), channel_id=1, source_target_pairs={{0,15},{1,0},{2,1},{3,2},{4,3},{5,4},{6,5},{7,6},{8,7},{9,8},{10,9... | collective-permute-start | bytes 589832 | tf_op jit(solution)/shard_map/ppermute | solution.py:368
  10.3 7.0 %collective-permute-start.3 = (bf16[432,256]{1,0:T(8,128)(2,1)}, bf16[432,256]{1,0:T(8,128)(2,1)S(1)}, u32[]{:S(2)}, u32[]{:S(2)}) collective-permute-start(bf16[432,256]{1,0:T(8,128)(2,1)} %rest_0_.5), channel_id=1, source_target_pairs={{0,4},{4,8},{8,12},{12,14},{14,10},{10,6},{6,2},{2,0},{1,3},{5,1},... | collective-permute-start | bytes 663560 | tf_op jit(solution)/shard_map/ppermute | solution.py:366
  15.3 11.1 %collective-permute-start.9 = (bf16[864,256]{1,0:T(8,128)(2,1)S(1)}, bf16[864,256]{1,0:T(8,128)(2,1)S(1)}, u32[]{:S(2)}, u32[]{:S(2)}) collective-permute-start(bf16[864,256]{1,0:T(8,128)(2,1)S(1)} %pad_maximum_fusion), channel_id=1, source_target_pairs={{0,1},{1,0},{2,3},{3,2},{4,5},{5,4},{6,7},{7,6},{8,9},{9,8},{10,11... | collective-permute-start | bytes 1327112 | tf_op jit(solution)/shard_map/ppermute | solution.py:372
  15.3 11.1 %collective-permute-start.8 = (bf16[864,256]{1,0:T(8,128)(2,1)S(1)}, bf16[864,256]{1,0:T(8,128)(2,1)S(1)}, u32[]{:S(2)}, u32[]{:S(2)}) collective-permute-start(bf16[864,256]{1,0:T(8,128)(2,1)S(1)} %pad_maximum_fusion), channel_id=1, source_target_pairs={{0,4},{4,8},{8,12},{12,14},{14,10},{10,6},{6,2},{2,0},{1,3},{5,1},... | collective-permute-start | bytes 1327112 | tf_op jit(solution)/shard_map/ppermute | solution.py:371
  16.4 7.7 %collective-permute-start.4 = (bf16[432,256]{1,0:T(8,128)(2,1)S(1)}, bf16[432,256]{1,0:T(8,128)(2,1)S(1)}, u32[]{:S(2)}, u32[]{:S(2)}) collective-permute-start(bf16[432,256]{1,0:T(8,128)(2,1)S(1)} %copy-done.2), channel_id=1, source_target_pairs={{1,4},{5,8},{9,12},{13,14},{15,10},{11,6},{7,2},{3,0},{0,3},{4,1},... | collective-permute-start | bytes 663560 | tf_op jit(solution)/shard_map/ppermute | solution.py:366
  24.1 6.6 %collective-permute-start.15 = (bf16[864,256]{1,0:T(8,128)(2,1)S(1)}, bf16[864,256]{1,0:T(8,128)(2,1)S(1)}, u32[]{:S(2)}, u32[]{:S(2)}) collective-permute-start(bf16[864,256]{1,0:T(8,128)(2,1)S(1)} %constant_dynamic-update-slice_fusion), channel_id=1, source_target_pairs={{0,1},{1,0},{2,3},{3,2},{4,5},{5,4},{6,7},{7,6},{8,9},{9,8},{10,11... | collective-permute-start | bytes 1327112 | tf_op jit(solution)/shard_map/ppermute | solution.py:402
  24.5 8.3 %collective-permute-start.5 = (bf16[864,256]{1,0:T(8,128)(2,1)S(1)}, bf16[864,256]{1,0:T(8,128)(2,1)S(1)}, u32[]{:S(2)}, u32[]{:S(2)}) collective-permute-start(bf16[864,256]{1,0:T(8,128)(2,1)S(1)} %constant_dynamic-update-slice_fusion), channel_id=1, source_target_pairs={{0,4},{4,8},{8,12},{12,14},{14,10},{10,6},{6,2},{2,0},{1,3},{5,1},... | collective-permute-start | bytes 1327112 | tf_op jit(solution)/shard_map/ppermute | solution.py:374
  26.4 11.1 %collective-permute-start.10 = (bf16[864,256]{1,0:T(8,128)(2,1)S(1)}, bf16[864,256]{1,0:T(8,128)(2,1)S(1)}, u32[]{:S(2)}, u32[]{:S(2)}) collective-permute-start(bf16[864,256]{1,0:T(8,128)(2,1)S(1)} %collective-permute-done.8.rest_4_), channel_id=1, source_target_pairs={{0,4},{4,8},{8,12},{12,14},{14,10},{10,6},{6,2},{2,0},{1,3},{5,1},... | collective-permute-start | bytes 1327112 | tf_op jit(solution)/shard_map/ppermute | solution.py:375
  28.8 8.7 %collective-permute-start.11 = (bf16[864,256]{1,0:T(8,128)(2,1)S(1)}, bf16[864,256]{1,0:T(8,128)(2,1)S(1)}, u32[]{:S(2)}, u32[]{:S(2)}) collective-permute-start(bf16[864,256]{1,0:T(8,128)(2,1)S(1)} %collective-permute-done.8.rest_4_), channel_id=1, source_target_pairs={{0,1},{1,0},{2,3},{3,2},{4,5},{5,4},{6,7},{7,6},{8,9},{9,8},{10,11... | collective-permute-start | bytes 1327112 | tf_op jit(solution)/shard_map/ppermute | solution.py:376
  28.8 8.7 %collective-permute-start.6 = (bf16[432,256]{1,0:T(8,128)(2,1)S(1)}, bf16[432,256]{1,0:T(8,128)(2,1)S(1)}, u32[]{:S(2)}, u32[]{:S(2)}) collective-permute-start(bf16[432,256]{1,0:T(8,128)(2,1)S(1)} %copy-done.4), channel_id=1, source_target_pairs={{0,1},{1,0},{2,3},{3,2},{4,5},{5,4},{6,7},{7,6},{8,9},{9,8},{10,11... | collective-permute-start | bytes 663560 | tf_op jit(solution)/shard_map/ppermute | solution.py:377
  32.8 12.4 %collective-permute-start.16 = (bf16[864,256]{1,0:T(8,128)(2,1)S(1)}, bf16[864,256]{1,0:T(8,128)(2,1)S(1)}, u32[]{:S(2)}, u32[]{:S(2)}) collective-permute-start(bf16[864,256]{1,0:T(8,128)(2,1)S(1)} %collective-permute-done.5.rest_15_.rest_4_), channel_id=1, source_target_pairs={{0,4},{4,8},{8,12},{12,14},{14,10},{10,6},{6,2},{2,0},{1,3},{5,1},... | collective-permute-start | bytes 1327112 | tf_op jit(solution)/shard_map/ppermute | solution.py:403
  37.6 7.1 %collective-permute-start.12 = (bf16[432,256]{1,0:T(8,128)(2,1)S(1)}, bf16[432,256]{1,0:T(8,128)(2,1)S(1)}, u32[]{:S(2)}, u32[]{:S(2)}) collective-permute-start(bf16[432,256]{1,0:T(8,128)(2,1)S(1)} %slice.120), channel_id=1, source_target_pairs={{0,4},{4,8},{8,12},{12,14},{14,10},{10,6},{6,2},{2,0},{1,3},{5,1},... | collective-permute-start | bytes 663560 | tf_op jit(solution)/shard_map/ppermute | solution.py:397
  39.5 5.6 %collective-permute-start.13 = (bf16[864,256]{1,0:T(8,128)(2,1)S(1)}, bf16[864,256]{1,0:T(8,128)(2,1)S(1)}, u32[]{:S(2)}, u32[]{:S(2)}) collective-permute-start(bf16[864,256]{1,0:T(8,128)(2,1)S(1)} %collective-permute-done.10.rest_5_), channel_id=1, source_target_pairs={{0,1},{1,0},{2,3},{3,2},{4,5},{5,4},{6,7},{7,6},{8,9},{9,8},{10,11... | collective-permute-start | bytes 1327112 | tf_op jit(solution)/shard_map/ppermute | solution.py:398
  39.5 8.9 %collective-permute-start.17 = (bf16[864,256]{1,0:T(8,128)(2,1)S(1)}, bf16[864,256]{1,0:T(8,128)(2,1)S(1)}, u32[]{:S(2)}, u32[]{:S(2)}) collective-permute-start(bf16[864,256]{1,0:T(8,128)(2,1)S(1)} %collective-permute-done.5.rest_15_.rest_4_), channel_id=1, source_target_pairs={{0,1},{1,0},{2,3},{3,2},{4,5},{5,4},{6,7},{7,6},{8,9},{9,8},{10,11... | collective-permute-start | bytes 1327112 | tf_op jit(solution)/shard_map/ppermute | solution.py:404
  44.6 1.5 %collective-permute-start.14 = (bf16[432,256]{1,0:T(8,128)(2,1)S(1)}, bf16[432,256]{1,0:T(8,128)(2,1)S(1)}, u32[]{:S(2)}, u32[]{:S(2)}) collective-permute-start(bf16[432,256]{1,0:T(8,128)(2,1)S(1)} %collective-permute-done.12.rest_6_), channel_id=1, source_target_pairs={{0,1},{1,0},{2,3},{3,2},{4,5},{5,4},{6,7},{7,6},{8,9},{9,8},{10,11... | collective-permute-start | bytes 663560 | tf_op jit(solution)/shard_map/ppermute | solution.py:398
  44.6 3.8 %collective-permute-start.18 = (bf16[432,256]{1,0:T(8,128)(2,1)S(1)}, bf16[432,256]{1,0:T(8,128)(2,1)S(1)}, u32[]{:S(2)}, u32[]{:S(2)}) collective-permute-start(bf16[432,256]{1,0:T(8,128)(2,1)S(1)} %copy-done.2), channel_id=1, source_target_pairs={{0,1},{1,0},{2,3},{3,2},{4,5},{5,4},{6,7},{7,6},{8,9},{9,8},{10,11... | collective-permute-start | bytes 663560 | tf_op jit(solution)/shard_map/ppermute | solution.py:405
  48.5 6.0 %collective-permute-start.19 = (bf16[432,256]{1,0:T(8,128)(2,1)S(1)}, bf16[432,256]{1,0:T(8,128)(2,1)S(1)}, u32[]{:S(2)}, u32[]{:S(2)}) collective-permute-start(bf16[432,256]{1,0:T(8,128)(2,1)S(1)} %slice.121), channel_id=1, source_target_pairs={{0,4},{4,8},{8,12},{12,14},{14,10},{10,6},{6,2},{2,0},{1,3},{5,1},... | collective-permute-start | bytes 663560 | tf_op jit(solution)/shard_map/ppermute | solution.py:421
  54.4 3.7 %collective-permute-start.20 = (bf16[3456,256]{1,0:T(8,128)(2,1)S(1)}, bf16[3456,256]{1,0:T(8,128)(2,1)S(1)}, u32[]{:S(2)}, u32[]{:S(2)}) collective-permute-start(bf16[3456,256]{1,0:T(8,128)(2,1)S(1)} %get-tuple-element.41), channel_id=1, source_target_pairs={{0,1},{1,0},{2,3},{3,2},{4,5},{5,4},{6,7},{7,6},{8,9},{9,8},{10,11... | collective-permute-start | bytes 5308424 | tf_op jit(solution)/shard_map/ppermute | solution.py:427
  54.4 5.7 %collective-permute-start.22 = (bf16[864,256]{1,0:T(8,128)(2,1)S(1)}, bf16[864,256]{1,0:T(8,128)(2,1)S(1)}, u32[]{:S(2)}, u32[]{:S(2)}) collective-permute-start(bf16[864,256]{1,0:T(8,128)(2,1)S(1)} %collective-permute-done.16.rest_16_.rest_5_), channel_id=1, source_target_pairs={{0,1},{1,0},{2,3},{3,2},{4,5},{5,4},{6,7},{7,6},{8,9},{9,8},{10,11... | collective-permute-start | bytes 1327112 | tf_op jit(solution)/shard_map/ppermute | solution.py:422
  55.0 5.2 %collective-permute-start.23 = (bf16[432,256]{1,0:T(8,128)(2,1)S(1)}, bf16[432,256]{1,0:T(8,128)(2,1)S(1)}, u32[]{:S(2)}, u32[]{:S(2)}) collective-permute-start(bf16[432,256]{1,0:T(8,128)(2,1)S(1)} %collective-permute-done.19.rest_17_.rest_6_), channel_id=1, source_target_pairs={{0,1},{1,0},{2,3},{3,2},{4,5},{5,4},{6,7},{7,6},{8,9},{9,8},{10,11... | collective-permute-start | bytes 663560 | tf_op jit(solution)/shard_map/ppermute | solution.py:422
  58.2 6.7 %collective-permute-start.21 = (bf16[432,256]{1,0:T(8,128)(2,1)S(1)}, bf16[432,256]{1,0:T(8,128)(2,1)S(1)}, u32[]{:S(2)}, u32[]{:S(2)}) collective-permute-start(bf16[432,256]{1,0:T(8,128)(2,1)S(1)} %add_convert_fusion.7), channel_id=1, source_target_pairs={{0,4},{4,8},{8,12},{12,14},{14,10},{10,6},{6,2},{2,0},{1,3},{5,1},... | collective-permute-start | bytes 663560 | tf_op jit(solution)/shard_map/ppermute | solution.py:443
  64.9 3.8 %collective-permute-start.24 = (bf16[3456,256]{1,0:T(8,128)(2,1)S(1)}, bf16[3456,256]{1,0:T(8,128)(2,1)S(1)}, u32[]{:S(2)}, u32[]{:S(2)}) collective-permute-start(bf16[3456,256]{1,0:T(8,128)(2,1)S(1)} %get-tuple-element.47), channel_id=1, source_target_pairs={{0,1},{1,0},{2,3},{3,2},{4,5},{5,4},{6,7},{7,6},{8,9},{9,8},{10,11... | collective-permute-start | bytes 5308424 | tf_op jit(solution)/shard_map/ppermute | solution.py:459
  65.1 10.9 %collective-permute-start.26 = (bf16[864,256]{1,0:T(8,128)(2,1)S(1)}, bf16[864,256]{1,0:T(8,128)(2,1)S(1)}, u32[]{:S(2)}, u32[]{:S(2)}) collective-permute-start(bf16[864,256]{1,0:T(8,128)(2,1)S(1)} %add_convert_fusion.4), channel_id=1, source_target_pairs={{0,4},{4,8},{8,12},{12,14},{14,10},{10,6},{6,2},{2,0},{1,3},{5,1},... | collective-permute-start | bytes 1327112 | tf_op jit(solution)/shard_map/ppermute | solution.py:461
  68.7 7.2 %collective-permute-start.25 = (bf16[432,256]{1,0:T(8,128)(2,1)S(1)}, bf16[432,256]{1,0:T(8,128)(2,1)S(1)}, u32[]{:S(2)}, u32[]{:S(2)}) collective-permute-start(bf16[432,256]{1,0:T(8,128)(2,1)S(1)} %add_convert_fusion.6), channel_id=1, source_target_pairs={{0,4},{4,8},{8,12},{12,14},{14,10},{10,6},{6,2},{2,0},{1,3},{5,1},... | collective-permute-start | bytes 663560 | tf_op jit(solution)/shard_map/ppermute | solution.py:462
  76.0 8.4 %collective-permute-start.27 = (bf16[864,256]{1,0:T(8,128)(2,1)S(1)}, bf16[864,256]{1,0:T(8,128)(2,1)S(1)}, u32[]{:S(2)}, u32[]{:S(2)}) collective-permute-start(bf16[864,256]{1,0:T(8,128)(2,1)S(1)} %add_convert_fusion.5), channel_id=1, source_target_pairs={{0,4},{4,8},{8,12},{12,14},{14,10},{10,6},{6,2},{2,0},{1,3},{5,1},... | collective-permute-start | bytes 1327112 | tf_op jit(solution)/shard_map/ppermute | solution.py:476
  78.7 10.5 %collective-permute-start.31 = (bf16[864,256]{1,0:T(8,128)(2,1)S(1)}, bf16[864,256]{1,0:T(8,128)(2,1)S(1)}, u32[]{:S(2)}, u32[]{:S(2)}) collective-permute-start(bf16[864,256]{1,0:T(8,128)(2,1)S(1)} %add_convert_fusion.1), channel_id=1, source_target_pairs={{0,4},{4,8},{8,12},{12,14},{14,10},{10,6},{6,2},{2,0},{1,3},{5,1},... | collective-permute-start | bytes 1327112 | tf_op jit(solution)/shard_map/ppermute | solution.py:477
  84.6 9.3 %collective-permute-start.28 = (bf16[864,256]{1,0:T(8,128)(2,1)S(1)}, bf16[864,256]{1,0:T(8,128)(2,1)S(1)}, u32[]{:S(2)}, u32[]{:S(2)}) collective-permute-start(bf16[864,256]{1,0:T(8,128)(2,1)S(1)} %add_convert_fusion.3), channel_id=1, source_target_pairs={{0,4},{4,8},{8,12},{12,14},{14,10},{10,6},{6,2},{2,0},{1,3},{5,1},... | collective-permute-start | bytes 1327112 | tf_op jit(solution)/shard_map/ppermute | solution.py:479
  89.3 7.2 %collective-permute-start.32 = (bf16[432,256]{1,0:T(8,128)(2,1)S(1)}, bf16[432,256]{1,0:T(8,128)(2,1)S(1)}, u32[]{:S(2)}, u32[]{:S(2)}) collective-permute-start(bf16[432,256]{1,0:T(8,128)(2,1)S(1)} %get-tuple-element.49), channel_id=1, source_target_pairs={{0,4},{4,8},{8,12},{12,14},{14,10},{10,6},{6,2},{2,0},{1,3},{5,1},... | collective-permute-start | bytes 663560 | tf_op jit(solution)/shard_map/ppermute | solution.py:440
  91.8 6.7 %collective-permute-start.33 = (bf16[432,256]{1,0:T(8,128)(2,1)S(1)}, bf16[432,256]{1,0:T(8,128)(2,1)S(1)}, u32[]{:S(2)}, u32[]{:S(2)}) collective-permute-start(bf16[432,256]{1,0:T(8,128)(2,1)S(1)} %get-tuple-element.50), channel_id=1, source_target_pairs={{0,5},{4,9},{8,13},{12,15},{14,11},{10,7},{6,3},{2,1},{1,2},{5,0},... | collective-permute-start | bytes 663560 | tf_op jit(solution)/shard_map/ppermute | solution.py:441
  94.1 6.9 %collective-permute-start.29 = (bf16[432,256]{1,0:T(8,128)(2,1)S(1)}, bf16[432,256]{1,0:T(8,128)(2,1)S(1)}, u32[]{:S(2)}, u32[]{:S(2)}) collective-permute-start(bf16[432,256]{1,0:T(8,128)(2,1)S(1)} %get-tuple-element.51), channel_id=1, source_target_pairs={{0,4},{4,8},{8,12},{12,14},{14,10},{10,6},{6,2},{2,0},{1,3},{5,1},... | collective-permute-start | bytes 663560 | tf_op jit(solution)/shard_map/ppermute | solution.py:440
  96.5 6.7 %collective-permute-start.30 = (bf16[432,256]{1,0:T(8,128)(2,1)S(1)}, bf16[432,256]{1,0:T(8,128)(2,1)S(1)}, u32[]{:S(2)}, u32[]{:S(2)}) collective-permute-start(bf16[432,256]{1,0:T(8,128)(2,1)S(1)} %get-tuple-element.52), channel_id=1, source_target_pairs={{0,5},{4,9},{8,13},{12,15},{14,11},{10,7},{6,3},{2,1},{1,2},{5,0},... | collective-permute-start | bytes 663560 | tf_op jit(solution)/shard_map/ppermute | solution.py:441

commit v5 on v4

--- a/solution.py
+++ b/solution.py
@@ -162,11 +162,10 @@
         store_shifted(sc_ref, x0, rows(value, side), ny, nz, channels)
 
 
-PIECES = (
+PAIRS = (
     (0, False, False),
     (0, False, True),
     (1, False, False),
-    (1, False, True),
     (2, False, False),
     (3, False, False),
     (4, False, False),
@@ -175,13 +174,14 @@
     (3, True, False),
     (4, True, False),
 )
-
-
-def fill_weight(pieces, w_ref):
+SHARDS = PAIRS[:2] + tuple((hop, False, flip) for hop in (1, 2, 3) for flip in (False, True)) + PAIRS[5:]
+
+
+def fill_weight(kinds, pieces, w_ref):
     tile = lax.axis_index("tiles")
     core = tile % 2
     rows = w_ref.shape[0] // 16
-    for piece, (hop, crossed, flip) in zip(pieces, PIECES):
+    for piece, (hop, crossed, flip) in zip(pieces, kinds):
         holder = 1 - core if crossed else core
         for half in range(piece.shape[0] // rows):
             start = shard_rows(tile, holder, hop, flip or half == 1, rows)
@@ -232,12 +232,13 @@
     return (value.reshape(-1, area, channels) * own).reshape(-1, channels)
 
 
-def first_kernel(n, sx_ref, mask_ref, *rest):
+def first_kernel(sx_ref, mask_ref, *rest):
+    n = len(PAIRS)
     pieces, (pre_ref, act_ref, act_t_ref, w_ref) = rest[:n], rest[n:]
     area, channels = mask_ref.shape[1:]
     ny = sx_ref.shape[1] - 2
     depth = pre_ref.shape[0] // area
-    fill_weight(pieces, w_ref)
+    fill_weight(PAIRS, pieces, w_ref)
     pre = conv(sx_ref, w_ref, 1, depth, ny, channels)
     pre_ref[...] = pre
     act = masked(pre * jax.nn.sigmoid(pre), mask_ref, 1).astype(BF)
@@ -259,12 +260,13 @@
     split_shards(g_ref, keep_ref, send_ref)
 
 
-def back_kernel(n, sc_ref, pre_ref, mask_ref, *rest):
+def back_kernel(sc_ref, pre_ref, mask_ref, *rest):
+    n = len(SHARDS)
     pieces, (sd_ref, w_ref) = rest[:n], rest[n:]
     area, channels = mask_ref.shape[1:]
     ny, nz = sc_ref.shape[1] - 2, sc_ref.shape[2]
     depth = pre_ref.shape[0] // area
-    fill_weight(pieces, w_ref)
+    fill_weight(SHARDS, pieces, w_ref)
     acc = None
     for p in range(3):
         for q in range(3):
@@ -296,13 +298,14 @@
     split_shards(g_ref, keep_ref, send_ref)
 
 
-def third_kernel(n, sx_ref, act_ref, mask_ref, *rest):
-    out_ref, w_ref, v_ref, sa_ref = rest[2 * n :]
+def third_kernel(sx_ref, act_ref, mask_ref, *rest):
+    n = len(PAIRS)
+    pieces, (out_ref, w_ref, v_ref, sa_ref) = rest[:-4], rest[-4:]
     area, channels = mask_ref.shape[1:]
     ny, nz = sx_ref.shape[1] - 2, sx_ref.shape[2]
     depth = act_ref.shape[0] // area
-    fill_weight(rest[:n], w_ref)
-    fill_weight(rest[n : 2 * n], v_ref)
+    fill_weight(PAIRS, pieces[:n], w_ref)
+    fill_weight(SHARDS, pieces[n:], v_ref)
     clear_edges(sa_ref, ny)
     store_shifted(sa_ref, 1, act_ref[...], ny, nz, channels)
     for x0, side in ((0, 0), (1 + depth, 2)):
@@ -362,19 +365,17 @@
         )(*operands)
 
     a1 = [onward(weight_one), gather_across(weight_one)]
-    weight_late = after(weight_two, a1[0])
-    b1 = [onward(weight_late), gather_across(weight_late)]
+    x1 = onward(after(weight_two, a1[0]))
     low = up(jnp.concatenate([features[-2:], cotangent[-1:]]))
     high = down(jnp.concatenate([features[:2], cotangent[:1]]))
-
-    a1_pair = after(jnp.concatenate(a1), low, high)
-    a2 = onward(a1_pair)
-    qa1 = sibling(a1_pair)
-    b1_pair = jnp.concatenate(b1)
-    b2 = onward(b1_pair)
-    a3 = onward(after(a2, qa1, b1_pair))
+    a1 = jnp.concatenate(a1)
+    a2 = onward(a1)
+    qa1 = sibling(a1)
+    y1 = gather_across(after(weight_two, a1))
+    a3 = onward(after(a2, x1, low, high))
     qa2 = sibling(a2)
     other_one = sibling(weight_one)
+    x2 = onward(after(x1, a2))
     sx, sc, in_t, near = kernel(
         prep_kernel,
         "prep",
@@ -394,17 +395,16 @@
         high,
         smem=1,
     )
-    a4 = onward(after(a3[:rows], qa2, other_one, sx))
+    a4 = onward(after(a3[:rows], y1, qa1, qa2, other_one, sx))
     qa3, qa4 = sibling(a3), sibling(a4)
-    ones = [weight_one, other_one, *a1, a2, a3, a4, qa1, qa2, qa3, qa4]
-    n = len(ones)
-
-    qb1 = sibling(b1_pair)
-    b3 = onward(after(b2, qb1))
-    qb2 = sibling(b2)
+    ones = [weight_one, other_one, a1, a2, a3, a4, qa1, qa2, qa3, qa4]
+
+    y2 = onward(after(y1, a3))
+    qb1 = sibling(jnp.concatenate([x1, y1]))
     other_two = sibling(weight_two)
+    x3 = onward(after(x2, qb1, other_two))
     pre, act, act_t = kernel(
-        functools.partial(first_kernel, n),
+        first_kernel,
         "first",
         8,
         1,
@@ -414,18 +414,17 @@
             shape((channels, depth * area), BF),
         ),
         [weights],
-        after(sx, b2),
+        after(sx, x2),
         near,
         *ones,
     )
-    b4 = onward(after(b3[:rows], qb2, other_two, act_t))
-    qb3, qb4 = sibling(b3), sibling(b4)
-    twos = [weight_two, other_two, *b1, b2, b3, b4, qb1, qb2, qb3, qb4]
+    qb2 = sibling(jnp.concatenate([x2, y2]))
     keep_two, send_two = kernel(
-        grad_two_kernel, "grad_two", 8, 1, shards, [weights], sc, after(act_t, b3)
-    )
-    got_two = sibling(after(send_two, b4))
-
+        grad_two_kernel, "grad_two", 8, 1, shards, [weights], sc, after(act_t, y2)
+    )
+    got_two = sibling(after(send_two, x3))
+    y3 = onward(after(y2, act_t))
+    x4 = onward(after(x3, qb2))
     def both(keep, got, lo, hi):
         return keep[lo * rows : hi * rows].astype(F32) + got[lo * rows : hi * rows].astype(F32)
 
@@ -440,9 +439,13 @@
         total = both(keep, got, 7, 8) + onward(message[:rows]).astype(F32)
         return (total + scatter_across(message[rows:]).astype(F32)) * loss_scale
 
-    two = onward(step(keep_two, got_two, None, 0))
+    message = step(keep_two, got_two, None, 0)
+    two = onward(message)
+    qb3 = sibling(jnp.concatenate([x3, after(y3, message)]))
+    qb4 = sibling(x4)
+    twos = [weight_two, other_two, x1, y1, x2, y2, x3, y3, x4, qb1, qb2, qb3, qb4]
     delta = kernel(
-        functools.partial(back_kernel, n),
+        back_kernel,
         "back",
         8,
         1,
@@ -461,7 +464,7 @@
     two = onward(step(keep_two, got_two, two, 1))
     one = onward(step(keep_one, got_one, None, 0))
     features_out = kernel(
-        functools.partial(third_kernel, n),
+        third_kernel,
         "third",
         14,
         4,

time: 104 us -> 108 us (1.038)
  starting transfers between devices: 41.2 us -> 46.6 us
  waiting for transfers between devices: 42.3 us -> 40 us
    ppermute x15 -> x17, waiting for transfers between devices: 21.9 us -> 13.9 us  [the longest x1 4.22 us: on_ring(): y1 = gather_across(after(weight_two, a1))]
    ppermute x15 -> x17, starting transfers between devices: 16.3 us -> 21.9 us  [the longest x1 2.68 us: on_ring(): x2 = onward(after(x1, a2))]
    ppermute x2, waiting for transfers between devices: 0.01 us -> 4.75 us  [on_ring(): a1 = [onward(weight_one), gather_across(weight_one)]]
    ppermute x1, waiting for transfers between devices: 3.58 us -> 5.08 us  [on_ring(): low = up(jnp.concatenate([features[-2:], cotangent[-1:]]))]
    ppermute x1, starting transfers between devices: 0.51 us -> 1.85 us  [on_ring(): other_one = sibling(weight_one)]
    ppermute x1, starting transfers between devices: 4.44 us -> 3.21 us  [on_ring(): high = down(jnp.concatenate([features[:2], cotangent[:1]]))]
  transfers between devices with their start and end apart: 34 -> 36, of which waited for: 17 -> 17; matrix products, arithmetic and copies ran while one was open for 4% -> 4% of each run, Pallas kernels for 14% -> 14%
where the time goes in v5:
time: 108 us; the launch traced here: 107 us
  starting transfers between devices  46.6 us (43%)
  waiting for transfers between devices  40 us (37%)
  Pallas kernels  14.8 us (14%)
  other arithmetic  2.93 us (3%)
  local copies, waits for them, and re-layouts  2 us (2%)
    pallas_call x6, Pallas kernels, kernel(): pl.pallas_call(body, name=name, out_shape=outs, in_specs=[pl.BlockSpec(me...  14.8 us
    ppermute x1, waiting for transfers between devices, on_ring(): low = up(jnp.concatenate([features[-2:], cotangent[-1:]]))  5.08 us
    ppermute x2, waiting for transfers between devices, on_ring(): a1 = [onward(weight_one), gather_across(weight_one)]  4.75 us
    ppermute x2, starting transfers between devices, finish(): total = both(keep, got, 7, 8) + onward(message[:rows]).astype(F32)  4.55 us
    ppermute x1, waiting for transfers between devices, on_ring(): one = onward(after(step(keep_one, got_one, one, 1), features_out, two))  4.27 us
    ppermute x1, waiting for transfers between devices, on_ring(): y1 = gather_across(after(weight_two, a1))  4.22 us
    ppermute x2, waiting for transfers between devices, finish(): return (total + scatter_across(message[rows:]).astype(F32)) * loss_scale  4.11 us
    ppermute x2, starting transfers between devices, on_ring(): a1 = [onward(weight_one), gather_across(weight_one)]  3.75 us
  transfers between devices with their start and end apart: 36, of which 17 were waited for; matrix products, arithmetic and copies ran while one was open for 4% of the time, Pallas kernels for 14%

profile of v5, /device:TPU:0, one launch (start us, length us, event | category | flops | bytes accessed | tf_op | source)
XLA Modules:
  0.0 107.3 jit_solution(4066610265600258207)
XLA Ops:
  0.7 3.1 %collective-permute-start.2 = (bf16[432,256]{1,0:T(8,128)(2,1)}, bf16[432,256]{1,0:T(8,128)(2,1)S(1)}, u32[]{:S(2)}, u32[]{:S(2)}) collective-permute-start(bf16[432,256]{1,0:T(8,128)(2,1)} %rest_0_.4), channel_id=1, source_target_pairs={{0,4},{4,8},{8,12},{12,14},{14,10},{10,6},{6,2},{2,0},{1,3},{5,1},... | collective-permute-start | bytes 663560 | tf_op jit(solution)/shard_map/ppermute | solution.py:367
  3.8 0.7 collective-permute-start.4
  4.4 1.0 fusion.2
  5.4 3.5 %collective-permute-done.2 = bf16[432,256]{1,0:T(8,128)(2,1)S(1)} collective-permute-done((bf16[432,256]{1,0:T(8,128)(2,1)}, bf16[432,256]{1,0:T(8,128)(2,1)S(1)}, u32[]{:S(2)}, u32[]{:S(2)}) %collective-permute-start.2) | collective-permute-done | bytes 221216 | tf_op jit(solution)/shard_map/ppermute | solution.py:367
  8.9 1.3 %collective-permute-done.4 = bf16[432,256]{1,0:T(8,128)(2,1)S(1)} collective-permute-done((bf16[432,256]{1,0:T(8,128)(2,1)}, bf16[432,256]{1,0:T(8,128)(2,1)S(1)}, u32[]{:S(2)}, u32[]{:S(2)}) %collective-permute-start.4) | collective-permute-done | bytes 221216 | tf_op jit(solution)/shard_map/ppermute | solution.py:367
  10.2 2.1 %collective-permute-start.5 = (bf16[864,256]{1,0:T(8,128)(2,1)S(1)}, bf16[864,256]{1,0:T(8,128)(2,1)S(1)}, u32[]{:S(2)}, u32[]{:S(2)}) collective-permute-start(bf16[864,256]{1,0:T(8,128)(2,1)S(1)} %constant_dynamic-update-slice_fusion.rest_2_), channel_id=1, source_target_pairs={{0,4},{4,8},{8,12},{12,14},{14,10},{10,6},{6,2},{2,0},{1,3},{5,1},... | collective-permute-start | bytes 1327112 | tf_op jit(solution)/shard_map/ppermute | solution.py:372
  12.3 0.9 fusion.3
  13.3 0.1 collective-permute-start
  13.3 1.6 %collective-permute-start.3 = (bf16[432,256]{1,0:T(8,128)(2,1)S(1)}, bf16[432,256]{1,0:T(8,128)(2,1)S(1)}, u32[]{:S(2)}, u32[]{:S(2)}) collective-permute-start(bf16[432,256]{1,0:T(8,128)(2,1)S(1)} %copy-done.2), channel_id=1, source_target_pairs={{0,4},{4,8},{8,12},{12,14},{14,10},{10,6},{6,2},{2,0},{1,3},{5,1},... | collective-permute-start | bytes 663560 | tf_op jit(solution)/shard_map/ppermute | solution.py:368
  15.0 3.2 %collective-permute-start.1 = (bf16[3,8,16,256]{3,2,1,0:T(8,128)(2,1)S(1)}, bf16[3,8,16,256]{3,2,1,0:T(8,128)(2,1)S(1)}, u32[]{:S(2)}, u32[]{:S(2)}) collective-permute-start(bf16[3,8,16,256]{3,2,1,0:T(8,128)(2,1)S(1)} %pad_maximum_fusion.4), channel_id=1, source_target_pairs={{0,15},{1,0},{2,1},{3,2},{4,3},{5,4},{6,5},{7,6},{8,7},{9,8},{10,9... | collective-permute-start | bytes 589832 | tf_op jit(solution)/shard_map/ppermute | solution.py:370
  18.2 5.1 %collective-permute-done.low = bf16[3,8,16,256]{3,2,1,0:T(8,128)(2,1)S(1)} collective-permute-done((bf16[3,8,16,256]{3,2,1,0:T(8,128)(2,1)S(1)}, bf16[3,8,16,256]{3,2,1,0:T(8,128)(2,1)S(1)}, u32[]{:S(2)}, u32[]{:S(2)}) %collective-permute-start) | collective-permute-done | bytes 196640 | tf_op jit(solution)/shard_map/ppermute | solution.py:369
  23.3 0.1 collective-permute-start.8
  23.4 1.7 %collective-permute-start.10 = (bf16[864,256]{1,0:T(8,128)(2,1)S(1)}, bf16[864,256]{1,0:T(8,128)(2,1)S(1)}, u32[]{:S(2)}, u32[]{:S(2)}) collective-permute-start(bf16[864,256]{1,0:T(8,128)(2,1)S(1)} %constant_dynamic-update-slice_fusion.rest_2_), channel_id=1, source_target_pairs={{0,1},{1,0},{2,3},{3,2},{4,5},{5,4},{6,7},{7,6},{8,9},{9,8},{10,11... | collective-permute-start | bytes 1327112 | tf_op jit(solution)/shard_map/ppermute | solution.py:373
  25.1 0.1 collective-permute-start.11
  25.1 0.3 collective-permute-start.9
  25.5 1.8 %collective-permute-start.7 = (bf16[432,256]{1,0:T(8,128)(2,1)S(1)}, bf16[432,256]{1,0:T(8,128)(2,1)S(1)}, u32[]{:S(2)}, u32[]{:S(2)}) collective-permute-start(bf16[432,256]{1,0:T(8,128)(2,1)S(1)} %copy-done.4), channel_id=1, source_target_pairs={{0,1},{1,0},{2,3},{3,2},{4,5},{5,4},{6,7},{7,6},{8,9},{9,8},{10,11... | collective-permute-start | bytes 663560 | tf_op jit(solution)/shard_map/ppermute | solution.py:377
  27.3 1.3 %prep.1 = (bf16[8,10,16,768]{3,2,1,0:T(8,128)(2,1)S(1)}, bf16[6,10,16,768]{3,2,1,0:T(8,128)(2,1)S(1)}, bf16[256,768]{1,0:T(8,128)(2,1)S(1)}, bf16[3,128,256]{2,1,0:T(8,128)(2,1)S(1)}) custom-call(s32[2,4,16]{2,1,0:T(4,128)S(1)} %bitcast.1, bf16[3,8,16,256]{3,2,1,0:T(8,128)(2,1)S(1)} %collective-permute-done.low, bf16[4,8,16,256]{3,2,1,0:T(8,128)(2,1)S(1)} %copy-done, ...), custom_call_target="tpu_custom_call" | custom-call | bytes 4194304 | tf_op jit(solution)/shard_map/prep/pallas_call | solution.py:353
  28.7 4.2 %collective-permute-done.9.rest_13_.rest_3_ = bf16[432,256]{1,0:T(8,128)(2,1)S(1)} collective-permute-done((bf16[432,256]{1,0:T(8,128)(2,1)S(1)}, bf16[432,256]{1,0:T(8,128)(2,1)S(1)}, u32[]{:S(2)}, u32[]{:S(2)}) %collective-permute-start.9) | collective-permute-done | bytes 221216 | tf_op jit(solution)/shard_map/ppermute | solution.py:374
  32.9 0.8 collective-permute-start.16
  33.7 0.3 collective-permute-done.8.rest_4_
  34.1 1.2 %collective-permute-start.12 = (bf16[432,256]{1,0:T(8,128)(2,1)S(1)}, bf16[432,256]{1,0:T(8,128)(2,1)S(1)}, u32[]{:S(2)}, u32[]{:S(2)}) collective-permute-start(bf16[432,256]{1,0:T(8,128)(2,1)S(1)} %slice.116), channel_id=1, source_target_pairs={{0,4},{4,8},{8,12},{12,14},{14,10},{10,6},{6,2},{2,0},{1,3},{5,1},... | collective-permute-start | bytes 663560 | tf_op jit(solution)/shard_map/ppermute | solution.py:398
  35.2 2.7 %collective-permute-start.6 = (bf16[432,256]{1,0:T(8,128)(2,1)S(1)}, bf16[432,256]{1,0:T(8,128)(2,1)S(1)}, u32[]{:S(2)}, u32[]{:S(2)}) collective-permute-start(bf16[432,256]{1,0:T(8,128)(2,1)S(1)} %collective-permute-done.3.rest_12_.rest_2_), channel_id=1, source_target_pairs={{0,4},{4,8},{8,12},{12,14},{14,10},{10,6},{6,2},{2,0},{1,3},{5,1},... | collective-permute-start | bytes 663560 | tf_op jit(solution)/shard_map/ppermute | solution.py:378
  37.9 2.1 %collective-permute-done.12.rest_5_ = bf16[432,256]{1,0:T(8,128)(2,1)S(1)} collective-permute-done((bf16[432,256]{1,0:T(8,128)(2,1)S(1)}, bf16[432,256]{1,0:T(8,128)(2,1)S(1)}, u32[]{:S(2)}, u32[]{:S(2)}) %collective-permute-start.12) | collective-permute-done | bytes 221216 | tf_op jit(solution)/shard_map/ppermute | solution.py:398
  40.1 2.4 %collective-permute-done.6.rest_14_.rest_4_ = bf16[432,256]{1,0:T(8,128)(2,1)S(1)} collective-permute-done((bf16[432,256]{1,0:T(8,128)(2,1)S(1)}, bf16[432,256]{1,0:T(8,128)(2,1)S(1)}, u32[]{:S(2)}, u32[]{:S(2)}) %collective-permute-start.6) | collective-permute-done | bytes 221216 | tf_op jit(solution)/shard_map/ppermute | solution.py:378
  42.4 1.4 %collective-permute-start.15 = (bf16[432,256]{1,0:T(8,128)(2,1)S(1)}, bf16[432,256]{1,0:T(8,128)(2,1)S(1)}, u32[]{:S(2)}, u32[]{:S(2)}) collective-permute-start(bf16[432,256]{1,0:T(8,128)(2,1)S(1)} %collective-permute-done.9.rest_13_.rest_3_), channel_id=1, source_target_pairs={{0,4},{4,8},{8,12},{12,14},{14,10},{10,6},{6,2},{2,0},{1,3},{5,1},... | collective-permute-start | bytes 663560 | tf_op jit(solution)/shard_map/ppermute | solution.py:402
  43.8 2.4 %collective-permute-start.18 = (bf16[432,256]{1,0:T(8,128)(2,1)S(1)}, bf16[432,256]{1,0:T(8,128)(2,1)S(1)}, u32[]{:S(2)}, u32[]{:S(2)}) collective-permute-start(bf16[432,256]{1,0:T(8,128)(2,1)S(1)} %collective-permute-done.6.rest_14_.rest_4_), channel_id=1, source_target_pairs={{0,4},{4,8},{8,12},{12,14},{14,10},{10,6},{6,2},{2,0},{1,3},{5,1},... | collective-permute-start | bytes 663560 | tf_op jit(solution)/shard_map/ppermute | solution.py:405
  46.2 2.3 %first.1 = (f32[512,256]{1,0:T(8,128)S(1)}, bf16[512,256]{1,0:T(8,128)(2,1)S(1)}, bf16[256,512]{1,0:T(8,128)(2,1)S(1)}) custom-call(bf16[8,10,16,768]{3,2,1,0:T(8,128)(2,1)S(1)} %get-tuple-element.33.sx_ref, bf16[3,128,256]{2,1,0:T(8,128)(2,1)S(1)} %get-tuple-element.34.mask_ref, bf16[432,256]{1,0:T(8,128)(2,1)S(1)} %copy-done.4, ...), custom_call_target="tpu_custom_call" | custom-call | flops 1811939328 | bytes 4194304 | tf_op jit(solution)/shard_map/first/pallas_call | solution.py:353
  48.6 2.2 %grad_two.1 = (bf16[3456,256]{1,0:T(8,128)(2,1)S(1)}, bf16[3456,256]{1,0:T(8,128)(2,1)S(1)}) custom-call(bf16[6,10,16,768]{3,2,1,0:T(8,128)(2,1)S(1)} %get-tuple-element.39.sc_ref, bf16[256,512]{1,0:T(8,128)(2,1)S(1)} %get-tuple-element.42.act_t_ref), custom_call_target="tpu_custom_call" | custom-call | flops 1811939328 | bytes 4194304 | tf_op jit(solution)/shard_map/grad_two/pallas_call | solution.py:353
  50.8 0.1 collective-permute-start.19
  50.9 0.6 collective-permute-start.22
  51.5 2.3 %collective-permute-start.21 = (bf16[432,256]{1,0:T(8,128)(2,1)S(1)}, bf16[432,256]{1,0:T(8,128)(2,1)S(1)}, u32[]{:S(2)}, u32[]{:S(2)}) collective-permute-start(bf16[432,256]{1,0:T(8,128)(2,1)S(1)} %collective-permute-done.15.rest_15_.rest_5_), channel_id=1, source_target_pairs={{0,4},{4,8},{8,12},{12,14},{14,10},{10,6},{6,2},{2,0},{1,3},{5,1},... | collective-permute-start | bytes 663560 | tf_op jit(solution)/shard_map/ppermute | solution.py:426
  53.8 1.4 %collective-permute-done.22.rest_20_.rest_10_ = bf16[864,256]{1,0:T(8,128)(2,1)S(1)} collective-permute-done((bf16[864,256]{1,0:T(8,128)(2,1)S(1)}, bf16[864,256]{1,0:T(8,128)(2,1)S(1)}, u32[]{:S(2)}, u32[]{:S(2)}) %collective-permute-start.22) | collective-permute-done | bytes 442400 | tf_op jit(solution)/shard_map/ppermute | solution.py:421
  55.2 2.3 %collective-permute-start.23 = (bf16[432,256]{1,0:T(8,128)(2,1)S(1)}, bf16[432,256]{1,0:T(8,128)(2,1)S(1)}, u32[]{:S(2)}, u32[]{:S(2)}) collective-permute-start(bf16[432,256]{1,0:T(8,128)(2,1)S(1)} %collective-permute-done.18.rest_16_.rest_6_), channel_id=1, source_target_pairs={{0,4},{4,8},{8,12},{12,14},{14,10},{10,6},{6,2},{2,0},{1,3},{5,1},... | collective-permute-start | bytes 663560 | tf_op jit(solution)/shard_map/ppermute | solution.py:427
  57.6 0.1 add_convert_fusion.7
  57.7 0.1 collective-permute-start.24
  57.7 3.5 %collective-permute-done.23.rest_18_.rest_8_ = bf16[432,256]{1,0:T(8,128)(2,1)S(1)} collective-permute-done((bf16[432,256]{1,0:T(8,128)(2,1)S(1)}, bf16[432,256]{1,0:T(8,128)(2,1)S(1)}, u32[]{:S(2)}, u32[]{:S(2)}) %collective-permute-start.23) | collective-permute-done | bytes 221216 | tf_op jit(solution)/shard_map/ppermute | solution.py:427
  61.3 2.2 %collective-permute-start.20 = (bf16[432,256]{1,0:T(8,128)(2,1)S(1)}, bf16[432,256]{1,0:T(8,128)(2,1)S(1)}, u32[]{:S(2)}, u32[]{:S(2)}) collective-permute-start(bf16[432,256]{1,0:T(8,128)(2,1)S(1)} %add_convert_fusion.7), channel_id=1, source_target_pairs={{0,4},{4,8},{8,12},{12,14},{14,10},{10,6},{6,2},{2,0},{1,3},{5,1},... | collective-permute-start | bytes 663560 | tf_op jit(solution)/shard_map/ppermute | solution.py:443
  63.5 2.4 %back.1.sd_ref = bf16[4,10,16,768]{3,2,1,0:T(8,128)(2,1)S(1)} custom-call(bf16[6,10,16,768]{3,2,1,0:T(8,128)(2,1)S(1)} %get-tuple-element.39.sc_ref, f32[512,256]{1,0:T(8,128)S(1)} %get-tuple-element.51.pre_ref, bf16[3,128,256]{2,1,0:T(8,128)(2,1)S(1)} %get-tuple-element.34.mask_ref, bf16[432,256]{1,0:T(8,128)(2,1)S(1)} %copy-done.2, ...), custom_call_target="tpu_custom_call" | custom-call | flops 1811939328 | bytes 4194304 | tf_op jit(solution)/shard_map/back/pallas_call | solution.py:353
  65.9 2.2 %grad_one.1 = (bf16[3456,256]{1,0:T(8,128)(2,1)S(1)}, bf16[3456,256]{1,0:T(8,128)(2,1)S(1)}) custom-call(bf16[4,10,16,768]{3,2,1,0:T(8,128)(2,1)S(1)} %back.1.sd_ref, bf16[256,768]{1,0:T(8,128)(2,1)S(1)} %get-tuple-element.52.int_ref), custom_call_target="tpu_custom_call" | custom-call | flops 1811939328 | bytes 4194304 | tf_op jit(solution)/shard_map/grad_one/pallas_call | solution.py:353
  68.2 0.1 collective-permute-start.26
  68.3 0.1 add_convert_fusion.4
  68.5 2.3 %collective-permute-start.28 = (bf16[864,256]{1,0:T(8,128)(2,1)S(1)}, bf16[864,256]{1,0:T(8,128)(2,1)S(1)}, u32[]{:S(2)}, u32[]{:S(2)}) collective-permute-start(bf16[864,256]{1,0:T(8,128)(2,1)S(1)} %add_convert_fusion.4), channel_id=1, source_target_pairs={{0,4},{4,8},{8,12},{12,14},{14,10},{10,6},{6,2},{2,0},{1,3},{5,1},... | collective-permute-start | bytes 1327112 | tf_op jit(solution)/shard_map/ppermute | solution.py:464
  70.7 1.2 %collective-permute-done.26 = bf16[3456,256]{1,0:T(8,128)(2,1)S(1)} collective-permute-done((bf16[3456,256]{1,0:T(8,128)(2,1)S(1)}, bf16[3456,256]{1,0:T(8,128)(2,1)S(1)}, u32[]{:S(2)}, u32[]{:S(2)}) %collective-permute-start.26) | collective-permute-done | bytes 1769504 | tf_op jit(solution)/shard_map/ppermute | solution.py:462
  72.0 2.5 %collective-permute-start.27 = (bf16[432,256]{1,0:T(8,128)(2,1)S(1)}, bf16[432,256]{1,0:T(8,128)(2,1)S(1)}, u32[]{:S(2)}, u32[]{:S(2)}) collective-permute-start(bf16[432,256]{1,0:T(8,128)(2,1)S(1)} %add_convert_fusion.6), channel_id=1, source_target_pairs={{0,4},{4,8},{8,12},{12,14},{14,10},{10,6},{6,2},{2,0},{1,3},{5,1},... | collective-permute-start | bytes 663560 | tf_op jit(solution)/shard_map/ppermute | solution.py:465
  74.5 4.3 %third.1 = bf16[4,8,16,256]{3,2,1,0:T(8,128)(2,1)} custom-call(bf16[8,10,16,768]{3,2,1,0:T(8,128)(2,1)S(1)} %get-tuple-element.33.sx_ref, bf16[512,256]{1,0:T(8,128)(2,1)S(1)} %get-tuple-element.47.act_ref, bf16[3,128,256]{2,1,0:T(8,128)(2,1)S(1)} %get-tuple-element.34.mask_ref, bf16[432,256]{1,0:T(8,128)(2,1)S(1)} %copy-done.4, ...), custom_call_target="tpu_custom_call" | custom-call | flops 7247757312 | bytes 4194304 | tf_op jit(solution)/shard_map/third/pallas_call | solution.py:353
  78.8 0.4 collective-permute-done.27
  79.2 0.1 add_convert_fusion.5
  79.3 2.3 %collective-permute-start.29 = (bf16[864,256]{1,0:T(8,128)(2,1)S(1)}, bf16[864,256]{1,0:T(8,128)(2,1)S(1)}, u32[]{:S(2)}, u32[]{:S(2)}) collective-permute-start(bf16[864,256]{1,0:T(8,128)(2,1)S(1)} %add_convert_fusion.5), channel_id=1, source_target_pairs={{0,4},{4,8},{8,12},{12,14},{14,10},{10,6},{6,2},{2,0},{1,3},{5,1},... | collective-permute-start | bytes 1327112 | tf_op jit(solution)/shard_map/ppermute | solution.py:479
  81.6 0.2 add_convert_fusion.1
  81.8 1.6 %collective-permute-start.33 = (bf16[864,256]{1,0:T(8,128)(2,1)S(1)}, bf16[864,256]{1,0:T(8,128)(2,1)S(1)}, u32[]{:S(2)}, u32[]{:S(2)}) collective-permute-start(bf16[864,256]{1,0:T(8,128)(2,1)S(1)} %add_convert_fusion.1), channel_id=1, source_target_pairs={{0,4},{4,8},{8,12},{12,14},{14,10},{10,6},{6,2},{2,0},{1,3},{5,1},... | collective-permute-start | bytes 1327112 | tf_op jit(solution)/shard_map/ppermute | solution.py:480
  83.4 4.3 %collective-permute-done.29 = bf16[864,256]{1,0:T(8,128)(2,1)S(1)} collective-permute-done((bf16[864,256]{1,0:T(8,128)(2,1)S(1)}, bf16[864,256]{1,0:T(8,128)(2,1)S(1)}, u32[]{:S(2)}, u32[]{:S(2)}) %collective-permute-start.29) | collective-permute-done | bytes 442400 | tf_op jit(solution)/shard_map/ppermute | solution.py:479
  87.7 0.2 add_convert_fusion.3
  87.9 2.3 %collective-permute-start.30 = (bf16[864,256]{1,0:T(8,128)(2,1)S(1)}, bf16[864,256]{1,0:T(8,128)(2,1)S(1)}, u32[]{:S(2)}, u32[]{:S(2)}) collective-permute-start(bf16[864,256]{1,0:T(8,128)(2,1)S(1)} %add_convert_fusion.3), channel_id=1, source_target_pairs={{0,4},{4,8},{8,12},{12,14},{14,10},{10,6},{6,2},{2,0},{1,3},{5,1},... | collective-permute-start | bytes 1327112 | tf_op jit(solution)/shard_map/ppermute | solution.py:482
  90.1 2.3 %collective-permute-done.33 = bf16[864,256]{1,0:T(8,128)(2,1)S(1)} collective-permute-done((bf16[864,256]{1,0:T(8,128)(2,1)S(1)}, bf16[864,256]{1,0:T(8,128)(2,1)S(1)}, u32[]{:S(2)}, u32[]{:S(2)}) %collective-permute-start.33) | collective-permute-done | bytes 442400 | tf_op jit(solution)/shard_map/ppermute | solution.py:480
  92.4 0.2 add_convert_fusion
  92.6 2.3 %collective-permute-start.34 = (bf16[432,256]{1,0:T(8,128)(2,1)S(1)}, bf16[432,256]{1,0:T(8,128)(2,1)S(1)}, u32[]{:S(2)}, u32[]{:S(2)}) collective-permute-start(bf16[432,256]{1,0:T(8,128)(2,1)S(1)} %get-tuple-element.57), channel_id=1, source_target_pairs={{0,4},{4,8},{8,12},{12,14},{14,10},{10,6},{6,2},{2,0},{1,3},{5,1},... | collective-permute-start | bytes 663560 | tf_op jit(solution)/shard_map/ppermute | solution.py:439
  94.9 2.3 %collective-permute-done.30 = bf16[864,256]{1,0:T(8,128)(2,1)S(1)} collective-permute-done((bf16[864,256]{1,0:T(8,128)(2,1)S(1)}, bf16[864,256]{1,0:T(8,128)(2,1)S(1)}, u32[]{:S(2)}, u32[]{:S(2)}) %collective-permute-start.30) | collective-permute-done | bytes 442400 | tf_op jit(solution)/shard_map/ppermute | solution.py:482
  97.2 0.2 add_convert_fusion.2
  97.4 2.3 %collective-permute-start.31 = (bf16[432,256]{1,0:T(8,128)(2,1)S(1)}, bf16[432,256]{1,0:T(8,128)(2,1)S(1)}, u32[]{:S(2)}, u32[]{:S(2)}) collective-permute-start(bf16[432,256]{1,0:T(8,128)(2,1)S(1)} %get-tuple-element.59), channel_id=1, source_target_pairs={{0,4},{4,8},{8,12},{12,14},{14,10},{10,6},{6,2},{2,0},{1,3},{5,1},... | collective-permute-start | bytes 663560 | tf_op jit(solution)/shard_map/ppermute | solution.py:439
  99.7 2.0 %collective-permute-done.35 = bf16[432,256]{1,0:T(8,128)(2,1)S(1)} collective-permute-done((bf16[432,256]{1,0:T(8,128)(2,1)S(1)}, bf16[432,256]{1,0:T(8,128)(2,1)S(1)}, u32[]{:S(2)}, u32[]{:S(2)}) %collective-permute-start.35) | collective-permute-done | bytes 221216 | tf_op jit(solution)/shard_map/ppermute | solution.py:440
  101.7 0.9 add_multiply_fusion
  102.5 1.7 %collective-permute-done.31 = bf16[432,256]{1,0:T(8,128)(2,1)S(1)} collective-permute-done((bf16[432,256]{1,0:T(8,128)(2,1)S(1)}, bf16[432,256]{1,0:T(8,128)(2,1)S(1)}, u32[]{:S(2)}, u32[]{:S(2)}) %collective-permute-start.31) | collective-permute-done | bytes 221216 | tf_op jit(solution)/shard_map/ppermute | solution.py:439
  104.3 2.1 %collective-permute-done.32 = bf16[432,256]{1,0:T(8,128)(2,1)S(1)} collective-permute-done((bf16[432,256]{1,0:T(8,128)(2,1)S(1)}, bf16[432,256]{1,0:T(8,128)(2,1)S(1)}, u32[]{:S(2)}, u32[]{:S(2)}) %collective-permute-start.32) | collective-permute-done | bytes 221216 | tf_op jit(solution)/shard_map/ppermute | solution.py:440
  106.4 0.9 add_multiply_fusion.1
  (46 shorter events, 0.4 us)
Async XLA Ops:
  0.6 24.9 %copy-start.4 = (bf16[432,256]{1,0:T(8,128)(2,1)S(1)}, bf16[432,256]{1,0:T(8,128)(2,1)}, u32[]{:S(2)}) copy-start(bf16[432,256]{1,0:T(8,128)(2,1)} %rest_0_.4) | copy-start | bytes 663556
  0.6 26.7 %copy-start = (bf16[4,8,16,256]{3,2,1,0:T(8,128)(2,1)S(1)}, bf16[4,8,16,256]{3,2,1,0:T(8,128)(2,1)}, u32[]{:S(2)}) copy-start(bf16[4,8,16,256]{3,2,1,0:T(8,128)(2,1)} %f_own.1) | copy-start | bytes 786436
  0.7 26.7 %copy-start.1 = (bf16[4,8,16,256]{3,2,1,0:T(8,128)(2,1)S(1)}, bf16[4,8,16,256]{3,2,1,0:T(8,128)(2,1)}, u32[]{:S(2)}) copy-start(bf16[4,8,16,256]{3,2,1,0:T(8,128)(2,1)} %c_own.1) | copy-start | bytes 786436
  0.7 12.7 %copy-start.2 = (bf16[432,256]{1,0:T(8,128)(2,1)S(1)}, bf16[432,256]{1,0:T(8,128)(2,1)}, u32[]{:S(2)}) copy-start(bf16[432,256]{1,0:T(8,128)(2,1)} %rest_0_.5) | copy-start | bytes 663556
  0.7 26.7 %copy-start.3 = (s32[16,2,4]{0,2,1:T(4,128)S(1)}, s32[16,2,4]{0,2,1:T(4,128)}, u32[]{:S(2)}) copy-start(s32[16,2,4]{0,2,1:T(4,128)} %param.9) | copy-start | bytes 1540
  0.7 8.2 %collective-permute-start.2 = (bf16[432,256]{1,0:T(8,128)(2,1)}, bf16[432,256]{1,0:T(8,128)(2,1)S(1)}, u32[]{:S(2)}, u32[]{:S(2)}) collective-permute-start(bf16[432,256]{1,0:T(8,128)(2,1)} %rest_0_.4), channel_id=1, source_target_pairs={{0,4},{4,8},{8,12},{12,14},{14,10},{10,6},{6,2},{2,0},{1,3},{5,1},... | collective-permute-start | bytes 663560 | tf_op jit(solution)/shard_map/ppermute | solution.py:367
  3.8 6.4 %collective-permute-start.4 = (bf16[432,256]{1,0:T(8,128)(2,1)}, bf16[432,256]{1,0:T(8,128)(2,1)S(1)}, u32[]{:S(2)}, u32[]{:S(2)}) collective-permute-start(bf16[432,256]{1,0:T(8,128)(2,1)} %rest_0_.4), channel_id=1, source_target_pairs={{1,4},{5,8},{9,12},{13,14},{15,10},{11,6},{7,2},{3,0},{0,3},{4,1},... | collective-permute-start | bytes 663560 | tf_op jit(solution)/shard_map/ppermute | solution.py:367
  10.2 13.1 %collective-permute-start.5 = (bf16[864,256]{1,0:T(8,128)(2,1)S(1)}, bf16[864,256]{1,0:T(8,128)(2,1)S(1)}, u32[]{:S(2)}, u32[]{:S(2)}) collective-permute-start(bf16[864,256]{1,0:T(8,128)(2,1)S(1)} %constant_dynamic-update-slice_fusion.rest_2_), channel_id=1, source_target_pairs={{0,4},{4,8},{8,12},{12,14},{14,10},{10,6},{6,2},{2,0},{1,3},{5,1},... | collective-permute-start | bytes 1327112 | tf_op jit(solution)/shard_map/ppermute | solution.py:372
  13.3 10.0 %collective-permute-start = (bf16[3,8,16,256]{3,2,1,0:T(8,128)(2,1)S(1)}, bf16[3,8,16,256]{3,2,1,0:T(8,128)(2,1)S(1)}, u32[]{:S(2)}, u32[]{:S(2)}) collective-permute-start(bf16[3,8,16,256]{3,2,1,0:T(8,128)(2,1)S(1)} %pad_maximum_fusion.3), channel_id=1, source_target_pairs={{0,1},{1,2},{2,3},{3,4},{4,5},{5,6},{6,7},{7,8},{8,9},{9,10},{10,1... | collective-permute-start | bytes 589832 | tf_op jit(solution)/shard_map/ppermute | solution.py:369
  13.3 9.9 %collective-permute-start.3 = (bf16[432,256]{1,0:T(8,128)(2,1)S(1)}, bf16[432,256]{1,0:T(8,128)(2,1)S(1)}, u32[]{:S(2)}, u32[]{:S(2)}) collective-permute-start(bf16[432,256]{1,0:T(8,128)(2,1)S(1)} %copy-done.2), channel_id=1, source_target_pairs={{0,4},{4,8},{8,12},{12,14},{14,10},{10,6},{6,2},{2,0},{1,3},{5,1},... | collective-permute-start | bytes 663560 | tf_op jit(solution)/shard_map/ppermute | solution.py:368
  15.0 8.3 %collective-permute-start.1 = (bf16[3,8,16,256]{3,2,1,0:T(8,128)(2,1)S(1)}, bf16[3,8,16,256]{3,2,1,0:T(8,128)(2,1)S(1)}, u32[]{:S(2)}, u32[]{:S(2)}) collective-permute-start(bf16[3,8,16,256]{3,2,1,0:T(8,128)(2,1)S(1)} %pad_maximum_fusion.4), channel_id=1, source_target_pairs={{0,15},{1,0},{2,1},{3,2},{4,3},{5,4},{6,5},{7,6},{8,7},{9,8},{10,9... | collective-permute-start | bytes 589832 | tf_op jit(solution)/shard_map/ppermute | solution.py:370
  23.3 10.7 %collective-permute-start.8 = (bf16[864,256]{1,0:T(8,128)(2,1)S(1)}, bf16[864,256]{1,0:T(8,128)(2,1)S(1)}, u32[]{:S(2)}, u32[]{:S(2)}) collective-permute-start(bf16[864,256]{1,0:T(8,128)(2,1)S(1)} %collective-permute-done.5.rest_3_), channel_id=1, source_target_pairs={{0,4},{4,8},{8,12},{12,14},{14,10},{10,6},{6,2},{2,0},{1,3},{5,1},... | collective-permute-start | bytes 1327112 | tf_op jit(solution)/shard_map/ppermute | solution.py:375
  23.4 10.7 %collective-permute-start.10 = (bf16[864,256]{1,0:T(8,128)(2,1)S(1)}, bf16[864,256]{1,0:T(8,128)(2,1)S(1)}, u32[]{:S(2)}, u32[]{:S(2)}) collective-permute-start(bf16[864,256]{1,0:T(8,128)(2,1)S(1)} %constant_dynamic-update-slice_fusion.rest_2_), channel_id=1, source_target_pairs={{0,1},{1,0},{2,3},{3,2},{4,5},{5,4},{6,7},{7,6},{8,9},{9,8},{10,11... | collective-permute-start | bytes 1327112 | tf_op jit(solution)/shard_map/ppermute | solution.py:373
  25.1 9.0 %collective-permute-start.11 = (bf16[864,256]{1,0:T(8,128)(2,1)S(1)}, bf16[864,256]{1,0:T(8,128)(2,1)S(1)}, u32[]{:S(2)}, u32[]{:S(2)}) collective-permute-start(bf16[864,256]{1,0:T(8,128)(2,1)S(1)} %collective-permute-done.5.rest_3_), channel_id=1, source_target_pairs={{0,1},{1,0},{2,3},{3,2},{4,5},{5,4},{6,7},{7,6},{8,9},{9,8},{10,11... | collective-permute-start | bytes 1327112 | tf_op jit(solution)/shard_map/ppermute | solution.py:376
  25.1 7.8 %collective-permute-start.9 = (bf16[432,256]{1,0:T(8,128)(2,1)S(1)}, bf16[432,256]{1,0:T(8,128)(2,1)S(1)}, u32[]{:S(2)}, u32[]{:S(2)}) collective-permute-start(bf16[432,256]{1,0:T(8,128)(2,1)S(1)} %copy-done.2), channel_id=1, source_target_pairs={{1,4},{5,8},{9,12},{13,14},{15,10},{11,6},{7,2},{3,0},{0,3},{4,1},... | collective-permute-start | bytes 663560 | tf_op jit(solution)/shard_map/ppermute | solution.py:374
  25.5 8.5 %collective-permute-start.7 = (bf16[432,256]{1,0:T(8,128)(2,1)S(1)}, bf16[432,256]{1,0:T(8,128)(2,1)S(1)}, u32[]{:S(2)}, u32[]{:S(2)}) collective-permute-start(bf16[432,256]{1,0:T(8,128)(2,1)S(1)} %copy-done.4), channel_id=1, source_target_pairs={{0,1},{1,0},{2,3},{3,2},{4,5},{5,4},{6,7},{7,6},{8,9},{9,8},{10,11... | collective-permute-start | bytes 663560 | tf_op jit(solution)/shard_map/ppermute | solution.py:377
  32.9 10.9 %collective-permute-start.16 = (bf16[864,256]{1,0:T(8,128)(2,1)S(1)}, bf16[864,256]{1,0:T(8,128)(2,1)S(1)}, u32[]{:S(2)}, u32[]{:S(2)}) collective-permute-start(bf16[864,256]{1,0:T(8,128)(2,1)S(1)} %pad_maximum_fusion), channel_id=1, source_target_pairs={{0,1},{1,0},{2,3},{3,2},{4,5},{5,4},{6,7},{7,6},{8,9},{9,8},{10,11... | collective-permute-start | bytes 1327112 | tf_op jit(solution)/shard_map/ppermute | solution.py:403
  34.1 6.0 %collective-permute-start.12 = (bf16[432,256]{1,0:T(8,128)(2,1)S(1)}, bf16[432,256]{1,0:T(8,128)(2,1)S(1)}, u32[]{:S(2)}, u32[]{:S(2)}) collective-permute-start(bf16[432,256]{1,0:T(8,128)(2,1)S(1)} %slice.116), channel_id=1, source_target_pairs={{0,4},{4,8},{8,12},{12,14},{14,10},{10,6},{6,2},{2,0},{1,3},{5,1},... | collective-permute-start | bytes 663560 | tf_op jit(solution)/shard_map/ppermute | solution.py:398
  35.2 11.0 %collective-permute-start.13 = (bf16[864,256]{1,0:T(8,128)(2,1)S(1)}, bf16[864,256]{1,0:T(8,128)(2,1)S(1)}, u32[]{:S(2)}, u32[]{:S(2)}) collective-permute-start(bf16[864,256]{1,0:T(8,128)(2,1)S(1)} %collective-permute-done.8.rest_4_), channel_id=1, source_target_pairs={{0,1},{1,0},{2,3},{3,2},{4,5},{5,4},{6,7},{7,6},{8,9},{9,8},{10,11... | collective-permute-start | bytes 1327112 | tf_op jit(solution)/shard_map/ppermute | solution.py:399
  35.2 7.2 %collective-permute-start.6 = (bf16[432,256]{1,0:T(8,128)(2,1)S(1)}, bf16[432,256]{1,0:T(8,128)(2,1)S(1)}, u32[]{:S(2)}, u32[]{:S(2)}) collective-permute-start(bf16[432,256]{1,0:T(8,128)(2,1)S(1)} %collective-permute-done.3.rest_12_.rest_2_), channel_id=1, source_target_pairs={{0,4},{4,8},{8,12},{12,14},{14,10},{10,6},{6,2},{2,0},{1,3},{5,1},... | collective-permute-start | bytes 663560 | tf_op jit(solution)/shard_map/ppermute | solution.py:378
  37.9 5.9 %collective-permute-start.17 = (bf16[432,256]{1,0:T(8,128)(2,1)S(1)}, bf16[432,256]{1,0:T(8,128)(2,1)S(1)}, u32[]{:S(2)}, u32[]{:S(2)}) collective-permute-start(bf16[432,256]{1,0:T(8,128)(2,1)S(1)} %copy-done.2), channel_id=1, source_target_pairs={{0,1},{1,0},{2,3},{3,2},{4,5},{5,4},{6,7},{7,6},{8,9},{9,8},{10,11... | collective-permute-start | bytes 663560 | tf_op jit(solution)/shard_map/ppermute | solution.py:404
  40.0 6.2 %collective-permute-start.14 = (bf16[432,256]{1,0:T(8,128)(2,1)S(1)}, bf16[432,256]{1,0:T(8,128)(2,1)S(1)}, u32[]{:S(2)}, u32[]{:S(2)}) collective-permute-start(bf16[432,256]{1,0:T(8,128)(2,1)S(1)} %collective-permute-done.12.rest_5_), channel_id=1, source_target_pairs={{0,1},{1,0},{2,3},{3,2},{4,5},{5,4},{6,7},{7,6},{8,9},{9,8},{10,11... | collective-permute-start | bytes 663560 | tf_op jit(solution)/shard_map/ppermute | solution.py:399
  42.4 6.1 %collective-permute-start.15 = (bf16[432,256]{1,0:T(8,128)(2,1)S(1)}, bf16[432,256]{1,0:T(8,128)(2,1)S(1)}, u32[]{:S(2)}, u32[]{:S(2)}) collective-permute-start(bf16[432,256]{1,0:T(8,128)(2,1)S(1)} %collective-permute-done.9.rest_13_.rest_3_), channel_id=1, source_target_pairs={{0,4},{4,8},{8,12},{12,14},{14,10},{10,6},{6,2},{2,0},{1,3},{5,1},... | collective-permute-start | bytes 663560 | tf_op jit(solution)/shard_map/ppermute | solution.py:402
  43.8 7.0 %collective-permute-start.18 = (bf16[432,256]{1,0:T(8,128)(2,1)S(1)}, bf16[432,256]{1,0:T(8,128)(2,1)S(1)}, u32[]{:S(2)}, u32[]{:S(2)}) collective-permute-start(bf16[432,256]{1,0:T(8,128)(2,1)S(1)} %collective-permute-done.6.rest_14_.rest_4_), channel_id=1, source_target_pairs={{0,4},{4,8},{8,12},{12,14},{14,10},{10,6},{6,2},{2,0},{1,3},{5,1},... | collective-permute-start | bytes 663560 | tf_op jit(solution)/shard_map/ppermute | solution.py:405
  50.8 6.7 %collective-permute-start.19 = (bf16[3456,256]{1,0:T(8,128)(2,1)S(1)}, bf16[3456,256]{1,0:T(8,128)(2,1)S(1)}, u32[]{:S(2)}, u32[]{:S(2)}) collective-permute-start(bf16[3456,256]{1,0:T(8,128)(2,1)S(1)} %get-tuple-element.46), channel_id=1, source_target_pairs={{0,1},{1,0},{2,3},{3,2},{4,5},{5,4},{6,7},{7,6},{8,9},{9,8},{10,11... | collective-permute-start | bytes 5308424 | tf_op jit(solution)/shard_map/ppermute | solution.py:425
  50.9 4.3 %collective-permute-start.22 = (bf16[864,256]{1,0:T(8,128)(2,1)S(1)}, bf16[864,256]{1,0:T(8,128)(2,1)S(1)}, u32[]{:S(2)}, u32[]{:S(2)}) collective-permute-start(bf16[864,256]{1,0:T(8,128)(2,1)S(1)} %pad_maximum_fusion.1), channel_id=1, source_target_pairs={{0,1},{1,0},{2,3},{3,2},{4,5},{5,4},{6,7},{7,6},{8,9},{9,8},{10,11... | collective-permute-start | bytes 1327112 | tf_op jit(solution)/shard_map/ppermute | solution.py:421
  51.5 6.1 %collective-permute-start.21 = (bf16[432,256]{1,0:T(8,128)(2,1)S(1)}, bf16[432,256]{1,0:T(8,128)(2,1)S(1)}, u32[]{:S(2)}, u32[]{:S(2)}) collective-permute-start(bf16[432,256]{1,0:T(8,128)(2,1)S(1)} %collective-permute-done.15.rest_15_.rest_5_), channel_id=1, source_target_pairs={{0,4},{4,8},{8,12},{12,14},{14,10},{10,6},{6,2},{2,0},{1,3},{5,1},... | collective-permute-start | bytes 663560 | tf_op jit(solution)/shard_map/ppermute | solution.py:426
  55.2 6.1 %collective-permute-start.23 = (bf16[432,256]{1,0:T(8,128)(2,1)S(1)}, bf16[432,256]{1,0:T(8,128)(2,1)S(1)}, u32[]{:S(2)}, u32[]{:S(2)}) collective-permute-start(bf16[432,256]{1,0:T(8,128)(2,1)S(1)} %collective-permute-done.18.rest_16_.rest_6_), channel_id=1, source_target_pairs={{0,4},{4,8},{8,12},{12,14},{14,10},{10,6},{6,2},{2,0},{1,3},{5,1},... | collective-permute-start | bytes 663560 | tf_op jit(solution)/shard_map/ppermute | solution.py:427
  57.7 5.8 %collective-permute-start.24 = (bf16[864,256]{1,0:T(8,128)(2,1)S(1)}, bf16[864,256]{1,0:T(8,128)(2,1)S(1)}, u32[]{:S(2)}, u32[]{:S(2)}) collective-permute-start(bf16[864,256]{1,0:T(8,128)(2,1)S(1)} %pad_maximum_fusion.2), channel_id=1, source_target_pairs={{0,1},{1,0},{2,3},{3,2},{4,5},{5,4},{6,7},{7,6},{8,9},{9,8},{10,11... | collective-permute-start | bytes 1327112 | tf_op jit(solution)/shard_map/ppermute | solution.py:444
  61.3 2.2 %collective-permute-start.25 = (bf16[432,256]{1,0:T(8,128)(2,1)S(1)}, bf16[432,256]{1,0:T(8,128)(2,1)S(1)}, u32[]{:S(2)}, u32[]{:S(2)}) collective-permute-start(bf16[432,256]{1,0:T(8,128)(2,1)S(1)} %collective-permute-done.23.rest_18_.rest_8_), channel_id=1, source_target_pairs={{0,1},{1,0},{2,3},{3,2},{4,5},{5,4},{6,7},{7,6},{8,9},{9,8},{10,11... | collective-permute-start | bytes 663560 | tf_op jit(solution)/shard_map/ppermute | solution.py:445
  61.3 6.9 %collective-permute-start.20 = (bf16[432,256]{1,0:T(8,128)(2,1)S(1)}, bf16[432,256]{1,0:T(8,128)(2,1)S(1)}, u32[]{:S(2)}, u32[]{:S(2)}) collective-permute-start(bf16[432,256]{1,0:T(8,128)(2,1)S(1)} %add_convert_fusion.7), channel_id=1, source_target_pairs={{0,4},{4,8},{8,12},{12,14},{14,10},{10,6},{6,2},{2,0},{1,3},{5,1},... | collective-permute-start | bytes 663560 | tf_op jit(solution)/shard_map/ppermute | solution.py:443
  68.2 3.8 %collective-permute-start.26 = (bf16[3456,256]{1,0:T(8,128)(2,1)S(1)}, bf16[3456,256]{1,0:T(8,128)(2,1)S(1)}, u32[]{:S(2)}, u32[]{:S(2)}) collective-permute-start(bf16[3456,256]{1,0:T(8,128)(2,1)S(1)} %get-tuple-element.55), channel_id=1, source_target_pairs={{0,1},{1,0},{2,3},{3,2},{4,5},{5,4},{6,7},{7,6},{8,9},{9,8},{10,11... | collective-permute-start | bytes 5308424 | tf_op jit(solution)/shard_map/ppermute | solution.py:462
  68.5 10.9 %collective-permute-start.28 = (bf16[864,256]{1,0:T(8,128)(2,1)S(1)}, bf16[864,256]{1,0:T(8,128)(2,1)S(1)}, u32[]{:S(2)}, u32[]{:S(2)}) collective-permute-start(bf16[864,256]{1,0:T(8,128)(2,1)S(1)} %add_convert_fusion.4), channel_id=1, source_target_pairs={{0,4},{4,8},{8,12},{12,14},{14,10},{10,6},{6,2},{2,0},{1,3},{5,1},... | collective-permute-start | bytes 1327112 | tf_op jit(solution)/shard_map/ppermute | solution.py:464
  72.0 7.2 %collective-permute-start.27 = (bf16[432,256]{1,0:T(8,128)(2,1)S(1)}, bf16[432,256]{1,0:T(8,128)(2,1)S(1)}, u32[]{:S(2)}, u32[]{:S(2)}) collective-permute-start(bf16[432,256]{1,0:T(8,128)(2,1)S(1)} %add_convert_fusion.6), channel_id=1, source_target_pairs={{0,4},{4,8},{8,12},{12,14},{14,10},{10,6},{6,2},{2,0},{1,3},{5,1},... | collective-permute-start | bytes 663560 | tf_op jit(solution)/shard_map/ppermute | solution.py:465
  79.3 8.4 %collective-permute-start.29 = (bf16[864,256]{1,0:T(8,128)(2,1)S(1)}, bf16[864,256]{1,0:T(8,128)(2,1)S(1)}, u32[]{:S(2)}, u32[]{:S(2)}) collective-permute-start(bf16[864,256]{1,0:T(8,128)(2,1)S(1)} %add_convert_fusion.5), channel_id=1, source_target_pairs={{0,4},{4,8},{8,12},{12,14},{14,10},{10,6},{6,2},{2,0},{1,3},{5,1},... | collective-permute-start | bytes 1327112 | tf_op jit(solution)/shard_map/ppermute | solution.py:479
  81.8 10.7 %collective-permute-start.33 = (bf16[864,256]{1,0:T(8,128)(2,1)S(1)}, bf16[864,256]{1,0:T(8,128)(2,1)S(1)}, u32[]{:S(2)}, u32[]{:S(2)}) collective-permute-start(bf16[864,256]{1,0:T(8,128)(2,1)S(1)} %add_convert_fusion.1), channel_id=1, source_target_pairs={{0,4},{4,8},{8,12},{12,14},{14,10},{10,6},{6,2},{2,0},{1,3},{5,1},... | collective-permute-start | bytes 1327112 | tf_op jit(solution)/shard_map/ppermute | solution.py:480
  87.9 9.3 %collective-permute-start.30 = (bf16[864,256]{1,0:T(8,128)(2,1)S(1)}, bf16[864,256]{1,0:T(8,128)(2,1)S(1)}, u32[]{:S(2)}, u32[]{:S(2)}) collective-permute-start(bf16[864,256]{1,0:T(8,128)(2,1)S(1)} %add_convert_fusion.3), channel_id=1, source_target_pairs={{0,4},{4,8},{8,12},{12,14},{14,10},{10,6},{6,2},{2,0},{1,3},{5,1},... | collective-permute-start | bytes 1327112 | tf_op jit(solution)/shard_map/ppermute | solution.py:482
  92.6 7.0 %collective-permute-start.34 = (bf16[432,256]{1,0:T(8,128)(2,1)S(1)}, bf16[432,256]{1,0:T(8,128)(2,1)S(1)}, u32[]{:S(2)}, u32[]{:S(2)}) collective-permute-start(bf16[432,256]{1,0:T(8,128)(2,1)S(1)} %get-tuple-element.57), channel_id=1, source_target_pairs={{0,4},{4,8},{8,12},{12,14},{14,10},{10,6},{6,2},{2,0},{1,3},{5,1},... | collective-permute-start | bytes 663560 | tf_op jit(solution)/shard_map/ppermute | solution.py:439
  94.9 6.7 %collective-permute-start.35 = (bf16[432,256]{1,0:T(8,128)(2,1)S(1)}, bf16[432,256]{1,0:T(8,128)(2,1)S(1)}, u32[]{:S(2)}, u32[]{:S(2)}) collective-permute-start(bf16[432,256]{1,0:T(8,128)(2,1)S(1)} %get-tuple-element.58), channel_id=1, source_target_pairs={{0,5},{4,9},{8,13},{12,15},{14,11},{10,7},{6,3},{2,1},{1,2},{5,0},... | collective-permute-start | bytes 663560 | tf_op jit(solution)/shard_map/ppermute | solution.py:440
  97.4 6.9 %collective-permute-start.31 = (bf16[432,256]{1,0:T(8,128)(2,1)S(1)}, bf16[432,256]{1,0:T(8,128)(2,1)S(1)}, u32[]{:S(2)}, u32[]{:S(2)}) collective-permute-start(bf16[432,256]{1,0:T(8,128)(2,1)S(1)} %get-tuple-element.59), channel_id=1, source_target_pairs={{0,4},{4,8},{8,12},{12,14},{14,10},{10,6},{6,2},{2,0},{1,3},{5,1},... | collective-permute-start | bytes 663560 | tf_op jit(solution)/shard_map/ppermute | solution.py:439
  99.7 6.7 %collective-permute-start.32 = (bf16[432,256]{1,0:T(8,128)(2,1)S(1)}, bf16[432,256]{1,0:T(8,128)(2,1)S(1)}, u32[]{:S(2)}, u32[]{:S(2)}) collective-permute-start(bf16[432,256]{1,0:T(8,128)(2,1)S(1)} %get-tuple-element.60), channel_id=1, source_target_pairs={{0,5},{4,9},{8,13},{12,15},{14,11},{10,7},{6,3},{2,1},{1,2},{5,0},... | collective-permute-start | bytes 663560 | tf_op jit(solution)/shard_map/ppermute | solution.py:440

commit v6 on v5

--- a/solution.py
+++ b/solution.py
@@ -163,29 +163,33 @@
 
 
 PAIRS = (
-    (0, False, False),
-    (0, False, True),
-    (1, False, False),
-    (2, False, False),
-    (3, False, False),
-    (4, False, False),
-    (1, True, False),
-    (2, True, False),
-    (3, True, False),
-    (4, True, False),
+    (False, ((0, False),)),
+    (False, ((0, True),)),
+) + tuple(
+    (crossed, rows)
+    for crossed in (False, True)
+    for rows in [((hop, False), (hop, True)) for hop in (1, 2, 3)] + [((4, False),)]
 )
-SHARDS = PAIRS[:2] + tuple((hop, False, flip) for hop in (1, 2, 3) for flip in (False, True)) + PAIRS[5:]
+SHARDS = (
+    PAIRS[:2]
+    + ((False, ((1, False),)), (False, ((1, True),)), (True, ((1, False), (1, True))))
+    + tuple(
+        (crossed, rows)
+        for crossed in (False, True)
+        for rows in (((2, False),), ((2, True), (3, False)), ((3, True), (4, False)))
+    )
+)
 
 
 def fill_weight(kinds, pieces, w_ref):
     tile = lax.axis_index("tiles")
     core = tile % 2
     rows = w_ref.shape[0] // 16
-    for piece, (hop, crossed, flip) in zip(pieces, kinds):
+    for piece, (crossed, parts) in zip(pieces, kinds):
         holder = 1 - core if crossed else core
-        for half in range(piece.shape[0] // rows):
-            start = shard_rows(tile, holder, hop, flip or half == 1, rows)
-            w_ref[pl.ds(start, rows)] = piece[half * rows : (half + 1) * rows]
+        for part, (hop, flip) in enumerate(parts):
+            start = shard_rows(tile, holder, hop, flip, rows)
+            w_ref[pl.ds(start, rows)] = piece[part * rows : (part + 1) * rows]
 
 
 def split_shards(g_ref, keep_ref, send_ref):
@@ -372,10 +376,10 @@
     a2 = onward(a1)
     qa1 = sibling(a1)
     y1 = gather_across(after(weight_two, a1))
-    a3 = onward(after(a2, x1, low, high))
+    a3 = onward(after(a2, x1))
     qa2 = sibling(a2)
     other_one = sibling(weight_one)
-    x2 = onward(after(x1, a2))
+    x2 = onward(after(x1, y1))
     sx, sc, in_t, near = kernel(
         prep_kernel,
         "prep",
@@ -395,14 +399,13 @@
         high,
         smem=1,
     )
-    a4 = onward(after(a3[:rows], y1, qa1, qa2, other_one, sx))
-    qa3, qa4 = sibling(a3), sibling(a4)
+    a4 = onward(after(a3[:rows], y1, qa1, qa2, other_one))
+    qa3, qa4 = sibling(a3), sibling(after(a4, low, high))
     ones = [weight_one, other_one, a1, a2, a3, a4, qa1, qa2, qa3, qa4]
 
-    y2 = onward(after(y1, a3))
+    m4 = onward(jnp.concatenate([y1, x2]))
     qb1 = sibling(jnp.concatenate([x1, y1]))
     other_two = sibling(weight_two)
-    x3 = onward(after(x2, qb1, other_two))
     pre, act, act_t = kernel(
         first_kernel,
         "first",
@@ -414,17 +417,18 @@
             shape((channels, depth * area), BF),
         ),
         [weights],
-        after(sx, x2),
+        after(sx, x2, qb1, other_two),
         near,
         *ones,
     )
-    qb2 = sibling(jnp.concatenate([x2, y2]))
+    qx2 = sibling(x2)
     keep_two, send_two = kernel(
-        grad_two_kernel, "grad_two", 8, 1, shards, [weights], sc, after(act_t, y2)
-    )
-    got_two = sibling(after(send_two, x3))
-    y3 = onward(after(y2, act_t))
-    x4 = onward(after(x3, qb2))
+        grad_two_kernel, "grad_two", 8, 1, shards, [weights], sc, act_t
+    )
+    got_two = sibling(after(send_two, m4, qx2))
+    m5 = onward(m4)
+    qm4 = sibling(m4)
+
     def both(keep, got, lo, hi):
         return keep[lo * rows : hi * rows].astype(F32) + got[lo * rows : hi * rows].astype(F32)
 
@@ -441,9 +445,8 @@
 
     message = step(keep_two, got_two, None, 0)
     two = onward(message)
-    qb3 = sibling(jnp.concatenate([x3, after(y3, message)]))
-    qb4 = sibling(x4)
-    twos = [weight_two, other_two, x1, y1, x2, y2, x3, y3, x4, qb1, qb2, qb3, qb4]
+    qm5 = sibling(after(m5, message))
+    twos = [weight_two, other_two, x1, y1, qb1, x2, m4, m5, qx2, qm4, qm5]
     delta = kernel(
         back_kernel,
         "back",

time: 108 us -> 108 us (level)
  waiting for transfers between devices: 40 us -> 55.9 us
  starting transfers between devices: 46.6 us -> 31 us
    ppermute x13 -> x11, waiting for transfers between devices: 9.72 us -> 16.9 us  [the longest x1 4.67 us: on_ring(): a3 = onward(after(a2, x1))]
    ppermute x1, waiting for transfers between devices: 0.01 us -> 6.64 us  [on_ring(): x1 = onward(after(weight_two, a1[0]))]
    ppermute x13 -> x11, starting transfers between devices: 13.1 us -> 7.77 us  [the longest x1 2.13 us: on_ring(): a4 = onward(after(a3[:rows], y1, qa1, qa2, other_one))]
    ppermute x1, waiting for transfers between devices: 5.08 us -> 0.01 us  [on_ring(): low = up(jnp.concatenate([features[-2:], cotangent[-1:]]))]
    ppermute x2, waiting for transfers between devices: 1.74 us -> 6.77 us  [finish(): total = both(keep, got, 7, 8) + onward(message[:rows]).astype(F32)]
    ppermute x1, waiting for transfers between devices: 4.22 us -> 0.01 us  [on_ring(): y1 = gather_across(after(weight_two, a1))]
    ppermute x2, waiting for transfers between devices: 4.11 us -> 0.03 us  [finish(): return (total + scatter_across(message[rows:]).astype(F32)) * loss_scale]
    ppermute x1, waiting for transfers between devices: 0.01 us -> 3.18 us  [on_ring(): high = down(jnp.concatenate([features[:2], cotangent[:1]]))]
  transfers between devices with their start and end apart: 36 -> 34, of which waited for: 17 -> 17; matrix products, arithmetic and copies ran while one was open for 4% -> 4% of each run, Pallas kernels for 14% -> 14%
where the time goes in v6:
time: 108 us
  waiting for transfers between devices  55.9 us (52%)
  starting transfers between devices  31 us (29%)
  Pallas kernels  14.8 us (14%)
  other arithmetic  2.97 us (3%)
  local copies, waits for them, and re-layouts  2 us (2%)
    pallas_call x6, Pallas kernels, kernel(): pl.pallas_call(body, name=name, out_shape=outs, in_specs=[pl.BlockSpec(me...  14.8 us
    ppermute x2, waiting for transfers between devices, finish(): total = both(keep, got, 7, 8) + onward(message[:rows]).astype(F32)  6.77 us
    ppermute x1, waiting for transfers between devices, on_ring(): x1 = onward(after(weight_two, a1[0]))  6.64 us
    ppermute x2, waiting for transfers between devices, on_ring(): a1 = [onward(weight_one), gather_across(weight_one)]  5.74 us
    ppermute x1, starting transfers between devices, on_ring(): high = down(jnp.concatenate([features[:2], cotangent[:1]]))  5.01 us
    ppermute x1, waiting for transfers between devices, on_ring(): one = onward(after(step(keep_one, got_one, one, 1), features_out, two))  4.98 us
    ppermute x1, waiting for transfers between devices, on_ring(): a3 = onward(after(a2, x1))  4.67 us
    ppermute x1, waiting for transfers between devices, on_ring(): m5 = onward(m4)  4.55 us
  transfers between devices with their start and end apart: 34, of which 17 were waited for; matrix products, arithmetic and copies ran while one was open for 4% of the time, Pallas kernels for 14%

profile of v6, /device:TPU:0, one launch (start us, length us, event | category | flops | bytes accessed | tf_op | source)
XLA Modules:
  0.0 107.6 jit_solution(16590316000358458837)
XLA Ops:
  0.6 3.1 %collective-permute-start.2 = (bf16[432,256]{1,0:T(8,128)(2,1)}, bf16[432,256]{1,0:T(8,128)(2,1)S(1)}, u32[]{:S(2)}, u32[]{:S(2)}) collective-permute-start(bf16[432,256]{1,0:T(8,128)(2,1)} %rest_0_.4), channel_id=1, source_target_pairs={{0,4},{4,8},{8,12},{12,14},{14,10},{10,6},{6,2},{2,0},{1,3},{5,1},... | collective-permute-start | bytes 663560 | tf_op jit(solution)/shard_map/ppermute | solution.py:371
  3.7 0.7 collective-permute-start.4
  4.4 4.5 %collective-permute-done.2 = bf16[432,256]{1,0:T(8,128)(2,1)S(1)} collective-permute-done((bf16[432,256]{1,0:T(8,128)(2,1)}, bf16[432,256]{1,0:T(8,128)(2,1)S(1)}, u32[]{:S(2)}, u32[]{:S(2)}) %collective-permute-start.2) | collective-permute-done | bytes 221216 | tf_op jit(solution)/shard_map/ppermute | solution.py:371
  8.9 1.3 %collective-permute-done.4 = bf16[432,256]{1,0:T(8,128)(2,1)S(1)} collective-permute-done((bf16[432,256]{1,0:T(8,128)(2,1)}, bf16[432,256]{1,0:T(8,128)(2,1)S(1)}, u32[]{:S(2)}, u32[]{:S(2)}) %collective-permute-start.4) | collective-permute-done | bytes 221216 | tf_op jit(solution)/shard_map/ppermute | solution.py:371
  10.2 0.0 copy-start.2
  10.2 2.1 %collective-permute-start.10 = (bf16[864,256]{1,0:T(8,128)(2,1)S(1)}, bf16[864,256]{1,0:T(8,128)(2,1)S(1)}, u32[]{:S(2)}, u32[]{:S(2)}) collective-permute-start(bf16[864,256]{1,0:T(8,128)(2,1)S(1)} %constant_dynamic-update-slice_fusion.rest_2_), channel_id=1, source_target_pairs={{0,4},{4,8},{8,12},{12,14},{14,10},{10,6},{6,2},{2,0},{1,3},{5,1},... | collective-permute-start | bytes 1327112 | tf_op jit(solution)/shard_map/ppermute | solution.py:376
  12.3 1.6 %collective-permute-start.3 = (bf16[432,256]{1,0:T(8,128)(2,1)}, bf16[432,256]{1,0:T(8,128)(2,1)S(1)}, u32[]{:S(2)}, u32[]{:S(2)}) collective-permute-start(bf16[432,256]{1,0:T(8,128)(2,1)} %rest_0_.5), channel_id=1, source_target_pairs={{0,4},{4,8},{8,12},{12,14},{14,10},{10,6},{6,2},{2,0},{1,3},{5,1},... | collective-permute-start | bytes 663560 | tf_op jit(solution)/shard_map/ppermute | solution.py:372
  13.9 0.2 collective-permute-start.5
  14.1 1.0 fusion.2
  15.1 1.5 %collective-permute-start.12 = (bf16[864,256]{1,0:T(8,128)(2,1)S(1)}, bf16[864,256]{1,0:T(8,128)(2,1)S(1)}, u32[]{:S(2)}, u32[]{:S(2)}) collective-permute-start(bf16[864,256]{1,0:T(8,128)(2,1)S(1)} %constant_dynamic-update-slice_fusion.rest_2_), channel_id=1, source_target_pairs={{0,1},{1,0},{2,3},{3,2},{4,5},{5,4},{6,7},{7,6},{8,9},{9,8},{10,11... | collective-permute-start | bytes 1327112 | tf_op jit(solution)/shard_map/ppermute | solution.py:377
  16.7 6.6 %collective-permute-done.3.rest_12_.rest_2_ = bf16[432,256]{1,0:T(8,128)(2,1)S(1)} collective-permute-done((bf16[432,256]{1,0:T(8,128)(2,1)}, bf16[432,256]{1,0:T(8,128)(2,1)S(1)}, u32[]{:S(2)}, u32[]{:S(2)}) %collective-permute-start.3) | collective-permute-done | bytes 221216 | tf_op jit(solution)/shard_map/ppermute | solution.py:372
  23.3 2.1 %collective-permute-start.6 = (bf16[432,256]{1,0:T(8,128)(2,1)S(1)}, bf16[432,256]{1,0:T(8,128)(2,1)S(1)}, u32[]{:S(2)}, u32[]{:S(2)}) collective-permute-start(bf16[432,256]{1,0:T(8,128)(2,1)S(1)} %collective-permute-done.3.rest_12_.rest_2_), channel_id=1, source_target_pairs={{0,4},{4,8},{8,12},{12,14},{14,10},{10,6},{6,2},{2,0},{1,3},{5,1},... | collective-permute-start | bytes 663560 | tf_op jit(solution)/shard_map/ppermute | solution.py:382
  25.4 1.6 %collective-permute-start.11 = (bf16[864,256]{1,0:T(8,128)(2,1)S(1)}, bf16[864,256]{1,0:T(8,128)(2,1)S(1)}, u32[]{:S(2)}, u32[]{:S(2)}) collective-permute-start(bf16[864,256]{1,0:T(8,128)(2,1)S(1)} %collective-permute-done.10.rest_3_), channel_id=1, source_target_pairs={{0,4},{4,8},{8,12},{12,14},{14,10},{10,6},{6,2},{2,0},{1,3},{5,1},... | collective-permute-start | bytes 1327112 | tf_op jit(solution)/shard_map/ppermute | solution.py:379
  27.0 0.9 fusion.3
  27.9 1.3 %collective-permute-done.6.rest_15_.rest_5_ = bf16[432,256]{1,0:T(8,128)(2,1)S(1)} collective-permute-done((bf16[432,256]{1,0:T(8,128)(2,1)S(1)}, bf16[432,256]{1,0:T(8,128)(2,1)S(1)}, u32[]{:S(2)}, u32[]{:S(2)}) %collective-permute-start.6) | collective-permute-done | bytes 221216 | tf_op jit(solution)/shard_map/ppermute | solution.py:382
  29.2 0.1 pad_maximum_fusion.1
  29.3 4.7 %collective-permute-done.11.rest_4_ = bf16[864,256]{1,0:T(8,128)(2,1)S(1)} collective-permute-done((bf16[864,256]{1,0:T(8,128)(2,1)S(1)}, bf16[864,256]{1,0:T(8,128)(2,1)S(1)}, u32[]{:S(2)}, u32[]{:S(2)}) %collective-permute-start.11) | collective-permute-done | bytes 442400 | tf_op jit(solution)/shard_map/ppermute | solution.py:379
  34.0 2.1 %collective-permute-start.14 = (bf16[432,256]{1,0:T(8,128)(2,1)S(1)}, bf16[432,256]{1,0:T(8,128)(2,1)S(1)}, u32[]{:S(2)}, u32[]{:S(2)}) collective-permute-start(bf16[432,256]{1,0:T(8,128)(2,1)S(1)} %slice.116), channel_id=1, source_target_pairs={{0,4},{4,8},{8,12},{12,14},{14,10},{10,6},{6,2},{2,0},{1,3},{5,1},... | collective-permute-start | bytes 663560 | tf_op jit(solution)/shard_map/ppermute | solution.py:402
  36.2 0.6 collective-permute-start.15
  36.8 5.0 %collective-permute-start.1 = (bf16[3,8,16,256]{3,2,1,0:T(8,128)(2,1)S(1)}, bf16[3,8,16,256]{3,2,1,0:T(8,128)(2,1)S(1)}, u32[]{:S(2)}, u32[]{:S(2)}) collective-permute-start(bf16[3,8,16,256]{3,2,1,0:T(8,128)(2,1)S(1)} %pad_maximum_fusion.3), channel_id=1, source_target_pairs={{0,15},{1,0},{2,1},{3,2},{4,3},{5,4},{6,5},{7,6},{8,7},{9,8},{10,9... | collective-permute-start | bytes 589832 | tf_op jit(solution)/shard_map/ppermute | solution.py:374
  41.8 3.2 %collective-permute-done.1.high = bf16[3,8,16,256]{3,2,1,0:T(8,128)(2,1)S(1)} collective-permute-done((bf16[3,8,16,256]{3,2,1,0:T(8,128)(2,1)S(1)}, bf16[3,8,16,256]{3,2,1,0:T(8,128)(2,1)S(1)}, u32[]{:S(2)}, u32[]{:S(2)}) %collective-permute-start.1) | collective-permute-done | bytes 196640 | tf_op jit(solution)/shard_map/ppermute | solution.py:374
  45.0 0.1 collective-permute-start.17
  45.1 1.3 %prep.1 = (bf16[8,10,16,768]{3,2,1,0:T(8,128)(2,1)S(1)}, bf16[6,10,16,768]{3,2,1,0:T(8,128)(2,1)S(1)}, bf16[256,768]{1,0:T(8,128)(2,1)S(1)}, bf16[3,128,256]{2,1,0:T(8,128)(2,1)S(1)}) custom-call(s32[2,4,16]{2,1,0:T(4,128)S(1)} %bitcast.1, bf16[3,8,16,256]{3,2,1,0:T(8,128)(2,1)S(1)} %collective-permute-done.low, bf16[4,8,16,256]{3,2,1,0:T(8,128)(2,1)S(1)} %copy-done, ...), custom_call_target="tpu_custom_call" | custom-call | bytes 4194304 | tf_op jit(solution)/shard_map/prep/pallas_call | solution.py:357
  46.4 0.5 collective-permute-start.18
  47.0 2.3 %first.1 = (f32[512,256]{1,0:T(8,128)S(1)}, bf16[512,256]{1,0:T(8,128)(2,1)S(1)}, bf16[256,512]{1,0:T(8,128)(2,1)S(1)}) custom-call(bf16[8,10,16,768]{3,2,1,0:T(8,128)(2,1)S(1)} %get-tuple-element.30.sx_ref, bf16[3,128,256]{2,1,0:T(8,128)(2,1)S(1)} %get-tuple-element.31.mask_ref, bf16[432,256]{1,0:T(8,128)(2,1)S(1)} %copy-done.4, ...), custom_call_target="tpu_custom_call" | custom-call | flops 1811939328 | bytes 4194304 | tf_op jit(solution)/shard_map/first/pallas_call | solution.py:357
  49.3 2.2 %grad_two.1 = (bf16[3456,256]{1,0:T(8,128)(2,1)S(1)}, bf16[3456,256]{1,0:T(8,128)(2,1)S(1)}) custom-call(bf16[6,10,16,768]{3,2,1,0:T(8,128)(2,1)S(1)} %get-tuple-element.36.sc_ref, bf16[256,512]{1,0:T(8,128)(2,1)S(1)} %get-tuple-element.37.act_t_ref), custom_call_target="tpu_custom_call" | custom-call | flops 1811939328 | bytes 4194304 | tf_op jit(solution)/shard_map/grad_two/pallas_call | solution.py:357
  51.5 1.8 %collective-permute-done.17.rest_16_.rest_6_ = bf16[864,256]{1,0:T(8,128)(2,1)S(1)} collective-permute-done((bf16[864,256]{1,0:T(8,128)(2,1)S(1)}, bf16[864,256]{1,0:T(8,128)(2,1)S(1)}, u32[]{:S(2)}, u32[]{:S(2)}) %collective-permute-start.17) | collective-permute-done | bytes 442400 | tf_op jit(solution)/shard_map/ppermute | solution.py:406
  53.3 0.1 collective-permute-start.21
  53.4 0.7 collective-permute-start.22
  54.1 2.9 %collective-permute-done.19 = bf16[3456,256]{1,0:T(8,128)(2,1)S(1)} collective-permute-done((bf16[3456,256]{1,0:T(8,128)(2,1)S(1)}, bf16[3456,256]{1,0:T(8,128)(2,1)S(1)}, u32[]{:S(2)}, u32[]{:S(2)}) %collective-permute-start.19) | collective-permute-done | bytes 1769504 | tf_op jit(solution)/shard_map/ppermute | solution.py:428
  57.0 0.1 add_convert_fusion.7
  57.1 4.6 %collective-permute-done.21.rest_17_.rest_7_ = bf16[864,256]{1,0:T(8,128)(2,1)S(1)} collective-permute-done((bf16[864,256]{1,0:T(8,128)(2,1)S(1)}, bf16[864,256]{1,0:T(8,128)(2,1)S(1)}, u32[]{:S(2)}, u32[]{:S(2)}) %collective-permute-start.21) | collective-permute-done | bytes 442400 | tf_op jit(solution)/shard_map/ppermute | solution.py:429
  61.6 0.1 collective-permute-start.20
  61.7 1.7 %collective-permute-done.23.rest_20_.rest_10_ = bf16[864,256]{1,0:T(8,128)(2,1)S(1)} collective-permute-done((bf16[864,256]{1,0:T(8,128)(2,1)S(1)}, bf16[864,256]{1,0:T(8,128)(2,1)S(1)}, u32[]{:S(2)}, u32[]{:S(2)}) %collective-permute-start.23) | collective-permute-done | bytes 442400 | tf_op jit(solution)/shard_map/ppermute | solution.py:448
  63.4 2.4 %back.1.sd_ref = bf16[4,10,16,768]{3,2,1,0:T(8,128)(2,1)S(1)} custom-call(bf16[6,10,16,768]{3,2,1,0:T(8,128)(2,1)S(1)} %get-tuple-element.36.sc_ref, f32[512,256]{1,0:T(8,128)S(1)} %get-tuple-element.43.pre_ref, bf16[3,128,256]{2,1,0:T(8,128)(2,1)S(1)} %get-tuple-element.31.mask_ref, bf16[432,256]{1,0:T(8,128)(2,1)S(1)} %copy-done.2, ...), custom_call_target="tpu_custom_call" | custom-call | flops 1811939328 | bytes 4194304 | tf_op jit(solution)/shard_map/back/pallas_call | solution.py:357
  65.8 2.3 %grad_one.1 = (bf16[3456,256]{1,0:T(8,128)(2,1)S(1)}, bf16[3456,256]{1,0:T(8,128)(2,1)S(1)}) custom-call(bf16[4,10,16,768]{3,2,1,0:T(8,128)(2,1)S(1)} %back.1.sd_ref, bf16[256,768]{1,0:T(8,128)(2,1)S(1)} %get-tuple-element.44.int_ref), custom_call_target="tpu_custom_call" | custom-call | flops 1811939328 | bytes 4194304 | tf_op jit(solution)/shard_map/grad_one/pallas_call | solution.py:357
  68.1 0.2 collective-permute-start.24
  68.3 0.2 add_convert_fusion.4
  68.5 0.7 collective-permute-start.26
  69.1 2.7 %collective-permute-done.24 = bf16[3456,256]{1,0:T(8,128)(2,1)S(1)} collective-permute-done((bf16[3456,256]{1,0:T(8,128)(2,1)S(1)}, bf16[3456,256]{1,0:T(8,128)(2,1)S(1)}, u32[]{:S(2)}, u32[]{:S(2)}) %collective-permute-start.24) | collective-permute-done | bytes 1769504 | tf_op jit(solution)/shard_map/ppermute | solution.py:465
  71.9 0.1 add_convert_fusion.6
  71.9 1.0 collective-permute-start.25
  72.9 4.3 %third.1 = bf16[4,8,16,256]{3,2,1,0:T(8,128)(2,1)} custom-call(bf16[8,10,16,768]{3,2,1,0:T(8,128)(2,1)S(1)} %get-tuple-element.30.sx_ref, bf16[512,256]{1,0:T(8,128)(2,1)S(1)} %get-tuple-element.41.act_ref, bf16[3,128,256]{2,1,0:T(8,128)(2,1)S(1)} %get-tuple-element.31.mask_ref, bf16[432,256]{1,0:T(8,128)(2,1)S(1)} %copy-done.4, ...), custom_call_target="tpu_custom_call" | custom-call | flops 7247757312 | bytes 4194304 | tf_op jit(solution)/shard_map/third/pallas_call | solution.py:357
  77.2 2.0 %collective-permute-done.25 = bf16[432,256]{1,0:T(8,128)(2,1)S(1)} collective-permute-done((bf16[432,256]{1,0:T(8,128)(2,1)S(1)}, bf16[432,256]{1,0:T(8,128)(2,1)S(1)}, u32[]{:S(2)}, u32[]{:S(2)}) %collective-permute-start.25) | collective-permute-done | bytes 221216 | tf_op jit(solution)/shard_map/ppermute | solution.py:468
  79.2 0.1 add_convert_fusion.5
  79.3 0.7 collective-permute-start.27
  80.0 0.2 add_convert_fusion.1
  80.2 2.5 %collective-permute-start.31 = (bf16[864,256]{1,0:T(8,128)(2,1)S(1)}, bf16[864,256]{1,0:T(8,128)(2,1)S(1)}, u32[]{:S(2)}, u32[]{:S(2)}) collective-permute-start(bf16[864,256]{1,0:T(8,128)(2,1)S(1)} %add_convert_fusion.1), channel_id=1, source_target_pairs={{0,4},{4,8},{8,12},{12,14},{14,10},{10,6},{6,2},{2,0},{1,3},{5,1},... | collective-permute-start | bytes 1327112 | tf_op jit(solution)/shard_map/ppermute | solution.py:483
  82.7 5.0 %collective-permute-done.27 = bf16[864,256]{1,0:T(8,128)(2,1)S(1)} collective-permute-done((bf16[864,256]{1,0:T(8,128)(2,1)S(1)}, bf16[864,256]{1,0:T(8,128)(2,1)S(1)}, u32[]{:S(2)}, u32[]{:S(2)}) %collective-permute-start.27) | collective-permute-done | bytes 442400 | tf_op jit(solution)/shard_map/ppermute | solution.py:482
  87.7 0.2 add_convert_fusion.3
  87.9 0.7 collective-permute-start.28
  88.5 3.9 %collective-permute-done.31 = bf16[864,256]{1,0:T(8,128)(2,1)S(1)} collective-permute-done((bf16[864,256]{1,0:T(8,128)(2,1)S(1)}, bf16[864,256]{1,0:T(8,128)(2,1)S(1)}, u32[]{:S(2)}, u32[]{:S(2)}) %collective-permute-start.31) | collective-permute-done | bytes 442400 | tf_op jit(solution)/shard_map/ppermute | solution.py:483
  92.4 0.2 add_convert_fusion
  92.7 0.1 collective-permute-start.33
  92.7 1.5 %collective-permute-start.32 = (bf16[432,256]{1,0:T(8,128)(2,1)S(1)}, bf16[432,256]{1,0:T(8,128)(2,1)S(1)}, u32[]{:S(2)}, u32[]{:S(2)}) collective-permute-start(bf16[432,256]{1,0:T(8,128)(2,1)S(1)} %get-tuple-element.49), channel_id=1, source_target_pairs={{0,4},{4,8},{8,12},{12,14},{14,10},{10,6},{6,2},{2,0},{1,3},{5,1},... | collective-permute-start | bytes 663560 | tf_op jit(solution)/shard_map/ppermute | solution.py:443
  94.3 2.9 %collective-permute-done.28 = bf16[864,256]{1,0:T(8,128)(2,1)S(1)} collective-permute-done((bf16[864,256]{1,0:T(8,128)(2,1)S(1)}, bf16[864,256]{1,0:T(8,128)(2,1)S(1)}, u32[]{:S(2)}, u32[]{:S(2)}) %collective-permute-start.28) | collective-permute-done | bytes 442400 | tf_op jit(solution)/shard_map/ppermute | solution.py:485
  97.2 0.2 add_convert_fusion.2
  97.4 0.1 collective-permute-start.30
  97.5 1.5 %collective-permute-start.29 = (bf16[432,256]{1,0:T(8,128)(2,1)S(1)}, bf16[432,256]{1,0:T(8,128)(2,1)S(1)}, u32[]{:S(2)}, u32[]{:S(2)}) collective-permute-start(bf16[432,256]{1,0:T(8,128)(2,1)S(1)} %get-tuple-element.51), channel_id=1, source_target_pairs={{0,4},{4,8},{8,12},{12,14},{14,10},{10,6},{6,2},{2,0},{1,3},{5,1},... | collective-permute-start | bytes 663560 | tf_op jit(solution)/shard_map/ppermute | solution.py:443
  99.0 2.9 %collective-permute-done.32 = bf16[432,256]{1,0:T(8,128)(2,1)S(1)} collective-permute-done((bf16[432,256]{1,0:T(8,128)(2,1)S(1)}, bf16[432,256]{1,0:T(8,128)(2,1)S(1)}, u32[]{:S(2)}, u32[]{:S(2)}) %collective-permute-start.32) | collective-permute-done | bytes 221216 | tf_op jit(solution)/shard_map/ppermute | solution.py:443
  101.9 0.9 add_multiply_fusion
  102.8 0.0 collective-permute-done.30
  102.8 3.8 %collective-permute-done.29 = bf16[432,256]{1,0:T(8,128)(2,1)S(1)} collective-permute-done((bf16[432,256]{1,0:T(8,128)(2,1)S(1)}, bf16[432,256]{1,0:T(8,128)(2,1)S(1)}, u32[]{:S(2)}, u32[]{:S(2)}) %collective-permute-start.29) | collective-permute-done | bytes 221216 | tf_op jit(solution)/shard_map/ppermute | solution.py:443
  106.7 0.9 add_multiply_fusion.1
  (40 shorter events, 0.2 us)
Async XLA Ops:
  0.6 8.2 %collective-permute-start.2 = (bf16[432,256]{1,0:T(8,128)(2,1)}, bf16[432,256]{1,0:T(8,128)(2,1)S(1)}, u32[]{:S(2)}, u32[]{:S(2)}) collective-permute-start(bf16[432,256]{1,0:T(8,128)(2,1)} %rest_0_.4), channel_id=1, source_target_pairs={{0,4},{4,8},{8,12},{12,14},{14,10},{10,6},{6,2},{2,0},{1,3},{5,1},... | collective-permute-start | bytes 663560 | tf_op jit(solution)/shard_map/ppermute | solution.py:371
  3.7 6.4 %collective-permute-start.4 = (bf16[432,256]{1,0:T(8,128)(2,1)}, bf16[432,256]{1,0:T(8,128)(2,1)S(1)}, u32[]{:S(2)}, u32[]{:S(2)}) collective-permute-start(bf16[432,256]{1,0:T(8,128)(2,1)} %rest_0_.4), channel_id=1, source_target_pairs={{1,4},{5,8},{9,12},{13,14},{15,10},{11,6},{7,2},{3,0},{0,3},{4,1},... | collective-permute-start | bytes 663560 | tf_op jit(solution)/shard_map/ppermute | solution.py:371
  10.2 31.6 %copy-start.2 = (bf16[432,256]{1,0:T(8,128)(2,1)S(1)}, bf16[432,256]{1,0:T(8,128)(2,1)}, u32[]{:S(2)}) copy-start(bf16[432,256]{1,0:T(8,128)(2,1)} %rest_0_.5) | copy-start | bytes 663556
  10.2 34.9 %copy-start = (bf16[4,8,16,256]{3,2,1,0:T(8,128)(2,1)S(1)}, bf16[4,8,16,256]{3,2,1,0:T(8,128)(2,1)}, u32[]{:S(2)}) copy-start(bf16[4,8,16,256]{3,2,1,0:T(8,128)(2,1)} %f_own.1) | copy-start | bytes 786436
  10.2 34.9 %copy-start.1 = (bf16[4,8,16,256]{3,2,1,0:T(8,128)(2,1)S(1)}, bf16[4,8,16,256]{3,2,1,0:T(8,128)(2,1)}, u32[]{:S(2)}) copy-start(bf16[4,8,16,256]{3,2,1,0:T(8,128)(2,1)} %c_own.1) | copy-start | bytes 786436
  10.2 34.9 %copy-start.3 = (s32[16,2,4]{0,2,1:T(4,128)S(1)}, s32[16,2,4]{0,2,1:T(4,128)}, u32[]{:S(2)}) copy-start(s32[16,2,4]{0,2,1:T(4,128)} %param.9) | copy-start | bytes 1540
  10.2 15.2 %collective-permute-start.10 = (bf16[864,256]{1,0:T(8,128)(2,1)S(1)}, bf16[864,256]{1,0:T(8,128)(2,1)S(1)}, u32[]{:S(2)}, u32[]{:S(2)}) collective-permute-start(bf16[864,256]{1,0:T(8,128)(2,1)S(1)} %constant_dynamic-update-slice_fusion.rest_2_), channel_id=1, source_target_pairs={{0,4},{4,8},{8,12},{12,14},{14,10},{10,6},{6,2},{2,0},{1,3},{5,1},... | collective-permute-start | bytes 1327112 | tf_op jit(solution)/shard_map/ppermute | solution.py:376
  12.3 21.7 %collective-permute-start.9 = (bf16[432,256]{1,0:T(8,128)(2,1)}, bf16[432,256]{1,0:T(8,128)(2,1)S(1)}, u32[]{:S(2)}, u32[]{:S(2)}) collective-permute-start(bf16[432,256]{1,0:T(8,128)(2,1)} %rest_0_.4), channel_id=1, source_target_pairs={{0,1},{1,0},{2,3},{3,2},{4,5},{5,4},{6,7},{7,6},{8,9},{9,8},{10,11... | collective-permute-start | bytes 663560 | tf_op jit(solution)/shard_map/ppermute | solution.py:381
  12.3 11.0 %collective-permute-start.3 = (bf16[432,256]{1,0:T(8,128)(2,1)}, bf16[432,256]{1,0:T(8,128)(2,1)S(1)}, u32[]{:S(2)}, u32[]{:S(2)}) collective-permute-start(bf16[432,256]{1,0:T(8,128)(2,1)} %rest_0_.5), channel_id=1, source_target_pairs={{0,4},{4,8},{8,12},{12,14},{14,10},{10,6},{6,2},{2,0},{1,3},{5,1},... | collective-permute-start | bytes 663560 | tf_op jit(solution)/shard_map/ppermute | solution.py:372
  13.9 9.4 %collective-permute-start.5 = (bf16[432,256]{1,0:T(8,128)(2,1)}, bf16[432,256]{1,0:T(8,128)(2,1)S(1)}, u32[]{:S(2)}, u32[]{:S(2)}) collective-permute-start(bf16[432,256]{1,0:T(8,128)(2,1)} %rest_0_.5), channel_id=1, source_target_pairs={{1,4},{5,8},{9,12},{13,14},{15,10},{11,6},{7,2},{3,0},{0,3},{4,1},... | collective-permute-start | bytes 663560 | tf_op jit(solution)/shard_map/ppermute | solution.py:378
  15.1 18.9 %collective-permute-start.12 = (bf16[864,256]{1,0:T(8,128)(2,1)S(1)}, bf16[864,256]{1,0:T(8,128)(2,1)S(1)}, u32[]{:S(2)}, u32[]{:S(2)}) collective-permute-start(bf16[864,256]{1,0:T(8,128)(2,1)S(1)} %constant_dynamic-update-slice_fusion.rest_2_), channel_id=1, source_target_pairs={{0,1},{1,0},{2,3},{3,2},{4,5},{5,4},{6,7},{7,6},{8,9},{9,8},{10,11... | collective-permute-start | bytes 1327112 | tf_op jit(solution)/shard_map/ppermute | solution.py:377
  23.3 5.9 %collective-permute-start.6 = (bf16[432,256]{1,0:T(8,128)(2,1)S(1)}, bf16[432,256]{1,0:T(8,128)(2,1)S(1)}, u32[]{:S(2)}, u32[]{:S(2)}) collective-permute-start(bf16[432,256]{1,0:T(8,128)(2,1)S(1)} %collective-permute-done.3.rest_12_.rest_2_), channel_id=1, source_target_pairs={{0,4},{4,8},{8,12},{12,14},{14,10},{10,6},{6,2},{2,0},{1,3},{5,1},... | collective-permute-start | bytes 663560 | tf_op jit(solution)/shard_map/ppermute | solution.py:382
  25.4 8.6 %collective-permute-start.11 = (bf16[864,256]{1,0:T(8,128)(2,1)S(1)}, bf16[864,256]{1,0:T(8,128)(2,1)S(1)}, u32[]{:S(2)}, u32[]{:S(2)}) collective-permute-start(bf16[864,256]{1,0:T(8,128)(2,1)S(1)} %collective-permute-done.10.rest_3_), channel_id=1, source_target_pairs={{0,4},{4,8},{8,12},{12,14},{14,10},{10,6},{6,2},{2,0},{1,3},{5,1},... | collective-permute-start | bytes 1327112 | tf_op jit(solution)/shard_map/ppermute | solution.py:379
  27.0 7.1 %collective-permute-start.13 = (bf16[864,256]{1,0:T(8,128)(2,1)S(1)}, bf16[864,256]{1,0:T(8,128)(2,1)S(1)}, u32[]{:S(2)}, u32[]{:S(2)}) collective-permute-start(bf16[864,256]{1,0:T(8,128)(2,1)S(1)} %collective-permute-done.10.rest_3_), channel_id=1, source_target_pairs={{0,1},{1,0},{2,3},{3,2},{4,5},{5,4},{6,7},{7,6},{8,9},{9,8},{10,11... | collective-permute-start | bytes 1327112 | tf_op jit(solution)/shard_map/ppermute | solution.py:380
  27.9 19.1 %copy-start.4 = (bf16[432,256]{1,0:T(8,128)(2,1)S(1)}, bf16[432,256]{1,0:T(8,128)(2,1)}, u32[]{:S(2)}) copy-start(bf16[432,256]{1,0:T(8,128)(2,1)} %rest_0_.4) | copy-start | bytes 663556
  29.2 12.6 %collective-permute-start = (bf16[3,8,16,256]{3,2,1,0:T(8,128)(2,1)S(1)}, bf16[3,8,16,256]{3,2,1,0:T(8,128)(2,1)S(1)}, u32[]{:S(2)}, u32[]{:S(2)}) collective-permute-start(bf16[3,8,16,256]{3,2,1,0:T(8,128)(2,1)S(1)} %pad_maximum_fusion.2), channel_id=1, source_target_pairs={{0,1},{1,2},{2,3},{3,4},{4,5},{5,6},{6,7},{7,8},{8,9},{9,10},{10,1... | collective-permute-start | bytes 589832 | tf_op jit(solution)/shard_map/ppermute | solution.py:373
  34.0 13.0 %collective-permute-start.7 = (bf16[864,256]{1,0:T(8,128)(2,1)S(1)}, bf16[864,256]{1,0:T(8,128)(2,1)S(1)}, u32[]{:S(2)}, u32[]{:S(2)}) collective-permute-start(bf16[864,256]{1,0:T(8,128)(2,1)S(1)} %get-tuple-element.58), channel_id=1, source_target_pairs={{0,1},{1,0},{2,3},{3,2},{4,5},{5,4},{6,7},{7,6},{8,9},{9,8},{10,11... | collective-permute-start | bytes 1327112 | tf_op jit(solution)/shard_map/ppermute | solution.py:407
  34.0 11.0 %collective-permute-start.14 = (bf16[432,256]{1,0:T(8,128)(2,1)S(1)}, bf16[432,256]{1,0:T(8,128)(2,1)S(1)}, u32[]{:S(2)}, u32[]{:S(2)}) collective-permute-start(bf16[432,256]{1,0:T(8,128)(2,1)S(1)} %slice.116), channel_id=1, source_target_pairs={{0,4},{4,8},{8,12},{12,14},{14,10},{10,6},{6,2},{2,0},{1,3},{5,1},... | collective-permute-start | bytes 663560 | tf_op jit(solution)/shard_map/ppermute | solution.py:402
  36.2 10.8 %collective-permute-start.15 = (bf16[864,256]{1,0:T(8,128)(2,1)S(1)}, bf16[864,256]{1,0:T(8,128)(2,1)S(1)}, u32[]{:S(2)}, u32[]{:S(2)}) collective-permute-start(bf16[864,256]{1,0:T(8,128)(2,1)S(1)} %collective-permute-done.11.rest_4_), channel_id=1, source_target_pairs={{0,1},{1,0},{2,3},{3,2},{4,5},{5,4},{6,7},{7,6},{8,9},{9,8},{10,11... | collective-permute-start | bytes 1327112 | tf_op jit(solution)/shard_map/ppermute | solution.py:403
  36.8 8.2 %collective-permute-start.1 = (bf16[3,8,16,256]{3,2,1,0:T(8,128)(2,1)S(1)}, bf16[3,8,16,256]{3,2,1,0:T(8,128)(2,1)S(1)}, u32[]{:S(2)}, u32[]{:S(2)}) collective-permute-start(bf16[3,8,16,256]{3,2,1,0:T(8,128)(2,1)S(1)} %pad_maximum_fusion.3), channel_id=1, source_target_pairs={{0,15},{1,0},{2,1},{3,2},{4,3},{5,4},{6,5},{7,6},{8,7},{9,8},{10,9... | collective-permute-start | bytes 589832 | tf_op jit(solution)/shard_map/ppermute | solution.py:374
  41.8 4.6 %collective-permute-start.8 = (bf16[432,256]{1,0:T(8,128)(2,1)S(1)}, bf16[432,256]{1,0:T(8,128)(2,1)S(1)}, u32[]{:S(2)}, u32[]{:S(2)}) collective-permute-start(bf16[432,256]{1,0:T(8,128)(2,1)S(1)} %copy-done.2), channel_id=1, source_target_pairs={{0,1},{1,0},{2,3},{3,2},{4,5},{5,4},{6,7},{7,6},{8,9},{9,8},{10,11... | collective-permute-start | bytes 663560 | tf_op jit(solution)/shard_map/ppermute | solution.py:408
  45.0 1.9 %collective-permute-start.16 = (bf16[432,256]{1,0:T(8,128)(2,1)S(1)}, bf16[432,256]{1,0:T(8,128)(2,1)S(1)}, u32[]{:S(2)}, u32[]{:S(2)}) collective-permute-start(bf16[432,256]{1,0:T(8,128)(2,1)S(1)} %collective-permute-done.14.rest_5_), channel_id=1, source_target_pairs={{0,1},{1,0},{2,3},{3,2},{4,5},{5,4},{6,7},{7,6},{8,9},{9,8},{10,11... | collective-permute-start | bytes 663560 | tf_op jit(solution)/shard_map/ppermute | solution.py:403
  45.0 8.3 %collective-permute-start.17 = (bf16[864,256]{1,0:T(8,128)(2,1)S(1)}, bf16[864,256]{1,0:T(8,128)(2,1)S(1)}, u32[]{:S(2)}, u32[]{:S(2)}) collective-permute-start(bf16[864,256]{1,0:T(8,128)(2,1)S(1)} %get-tuple-element.57), channel_id=1, source_target_pairs={{0,4},{4,8},{8,12},{12,14},{14,10},{10,6},{6,2},{2,0},{1,3},{5,1},... | collective-permute-start | bytes 1327112 | tf_op jit(solution)/shard_map/ppermute | solution.py:406
  46.4 5.1 %collective-permute-start.18 = (bf16[432,256]{1,0:T(8,128)(2,1)S(1)}, bf16[432,256]{1,0:T(8,128)(2,1)S(1)}, u32[]{:S(2)}, u32[]{:S(2)}) collective-permute-start(bf16[432,256]{1,0:T(8,128)(2,1)S(1)} %collective-permute-done.6.rest_15_.rest_5_), channel_id=1, source_target_pairs={{0,1},{1,0},{2,3},{3,2},{4,5},{5,4},{6,7},{7,6},{8,9},{9,8},{10,11... | collective-permute-start | bytes 663560 | tf_op jit(solution)/shard_map/ppermute | solution.py:424
  53.3 3.7 %collective-permute-start.19 = (bf16[3456,256]{1,0:T(8,128)(2,1)S(1)}, bf16[3456,256]{1,0:T(8,128)(2,1)S(1)}, u32[]{:S(2)}, u32[]{:S(2)}) collective-permute-start(bf16[3456,256]{1,0:T(8,128)(2,1)S(1)} %get-tuple-element.40), channel_id=1, source_target_pairs={{0,1},{1,0},{2,3},{3,2},{4,5},{5,4},{6,7},{7,6},{8,9},{9,8},{10,11... | collective-permute-start | bytes 5308424 | tf_op jit(solution)/shard_map/ppermute | solution.py:428
  53.3 8.3 %collective-permute-start.21 = (bf16[864,256]{1,0:T(8,128)(2,1)S(1)}, bf16[864,256]{1,0:T(8,128)(2,1)S(1)}, u32[]{:S(2)}, u32[]{:S(2)}) collective-permute-start(bf16[864,256]{1,0:T(8,128)(2,1)S(1)} %collective-permute-done.17.rest_16_.rest_6_), channel_id=1, source_target_pairs={{0,4},{4,8},{8,12},{12,14},{14,10},{10,6},{6,2},{2,0},{1,3},{5,1},... | collective-permute-start | bytes 1327112 | tf_op jit(solution)/shard_map/ppermute | solution.py:429
  53.4 8.3 %collective-permute-start.22 = (bf16[864,256]{1,0:T(8,128)(2,1)S(1)}, bf16[864,256]{1,0:T(8,128)(2,1)S(1)}, u32[]{:S(2)}, u32[]{:S(2)}) collective-permute-start(bf16[864,256]{1,0:T(8,128)(2,1)S(1)} %collective-permute-done.17.rest_16_.rest_6_), channel_id=1, source_target_pairs={{0,1},{1,0},{2,3},{3,2},{4,5},{5,4},{6,7},{7,6},{8,9},{9,8},{10,11... | collective-permute-start | bytes 1327112 | tf_op jit(solution)/shard_map/ppermute | solution.py:430
  61.6 1.8 %collective-permute-start.23 = (bf16[864,256]{1,0:T(8,128)(2,1)S(1)}, bf16[864,256]{1,0:T(8,128)(2,1)S(1)}, u32[]{:S(2)}, u32[]{:S(2)}) collective-permute-start(bf16[864,256]{1,0:T(8,128)(2,1)S(1)} %collective-permute-done.21.rest_17_.rest_7_), channel_id=1, source_target_pairs={{0,1},{1,0},{2,3},{3,2},{4,5},{5,4},{6,7},{7,6},{8,9},{9,8},{10,11... | collective-permute-start | bytes 1327112 | tf_op jit(solution)/shard_map/ppermute | solution.py:448
  61.6 6.5 %collective-permute-start.20 = (bf16[432,256]{1,0:T(8,128)(2,1)S(1)}, bf16[432,256]{1,0:T(8,128)(2,1)S(1)}, u32[]{:S(2)}, u32[]{:S(2)}) collective-permute-start(bf16[432,256]{1,0:T(8,128)(2,1)S(1)} %add_convert_fusion.7), channel_id=1, source_target_pairs={{0,4},{4,8},{8,12},{12,14},{14,10},{10,6},{6,2},{2,0},{1,3},{5,1},... | collective-permute-start | bytes 663560 | tf_op jit(solution)/shard_map/ppermute | solution.py:447
  68.1 3.8 %collective-permute-start.24 = (bf16[3456,256]{1,0:T(8,128)(2,1)S(1)}, bf16[3456,256]{1,0:T(8,128)(2,1)S(1)}, u32[]{:S(2)}, u32[]{:S(2)}) collective-permute-start(bf16[3456,256]{1,0:T(8,128)(2,1)S(1)} %get-tuple-element.47), channel_id=1, source_target_pairs={{0,1},{1,0},{2,3},{3,2},{4,5},{5,4},{6,7},{7,6},{8,9},{9,8},{10,11... | collective-permute-start | bytes 5308424 | tf_op jit(solution)/shard_map/ppermute | solution.py:465
  68.5 10.9 %collective-permute-start.26 = (bf16[864,256]{1,0:T(8,128)(2,1)S(1)}, bf16[864,256]{1,0:T(8,128)(2,1)S(1)}, u32[]{:S(2)}, u32[]{:S(2)}) collective-permute-start(bf16[864,256]{1,0:T(8,128)(2,1)S(1)} %add_convert_fusion.4), channel_id=1, source_target_pairs={{0,4},{4,8},{8,12},{12,14},{14,10},{10,6},{6,2},{2,0},{1,3},{5,1},... | collective-permute-start | bytes 1327112 | tf_op jit(solution)/shard_map/ppermute | solution.py:467
  71.9 7.3 %collective-permute-start.25 = (bf16[432,256]{1,0:T(8,128)(2,1)S(1)}, bf16[432,256]{1,0:T(8,128)(2,1)S(1)}, u32[]{:S(2)}, u32[]{:S(2)}) collective-permute-start(bf16[432,256]{1,0:T(8,128)(2,1)S(1)} %add_convert_fusion.6), channel_id=1, source_target_pairs={{0,4},{4,8},{8,12},{12,14},{14,10},{10,6},{6,2},{2,0},{1,3},{5,1},... | collective-permute-start | bytes 663560 | tf_op jit(solution)/shard_map/ppermute | solution.py:468
  79.3 8.4 %collective-permute-start.27 = (bf16[864,256]{1,0:T(8,128)(2,1)S(1)}, bf16[864,256]{1,0:T(8,128)(2,1)S(1)}, u32[]{:S(2)}, u32[]{:S(2)}) collective-permute-start(bf16[864,256]{1,0:T(8,128)(2,1)S(1)} %add_convert_fusion.5), channel_id=1, source_target_pairs={{0,4},{4,8},{8,12},{12,14},{14,10},{10,6},{6,2},{2,0},{1,3},{5,1},... | collective-permute-start | bytes 1327112 | tf_op jit(solution)/shard_map/ppermute | solution.py:482
  80.2 12.3 %collective-permute-start.31 = (bf16[864,256]{1,0:T(8,128)(2,1)S(1)}, bf16[864,256]{1,0:T(8,128)(2,1)S(1)}, u32[]{:S(2)}, u32[]{:S(2)}) collective-permute-start(bf16[864,256]{1,0:T(8,128)(2,1)S(1)} %add_convert_fusion.1), channel_id=1, source_target_pairs={{0,4},{4,8},{8,12},{12,14},{14,10},{10,6},{6,2},{2,0},{1,3},{5,1},... | collective-permute-start | bytes 1327112 | tf_op jit(solution)/shard_map/ppermute | solution.py:483
  87.9 9.3 %collective-permute-start.28 = (bf16[864,256]{1,0:T(8,128)(2,1)S(1)}, bf16[864,256]{1,0:T(8,128)(2,1)S(1)}, u32[]{:S(2)}, u32[]{:S(2)}) collective-permute-start(bf16[864,256]{1,0:T(8,128)(2,1)S(1)} %add_convert_fusion.3), channel_id=1, source_target_pairs={{0,4},{4,8},{8,12},{12,14},{14,10},{10,6},{6,2},{2,0},{1,3},{5,1},... | collective-permute-start | bytes 1327112 | tf_op jit(solution)/shard_map/ppermute | solution.py:485
  92.7 6.3 %collective-permute-start.33 = (bf16[432,256]{1,0:T(8,128)(2,1)S(1)}, bf16[432,256]{1,0:T(8,128)(2,1)S(1)}, u32[]{:S(2)}, u32[]{:S(2)}) collective-permute-start(bf16[432,256]{1,0:T(8,128)(2,1)S(1)} %get-tuple-element.50), channel_id=1, source_target_pairs={{0,5},{4,9},{8,13},{12,15},{14,11},{10,7},{6,3},{2,1},{1,2},{5,0},... | collective-permute-start | bytes 663560 | tf_op jit(solution)/shard_map/ppermute | solution.py:444
  92.7 9.2 %collective-permute-start.32 = (bf16[432,256]{1,0:T(8,128)(2,1)S(1)}, bf16[432,256]{1,0:T(8,128)(2,1)S(1)}, u32[]{:S(2)}, u32[]{:S(2)}) collective-permute-start(bf16[432,256]{1,0:T(8,128)(2,1)S(1)} %get-tuple-element.49), channel_id=1, source_target_pairs={{0,4},{4,8},{8,12},{12,14},{14,10},{10,6},{6,2},{2,0},{1,3},{5,1},... | collective-permute-start | bytes 663560 | tf_op jit(solution)/shard_map/ppermute | solution.py:443
  97.4 5.5 %collective-permute-start.30 = (bf16[432,256]{1,0:T(8,128)(2,1)S(1)}, bf16[432,256]{1,0:T(8,128)(2,1)S(1)}, u32[]{:S(2)}, u32[]{:S(2)}) collective-permute-start(bf16[432,256]{1,0:T(8,128)(2,1)S(1)} %get-tuple-element.52), channel_id=1, source_target_pairs={{0,5},{4,9},{8,13},{12,15},{14,11},{10,7},{6,3},{2,1},{1,2},{5,0},... | collective-permute-start | bytes 663560 | tf_op jit(solution)/shard_map/ppermute | solution.py:444
  97.5 9.2 %collective-permute-start.29 = (bf16[432,256]{1,0:T(8,128)(2,1)S(1)}, bf16[432,256]{1,0:T(8,128)(2,1)S(1)}, u32[]{:S(2)}, u32[]{:S(2)}) collective-permute-start(bf16[432,256]{1,0:T(8,128)(2,1)S(1)} %get-tuple-element.51), channel_id=1, source_target_pairs={{0,4},{4,8},{8,12},{12,14},{14,10},{10,6},{6,2},{2,0},{1,3},{5,1},... | collective-permute-start | bytes 663560 | tf_op jit(solution)/shard_map/ppermute | solution.py:443

commit v7 on v3

--- a/solution.py
+++ b/solution.py
@@ -162,29 +162,17 @@
         store_shifted(sc_ref, x0, rows(value, side), ny, nz, channels)
 
 
-PIECES = (
-    (0, False, False),
-    (0, False, True),
-    (1, False, False),
-    (1, False, True),
-    (2, False, False),
-    (3, False, False),
-    (4, False, False),
-    (1, True, False),
-    (2, True, False),
-    (3, True, False),
-    (4, True, False),
-)
+PIECES = tuple((hop, False) for hop in range(5)) + tuple((hop, True) for hop in range(1, 5))
 
 
 def fill_weight(pieces, w_ref):
     tile = lax.axis_index("tiles")
     core = tile % 2
     rows = w_ref.shape[0] // 16
-    for piece, (hop, crossed, flip) in zip(pieces, PIECES):
+    for piece, (hop, crossed) in zip(pieces, PIECES):
         holder = 1 - core if crossed else core
         for half in range(piece.shape[0] // rows):
-            start = shard_rows(tile, holder, hop, flip or half == 1, rows)
+            start = shard_rows(tile, holder, hop, half == 1, rows)
             w_ref[pl.ds(start, rows)] = piece[half * rows : (half + 1) * rows]
 
 
@@ -338,7 +326,7 @@
             ]
         )
 
-    onward, gather_across, scatter_across = along_ring(0, 0), along_ring(1, 0), along_ring(0, 1)
+    onward, scatter_across = along_ring(0, 0), along_ring(0, 1)
     sibling = permute([(i, i ^ 1) for i in range(tiles)])
     up = permute([(i, (i + 1) % tiles) for i in range(tiles)])
     down = permute([(i, (i - 1) % tiles) for i in range(tiles)])
@@ -357,25 +345,20 @@
             scratch_shapes=scratches,
             compiler_params=pltpu.CompilerParams(vmem_limit_bytes=mib << 20),
             cost_estimate=pl.CostEstimate(
-                flops=4 * convs * flops, transcendentals=0, bytes_accessed=4 << 20
+                flops=convs * flops, transcendentals=0, bytes_accessed=4 << 20
             ),
         )(*operands)
 
-    a1 = [onward(weight_one), gather_across(weight_one)]
-    weight_late = after(weight_two, weight_one)
-    b1 = [onward(weight_late), gather_across(weight_late)]
-    features_late, cot_late, _ = lax.optimization_barrier((features, cotangent, a1[0]))
+    a0 = jnp.concatenate([weight_one, sibling(weight_one)])
+    b0 = jnp.concatenate([after(weight_two, a0), sibling(weight_two)])
+    features_late, cot_late, _ = lax.optimization_barrier((features, cotangent, b0))
     low = up(jnp.concatenate([features_late[-2:], cot_late[-1:]]))
     high = down(jnp.concatenate([features_late[:2], cot_late[:1]]))
 
-    a1_pair = jnp.concatenate(a1)
-    a2 = onward(a1_pair)
-    qa1 = sibling(a1_pair)
-    b1_pair = jnp.concatenate(b1)
-    b2 = onward(after(b1_pair, low, high))
-    a3 = onward(after(a2, qa1, b1_pair))
-    qa2 = sibling(a2)
-    other_one = sibling(weight_one)
+    a1, b1 = onward(a0), onward(b0)
+    a2, qa1 = onward(a1), sibling(a1)
+    b2, qb1 = onward(b1), sibling(b1)
+    a3, qa2 = onward(after(a2, b1, low, high, qa1)), sibling(a2)
     sx, sc, in_t, near = kernel(
         prep_kernel,
         "prep",
@@ -395,15 +378,14 @@
         high,
         smem=1,
     )
-    a4 = onward(after(a3[:rows], qa2, other_one, sx))
-    qa3, qa4 = sibling(a3), sibling(a4)
-    ones = [weight_one, other_one, *a1, a2, a3, a4, qa1, qa2, qa3, qa4]
+    b3, qb2 = onward(after(b2, qb1)), sibling(b2)
+    a4, qa3 = onward(after(a3[:rows], b2, sx, qa2)), sibling(a3)
+    b4, qb3 = onward(after(b3[:rows], qb2)), sibling(b3)
+    qa4, qb4 = sibling(a4), sibling(b4)
+    ones = [a0, a1, a2, a3, a4, qa1, qa2, qa3, qa4]
+    twos = [b0, b1, b2, b3, b4, qb1, qb2, qb3, qb4]
     n = len(ones)
 
-    qb1 = sibling(b1_pair)
-    b3 = onward(after(b2, qb1))
-    qb2 = sibling(b2)
-    other_two = sibling(weight_two)
     pre, act, act_t = kernel(
         functools.partial(first_kernel, n),
         "first",
@@ -415,17 +397,14 @@
             shape((channels, depth * area), BF),
         ),
         [weights],
-        after(sx, b2),
+        after(sx, b4),
         near,
         *ones,
     )
-    b4 = onward(after(b3[:rows], qb2, other_two))
-    qb3, qb4 = sibling(b3), sibling(b4)
-    twos = [weight_two, other_two, *b1, b2, b3, b4, qb1, qb2, qb3, qb4]
     keep_two, send_two = kernel(
-        grad_two_kernel, "grad_two", 8, 1, shards, [weights], sc, after(act_t, b3)
-    )
-    got_two = sibling(after(send_two, b4))
+        grad_two_kernel, "grad_two", 8, 1, shards, [weights], sc, act_t
+    )
+    got_two = sibling(send_two)
 
     def both(keep, got, lo, hi):
         return keep[lo * rows : hi * rows].astype(F32) + got[lo * rows : hi * rows].astype(F32)
@@ -441,7 +420,6 @@
         total = both(keep, got, 7, 8) + onward(message[:rows]).astype(F32)
         return (total + scatter_across(message[rows:]).astype(F32)) * loss_scale
 
-    two = onward(step(keep_two, got_two, None, 0))
     delta = kernel(
         functools.partial(back_kernel, n),
         "back",
@@ -457,9 +435,8 @@
     keep_one, send_one = kernel(
         grad_one_kernel, "grad_one", 8, 1, shards, [weights], delta, in_t
     )
-    got_one = sibling(after(send_one, two))
-    act_late = after(act, two)
-    two = onward(step(keep_two, got_two, two, 1))
+    two = onward(step(keep_two, after(got_two, keep_one), None, 0))
+    got_one = sibling(send_one)
     one = onward(step(keep_one, got_one, None, 0))
     features_out = kernel(
         functools.partial(third_kernel, n),
@@ -469,15 +446,16 @@
         shape(features.shape, BF),
         [weights, weights, scratch((depth + 2, ny + 2, nz, 3 * channels), BF)],
         sx,
-        act_late,
+        after(act, two),
         near,
         *ones,
         *twos,
     )
-    one = onward(after(step(keep_one, got_one, one, 1), features_out, two))
-    two = onward(step(keep_two, got_two, two, 2))
+    two = onward(step(keep_two, got_two, two, 1))
+    one = onward(step(keep_one, got_one, one, 1))
+    two = onward(step(keep_two, got_two, after(two, features_out), 2))
+    one = onward(step(keep_one, got_one, one, 2))
     grad_two = finish(keep_two, got_two, step(keep_two, got_two, two, 3))
-    one = onward(step(keep_one, got_one, one, 2))
     return (features_out, finish(keep_one, got_one, step(keep_one, got_one, one, 3)), grad_two)
 
 

time: 103 us -> 96.1 us (0.933)
  waiting for transfers between devices: 61.9 us -> 41.6 us
  starting transfers between devices: 19.8 us -> 33.8 us
    ppermute x25 -> x23, waiting for transfers between devices: 44.2 us -> 22.5 us  [the longest x2 5.95 us: on_ring(): a1, b1 = (onward(a0), onward(b0))]
    ppermute x25 -> x23, starting transfers between devices: 12.3 us -> 25 us  [the longest x2 4.63 us: on_ring(): a1, b1 = (onward(a0), onward(b0))]
    ppermute x1, starting transfers between devices: 4.48 us -> 0.01 us  [on_ring(): high = down(jnp.concatenate([features_late[:2], cot_late[:1]]))]
    ppermute x1, waiting for transfers between devices: 0.01 us -> 3.84 us  [on_ring(): high = down(jnp.concatenate([features_late[:2], cot_late[:1]]))]
    ppermute x2, starting transfers between devices: 1.12 us -> 4.79 us  [finish(): total = both(keep, got, 7, 8) + onward(message[:rows]).astype(F32)]
    ppermute x2, waiting for transfers between devices: 4.4 us -> 1.62 us  [finish(): total = both(keep, got, 7, 8) + onward(message[:rows]).astype(F32)]
    ppermute x2, waiting for transfers between devices: 2.1 us -> 4.23 us  [finish(): return (total + scatter_across(message[rows:]).astype(F32)) * loss_scale]
    slice x2, local copies, waits for them, and re-layouts: 1.91 us -> 0.03 us  [on_ring(): high = down(jnp.concatenate([features_late[:2], cot_late[:1]]))]
  transfers between devices with their start and end apart: 34 -> 32, of which waited for: 18 -> 18; matrix products, arithmetic and copies ran while one was open for 4% -> 4% of each run, Pallas kernels for 14% -> 15%
where the time goes in v7:
time: 96.1 us; the launch traced here: 96 us
  waiting for transfers between devices  41.6 us (43%)
  starting transfers between devices  33.8 us (35%)
  Pallas kernels  14.8 us (15%)
  other arithmetic  2.89 us (3%)
  local copies, waits for them, and re-layouts  2.07 us (2%)
    pallas_call x6, Pallas kernels, kernel(): pl.pallas_call(body, name=name, out_shape=outs, in_specs=[pl.BlockSpec(me...  14.8 us
    ppermute x2, waiting for transfers between devices, on_ring(): a1, b1 = (onward(a0), onward(b0))  5.95 us
    ppermute x1, waiting for transfers between devices, on_ring(): low = up(jnp.concatenate([features_late[-2:], cot_late[-1:]]))  5.28 us
    ppermute x2, starting transfers between devices, finish(): total = both(keep, got, 7, 8) + onward(message[:rows]).astype(F32)  4.79 us
    ppermute x2, starting transfers between devices, on_ring(): a1, b1 = (onward(a0), onward(b0))  4.63 us
    ppermute x2, waiting for transfers between devices, finish(): return (total + scatter_across(message[rows:]).astype(F32)) * loss_scale  4.23 us
    ppermute x1, waiting for transfers between devices, on_ring(): high = down(jnp.concatenate([features_late[:2], cot_late[:1]]))  3.84 us
    ppermute x1, waiting for transfers between devices, on_ring(): two = onward(step(keep_two, got_two, after(two, features_out), 2))  3.32 us
  transfers between devices with their start and end apart: 32, of which 18 were waited for; matrix products, arithmetic and copies ran while one was open for 4% of the time, Pallas kernels for 15%

profile of v7, /device:TPU:0, one launch (start us, length us, event | category | flops | bytes accessed | tf_op | source)
XLA Modules:
  0.0 96.0 jit_solution(14178591150903510935)
XLA Ops:
  0.7 0.5 collective-permute-start
  1.2 0.1 collective-permute-start.1
  1.3 0.9 constant_dynamic-update-slice_fusion.1
  2.2 0.3 collective-permute-done
  2.5 3.0 %collective-permute-start.10 = (bf16[864,256]{1,0:T(8,128)(2,1)S(1)}, bf16[864,256]{1,0:T(8,128)(2,1)S(1)}, u32[]{:S(2)}, u32[]{:S(2)}) collective-permute-start(bf16[864,256]{1,0:T(8,128)(2,1)S(1)} %constant_dynamic-update-slice_fusion.rest_0_), channel_id=1, source_target_pairs={{0,4},{4,8},{8,12},{12,14},{14,10},{10,6},{6,2},{2,0},{1,3},{5,1},... | collective-permute-start | bytes 1327112 | tf_op jit(solution)/shard_map/ppermute | solution.py:358
  5.5 0.9 constant_dynamic-update-slice_fusion.3
  6.5 1.6 %collective-permute-start.4 = (bf16[864,256]{1,0:T(8,128)(2,1)S(1)}, bf16[864,256]{1,0:T(8,128)(2,1)S(1)}, u32[]{:S(2)}, u32[]{:S(2)}) collective-permute-start(bf16[864,256]{1,0:T(8,128)(2,1)S(1)} %constant_dynamic-update-slice_fusion.2.rest_0_.rest_9_), channel_id=1, source_target_pairs={{0,4},{4,8},{8,12},{12,14},{14,10},{10,6},{6,2},{2,0},{1,3},{5,1},... | collective-permute-start | bytes 1327112 | tf_op jit(solution)/shard_map/ppermute | solution.py:358
  8.2 3.6 %collective-permute-done.10.rest_1_ = bf16[864,256]{1,0:T(8,128)(2,1)S(1)} collective-permute-done((bf16[864,256]{1,0:T(8,128)(2,1)S(1)}, bf16[864,256]{1,0:T(8,128)(2,1)S(1)}, u32[]{:S(2)}, u32[]{:S(2)}) %collective-permute-start.10) | collective-permute-done | bytes 442400 | tf_op jit(solution)/shard_map/ppermute | solution.py:358
  11.7 2.1 %collective-permute-start.11 = (bf16[864,256]{1,0:T(8,128)(2,1)S(1)}, bf16[864,256]{1,0:T(8,128)(2,1)S(1)}, u32[]{:S(2)}, u32[]{:S(2)}) collective-permute-start(bf16[864,256]{1,0:T(8,128)(2,1)S(1)} %collective-permute-done.10.rest_1_), channel_id=1, source_target_pairs={{0,4},{4,8},{8,12},{12,14},{14,10},{10,6},{6,2},{2,0},{1,3},{5,1},... | collective-permute-start | bytes 1327112 | tf_op jit(solution)/shard_map/ppermute | solution.py:359
  13.8 0.2 collective-permute-start.2
  14.1 2.4 %collective-permute-done.4.rest_1_.rest_10_ = bf16[864,256]{1,0:T(8,128)(2,1)S(1)} collective-permute-done((bf16[864,256]{1,0:T(8,128)(2,1)S(1)}, bf16[864,256]{1,0:T(8,128)(2,1)S(1)}, u32[]{:S(2)}, u32[]{:S(2)}) %collective-permute-start.4) | collective-permute-done | bytes 442400 | tf_op jit(solution)/shard_map/ppermute | solution.py:358
  16.5 2.1 %collective-permute-start.5 = (bf16[864,256]{1,0:T(8,128)(2,1)S(1)}, bf16[864,256]{1,0:T(8,128)(2,1)S(1)}, u32[]{:S(2)}, u32[]{:S(2)}) collective-permute-start(bf16[864,256]{1,0:T(8,128)(2,1)S(1)} %collective-permute-done.4.rest_1_.rest_10_), channel_id=1, source_target_pairs={{0,4},{4,8},{8,12},{12,14},{14,10},{10,6},{6,2},{2,0},{1,3},{5,1},... | collective-permute-start | bytes 1327112 | tf_op jit(solution)/shard_map/ppermute | solution.py:360
  18.6 5.3 %collective-permute-done.2.low = bf16[3,8,16,256]{3,2,1,0:T(8,128)(2,1)S(1)} collective-permute-done((bf16[3,8,16,256]{3,2,1,0:T(8,128)(2,1)S(1)}, bf16[3,8,16,256]{3,2,1,0:T(8,128)(2,1)S(1)}, u32[]{:S(2)}, u32[]{:S(2)}) %collective-permute-start.2) | collective-permute-done | bytes 196640 | tf_op jit(solution)/shard_map/ppermute | solution.py:355
  23.9 0.0 collective-permute-start.3
  23.9 3.8 %collective-permute-done.3.high = bf16[3,8,16,256]{3,2,1,0:T(8,128)(2,1)S(1)} collective-permute-done((bf16[3,8,16,256]{3,2,1,0:T(8,128)(2,1)S(1)}, bf16[3,8,16,256]{3,2,1,0:T(8,128)(2,1)S(1)}, u32[]{:S(2)}, u32[]{:S(2)}) %collective-permute-start.3) | collective-permute-done | bytes 196640 | tf_op jit(solution)/shard_map/ppermute | solution.py:356
  27.7 1.2 %collective-permute-start.13 = (bf16[864,256]{1,0:T(8,128)(2,1)S(1)}, bf16[864,256]{1,0:T(8,128)(2,1)S(1)}, u32[]{:S(2)}, u32[]{:S(2)}) collective-permute-start(bf16[864,256]{1,0:T(8,128)(2,1)S(1)} %collective-permute-done.11.rest_2_), channel_id=1, source_target_pairs={{0,4},{4,8},{8,12},{12,14},{14,10},{10,6},{6,2},{2,0},{1,3},{5,1},... | collective-permute-start | bytes 1327112 | tf_op jit(solution)/shard_map/ppermute | solution.py:361
  28.9 1.5 %collective-permute-start.14 = (bf16[864,256]{1,0:T(8,128)(2,1)S(1)}, bf16[864,256]{1,0:T(8,128)(2,1)S(1)}, u32[]{:S(2)}, u32[]{:S(2)}) collective-permute-start(bf16[864,256]{1,0:T(8,128)(2,1)S(1)} %collective-permute-done.11.rest_2_), channel_id=1, source_target_pairs={{0,1},{1,0},{2,3},{3,2},{4,5},{5,4},{6,7},{7,6},{8,9},{9,8},{10,11... | collective-permute-start | bytes 1327112 | tf_op jit(solution)/shard_map/ppermute | solution.py:361
  30.4 1.4 %collective-permute-start.7 = (bf16[864,256]{1,0:T(8,128)(2,1)S(1)}, bf16[864,256]{1,0:T(8,128)(2,1)S(1)}, u32[]{:S(2)}, u32[]{:S(2)}) collective-permute-start(bf16[864,256]{1,0:T(8,128)(2,1)S(1)} %collective-permute-done.5.rest_2_.rest_11_), channel_id=1, source_target_pairs={{0,4},{4,8},{8,12},{12,14},{14,10},{10,6},{6,2},{2,0},{1,3},{5,1},... | collective-permute-start | bytes 1327112 | tf_op jit(solution)/shard_map/ppermute | solution.py:381
  31.8 0.9 collective-permute-start.8
  32.7 1.3 %prep.1 = (bf16[8,10,16,768]{3,2,1,0:T(8,128)(2,1)S(1)}, bf16[6,10,16,768]{3,2,1,0:T(8,128)(2,1)S(1)}, bf16[256,768]{1,0:T(8,128)(2,1)S(1)}, bf16[3,128,256]{2,1,0:T(8,128)(2,1)S(1)}) custom-call(s32[2,4,16]{2,1,0:T(4,128)S(1)} %bitcast.1, bf16[3,8,16,256]{3,2,1,0:T(8,128)(2,1)S(1)} %collective-permute-done.2.low, bf16[4,8,16,256]{3,2,1,0:T(8,128)(2,1)S(1)} %copy-done, ...), custom_call_target="tpu_custom_call" | custom-call | bytes 4194304 | tf_op jit(solution)/shard_map/prep/pallas_call | solution.py:338
  34.0 2.0 %collective-permute-done.13.rest_3_ = bf16[864,256]{1,0:T(8,128)(2,1)S(1)} collective-permute-done((bf16[864,256]{1,0:T(8,128)(2,1)S(1)}, bf16[864,256]{1,0:T(8,128)(2,1)S(1)}, u32[]{:S(2)}, u32[]{:S(2)}) %collective-permute-start.13) | collective-permute-done | bytes 442400 | tf_op jit(solution)/shard_map/ppermute | solution.py:361
  36.0 1.3 %collective-permute-start.15 = (bf16[432,256]{1,0:T(8,128)(2,1)S(1)}, bf16[432,256]{1,0:T(8,128)(2,1)S(1)}, u32[]{:S(2)}, u32[]{:S(2)}) collective-permute-start(bf16[432,256]{1,0:T(8,128)(2,1)S(1)} %slice.121), channel_id=1, source_target_pairs={{0,4},{4,8},{8,12},{12,14},{14,10},{10,6},{6,2},{2,0},{1,3},{5,1},... | collective-permute-start | bytes 663560 | tf_op jit(solution)/shard_map/ppermute | solution.py:382
  37.3 0.6 collective-permute-start.16
  37.9 2.8 %collective-permute-done.7.rest_3_.rest_12_ = bf16[864,256]{1,0:T(8,128)(2,1)S(1)} collective-permute-done((bf16[864,256]{1,0:T(8,128)(2,1)S(1)}, bf16[864,256]{1,0:T(8,128)(2,1)S(1)}, u32[]{:S(2)}, u32[]{:S(2)}) %collective-permute-start.7) | collective-permute-done | bytes 442400 | tf_op jit(solution)/shard_map/ppermute | solution.py:381
  40.8 1.3 %collective-permute-start.9 = (bf16[432,256]{1,0:T(8,128)(2,1)S(1)}, bf16[432,256]{1,0:T(8,128)(2,1)S(1)}, u32[]{:S(2)}, u32[]{:S(2)}) collective-permute-start(bf16[432,256]{1,0:T(8,128)(2,1)S(1)} %slice.120), channel_id=1, source_target_pairs={{0,4},{4,8},{8,12},{12,14},{14,10},{10,6},{6,2},{2,0},{1,3},{5,1},... | collective-permute-start | bytes 663560 | tf_op jit(solution)/shard_map/ppermute | solution.py:383
  42.1 1.0 %collective-permute-done.15.rest_4_ = bf16[432,256]{1,0:T(8,128)(2,1)S(1)} collective-permute-done((bf16[432,256]{1,0:T(8,128)(2,1)S(1)}, bf16[432,256]{1,0:T(8,128)(2,1)S(1)}, u32[]{:S(2)}, u32[]{:S(2)}) %collective-permute-start.15) | collective-permute-done | bytes 221216 | tf_op jit(solution)/shard_map/ppermute | solution.py:382
  43.1 1.4 %collective-permute-start.17 = (bf16[432,256]{1,0:T(8,128)(2,1)S(1)}, bf16[432,256]{1,0:T(8,128)(2,1)S(1)}, u32[]{:S(2)}, u32[]{:S(2)}) collective-permute-start(bf16[432,256]{1,0:T(8,128)(2,1)S(1)} %collective-permute-done.15.rest_4_), channel_id=1, source_target_pairs={{0,1},{1,0},{2,3},{3,2},{4,5},{5,4},{6,7},{7,6},{8,9},{9,8},{10,11... | collective-permute-start | bytes 663560 | tf_op jit(solution)/shard_map/ppermute | solution.py:384
  44.6 0.0 collective-permute-start.19
  44.6 2.2 %collective-permute-done.9.rest_4_.rest_13_ = bf16[432,256]{1,0:T(8,128)(2,1)S(1)} collective-permute-done((bf16[432,256]{1,0:T(8,128)(2,1)S(1)}, bf16[432,256]{1,0:T(8,128)(2,1)S(1)}, u32[]{:S(2)}, u32[]{:S(2)}) %collective-permute-start.9) | collective-permute-done | bytes 221216 | tf_op jit(solution)/shard_map/ppermute | solution.py:383
  46.8 0.3 collective-permute-start.20
  47.1 2.3 %first.1 = (f32[512,256]{1,0:T(8,128)S(1)}, bf16[512,256]{1,0:T(8,128)(2,1)S(1)}, bf16[256,512]{1,0:T(8,128)(2,1)S(1)}) custom-call(bf16[8,10,16,768]{3,2,1,0:T(8,128)(2,1)S(1)} %get-tuple-element.31.sx_ref, bf16[3,128,256]{2,1,0:T(8,128)(2,1)S(1)} %get-tuple-element.32.mask_ref, bf16[864,256]{1,0:T(8,128)(2,1)S(1)} %constant_dynamic-update-slice_fusion.rest_0_, ...), custom_call_target="tpu_custom_call" | custom-call | flops 1811939328 | bytes 4194304 | tf_op jit(solution)/shard_map/first/pallas_call | solution.py:338
  49.4 2.2 %grad_two.1 = (bf16[3456,256]{1,0:T(8,128)(2,1)S(1)}, bf16[3456,256]{1,0:T(8,128)(2,1)S(1)}) custom-call(bf16[6,10,16,768]{3,2,1,0:T(8,128)(2,1)S(1)} %get-tuple-element.36.sc_ref, bf16[256,512]{1,0:T(8,128)(2,1)S(1)} %get-tuple-element.37.act_t_ref), custom_call_target="tpu_custom_call" | custom-call | flops 1811939328 | bytes 4194304 | tf_op jit(solution)/shard_map/grad_two/pallas_call | solution.py:338
  51.6 0.3 collective-permute-start.18
  51.9 2.4 %back.1.sd_ref = bf16[4,10,16,768]{3,2,1,0:T(8,128)(2,1)S(1)} custom-call(bf16[6,10,16,768]{3,2,1,0:T(8,128)(2,1)S(1)} %get-tuple-element.36.sc_ref, f32[512,256]{1,0:T(8,128)S(1)} %get-tuple-element.40.pre_ref, bf16[3,128,256]{2,1,0:T(8,128)(2,1)S(1)} %get-tuple-element.32.mask_ref, ...), custom_call_target="tpu_custom_call" | custom-call | flops 1811939328 | bytes 4194304 | tf_op jit(solution)/shard_map/back/pallas_call | solution.py:338
  54.4 2.3 %grad_one.1 = (bf16[3456,256]{1,0:T(8,128)(2,1)S(1)}, bf16[3456,256]{1,0:T(8,128)(2,1)S(1)}) custom-call(bf16[4,10,16,768]{3,2,1,0:T(8,128)(2,1)S(1)} %back.1.sd_ref, bf16[256,768]{1,0:T(8,128)(2,1)S(1)} %get-tuple-element.41.int_ref), custom_call_target="tpu_custom_call" | custom-call | flops 1811939328 | bytes 4194304 | tf_op jit(solution)/shard_map/grad_one/pallas_call | solution.py:338
  56.6 0.3 collective-permute-start.22
  57.0 0.1 add_convert_fusion.7
  57.0 1.0 %collective-permute-start.21 = (bf16[432,256]{1,0:T(8,128)(2,1)S(1)}, bf16[432,256]{1,0:T(8,128)(2,1)S(1)}, u32[]{:S(2)}, u32[]{:S(2)}) collective-permute-start(bf16[432,256]{1,0:T(8,128)(2,1)S(1)} %add_convert_fusion.7), channel_id=1, source_target_pairs={{0,4},{4,8},{8,12},{12,14},{14,10},{10,6},{6,2},{2,0},{1,3},{5,1},... | collective-permute-start | bytes 663560 | tf_op jit(solution)/shard_map/ppermute | solution.py:438
  58.1 2.3 %collective-permute-done.22 = bf16[3456,256]{1,0:T(8,128)(2,1)S(1)} collective-permute-done((bf16[3456,256]{1,0:T(8,128)(2,1)S(1)}, bf16[3456,256]{1,0:T(8,128)(2,1)S(1)}, u32[]{:S(2)}, u32[]{:S(2)}) %collective-permute-start.22) | collective-permute-done | bytes 1769504 | tf_op jit(solution)/shard_map/ppermute | solution.py:439
  60.4 0.1 add_convert_fusion.6
  60.4 1.3 %collective-permute-start.23 = (bf16[432,256]{1,0:T(8,128)(2,1)S(1)}, bf16[432,256]{1,0:T(8,128)(2,1)S(1)}, u32[]{:S(2)}, u32[]{:S(2)}) collective-permute-start(bf16[432,256]{1,0:T(8,128)(2,1)S(1)} %add_convert_fusion.6), channel_id=1, source_target_pairs={{0,4},{4,8},{8,12},{12,14},{14,10},{10,6},{6,2},{2,0},{1,3},{5,1},... | collective-permute-start | bytes 663560 | tf_op jit(solution)/shard_map/ppermute | solution.py:440
  61.7 1.3 %collective-permute-done.21 = bf16[432,256]{1,0:T(8,128)(2,1)S(1)} collective-permute-done((bf16[432,256]{1,0:T(8,128)(2,1)S(1)}, bf16[432,256]{1,0:T(8,128)(2,1)S(1)}, u32[]{:S(2)}, u32[]{:S(2)}) %collective-permute-start.21) | collective-permute-done | bytes 221216 | tf_op jit(solution)/shard_map/ppermute | solution.py:438
  63.0 0.1 add_convert_fusion.2
  63.2 1.3 %collective-permute-start.28 = (bf16[864,256]{1,0:T(8,128)(2,1)S(1)}, bf16[864,256]{1,0:T(8,128)(2,1)S(1)}, u32[]{:S(2)}, u32[]{:S(2)}) collective-permute-start(bf16[864,256]{1,0:T(8,128)(2,1)S(1)} %add_convert_fusion.2), channel_id=1, source_target_pairs={{0,4},{4,8},{8,12},{12,14},{14,10},{10,6},{6,2},{2,0},{1,3},{5,1},... | collective-permute-start | bytes 1327112 | tf_op jit(solution)/shard_map/ppermute | solution.py:454
  64.4 2.0 %collective-permute-done.23 = bf16[432,256]{1,0:T(8,128)(2,1)S(1)} collective-permute-done((bf16[432,256]{1,0:T(8,128)(2,1)S(1)}, bf16[432,256]{1,0:T(8,128)(2,1)S(1)}, u32[]{:S(2)}, u32[]{:S(2)}) %collective-permute-start.23) | collective-permute-done | bytes 221216 | tf_op jit(solution)/shard_map/ppermute | solution.py:440
  66.4 0.2 add_convert_fusion.5
  66.6 1.5 %collective-permute-start.24 = (bf16[864,256]{1,0:T(8,128)(2,1)S(1)}, bf16[864,256]{1,0:T(8,128)(2,1)S(1)}, u32[]{:S(2)}, u32[]{:S(2)}) collective-permute-start(bf16[864,256]{1,0:T(8,128)(2,1)S(1)} %add_convert_fusion.5), channel_id=1, source_target_pairs={{0,4},{4,8},{8,12},{12,14},{14,10},{10,6},{6,2},{2,0},{1,3},{5,1},... | collective-permute-start | bytes 1327112 | tf_op jit(solution)/shard_map/ppermute | solution.py:455
  68.1 4.2 %third.1 = bf16[4,8,16,256]{3,2,1,0:T(8,128)(2,1)} custom-call(bf16[8,10,16,768]{3,2,1,0:T(8,128)(2,1)S(1)} %get-tuple-element.31.sx_ref, bf16[512,256]{1,0:T(8,128)(2,1)S(1)} %get-tuple-element.44.act_ref, bf16[3,128,256]{2,1,0:T(8,128)(2,1)S(1)} %get-tuple-element.32.mask_ref, bf16[864,256]{1,0:T(8,128)(2,1)S(1)} %constant_dynamic-update-slice_fusion.rest_0_, ...), custom_call_target="tpu_custom_call" | custom-call | flops 1811939328 | bytes 4194304 | tf_op jit(solution)/shard_map/third/pallas_call | solution.py:338
  72.3 0.2 add_convert_fusion.1
  72.5 2.5 %collective-permute-start.29 = (bf16[864,256]{1,0:T(8,128)(2,1)S(1)}, bf16[864,256]{1,0:T(8,128)(2,1)S(1)}, u32[]{:S(2)}, u32[]{:S(2)}) collective-permute-start(bf16[864,256]{1,0:T(8,128)(2,1)S(1)} %add_convert_fusion.1), channel_id=1, source_target_pairs={{0,4},{4,8},{8,12},{12,14},{14,10},{10,6},{6,2},{2,0},{1,3},{5,1},... | collective-permute-start | bytes 1327112 | tf_op jit(solution)/shard_map/ppermute | solution.py:456
  75.0 1.2 %collective-permute-done.24 = bf16[864,256]{1,0:T(8,128)(2,1)S(1)} collective-permute-done((bf16[864,256]{1,0:T(8,128)(2,1)S(1)}, bf16[864,256]{1,0:T(8,128)(2,1)S(1)}, u32[]{:S(2)}, u32[]{:S(2)}) %collective-permute-start.24) | collective-permute-done | bytes 442400 | tf_op jit(solution)/shard_map/ppermute | solution.py:455
  76.2 0.2 add_convert_fusion.4
  76.4 1.3 %collective-permute-start.25 = (bf16[864,256]{1,0:T(8,128)(2,1)S(1)}, bf16[864,256]{1,0:T(8,128)(2,1)S(1)}, u32[]{:S(2)}, u32[]{:S(2)}) collective-permute-start(bf16[864,256]{1,0:T(8,128)(2,1)S(1)} %add_convert_fusion.4), channel_id=1, source_target_pairs={{0,4},{4,8},{8,12},{12,14},{14,10},{10,6},{6,2},{2,0},{1,3},{5,1},... | collective-permute-start | bytes 1327112 | tf_op jit(solution)/shard_map/ppermute | solution.py:457
  77.7 3.3 %collective-permute-done.29 = bf16[864,256]{1,0:T(8,128)(2,1)S(1)} collective-permute-done((bf16[864,256]{1,0:T(8,128)(2,1)S(1)}, bf16[864,256]{1,0:T(8,128)(2,1)S(1)}, u32[]{:S(2)}, u32[]{:S(2)}) %collective-permute-start.29) | collective-permute-done | bytes 442400 | tf_op jit(solution)/shard_map/ppermute | solution.py:456
  81.0 0.2 add_convert_fusion
  81.2 2.4 %collective-permute-start.30 = (bf16[432,256]{1,0:T(8,128)(2,1)S(1)}, bf16[432,256]{1,0:T(8,128)(2,1)S(1)}, u32[]{:S(2)}, u32[]{:S(2)}) collective-permute-start(bf16[432,256]{1,0:T(8,128)(2,1)S(1)} %get-tuple-element.47), channel_id=1, source_target_pairs={{0,4},{4,8},{8,12},{12,14},{14,10},{10,6},{6,2},{2,0},{1,3},{5,1},... | collective-permute-start | bytes 663560 | tf_op jit(solution)/shard_map/ppermute | solution.py:420
  83.6 2.1 %collective-permute-done.25 = bf16[864,256]{1,0:T(8,128)(2,1)S(1)} collective-permute-done((bf16[864,256]{1,0:T(8,128)(2,1)S(1)}, bf16[864,256]{1,0:T(8,128)(2,1)S(1)}, u32[]{:S(2)}, u32[]{:S(2)}) %collective-permute-start.25) | collective-permute-done | bytes 442400 | tf_op jit(solution)/shard_map/ppermute | solution.py:457
  85.7 0.2 add_convert_fusion.3
  85.9 2.4 %collective-permute-start.26 = (bf16[432,256]{1,0:T(8,128)(2,1)S(1)}, bf16[432,256]{1,0:T(8,128)(2,1)S(1)}, u32[]{:S(2)}, u32[]{:S(2)}) collective-permute-start(bf16[432,256]{1,0:T(8,128)(2,1)S(1)} %get-tuple-element.49), channel_id=1, source_target_pairs={{0,4},{4,8},{8,12},{12,14},{14,10},{10,6},{6,2},{2,0},{1,3},{5,1},... | collective-permute-start | bytes 663560 | tf_op jit(solution)/shard_map/ppermute | solution.py:420
  88.3 2.0 %collective-permute-done.31 = bf16[432,256]{1,0:T(8,128)(2,1)S(1)} collective-permute-done((bf16[432,256]{1,0:T(8,128)(2,1)S(1)}, bf16[432,256]{1,0:T(8,128)(2,1)S(1)}, u32[]{:S(2)}, u32[]{:S(2)}) %collective-permute-start.31) | collective-permute-done | bytes 221216 | tf_op jit(solution)/shard_map/ppermute | solution.py:421
  90.3 0.9 add_multiply_fusion
  91.2 1.6 %collective-permute-done.26 = bf16[432,256]{1,0:T(8,128)(2,1)S(1)} collective-permute-done((bf16[432,256]{1,0:T(8,128)(2,1)S(1)}, bf16[432,256]{1,0:T(8,128)(2,1)S(1)}, u32[]{:S(2)}, u32[]{:S(2)}) %collective-permute-start.26) | collective-permute-done | bytes 221216 | tf_op jit(solution)/shard_map/ppermute | solution.py:420
  92.8 2.2 %collective-permute-done.27 = bf16[432,256]{1,0:T(8,128)(2,1)S(1)} collective-permute-done((bf16[432,256]{1,0:T(8,128)(2,1)S(1)}, bf16[432,256]{1,0:T(8,128)(2,1)S(1)}, u32[]{:S(2)}, u32[]{:S(2)}) %collective-permute-start.27) | collective-permute-done | bytes 221216 | tf_op jit(solution)/shard_map/ppermute | solution.py:421
  95.1 0.9 add_multiply_fusion.1
  (34 shorter events, 0.3 us)
Async XLA Ops:
  0.6 7.5 %copy-start.1 = (bf16[4,8,16,256]{3,2,1,0:T(8,128)(2,1)S(1)}, bf16[4,8,16,256]{3,2,1,0:T(8,128)(2,1)}, u32[]{:S(2)}) copy-start(bf16[4,8,16,256]{3,2,1,0:T(8,128)(2,1)} %c_own.1) | copy-start | bytes 786436
  0.6 7.5 %copy-start = (bf16[4,8,16,256]{3,2,1,0:T(8,128)(2,1)S(1)}, bf16[4,8,16,256]{3,2,1,0:T(8,128)(2,1)}, u32[]{:S(2)}) copy-start(bf16[4,8,16,256]{3,2,1,0:T(8,128)(2,1)} %f_own.1) | copy-start | bytes 786436
  0.7 32.0 %copy-start.2 = (s32[16,2,4]{0,2,1:T(4,128)S(1)}, s32[16,2,4]{0,2,1:T(4,128)}, u32[]{:S(2)}) copy-start(s32[16,2,4]{0,2,1:T(4,128)} %param.9) | copy-start | bytes 1540
  0.7 1.8 %collective-permute-start = (bf16[432,256]{1,0:T(8,128)(2,1)}, bf16[432,256]{1,0:T(8,128)(2,1)S(1)}, u32[]{:S(2)}, u32[]{:S(2)}) collective-permute-start(bf16[432,256]{1,0:T(8,128)(2,1)} %param.6), channel_id=1, source_target_pairs={{0,1},{1,0},{2,3},{3,2},{4,5},{5,4},{6,7},{7,6},{8,9},{9,8},{10,11... | collective-permute-start | bytes 663560 | tf_op jit(solution)/shard_map/ppermute | solution.py:352
  1.2 5.3 %collective-permute-start.1 = (bf16[432,256]{1,0:T(8,128)(2,1)}, bf16[432,256]{1,0:T(8,128)(2,1)S(1)}, u32[]{:S(2)}, u32[]{:S(2)}) collective-permute-start(bf16[432,256]{1,0:T(8,128)(2,1)} %param.7), channel_id=1, source_target_pairs={{0,1},{1,0},{2,3},{3,2},{4,5},{5,4},{6,7},{7,6},{8,9},{9,8},{10,11... | collective-permute-start | bytes 663560 | tf_op jit(solution)/shard_map/ppermute | solution.py:353
  2.5 9.2 %collective-permute-start.10 = (bf16[864,256]{1,0:T(8,128)(2,1)S(1)}, bf16[864,256]{1,0:T(8,128)(2,1)S(1)}, u32[]{:S(2)}, u32[]{:S(2)}) collective-permute-start(bf16[864,256]{1,0:T(8,128)(2,1)S(1)} %constant_dynamic-update-slice_fusion.rest_0_), channel_id=1, source_target_pairs={{0,4},{4,8},{8,12},{12,14},{14,10},{10,6},{6,2},{2,0},{1,3},{5,1},... | collective-permute-start | bytes 1327112 | tf_op jit(solution)/shard_map/ppermute | solution.py:358
  6.5 10.0 %collective-permute-start.4 = (bf16[864,256]{1,0:T(8,128)(2,1)S(1)}, bf16[864,256]{1,0:T(8,128)(2,1)S(1)}, u32[]{:S(2)}, u32[]{:S(2)}) collective-permute-start(bf16[864,256]{1,0:T(8,128)(2,1)S(1)} %constant_dynamic-update-slice_fusion.2.rest_0_.rest_9_), channel_id=1, source_target_pairs={{0,4},{4,8},{8,12},{12,14},{14,10},{10,6},{6,2},{2,0},{1,3},{5,1},... | collective-permute-start | bytes 1327112 | tf_op jit(solution)/shard_map/ppermute | solution.py:358
  11.7 16.0 %collective-permute-start.12 = (bf16[864,256]{1,0:T(8,128)(2,1)S(1)}, bf16[864,256]{1,0:T(8,128)(2,1)S(1)}, u32[]{:S(2)}, u32[]{:S(2)}) collective-permute-start(bf16[864,256]{1,0:T(8,128)(2,1)S(1)} %collective-permute-done.10.rest_1_), channel_id=1, source_target_pairs={{0,1},{1,0},{2,3},{3,2},{4,5},{5,4},{6,7},{7,6},{8,9},{9,8},{10,11... | collective-permute-start | bytes 1327112 | tf_op jit(solution)/shard_map/ppermute | solution.py:359
  11.7 16.0 %collective-permute-start.11 = (bf16[864,256]{1,0:T(8,128)(2,1)S(1)}, bf16[864,256]{1,0:T(8,128)(2,1)S(1)}, u32[]{:S(2)}, u32[]{:S(2)}) collective-permute-start(bf16[864,256]{1,0:T(8,128)(2,1)S(1)} %collective-permute-done.10.rest_1_), channel_id=1, source_target_pairs={{0,4},{4,8},{8,12},{12,14},{14,10},{10,6},{6,2},{2,0},{1,3},{5,1},... | collective-permute-start | bytes 1327112 | tf_op jit(solution)/shard_map/ppermute | solution.py:359
  13.8 10.0 %collective-permute-start.2 = (bf16[3,8,16,256]{3,2,1,0:T(8,128)(2,1)S(1)}, bf16[3,8,16,256]{3,2,1,0:T(8,128)(2,1)S(1)}, u32[]{:S(2)}, u32[]{:S(2)}) collective-permute-start(bf16[3,8,16,256]{3,2,1,0:T(8,128)(2,1)S(1)} %pad_maximum_fusion), channel_id=1, source_target_pairs={{0,1},{1,2},{2,3},{3,4},{4,5},{5,6},{6,7},{7,8},{8,9},{9,10},{10,1... | collective-permute-start | bytes 589832 | tf_op jit(solution)/shard_map/ppermute | solution.py:355
  16.5 13.9 %collective-permute-start.6 = (bf16[864,256]{1,0:T(8,128)(2,1)S(1)}, bf16[864,256]{1,0:T(8,128)(2,1)S(1)}, u32[]{:S(2)}, u32[]{:S(2)}) collective-permute-start(bf16[864,256]{1,0:T(8,128)(2,1)S(1)} %collective-permute-done.4.rest_1_.rest_10_), channel_id=1, source_target_pairs={{0,1},{1,0},{2,3},{3,2},{4,5},{5,4},{6,7},{7,6},{8,9},{9,8},{10,11... | collective-permute-start | bytes 1327112 | tf_op jit(solution)/shard_map/ppermute | solution.py:360
  16.5 13.9 %collective-permute-start.5 = (bf16[864,256]{1,0:T(8,128)(2,1)S(1)}, bf16[864,256]{1,0:T(8,128)(2,1)S(1)}, u32[]{:S(2)}, u32[]{:S(2)}) collective-permute-start(bf16[864,256]{1,0:T(8,128)(2,1)S(1)} %collective-permute-done.4.rest_1_.rest_10_), channel_id=1, source_target_pairs={{0,4},{4,8},{8,12},{12,14},{14,10},{10,6},{6,2},{2,0},{1,3},{5,1},... | collective-permute-start | bytes 1327112 | tf_op jit(solution)/shard_map/ppermute | solution.py:360
  23.9 3.8 %collective-permute-start.3 = (bf16[3,8,16,256]{3,2,1,0:T(8,128)(2,1)S(1)}, bf16[3,8,16,256]{3,2,1,0:T(8,128)(2,1)S(1)}, u32[]{:S(2)}, u32[]{:S(2)}) collective-permute-start(bf16[3,8,16,256]{3,2,1,0:T(8,128)(2,1)S(1)} %pad_maximum_fusion.1), channel_id=1, source_target_pairs={{0,15},{1,0},{2,1},{3,2},{4,3},{5,4},{6,5},{7,6},{8,7},{9,8},{10,9... | collective-permute-start | bytes 589832 | tf_op jit(solution)/shard_map/ppermute | solution.py:356
  27.7 8.3 %collective-permute-start.13 = (bf16[864,256]{1,0:T(8,128)(2,1)S(1)}, bf16[864,256]{1,0:T(8,128)(2,1)S(1)}, u32[]{:S(2)}, u32[]{:S(2)}) collective-permute-start(bf16[864,256]{1,0:T(8,128)(2,1)S(1)} %collective-permute-done.11.rest_2_), channel_id=1, source_target_pairs={{0,4},{4,8},{8,12},{12,14},{14,10},{10,6},{6,2},{2,0},{1,3},{5,1},... | collective-permute-start | bytes 1327112 | tf_op jit(solution)/shard_map/ppermute | solution.py:361
  28.9 7.2 %collective-permute-start.14 = (bf16[864,256]{1,0:T(8,128)(2,1)S(1)}, bf16[864,256]{1,0:T(8,128)(2,1)S(1)}, u32[]{:S(2)}, u32[]{:S(2)}) collective-permute-start(bf16[864,256]{1,0:T(8,128)(2,1)S(1)} %collective-permute-done.11.rest_2_), channel_id=1, source_target_pairs={{0,1},{1,0},{2,3},{3,2},{4,5},{5,4},{6,7},{7,6},{8,9},{9,8},{10,11... | collective-permute-start | bytes 1327112 | tf_op jit(solution)/shard_map/ppermute | solution.py:361
  30.4 10.4 %collective-permute-start.7 = (bf16[864,256]{1,0:T(8,128)(2,1)S(1)}, bf16[864,256]{1,0:T(8,128)(2,1)S(1)}, u32[]{:S(2)}, u32[]{:S(2)}) collective-permute-start(bf16[864,256]{1,0:T(8,128)(2,1)S(1)} %collective-permute-done.5.rest_2_.rest_11_), channel_id=1, source_target_pairs={{0,4},{4,8},{8,12},{12,14},{14,10},{10,6},{6,2},{2,0},{1,3},{5,1},... | collective-permute-start | bytes 1327112 | tf_op jit(solution)/shard_map/ppermute | solution.py:381
  31.8 9.0 %collective-permute-start.8 = (bf16[864,256]{1,0:T(8,128)(2,1)S(1)}, bf16[864,256]{1,0:T(8,128)(2,1)S(1)}, u32[]{:S(2)}, u32[]{:S(2)}) collective-permute-start(bf16[864,256]{1,0:T(8,128)(2,1)S(1)} %collective-permute-done.5.rest_2_.rest_11_), channel_id=1, source_target_pairs={{0,1},{1,0},{2,3},{3,2},{4,5},{5,4},{6,7},{7,6},{8,9},{9,8},{10,11... | collective-permute-start | bytes 1327112 | tf_op jit(solution)/shard_map/ppermute | solution.py:381
  36.0 7.1 %collective-permute-start.15 = (bf16[432,256]{1,0:T(8,128)(2,1)S(1)}, bf16[432,256]{1,0:T(8,128)(2,1)S(1)}, u32[]{:S(2)}, u32[]{:S(2)}) collective-permute-start(bf16[432,256]{1,0:T(8,128)(2,1)S(1)} %slice.121), channel_id=1, source_target_pairs={{0,4},{4,8},{8,12},{12,14},{14,10},{10,6},{6,2},{2,0},{1,3},{5,1},... | collective-permute-start | bytes 663560 | tf_op jit(solution)/shard_map/ppermute | solution.py:382
  37.3 9.7 %collective-permute-start.16 = (bf16[864,256]{1,0:T(8,128)(2,1)S(1)}, bf16[864,256]{1,0:T(8,128)(2,1)S(1)}, u32[]{:S(2)}, u32[]{:S(2)}) collective-permute-start(bf16[864,256]{1,0:T(8,128)(2,1)S(1)} %collective-permute-done.13.rest_3_), channel_id=1, source_target_pairs={{0,1},{1,0},{2,3},{3,2},{4,5},{5,4},{6,7},{7,6},{8,9},{9,8},{10,11... | collective-permute-start | bytes 1327112 | tf_op jit(solution)/shard_map/ppermute | solution.py:382
  40.8 6.0 %collective-permute-start.9 = (bf16[432,256]{1,0:T(8,128)(2,1)S(1)}, bf16[432,256]{1,0:T(8,128)(2,1)S(1)}, u32[]{:S(2)}, u32[]{:S(2)}) collective-permute-start(bf16[432,256]{1,0:T(8,128)(2,1)S(1)} %slice.120), channel_id=1, source_target_pairs={{0,4},{4,8},{8,12},{12,14},{14,10},{10,6},{6,2},{2,0},{1,3},{5,1},... | collective-permute-start | bytes 663560 | tf_op jit(solution)/shard_map/ppermute | solution.py:383
  43.1 3.9 %collective-permute-start.17 = (bf16[432,256]{1,0:T(8,128)(2,1)S(1)}, bf16[432,256]{1,0:T(8,128)(2,1)S(1)}, u32[]{:S(2)}, u32[]{:S(2)}) collective-permute-start(bf16[432,256]{1,0:T(8,128)(2,1)S(1)} %collective-permute-done.15.rest_4_), channel_id=1, source_target_pairs={{0,1},{1,0},{2,3},{3,2},{4,5},{5,4},{6,7},{7,6},{8,9},{9,8},{10,11... | collective-permute-start | bytes 663560 | tf_op jit(solution)/shard_map/ppermute | solution.py:384
  44.6 7.4 %collective-permute-start.19 = (bf16[864,256]{1,0:T(8,128)(2,1)S(1)}, bf16[864,256]{1,0:T(8,128)(2,1)S(1)}, u32[]{:S(2)}, u32[]{:S(2)}) collective-permute-start(bf16[864,256]{1,0:T(8,128)(2,1)S(1)} %collective-permute-done.7.rest_3_.rest_12_), channel_id=1, source_target_pairs={{0,1},{1,0},{2,3},{3,2},{4,5},{5,4},{6,7},{7,6},{8,9},{9,8},{10,11... | collective-permute-start | bytes 1327112 | tf_op jit(solution)/shard_map/ppermute | solution.py:383
  46.8 5.2 %collective-permute-start.20 = (bf16[432,256]{1,0:T(8,128)(2,1)S(1)}, bf16[432,256]{1,0:T(8,128)(2,1)S(1)}, u32[]{:S(2)}, u32[]{:S(2)}) collective-permute-start(bf16[432,256]{1,0:T(8,128)(2,1)S(1)} %collective-permute-done.9.rest_4_.rest_13_), channel_id=1, source_target_pairs={{0,1},{1,0},{2,3},{3,2},{4,5},{5,4},{6,7},{7,6},{8,9},{9,8},{10,11... | collective-permute-start | bytes 663560 | tf_op jit(solution)/shard_map/ppermute | solution.py:384
  51.6 5.3 %collective-permute-start.18 = (bf16[3456,256]{1,0:T(8,128)(2,1)S(1)}, bf16[3456,256]{1,0:T(8,128)(2,1)S(1)}, u32[]{:S(2)}, u32[]{:S(2)}) collective-permute-start(bf16[3456,256]{1,0:T(8,128)(2,1)S(1)} %get-tuple-element.39), channel_id=1, source_target_pairs={{0,1},{1,0},{2,3},{3,2},{4,5},{5,4},{6,7},{7,6},{8,9},{9,8},{10,11... | collective-permute-start | bytes 5308424 | tf_op jit(solution)/shard_map/ppermute | solution.py:407
  56.6 3.8 %collective-permute-start.22 = (bf16[3456,256]{1,0:T(8,128)(2,1)S(1)}, bf16[3456,256]{1,0:T(8,128)(2,1)S(1)}, u32[]{:S(2)}, u32[]{:S(2)}) collective-permute-start(bf16[3456,256]{1,0:T(8,128)(2,1)S(1)} %get-tuple-element.45), channel_id=1, source_target_pairs={{0,1},{1,0},{2,3},{3,2},{4,5},{5,4},{6,7},{7,6},{8,9},{9,8},{10,11... | collective-permute-start | bytes 5308424 | tf_op jit(solution)/shard_map/ppermute | solution.py:439
  57.0 6.0 %collective-permute-start.21 = (bf16[432,256]{1,0:T(8,128)(2,1)S(1)}, bf16[432,256]{1,0:T(8,128)(2,1)S(1)}, u32[]{:S(2)}, u32[]{:S(2)}) collective-permute-start(bf16[432,256]{1,0:T(8,128)(2,1)S(1)} %add_convert_fusion.7), channel_id=1, source_target_pairs={{0,4},{4,8},{8,12},{12,14},{14,10},{10,6},{6,2},{2,0},{1,3},{5,1},... | collective-permute-start | bytes 663560 | tf_op jit(solution)/shard_map/ppermute | solution.py:438
  60.4 6.0 %collective-permute-start.23 = (bf16[432,256]{1,0:T(8,128)(2,1)S(1)}, bf16[432,256]{1,0:T(8,128)(2,1)S(1)}, u32[]{:S(2)}, u32[]{:S(2)}) collective-permute-start(bf16[432,256]{1,0:T(8,128)(2,1)S(1)} %add_convert_fusion.6), channel_id=1, source_target_pairs={{0,4},{4,8},{8,12},{12,14},{14,10},{10,6},{6,2},{2,0},{1,3},{5,1},... | collective-permute-start | bytes 663560 | tf_op jit(solution)/shard_map/ppermute | solution.py:440
  63.2 9.1 %collective-permute-start.28 = (bf16[864,256]{1,0:T(8,128)(2,1)S(1)}, bf16[864,256]{1,0:T(8,128)(2,1)S(1)}, u32[]{:S(2)}, u32[]{:S(2)}) collective-permute-start(bf16[864,256]{1,0:T(8,128)(2,1)S(1)} %add_convert_fusion.2), channel_id=1, source_target_pairs={{0,4},{4,8},{8,12},{12,14},{14,10},{10,6},{6,2},{2,0},{1,3},{5,1},... | collective-permute-start | bytes 1327112 | tf_op jit(solution)/shard_map/ppermute | solution.py:454
  66.6 9.7 %collective-permute-start.24 = (bf16[864,256]{1,0:T(8,128)(2,1)S(1)}, bf16[864,256]{1,0:T(8,128)(2,1)S(1)}, u32[]{:S(2)}, u32[]{:S(2)}) collective-permute-start(bf16[864,256]{1,0:T(8,128)(2,1)S(1)} %add_convert_fusion.5), channel_id=1, source_target_pairs={{0,4},{4,8},{8,12},{12,14},{14,10},{10,6},{6,2},{2,0},{1,3},{5,1},... | collective-permute-start | bytes 1327112 | tf_op jit(solution)/shard_map/ppermute | solution.py:455
  72.5 8.5 %collective-permute-start.29 = (bf16[864,256]{1,0:T(8,128)(2,1)S(1)}, bf16[864,256]{1,0:T(8,128)(2,1)S(1)}, u32[]{:S(2)}, u32[]{:S(2)}) collective-permute-start(bf16[864,256]{1,0:T(8,128)(2,1)S(1)} %add_convert_fusion.1), channel_id=1, source_target_pairs={{0,4},{4,8},{8,12},{12,14},{14,10},{10,6},{6,2},{2,0},{1,3},{5,1},... | collective-permute-start | bytes 1327112 | tf_op jit(solution)/shard_map/ppermute | solution.py:456
  76.4 9.3 %collective-permute-start.25 = (bf16[864,256]{1,0:T(8,128)(2,1)S(1)}, bf16[864,256]{1,0:T(8,128)(2,1)S(1)}, u32[]{:S(2)}, u32[]{:S(2)}) collective-permute-start(bf16[864,256]{1,0:T(8,128)(2,1)S(1)} %add_convert_fusion.4), channel_id=1, source_target_pairs={{0,4},{4,8},{8,12},{12,14},{14,10},{10,6},{6,2},{2,0},{1,3},{5,1},... | collective-permute-start | bytes 1327112 | tf_op jit(solution)/shard_map/ppermute | solution.py:457
  81.2 7.1 %collective-permute-start.30 = (bf16[432,256]{1,0:T(8,128)(2,1)S(1)}, bf16[432,256]{1,0:T(8,128)(2,1)S(1)}, u32[]{:S(2)}, u32[]{:S(2)}) collective-permute-start(bf16[432,256]{1,0:T(8,128)(2,1)S(1)} %get-tuple-element.47), channel_id=1, source_target_pairs={{0,4},{4,8},{8,12},{12,14},{14,10},{10,6},{6,2},{2,0},{1,3},{5,1},... | collective-permute-start | bytes 663560 | tf_op jit(solution)/shard_map/ppermute | solution.py:420
  83.6 6.7 %collective-permute-start.31 = (bf16[432,256]{1,0:T(8,128)(2,1)S(1)}, bf16[432,256]{1,0:T(8,128)(2,1)S(1)}, u32[]{:S(2)}, u32[]{:S(2)}) collective-permute-start(bf16[432,256]{1,0:T(8,128)(2,1)S(1)} %get-tuple-element.48), channel_id=1, source_target_pairs={{0,5},{4,9},{8,13},{12,15},{14,11},{10,7},{6,3},{2,1},{1,2},{5,0},... | collective-permute-start | bytes 663560 | tf_op jit(solution)/shard_map/ppermute | solution.py:421
  85.9 6.9 %collective-permute-start.26 = (bf16[432,256]{1,0:T(8,128)(2,1)S(1)}, bf16[432,256]{1,0:T(8,128)(2,1)S(1)}, u32[]{:S(2)}, u32[]{:S(2)}) collective-permute-start(bf16[432,256]{1,0:T(8,128)(2,1)S(1)} %get-tuple-element.49), channel_id=1, source_target_pairs={{0,4},{4,8},{8,12},{12,14},{14,10},{10,6},{6,2},{2,0},{1,3},{5,1},... | collective-permute-start | bytes 663560 | tf_op jit(solution)/shard_map/ppermute | solution.py:420
  88.3 6.7 %collective-permute-start.27 = (bf16[432,256]{1,0:T(8,128)(2,1)S(1)}, bf16[432,256]{1,0:T(8,128)(2,1)S(1)}, u32[]{:S(2)}, u32[]{:S(2)}) collective-permute-start(bf16[432,256]{1,0:T(8,128)(2,1)S(1)} %get-tuple-element.50), channel_id=1, source_target_pairs={{0,5},{4,9},{8,13},{12,15},{14,11},{10,7},{6,3},{2,1},{1,2},{5,0},... | collective-permute-start | bytes 663560 | tf_op jit(solution)/shard_map/ppermute | solution.py:421

commit v8 on v7

--- a/solution.py
+++ b/solution.py
@@ -356,9 +356,9 @@
     high = down(jnp.concatenate([features_late[:2], cot_late[:1]]))
 
     a1, b1 = onward(a0), onward(b0)
-    a2, qa1 = onward(a1), sibling(a1)
-    b2, qb1 = onward(b1), sibling(b1)
-    a3, qa2 = onward(after(a2, b1, low, high, qa1)), sibling(a2)
+    a2, qa1 = onward(a1), sibling(after(a1, low, high))
+    b2, qb1 = onward(b1), sibling(after(b1, low, high))
+    a3, qa2 = onward(after(a2, b1, low, high)), sibling(a2)
     sx, sc, in_t, near = kernel(
         prep_kernel,
         "prep",
@@ -378,9 +378,9 @@
         high,
         smem=1,
     )
-    b3, qb2 = onward(after(b2, qb1)), sibling(b2)
-    a4, qa3 = onward(after(a3[:rows], b2, sx, qa2)), sibling(a3)
-    b4, qb3 = onward(after(b3[:rows], qb2)), sibling(b3)
+    a4, qa3 = onward(after(a3[:rows], b2, sx, qa1, qa2)), sibling(a3)
+    b3, qb2 = onward(after(b2, qb1, qa3)), sibling(b2)
+    b4, qb3 = onward(b3[:rows]), sibling(b3)
     qa4, qb4 = sibling(a4), sibling(b4)
     ones = [a0, a1, a2, a3, a4, qa1, qa2, qa3, qa4]
     twos = [b0, b1, b2, b3, b4, qb1, qb2, qb3, qb4]
@@ -397,14 +397,14 @@
             shape((channels, depth * area), BF),
         ),
         [weights],
-        after(sx, b4),
+        sx,
         near,
         *ones,
     )
     keep_two, send_two = kernel(
         grad_two_kernel, "grad_two", 8, 1, shards, [weights], sc, act_t
     )
-    got_two = sibling(send_two)
+    got_two = sibling(after(send_two, b3))
 
     def both(keep, got, lo, hi):
         return keep[lo * rows : hi * rows].astype(F32) + got[lo * rows : hi * rows].astype(F32)
@@ -435,14 +435,14 @@
     keep_one, send_one = kernel(
         grad_one_kernel, "grad_one", 8, 1, shards, [weights], delta, in_t
     )
-    two = onward(step(keep_two, after(got_two, keep_one), None, 0))
-    got_one = sibling(send_one)
+    two = onward(step(keep_two, got_two, None, 0))
+    got_one = sibling(after(send_one, two))
     one = onward(step(keep_one, got_one, None, 0))
     features_out = kernel(
         functools.partial(third_kernel, n),
         "third",
         14,
-        1,
+        4,
         shape(features.shape, BF),
         [weights, weights, scratch((depth + 2, ny + 2, nz, 3 * channels), BF)],
         sx,

time: 96.1 us -> 105 us (1.093)
  waiting for transfers between devices: 41.6 us -> 52.5 us
  starting transfers between devices: 33.8 us -> 31.3 us
    ppermute x15, waiting for transfers between devices: 11.7 us -> 22.2 us  [the longest x2 5.29 us: on_ring(): a3, qa2 = (onward(after(a2, b1, low, high)), sibling(a2))]
    ppermute x2, waiting for transfers between devices: 1.62 us -> 6.36 us  [finish(): total = both(keep, got, 7, 8) + onward(message[:rows]).astype(F32)]
    ppermute x1, starting transfers between devices: 0.01 us -> 4.48 us  [on_ring(): high = down(jnp.concatenate([features_late[:2], cot_late[:1]]))]
    ppermute x2, waiting for transfers between devices: 4.23 us -> 0.02 us  [finish(): return (total + scatter_across(message[rows:]).astype(F32)) * loss_scale]
    ppermute x1, waiting for transfers between devices: 3.84 us -> 0.01 us  [on_ring(): high = down(jnp.concatenate([features_late[:2], cot_late[:1]]))]
    ppermute x1, waiting for transfers between devices: 1.22 us -> 5.04 us  [on_ring(): one = onward(step(keep_one, got_one, one, 1))]
    ppermute x2, waiting for transfers between devices: 5.95 us -> 3.59 us  [on_ring(): a1, b1 = (onward(a0), onward(b0))]
    ppermute x15, starting transfers between devices: 14 us -> 12 us  [the longest x2 2.3 us: on_ring(): b3, qb2 = (onward(after(b2, qb1, qa3)), sibling(b2))]
  transfers between devices with their start and end apart: 32 -> 32, of which waited for: 18 -> 17; matrix products, arithmetic and copies ran while one was open for 4% -> 4% of each run, Pallas kernels for 15% -> 14%
where the time goes in v8:
time: 105 us; the launch traced here: 104 us
  waiting for transfers between devices  52.5 us (50%)
  starting transfers between devices  31.3 us (30%)
  Pallas kernels  14.8 us (14%)
  other arithmetic  2.9 us (3%)
  local copies, waits for them, and re-layouts  2.07 us (2%)
    pallas_call x6, Pallas kernels, kernel(): pl.pallas_call(body, name=name, out_shape=outs, in_specs=[pl.BlockSpec(me...  14.8 us
    ppermute x2, waiting for transfers between devices, finish(): total = both(keep, got, 7, 8) + onward(message[:rows]).astype(F32)  6.36 us
    ppermute x1, waiting for transfers between devices, on_ring(): low = up(jnp.concatenate([features_late[-2:], cot_late[-1:]]))  5.45 us
    ppermute x2, waiting for transfers between devices, on_ring(): a3, qa2 = (onward(after(a2, b1, low, high)), sibling(a2))  5.29 us
    ppermute x1, waiting for transfers between devices, on_ring(): one = onward(step(keep_one, got_one, one, 1))  5.04 us
    ppermute x2, waiting for transfers between devices, on_ring(): a4, qa3 = (onward(after(a3[:rows], b2, sx, qa1, qa2)), sibling(a3))  5.01 us
    ppermute x2, starting transfers between devices, on_ring(): a1, b1 = (onward(a0), onward(b0))  4.63 us
    ppermute x1, starting transfers between devices, on_ring(): high = down(jnp.concatenate([features_late[:2], cot_late[:1]]))  4.48 us
  transfers between devices with their start and end apart: 32, of which 17 were waited for; matrix products, arithmetic and copies ran while one was open for 4% of the time, Pallas kernels for 14%

profile of v8, /device:TPU:0, one launch (start us, length us, event | category | flops | bytes accessed | tf_op | source)
XLA Modules:
  0.0 104.4 jit_solution(15250421196003017750)
XLA Ops:
  0.7 0.5 collective-permute-start
  1.2 0.1 collective-permute-start.1
  1.3 0.9 constant_dynamic-update-slice_fusion.1
  2.2 0.3 collective-permute-done
  2.5 3.0 %collective-permute-start.4 = (bf16[864,256]{1,0:T(8,128)(2,1)S(1)}, bf16[864,256]{1,0:T(8,128)(2,1)S(1)}, u32[]{:S(2)}, u32[]{:S(2)}) collective-permute-start(bf16[864,256]{1,0:T(8,128)(2,1)S(1)} %constant_dynamic-update-slice_fusion.rest_0_), channel_id=1, source_target_pairs={{0,4},{4,8},{8,12},{12,14},{14,10},{10,6},{6,2},{2,0},{1,3},{5,1},... | collective-permute-start | bytes 1327112 | tf_op jit(solution)/shard_map/ppermute | solution.py:358
  5.5 0.9 constant_dynamic-update-slice_fusion.3
  6.5 0.0 collective-permute-done.1
  6.5 1.6 %collective-permute-start.6 = (bf16[864,256]{1,0:T(8,128)(2,1)S(1)}, bf16[864,256]{1,0:T(8,128)(2,1)S(1)}, u32[]{:S(2)}, u32[]{:S(2)}) collective-permute-start(bf16[864,256]{1,0:T(8,128)(2,1)S(1)} %constant_dynamic-update-slice_fusion.2.rest_9_.rest_0_), channel_id=1, source_target_pairs={{0,4},{4,8},{8,12},{12,14},{14,10},{10,6},{6,2},{2,0},{1,3},{5,1},... | collective-permute-start | bytes 1327112 | tf_op jit(solution)/shard_map/ppermute | solution.py:358
  8.2 3.6 %collective-permute-done.4.rest_1_ = bf16[864,256]{1,0:T(8,128)(2,1)S(1)} collective-permute-done((bf16[864,256]{1,0:T(8,128)(2,1)S(1)}, bf16[864,256]{1,0:T(8,128)(2,1)S(1)}, u32[]{:S(2)}, u32[]{:S(2)}) %collective-permute-start.4) | collective-permute-done | bytes 442400 | tf_op jit(solution)/shard_map/ppermute | solution.py:358
  11.7 2.1 %collective-permute-start.5 = (bf16[864,256]{1,0:T(8,128)(2,1)S(1)}, bf16[864,256]{1,0:T(8,128)(2,1)S(1)}, u32[]{:S(2)}, u32[]{:S(2)}) collective-permute-start(bf16[864,256]{1,0:T(8,128)(2,1)S(1)} %collective-permute-done.4.rest_1_), channel_id=1, source_target_pairs={{0,4},{4,8},{8,12},{12,14},{14,10},{10,6},{6,2},{2,0},{1,3},{5,1},... | collective-permute-start | bytes 1327112 | tf_op jit(solution)/shard_map/ppermute | solution.py:359
  13.9 0.1 collective-permute-start.2
  14.0 4.5 %collective-permute-start.3 = (bf16[3,8,16,256]{3,2,1,0:T(8,128)(2,1)S(1)}, bf16[3,8,16,256]{3,2,1,0:T(8,128)(2,1)S(1)}, u32[]{:S(2)}, u32[]{:S(2)}) collective-permute-start(bf16[3,8,16,256]{3,2,1,0:T(8,128)(2,1)S(1)} %pad_maximum_fusion.1), channel_id=1, source_target_pairs={{0,15},{1,0},{2,1},{3,2},{4,3},{5,4},{6,5},{7,6},{8,7},{9,8},{10,9... | collective-permute-start | bytes 589832 | tf_op jit(solution)/shard_map/ppermute | solution.py:356
  18.4 5.4 %collective-permute-done.2.low = bf16[3,8,16,256]{3,2,1,0:T(8,128)(2,1)S(1)} collective-permute-done((bf16[3,8,16,256]{3,2,1,0:T(8,128)(2,1)S(1)}, bf16[3,8,16,256]{3,2,1,0:T(8,128)(2,1)S(1)}, u32[]{:S(2)}, u32[]{:S(2)}) %collective-permute-start.2) | collective-permute-done | bytes 196640 | tf_op jit(solution)/shard_map/ppermute | solution.py:355
  23.9 0.0 collective-permute-done.3.high
  23.9 0.0 collective-permute-done.6.rest_10_.rest_1_
  23.9 1.7 %collective-permute-start.7 = (bf16[864,256]{1,0:T(8,128)(2,1)S(1)}, bf16[864,256]{1,0:T(8,128)(2,1)S(1)}, u32[]{:S(2)}, u32[]{:S(2)}) collective-permute-start(bf16[864,256]{1,0:T(8,128)(2,1)S(1)} %collective-permute-done.5.rest_2_), channel_id=1, source_target_pairs={{0,4},{4,8},{8,12},{12,14},{14,10},{10,6},{6,2},{2,0},{1,3},{5,1},... | collective-permute-start | bytes 1327112 | tf_op jit(solution)/shard_map/ppermute | solution.py:361
  25.6 1.6 %collective-permute-start.8 = (bf16[864,256]{1,0:T(8,128)(2,1)S(1)}, bf16[864,256]{1,0:T(8,128)(2,1)S(1)}, u32[]{:S(2)}, u32[]{:S(2)}) collective-permute-start(bf16[864,256]{1,0:T(8,128)(2,1)S(1)} %collective-permute-done.6.rest_10_.rest_1_), channel_id=1, source_target_pairs={{0,4},{4,8},{8,12},{12,14},{14,10},{10,6},{6,2},{2,0},{1,3},{5,1},... | collective-permute-start | bytes 1327112 | tf_op jit(solution)/shard_map/ppermute | solution.py:360
  27.2 0.5 collective-permute-start.10
  27.7 5.3 %collective-permute-done.7.rest_3_ = bf16[864,256]{1,0:T(8,128)(2,1)S(1)} collective-permute-done((bf16[864,256]{1,0:T(8,128)(2,1)S(1)}, bf16[864,256]{1,0:T(8,128)(2,1)S(1)}, u32[]{:S(2)}, u32[]{:S(2)}) %collective-permute-start.7) | collective-permute-done | bytes 442400 | tf_op jit(solution)/shard_map/ppermute | solution.py:361
  33.0 1.3 %prep.1 = (bf16[8,10,16,768]{3,2,1,0:T(8,128)(2,1)S(1)}, bf16[6,10,16,768]{3,2,1,0:T(8,128)(2,1)S(1)}, bf16[256,768]{1,0:T(8,128)(2,1)S(1)}, bf16[3,128,256]{2,1,0:T(8,128)(2,1)S(1)}) custom-call(s32[2,4,16]{2,1,0:T(4,128)S(1)} %bitcast.1, bf16[3,8,16,256]{3,2,1,0:T(8,128)(2,1)S(1)} %collective-permute-done.2.low, bf16[4,8,16,256]{3,2,1,0:T(8,128)(2,1)S(1)} %copy-done, ...), custom_call_target="tpu_custom_call" | custom-call | bytes 4194304 | tf_op jit(solution)/shard_map/prep/pallas_call | solution.py:338
  34.3 3.4 %collective-permute-done.8.rest_11_.rest_2_ = bf16[864,256]{1,0:T(8,128)(2,1)S(1)} collective-permute-done((bf16[864,256]{1,0:T(8,128)(2,1)S(1)}, bf16[864,256]{1,0:T(8,128)(2,1)S(1)}, u32[]{:S(2)}, u32[]{:S(2)}) %collective-permute-start.8) | collective-permute-done | bytes 442400 | tf_op jit(solution)/shard_map/ppermute | solution.py:360
  37.7 0.9 collective-permute-start.11
  38.6 5.0 %collective-permute-done.11.rest_4_ = bf16[432,256]{1,0:T(8,128)(2,1)S(1)} collective-permute-done((bf16[432,256]{1,0:T(8,128)(2,1)S(1)}, bf16[432,256]{1,0:T(8,128)(2,1)S(1)}, u32[]{:S(2)}, u32[]{:S(2)}) %collective-permute-start.11) | collective-permute-done | bytes 221216 | tf_op jit(solution)/shard_map/ppermute | solution.py:381
  43.7 1.0 collective-permute-start.15
  44.6 0.5 collective-permute-done.13.rest_8_
  45.1 2.3 %first.1 = (f32[512,256]{1,0:T(8,128)S(1)}, bf16[512,256]{1,0:T(8,128)(2,1)S(1)}, bf16[256,512]{1,0:T(8,128)(2,1)S(1)}) custom-call(bf16[8,10,16,768]{3,2,1,0:T(8,128)(2,1)S(1)} %get-tuple-element.29.sx_ref, bf16[3,128,256]{2,1,0:T(8,128)(2,1)S(1)} %get-tuple-element.30.mask_ref, bf16[864,256]{1,0:T(8,128)(2,1)S(1)} %constant_dynamic-update-slice_fusion.rest_0_, ...), custom_call_target="tpu_custom_call" | custom-call | flops 1811939328 | bytes 4194304 | tf_op jit(solution)/shard_map/first/pallas_call | solution.py:338
  47.5 2.2 %grad_two.1 = (bf16[3456,256]{1,0:T(8,128)(2,1)S(1)}, bf16[3456,256]{1,0:T(8,128)(2,1)S(1)}) custom-call(bf16[6,10,16,768]{3,2,1,0:T(8,128)(2,1)S(1)} %get-tuple-element.35.sc_ref, bf16[256,512]{1,0:T(8,128)(2,1)S(1)} %get-tuple-element.36.act_t_ref), custom_call_target="tpu_custom_call" | custom-call | flops 1811939328 | bytes 4194304 | tf_op jit(solution)/shard_map/grad_two/pallas_call | solution.py:338
  49.7 2.3 %collective-permute-done.15.rest_12_.rest_3_ = bf16[864,256]{1,0:T(8,128)(2,1)S(1)} collective-permute-done((bf16[864,256]{1,0:T(8,128)(2,1)S(1)}, bf16[864,256]{1,0:T(8,128)(2,1)S(1)}, u32[]{:S(2)}, u32[]{:S(2)}) %collective-permute-start.15) | collective-permute-done | bytes 442400 | tf_op jit(solution)/shard_map/ppermute | solution.py:382
  52.0 1.0 collective-permute-start.18
  53.0 1.3 %collective-permute-start.19 = (bf16[864,256]{1,0:T(8,128)(2,1)S(1)}, bf16[864,256]{1,0:T(8,128)(2,1)S(1)}, u32[]{:S(2)}, u32[]{:S(2)}) collective-permute-start(bf16[864,256]{1,0:T(8,128)(2,1)S(1)} %collective-permute-done.8.rest_11_.rest_2_), channel_id=1, source_target_pairs={{0,1},{1,0},{2,3},{3,2},{4,5},{5,4},{6,7},{7,6},{8,9},{9,8},{10,11... | collective-permute-start | bytes 1327112 | tf_op jit(solution)/shard_map/ppermute | solution.py:382
  54.3 3.7 %collective-permute-done.18.rest_13_.rest_4_ = bf16[432,256]{1,0:T(8,128)(2,1)S(1)} collective-permute-done((bf16[432,256]{1,0:T(8,128)(2,1)S(1)}, bf16[432,256]{1,0:T(8,128)(2,1)S(1)}, u32[]{:S(2)}, u32[]{:S(2)}) %collective-permute-start.18) | collective-permute-done | bytes 221216 | tf_op jit(solution)/shard_map/ppermute | solution.py:383
  58.0 0.1 add_convert_fusion.7
  58.1 1.0 collective-permute-start.17
  59.1 0.4 collective-permute-done.21.rest_17_.rest_8_
  59.5 2.4 %back.1.sd_ref = bf16[4,10,16,768]{3,2,1,0:T(8,128)(2,1)S(1)} custom-call(bf16[6,10,16,768]{3,2,1,0:T(8,128)(2,1)S(1)} %get-tuple-element.35.sc_ref, f32[512,256]{1,0:T(8,128)S(1)} %get-tuple-element.43.pre_ref, bf16[3,128,256]{2,1,0:T(8,128)(2,1)S(1)} %get-tuple-element.30.mask_ref, ...), custom_call_target="tpu_custom_call" | custom-call | flops 1811939328 | bytes 4194304 | tf_op jit(solution)/shard_map/back/pallas_call | solution.py:338
  61.9 2.3 %grad_one.1 = (bf16[3456,256]{1,0:T(8,128)(2,1)S(1)}, bf16[3456,256]{1,0:T(8,128)(2,1)S(1)}) custom-call(bf16[4,10,16,768]{3,2,1,0:T(8,128)(2,1)S(1)} %back.1.sd_ref, bf16[256,768]{1,0:T(8,128)(2,1)S(1)} %get-tuple-element.44.int_ref), custom_call_target="tpu_custom_call" | custom-call | flops 1811939328 | bytes 4194304 | tf_op jit(solution)/shard_map/grad_one/pallas_call | solution.py:338
  64.2 1.0 collective-permute-start.22
  65.2 0.2 add_convert_fusion.2
  65.3 0.6 collective-permute-start.28
  65.9 2.6 %collective-permute-done.22 = bf16[3456,256]{1,0:T(8,128)(2,1)S(1)} collective-permute-done((bf16[3456,256]{1,0:T(8,128)(2,1)S(1)}, bf16[3456,256]{1,0:T(8,128)(2,1)S(1)}, u32[]{:S(2)}, u32[]{:S(2)}) %collective-permute-start.22) | collective-permute-done | bytes 1769504 | tf_op jit(solution)/shard_map/ppermute | solution.py:439
  68.5 0.1 add_convert_fusion.6
  68.5 1.1 %collective-permute-start.23 = (bf16[432,256]{1,0:T(8,128)(2,1)S(1)}, bf16[432,256]{1,0:T(8,128)(2,1)S(1)}, u32[]{:S(2)}, u32[]{:S(2)}) collective-permute-start(bf16[432,256]{1,0:T(8,128)(2,1)S(1)} %add_convert_fusion.6), channel_id=1, source_target_pairs={{0,4},{4,8},{8,12},{12,14},{14,10},{10,6},{6,2},{2,0},{1,3},{5,1},... | collective-permute-start | bytes 663560 | tf_op jit(solution)/shard_map/ppermute | solution.py:440
  69.7 4.2 %third.1 = bf16[4,8,16,256]{3,2,1,0:T(8,128)(2,1)} custom-call(bf16[8,10,16,768]{3,2,1,0:T(8,128)(2,1)S(1)} %get-tuple-element.29.sx_ref, bf16[512,256]{1,0:T(8,128)(2,1)S(1)} %get-tuple-element.42.act_ref, bf16[3,128,256]{2,1,0:T(8,128)(2,1)S(1)} %get-tuple-element.30.mask_ref, bf16[864,256]{1,0:T(8,128)(2,1)S(1)} %constant_dynamic-update-slice_fusion.rest_0_, ...), custom_call_target="tpu_custom_call" | custom-call | flops 7247757312 | bytes 4194304 | tf_op jit(solution)/shard_map/third/pallas_call | solution.py:338
  73.9 2.2 %collective-permute-done.23 = bf16[432,256]{1,0:T(8,128)(2,1)S(1)} collective-permute-done((bf16[432,256]{1,0:T(8,128)(2,1)S(1)}, bf16[432,256]{1,0:T(8,128)(2,1)S(1)}, u32[]{:S(2)}, u32[]{:S(2)}) %collective-permute-start.23) | collective-permute-done | bytes 221216 | tf_op jit(solution)/shard_map/ppermute | solution.py:440
  76.1 0.1 add_convert_fusion.5
  76.2 0.6 collective-permute-start.24
  76.8 0.2 add_convert_fusion.1
  77.0 2.5 %collective-permute-start.29 = (bf16[864,256]{1,0:T(8,128)(2,1)S(1)}, bf16[864,256]{1,0:T(8,128)(2,1)S(1)}, u32[]{:S(2)}, u32[]{:S(2)}) collective-permute-start(bf16[864,256]{1,0:T(8,128)(2,1)S(1)} %add_convert_fusion.1), channel_id=1, source_target_pairs={{0,4},{4,8},{8,12},{12,14},{14,10},{10,6},{6,2},{2,0},{1,3},{5,1},... | collective-permute-start | bytes 1327112 | tf_op jit(solution)/shard_map/ppermute | solution.py:456
  79.5 5.0 %collective-permute-done.24 = bf16[864,256]{1,0:T(8,128)(2,1)S(1)} collective-permute-done((bf16[864,256]{1,0:T(8,128)(2,1)S(1)}, bf16[864,256]{1,0:T(8,128)(2,1)S(1)}, u32[]{:S(2)}, u32[]{:S(2)}) %collective-permute-start.24) | collective-permute-done | bytes 442400 | tf_op jit(solution)/shard_map/ppermute | solution.py:455
  84.6 0.2 add_convert_fusion.4
  84.7 0.6 collective-permute-start.25
  85.3 4.0 %collective-permute-done.29 = bf16[864,256]{1,0:T(8,128)(2,1)S(1)} collective-permute-done((bf16[864,256]{1,0:T(8,128)(2,1)S(1)}, bf16[864,256]{1,0:T(8,128)(2,1)S(1)}, u32[]{:S(2)}, u32[]{:S(2)}) %collective-permute-start.29) | collective-permute-done | bytes 442400 | tf_op jit(solution)/shard_map/ppermute | solution.py:456
  89.3 0.2 add_convert_fusion
  89.5 0.2 collective-permute-start.31
  89.7 1.8 %collective-permute-start.30 = (bf16[432,256]{1,0:T(8,128)(2,1)S(1)}, bf16[432,256]{1,0:T(8,128)(2,1)S(1)}, u32[]{:S(2)}, u32[]{:S(2)}) collective-permute-start(bf16[432,256]{1,0:T(8,128)(2,1)S(1)} %get-tuple-element.49), channel_id=1, source_target_pairs={{0,4},{4,8},{8,12},{12,14},{14,10},{10,6},{6,2},{2,0},{1,3},{5,1},... | collective-permute-start | bytes 663560 | tf_op jit(solution)/shard_map/ppermute | solution.py:420
  91.5 2.5 %collective-permute-done.25 = bf16[864,256]{1,0:T(8,128)(2,1)S(1)} collective-permute-done((bf16[864,256]{1,0:T(8,128)(2,1)S(1)}, bf16[864,256]{1,0:T(8,128)(2,1)S(1)}, u32[]{:S(2)}, u32[]{:S(2)}) %collective-permute-start.25) | collective-permute-done | bytes 442400 | tf_op jit(solution)/shard_map/ppermute | solution.py:457
  94.0 0.2 add_convert_fusion.3
  94.2 0.2 collective-permute-start.27
  94.5 1.8 %collective-permute-start.26 = (bf16[432,256]{1,0:T(8,128)(2,1)S(1)}, bf16[432,256]{1,0:T(8,128)(2,1)S(1)}, u32[]{:S(2)}, u32[]{:S(2)}) collective-permute-start(bf16[432,256]{1,0:T(8,128)(2,1)S(1)} %get-tuple-element.51), channel_id=1, source_target_pairs={{0,4},{4,8},{8,12},{12,14},{14,10},{10,6},{6,2},{2,0},{1,3},{5,1},... | collective-permute-start | bytes 663560 | tf_op jit(solution)/shard_map/ppermute | solution.py:420
  96.2 2.5 %collective-permute-done.30 = bf16[432,256]{1,0:T(8,128)(2,1)S(1)} collective-permute-done((bf16[432,256]{1,0:T(8,128)(2,1)S(1)}, bf16[432,256]{1,0:T(8,128)(2,1)S(1)}, u32[]{:S(2)}, u32[]{:S(2)}) %collective-permute-start.30) | collective-permute-done | bytes 221216 | tf_op jit(solution)/shard_map/ppermute | solution.py:420
  98.8 0.9 add_multiply_fusion
  99.7 0.0 collective-permute-done.27
  99.7 3.8 %collective-permute-done.26 = bf16[432,256]{1,0:T(8,128)(2,1)S(1)} collective-permute-done((bf16[432,256]{1,0:T(8,128)(2,1)S(1)}, bf16[432,256]{1,0:T(8,128)(2,1)S(1)}, u32[]{:S(2)}, u32[]{:S(2)}) %collective-permute-start.26) | collective-permute-done | bytes 221216 | tf_op jit(solution)/shard_map/ppermute | solution.py:420
  103.5 0.9 add_multiply_fusion.1
  (34 shorter events, 0.3 us)
Async XLA Ops:
  0.6 7.5 %copy-start = (bf16[4,8,16,256]{3,2,1,0:T(8,128)(2,1)S(1)}, bf16[4,8,16,256]{3,2,1,0:T(8,128)(2,1)}, u32[]{:S(2)}) copy-start(bf16[4,8,16,256]{3,2,1,0:T(8,128)(2,1)} %f_own.1) | copy-start | bytes 786436
  0.6 13.2 %copy-start.1 = (bf16[4,8,16,256]{3,2,1,0:T(8,128)(2,1)S(1)}, bf16[4,8,16,256]{3,2,1,0:T(8,128)(2,1)}, u32[]{:S(2)}) copy-start(bf16[4,8,16,256]{3,2,1,0:T(8,128)(2,1)} %c_own.1) | copy-start | bytes 786436
  0.7 32.3 %copy-start.2 = (s32[16,2,4]{0,2,1:T(4,128)S(1)}, s32[16,2,4]{0,2,1:T(4,128)}, u32[]{:S(2)}) copy-start(s32[16,2,4]{0,2,1:T(4,128)} %param.9) | copy-start | bytes 1540
  0.7 1.8 %collective-permute-start = (bf16[432,256]{1,0:T(8,128)(2,1)}, bf16[432,256]{1,0:T(8,128)(2,1)S(1)}, u32[]{:S(2)}, u32[]{:S(2)}) collective-permute-start(bf16[432,256]{1,0:T(8,128)(2,1)} %param.6), channel_id=1, source_target_pairs={{0,1},{1,0},{2,3},{3,2},{4,5},{5,4},{6,7},{7,6},{8,9},{9,8},{10,11... | collective-permute-start | bytes 663560 | tf_op jit(solution)/shard_map/ppermute | solution.py:352
  1.2 5.3 %collective-permute-start.1 = (bf16[432,256]{1,0:T(8,128)(2,1)}, bf16[432,256]{1,0:T(8,128)(2,1)S(1)}, u32[]{:S(2)}, u32[]{:S(2)}) collective-permute-start(bf16[432,256]{1,0:T(8,128)(2,1)} %param.7), channel_id=1, source_target_pairs={{0,1},{1,0},{2,3},{3,2},{4,5},{5,4},{6,7},{7,6},{8,9},{9,8},{10,11... | collective-permute-start | bytes 663560 | tf_op jit(solution)/shard_map/ppermute | solution.py:353
  2.5 9.2 %collective-permute-start.4 = (bf16[864,256]{1,0:T(8,128)(2,1)S(1)}, bf16[864,256]{1,0:T(8,128)(2,1)S(1)}, u32[]{:S(2)}, u32[]{:S(2)}) collective-permute-start(bf16[864,256]{1,0:T(8,128)(2,1)S(1)} %constant_dynamic-update-slice_fusion.rest_0_), channel_id=1, source_target_pairs={{0,4},{4,8},{8,12},{12,14},{14,10},{10,6},{6,2},{2,0},{1,3},{5,1},... | collective-permute-start | bytes 1327112 | tf_op jit(solution)/shard_map/ppermute | solution.py:358
  6.5 17.4 %collective-permute-start.6 = (bf16[864,256]{1,0:T(8,128)(2,1)S(1)}, bf16[864,256]{1,0:T(8,128)(2,1)S(1)}, u32[]{:S(2)}, u32[]{:S(2)}) collective-permute-start(bf16[864,256]{1,0:T(8,128)(2,1)S(1)} %constant_dynamic-update-slice_fusion.2.rest_9_.rest_0_), channel_id=1, source_target_pairs={{0,4},{4,8},{8,12},{12,14},{14,10},{10,6},{6,2},{2,0},{1,3},{5,1},... | collective-permute-start | bytes 1327112 | tf_op jit(solution)/shard_map/ppermute | solution.py:358
  11.7 12.1 %collective-permute-start.5 = (bf16[864,256]{1,0:T(8,128)(2,1)S(1)}, bf16[864,256]{1,0:T(8,128)(2,1)S(1)}, u32[]{:S(2)}, u32[]{:S(2)}) collective-permute-start(bf16[864,256]{1,0:T(8,128)(2,1)S(1)} %collective-permute-done.4.rest_1_), channel_id=1, source_target_pairs={{0,4},{4,8},{8,12},{12,14},{14,10},{10,6},{6,2},{2,0},{1,3},{5,1},... | collective-permute-start | bytes 1327112 | tf_op jit(solution)/shard_map/ppermute | solution.py:359
  13.9 10.0 %collective-permute-start.2 = (bf16[3,8,16,256]{3,2,1,0:T(8,128)(2,1)S(1)}, bf16[3,8,16,256]{3,2,1,0:T(8,128)(2,1)S(1)}, u32[]{:S(2)}, u32[]{:S(2)}) collective-permute-start(bf16[3,8,16,256]{3,2,1,0:T(8,128)(2,1)S(1)} %pad_maximum_fusion), channel_id=1, source_target_pairs={{0,1},{1,2},{2,3},{3,4},{4,5},{5,6},{6,7},{7,8},{8,9},{9,10},{10,1... | collective-permute-start | bytes 589832 | tf_op jit(solution)/shard_map/ppermute | solution.py:355
  14.0 9.9 %collective-permute-start.3 = (bf16[3,8,16,256]{3,2,1,0:T(8,128)(2,1)S(1)}, bf16[3,8,16,256]{3,2,1,0:T(8,128)(2,1)S(1)}, u32[]{:S(2)}, u32[]{:S(2)}) collective-permute-start(bf16[3,8,16,256]{3,2,1,0:T(8,128)(2,1)S(1)} %pad_maximum_fusion.1), channel_id=1, source_target_pairs={{0,15},{1,0},{2,1},{3,2},{4,3},{5,4},{6,5},{7,6},{8,7},{9,8},{10,9... | collective-permute-start | bytes 589832 | tf_op jit(solution)/shard_map/ppermute | solution.py:356
  23.9 9.1 %collective-permute-start.7 = (bf16[864,256]{1,0:T(8,128)(2,1)S(1)}, bf16[864,256]{1,0:T(8,128)(2,1)S(1)}, u32[]{:S(2)}, u32[]{:S(2)}) collective-permute-start(bf16[864,256]{1,0:T(8,128)(2,1)S(1)} %collective-permute-done.5.rest_2_), channel_id=1, source_target_pairs={{0,4},{4,8},{8,12},{12,14},{14,10},{10,6},{6,2},{2,0},{1,3},{5,1},... | collective-permute-start | bytes 1327112 | tf_op jit(solution)/shard_map/ppermute | solution.py:361
  25.6 12.1 %collective-permute-start.8 = (bf16[864,256]{1,0:T(8,128)(2,1)S(1)}, bf16[864,256]{1,0:T(8,128)(2,1)S(1)}, u32[]{:S(2)}, u32[]{:S(2)}) collective-permute-start(bf16[864,256]{1,0:T(8,128)(2,1)S(1)} %collective-permute-done.6.rest_10_.rest_1_), channel_id=1, source_target_pairs={{0,4},{4,8},{8,12},{12,14},{14,10},{10,6},{6,2},{2,0},{1,3},{5,1},... | collective-permute-start | bytes 1327112 | tf_op jit(solution)/shard_map/ppermute | solution.py:360
  27.2 10.5 %collective-permute-start.9 = (bf16[864,256]{1,0:T(8,128)(2,1)S(1)}, bf16[864,256]{1,0:T(8,128)(2,1)S(1)}, u32[]{:S(2)}, u32[]{:S(2)}) collective-permute-start(bf16[864,256]{1,0:T(8,128)(2,1)S(1)} %collective-permute-done.4.rest_1_), channel_id=1, source_target_pairs={{0,1},{1,0},{2,3},{3,2},{4,5},{5,4},{6,7},{7,6},{8,9},{9,8},{10,11... | collective-permute-start | bytes 1327112 | tf_op jit(solution)/shard_map/ppermute | solution.py:359
  27.2 10.5 %collective-permute-start.10 = (bf16[864,256]{1,0:T(8,128)(2,1)S(1)}, bf16[864,256]{1,0:T(8,128)(2,1)S(1)}, u32[]{:S(2)}, u32[]{:S(2)}) collective-permute-start(bf16[864,256]{1,0:T(8,128)(2,1)S(1)} %collective-permute-done.5.rest_2_), channel_id=1, source_target_pairs={{0,1},{1,0},{2,3},{3,2},{4,5},{5,4},{6,7},{7,6},{8,9},{9,8},{10,11... | collective-permute-start | bytes 1327112 | tf_op jit(solution)/shard_map/ppermute | solution.py:361
  27.7 16.0 %collective-permute-start.14 = (bf16[864,256]{1,0:T(8,128)(2,1)S(1)}, bf16[864,256]{1,0:T(8,128)(2,1)S(1)}, u32[]{:S(2)}, u32[]{:S(2)}) collective-permute-start(bf16[864,256]{1,0:T(8,128)(2,1)S(1)} %collective-permute-done.6.rest_10_.rest_1_), channel_id=1, source_target_pairs={{0,1},{1,0},{2,3},{3,2},{4,5},{5,4},{6,7},{7,6},{8,9},{9,8},{10,11... | collective-permute-start | bytes 1327112 | tf_op jit(solution)/shard_map/ppermute | solution.py:360
  33.0 10.7 %collective-permute-start.12 = (bf16[864,256]{1,0:T(8,128)(2,1)S(1)}, bf16[864,256]{1,0:T(8,128)(2,1)S(1)}, u32[]{:S(2)}, u32[]{:S(2)}) collective-permute-start(bf16[864,256]{1,0:T(8,128)(2,1)S(1)} %collective-permute-done.7.rest_3_), channel_id=1, source_target_pairs={{0,1},{1,0},{2,3},{3,2},{4,5},{5,4},{6,7},{7,6},{8,9},{9,8},{10,11... | collective-permute-start | bytes 1327112 | tf_op jit(solution)/shard_map/ppermute | solution.py:381
  37.7 5.9 %collective-permute-start.11 = (bf16[432,256]{1,0:T(8,128)(2,1)S(1)}, bf16[432,256]{1,0:T(8,128)(2,1)S(1)}, u32[]{:S(2)}, u32[]{:S(2)}) collective-permute-start(bf16[432,256]{1,0:T(8,128)(2,1)S(1)} %slice.120), channel_id=1, source_target_pairs={{0,4},{4,8},{8,12},{12,14},{14,10},{10,6},{6,2},{2,0},{1,3},{5,1},... | collective-permute-start | bytes 663560 | tf_op jit(solution)/shard_map/ppermute | solution.py:381
  43.6 1.5 %collective-permute-start.13 = (bf16[432,256]{1,0:T(8,128)(2,1)S(1)}, bf16[432,256]{1,0:T(8,128)(2,1)S(1)}, u32[]{:S(2)}, u32[]{:S(2)}) collective-permute-start(bf16[432,256]{1,0:T(8,128)(2,1)S(1)} %collective-permute-done.11.rest_4_), channel_id=1, source_target_pairs={{0,1},{1,0},{2,3},{3,2},{4,5},{5,4},{6,7},{7,6},{8,9},{9,8},{10,11... | collective-permute-start | bytes 663560 | tf_op jit(solution)/shard_map/ppermute | solution.py:384
  43.7 8.4 %collective-permute-start.15 = (bf16[864,256]{1,0:T(8,128)(2,1)S(1)}, bf16[864,256]{1,0:T(8,128)(2,1)S(1)}, u32[]{:S(2)}, u32[]{:S(2)}) collective-permute-start(bf16[864,256]{1,0:T(8,128)(2,1)S(1)} %collective-permute-done.8.rest_11_.rest_2_), channel_id=1, source_target_pairs={{0,4},{4,8},{8,12},{12,14},{14,10},{10,6},{6,2},{2,0},{1,3},{5,1},... | collective-permute-start | bytes 1327112 | tf_op jit(solution)/shard_map/ppermute | solution.py:382
  52.0 6.0 %collective-permute-start.16 = (bf16[3456,256]{1,0:T(8,128)(2,1)S(1)}, bf16[3456,256]{1,0:T(8,128)(2,1)S(1)}, u32[]{:S(2)}, u32[]{:S(2)}) collective-permute-start(bf16[3456,256]{1,0:T(8,128)(2,1)S(1)} %get-tuple-element.41), channel_id=1, source_target_pairs={{0,1},{1,0},{2,3},{3,2},{4,5},{5,4},{6,7},{7,6},{8,9},{9,8},{10,11... | collective-permute-start | bytes 5308424 | tf_op jit(solution)/shard_map/ppermute | solution.py:407
  52.0 6.0 %collective-permute-start.18 = (bf16[432,256]{1,0:T(8,128)(2,1)S(1)}, bf16[432,256]{1,0:T(8,128)(2,1)S(1)}, u32[]{:S(2)}, u32[]{:S(2)}) collective-permute-start(bf16[432,256]{1,0:T(8,128)(2,1)S(1)} %slice.122), channel_id=1, source_target_pairs={{0,4},{4,8},{8,12},{12,14},{14,10},{10,6},{6,2},{2,0},{1,3},{5,1},... | collective-permute-start | bytes 663560 | tf_op jit(solution)/shard_map/ppermute | solution.py:383
  53.0 6.1 %collective-permute-start.19 = (bf16[864,256]{1,0:T(8,128)(2,1)S(1)}, bf16[864,256]{1,0:T(8,128)(2,1)S(1)}, u32[]{:S(2)}, u32[]{:S(2)}) collective-permute-start(bf16[864,256]{1,0:T(8,128)(2,1)S(1)} %collective-permute-done.8.rest_11_.rest_2_), channel_id=1, source_target_pairs={{0,1},{1,0},{2,3},{3,2},{4,5},{5,4},{6,7},{7,6},{8,9},{9,8},{10,11... | collective-permute-start | bytes 1327112 | tf_op jit(solution)/shard_map/ppermute | solution.py:382
  54.3 4.7 %collective-permute-start.20 = (bf16[864,256]{1,0:T(8,128)(2,1)S(1)}, bf16[864,256]{1,0:T(8,128)(2,1)S(1)}, u32[]{:S(2)}, u32[]{:S(2)}) collective-permute-start(bf16[864,256]{1,0:T(8,128)(2,1)S(1)} %collective-permute-done.15.rest_12_.rest_3_), channel_id=1, source_target_pairs={{0,1},{1,0},{2,3},{3,2},{4,5},{5,4},{6,7},{7,6},{8,9},{9,8},{10,11... | collective-permute-start | bytes 1327112 | tf_op jit(solution)/shard_map/ppermute | solution.py:383
  58.0 1.5 %collective-permute-start.21 = (bf16[432,256]{1,0:T(8,128)(2,1)S(1)}, bf16[432,256]{1,0:T(8,128)(2,1)S(1)}, u32[]{:S(2)}, u32[]{:S(2)}) collective-permute-start(bf16[432,256]{1,0:T(8,128)(2,1)S(1)} %collective-permute-done.18.rest_13_.rest_4_), channel_id=1, source_target_pairs={{0,1},{1,0},{2,3},{3,2},{4,5},{5,4},{6,7},{7,6},{8,9},{9,8},{10,11... | collective-permute-start | bytes 663560 | tf_op jit(solution)/shard_map/ppermute | solution.py:384
  58.1 6.1 %collective-permute-start.17 = (bf16[432,256]{1,0:T(8,128)(2,1)S(1)}, bf16[432,256]{1,0:T(8,128)(2,1)S(1)}, u32[]{:S(2)}, u32[]{:S(2)}) collective-permute-start(bf16[432,256]{1,0:T(8,128)(2,1)S(1)} %add_convert_fusion.7), channel_id=1, source_target_pairs={{0,4},{4,8},{8,12},{12,14},{14,10},{10,6},{6,2},{2,0},{1,3},{5,1},... | collective-permute-start | bytes 663560 | tf_op jit(solution)/shard_map/ppermute | solution.py:438
  64.2 4.3 %collective-permute-start.22 = (bf16[3456,256]{1,0:T(8,128)(2,1)S(1)}, bf16[3456,256]{1,0:T(8,128)(2,1)S(1)}, u32[]{:S(2)}, u32[]{:S(2)}) collective-permute-start(bf16[3456,256]{1,0:T(8,128)(2,1)S(1)} %get-tuple-element.47), channel_id=1, source_target_pairs={{0,1},{1,0},{2,3},{3,2},{4,5},{5,4},{6,7},{7,6},{8,9},{9,8},{10,11... | collective-permute-start | bytes 5308424 | tf_op jit(solution)/shard_map/ppermute | solution.py:439
  65.3 8.6 %collective-permute-start.28 = (bf16[864,256]{1,0:T(8,128)(2,1)S(1)}, bf16[864,256]{1,0:T(8,128)(2,1)S(1)}, u32[]{:S(2)}, u32[]{:S(2)}) collective-permute-start(bf16[864,256]{1,0:T(8,128)(2,1)S(1)} %add_convert_fusion.2), channel_id=1, source_target_pairs={{0,4},{4,8},{8,12},{12,14},{14,10},{10,6},{6,2},{2,0},{1,3},{5,1},... | collective-permute-start | bytes 1327112 | tf_op jit(solution)/shard_map/ppermute | solution.py:454
  68.5 7.5 %collective-permute-start.23 = (bf16[432,256]{1,0:T(8,128)(2,1)S(1)}, bf16[432,256]{1,0:T(8,128)(2,1)S(1)}, u32[]{:S(2)}, u32[]{:S(2)}) collective-permute-start(bf16[432,256]{1,0:T(8,128)(2,1)S(1)} %add_convert_fusion.6), channel_id=1, source_target_pairs={{0,4},{4,8},{8,12},{12,14},{14,10},{10,6},{6,2},{2,0},{1,3},{5,1},... | collective-permute-start | bytes 663560 | tf_op jit(solution)/shard_map/ppermute | solution.py:440
  76.2 8.4 %collective-permute-start.24 = (bf16[864,256]{1,0:T(8,128)(2,1)S(1)}, bf16[864,256]{1,0:T(8,128)(2,1)S(1)}, u32[]{:S(2)}, u32[]{:S(2)}) collective-permute-start(bf16[864,256]{1,0:T(8,128)(2,1)S(1)} %add_convert_fusion.5), channel_id=1, source_target_pairs={{0,4},{4,8},{8,12},{12,14},{14,10},{10,6},{6,2},{2,0},{1,3},{5,1},... | collective-permute-start | bytes 1327112 | tf_op jit(solution)/shard_map/ppermute | solution.py:455
  77.0 12.3 %collective-permute-start.29 = (bf16[864,256]{1,0:T(8,128)(2,1)S(1)}, bf16[864,256]{1,0:T(8,128)(2,1)S(1)}, u32[]{:S(2)}, u32[]{:S(2)}) collective-permute-start(bf16[864,256]{1,0:T(8,128)(2,1)S(1)} %add_convert_fusion.1), channel_id=1, source_target_pairs={{0,4},{4,8},{8,12},{12,14},{14,10},{10,6},{6,2},{2,0},{1,3},{5,1},... | collective-permute-start | bytes 1327112 | tf_op jit(solution)/shard_map/ppermute | solution.py:456
  84.7 9.3 %collective-permute-start.25 = (bf16[864,256]{1,0:T(8,128)(2,1)S(1)}, bf16[864,256]{1,0:T(8,128)(2,1)S(1)}, u32[]{:S(2)}, u32[]{:S(2)}) collective-permute-start(bf16[864,256]{1,0:T(8,128)(2,1)S(1)} %add_convert_fusion.4), channel_id=1, source_target_pairs={{0,4},{4,8},{8,12},{12,14},{14,10},{10,6},{6,2},{2,0},{1,3},{5,1},... | collective-permute-start | bytes 1327112 | tf_op jit(solution)/shard_map/ppermute | solution.py:457
  89.5 6.7 %collective-permute-start.31 = (bf16[432,256]{1,0:T(8,128)(2,1)S(1)}, bf16[432,256]{1,0:T(8,128)(2,1)S(1)}, u32[]{:S(2)}, u32[]{:S(2)}) collective-permute-start(bf16[432,256]{1,0:T(8,128)(2,1)S(1)} %get-tuple-element.50), channel_id=1, source_target_pairs={{0,5},{4,9},{8,13},{12,15},{14,11},{10,7},{6,3},{2,1},{1,2},{5,0},... | collective-permute-start | bytes 663560 | tf_op jit(solution)/shard_map/ppermute | solution.py:421
  89.7 9.0 %collective-permute-start.30 = (bf16[432,256]{1,0:T(8,128)(2,1)S(1)}, bf16[432,256]{1,0:T(8,128)(2,1)S(1)}, u32[]{:S(2)}, u32[]{:S(2)}) collective-permute-start(bf16[432,256]{1,0:T(8,128)(2,1)S(1)} %get-tuple-element.49), channel_id=1, source_target_pairs={{0,4},{4,8},{8,12},{12,14},{14,10},{10,6},{6,2},{2,0},{1,3},{5,1},... | collective-permute-start | bytes 663560 | tf_op jit(solution)/shard_map/ppermute | solution.py:420
  94.2 5.4 %collective-permute-start.27 = (bf16[432,256]{1,0:T(8,128)(2,1)S(1)}, bf16[432,256]{1,0:T(8,128)(2,1)S(1)}, u32[]{:S(2)}, u32[]{:S(2)}) collective-permute-start(bf16[432,256]{1,0:T(8,128)(2,1)S(1)} %get-tuple-element.52), channel_id=1, source_target_pairs={{0,5},{4,9},{8,13},{12,15},{14,11},{10,7},{6,3},{2,1},{1,2},{5,0},... | collective-permute-start | bytes 663560 | tf_op jit(solution)/shard_map/ppermute | solution.py:421
  94.5 9.1 %collective-permute-start.26 = (bf16[432,256]{1,0:T(8,128)(2,1)S(1)}, bf16[432,256]{1,0:T(8,128)(2,1)S(1)}, u32[]{:S(2)}, u32[]{:S(2)}) collective-permute-start(bf16[432,256]{1,0:T(8,128)(2,1)S(1)} %get-tuple-element.51), channel_id=1, source_target_pairs={{0,4},{4,8},{8,12},{12,14},{14,10},{10,6},{6,2},{2,0},{1,3},{5,1},... | collective-permute-start | bytes 663560 | tf_op jit(solution)/shard_map/ppermute | solution.py:420

commit v9 on v7

--- a/solution.py
+++ b/solution.py
@@ -326,7 +326,7 @@
             ]
         )
 
-    onward, scatter_across = along_ring(0, 0), along_ring(0, 1)
+    onward, gather_across, scatter_across = along_ring(0, 0), along_ring(1, 0), along_ring(0, 1)
     sibling = permute([(i, i ^ 1) for i in range(tiles)])
     up = permute([(i, (i + 1) % tiles) for i in range(tiles)])
     down = permute([(i, (i - 1) % tiles) for i in range(tiles)])
@@ -350,12 +350,13 @@
         )(*operands)
 
     a0 = jnp.concatenate([weight_one, sibling(weight_one)])
-    b0 = jnp.concatenate([after(weight_two, a0), sibling(weight_two)])
+    b0 = jnp.concatenate([weight_two, sibling(weight_two)])
     features_late, cot_late, _ = lax.optimization_barrier((features, cotangent, b0))
     low = up(jnp.concatenate([features_late[-2:], cot_late[-1:]]))
     high = down(jnp.concatenate([features_late[:2], cot_late[:1]]))
 
-    a1, b1 = onward(a0), onward(b0)
+    a1 = jnp.concatenate([onward(weight_one), gather_across(weight_one)])
+    b1 = jnp.concatenate([onward(weight_two), gather_across(weight_two)])
     a2, qa1 = onward(a1), sibling(a1)
     b2, qb1 = onward(b1), sibling(b1)
     a3, qa2 = onward(after(a2, b1, low, high, qa1)), sibling(a2)

time: 96.1 us -> 94.4 us (0.982)
  starting transfers between devices: 33.8 us -> 24.3 us
  waiting for transfers between devices: 41.6 us -> 49.8 us
    ppermute x2, starting transfers between devices: 4.79 us -> 2.64 us  [finish(): total = both(keep, got, 7, 8) + onward(message[:rows]).astype(F32)]
    ppermute x3 -> x5, waiting for transfers between devices: 5.96 us -> 3.85 us  [the longest x2 2.32 us: on_ring(): a1 = jnp.concatenate([onward(weight_one), gather_across(weight_one)])]
    ppermute x3 -> x5, starting transfers between devices: 4.7 us -> 6.4 us  [the longest x2 3.75 us: on_ring(): a1 = jnp.concatenate([onward(weight_one), gather_across(weight_one)])]
    ppermute x2, waiting for transfers between devices: 1.62 us -> 3.26 us  [finish(): total = both(keep, got, 7, 8) + onward(message[:rows]).astype(F32)]
    ppermute x2, waiting for transfers between devices: 4.23 us -> 2.87 us  [finish(): return (total + scatter_across(message[rows:]).astype(F32)) * loss_scale]
    ppermute x2, waiting for transfers between devices: 2.01 us -> 3.34 us  [on_ring(): a3, qa2 = (onward(after(a2, b1, low, high, qa1)), sibling(a2))]
    ppermute x1, waiting for transfers between devices: 2.01 us -> 3.2 us  [on_ring(): one = onward(step(keep_one, got_one, None, 0))]
    ppermute x2, starting transfers between devices: 1.71 us -> 0.54 us  [on_ring(): qa4, qb4 = (sibling(a4), sibling(b4))]
  transfers between devices with their start and end apart: 32 -> 34, of which waited for: 18 -> 20; matrix products, arithmetic and copies ran while one was open for 4% -> 3% of each run, Pallas kernels for 15% -> 16%
where the time goes in v9:
time: 94.4 us; the launch traced here: 93.9 us
  waiting for transfers between devices  49.8 us (53%)
  starting transfers between devices  24.3 us (26%)
  Pallas kernels  14.8 us (16%)
  other arithmetic  2.89 us (3%)
  local copies, waits for them, and re-layouts  1.24 us (1%)
    pallas_call x6, Pallas kernels, kernel(): pl.pallas_call(body, name=name, out_shape=outs, in_specs=[pl.BlockSpec(me...  14.8 us
    ppermute x1, waiting for transfers between devices, on_ring(): low = up(jnp.concatenate([features_late[-2:], cot_late[-1:]]))  6.39 us
    ppermute x1, waiting for transfers between devices, on_ring(): two = onward(step(keep_two, got_two, after(two, features_out), 2))  4.26 us
    ppermute x2, starting transfers between devices, on_ring(): a1 = jnp.concatenate([onward(weight_one), gather_across(weight_one)])  3.75 us
    ppermute x2, waiting for transfers between devices, on_ring(): b3, qb2 = (onward(after(b2, qb1)), sibling(b2))  3.66 us
    ppermute x2, waiting for transfers between devices, on_ring(): a3, qa2 = (onward(after(a2, b1, low, high, qa1)), sibling(a2))  3.34 us
    ppermute x1, waiting for transfers between devices, on_ring(): got_one = sibling(send_one)  3.28 us
    ppermute x2, waiting for transfers between devices, finish(): total = both(keep, got, 7, 8) + onward(message[:rows]).astype(F32)  3.26 us
  transfers between devices with their start and end apart: 34, of which 20 were waited for; matrix products, arithmetic and copies ran while one was open for 3% of the time, Pallas kernels for 16%

profile of v9, /device:TPU:0, one launch (start us, length us, event | category | flops | bytes accessed | tf_op | source)
XLA Modules:
  0.0 93.9 jit_solution(18150615034388877996)
XLA Ops:
  0.7 3.1 %collective-permute-start.11 = (bf16[432,256]{1,0:T(8,128)(2,1)}, bf16[432,256]{1,0:T(8,128)(2,1)S(1)}, u32[]{:S(2)}, u32[]{:S(2)}) collective-permute-start(bf16[432,256]{1,0:T(8,128)(2,1)} %param.6), channel_id=1, source_target_pairs={{0,4},{4,8},{8,12},{12,14},{14,10},{10,6},{6,2},{2,0},{1,3},{5,1},... | collective-permute-start | bytes 663560 | tf_op jit(solution)/shard_map/ppermute | solution.py:358
  3.7 0.7 collective-permute-start.12
  4.4 1.0 %collective-permute-start = (bf16[432,256]{1,0:T(8,128)(2,1)}, bf16[432,256]{1,0:T(8,128)(2,1)S(1)}, u32[]{:S(2)}, u32[]{:S(2)}) collective-permute-start(bf16[432,256]{1,0:T(8,128)(2,1)} %param.7), channel_id=1, source_target_pairs={{0,1},{1,0},{2,3},{3,2},{4,5},{5,4},{6,7},{7,6},{8,9},{9,8},{10,11... | collective-permute-start | bytes 663560 | tf_op jit(solution)/shard_map/ppermute | solution.py:353
  5.4 0.7 collective-permute-start.4
  6.1 1.0 %collective-permute-start.3 = (bf16[432,256]{1,0:T(8,128)(2,1)}, bf16[432,256]{1,0:T(8,128)(2,1)S(1)}, u32[]{:S(2)}, u32[]{:S(2)}) collective-permute-start(bf16[432,256]{1,0:T(8,128)(2,1)} %param.7), channel_id=1, source_target_pairs={{0,4},{4,8},{8,12},{12,14},{14,10},{10,6},{6,2},{2,0},{1,3},{5,1},... | collective-permute-start | bytes 663560 | tf_op jit(solution)/shard_map/ppermute | solution.py:359
  7.1 1.0 %constant_dynamic-update-slice_fusion.1 = bf16[864,256]{1,0:T(8,128)(2,1)S(1)} fusion(bf16[432,256]{1,0:T(8,128)(2,1)} %param.7), kind=kLoop, calls=%fused_computation.13 | loop fusion | bytes 442368
  8.0 0.8 collective-permute-done.11
  8.9 1.5 %collective-permute-done.12 = bf16[432,256]{1,0:T(8,128)(2,1)S(1)} collective-permute-done((bf16[432,256]{1,0:T(8,128)(2,1)}, bf16[432,256]{1,0:T(8,128)(2,1)S(1)}, u32[]{:S(2)}, u32[]{:S(2)}) %collective-permute-start.12) | collective-permute-done | bytes 221216 | tf_op jit(solution)/shard_map/ppermute | solution.py:358
  10.4 0.7 collective-permute-start.14
  11.1 2.3 %collective-permute-start.13 = (bf16[864,256]{1,0:T(8,128)(2,1)S(1)}, bf16[864,256]{1,0:T(8,128)(2,1)S(1)}, u32[]{:S(2)}, u32[]{:S(2)}) collective-permute-start(bf16[864,256]{1,0:T(8,128)(2,1)S(1)} %constant_dynamic-update-slice_fusion.6.rest_1_), channel_id=1, source_target_pairs={{0,4},{4,8},{8,12},{12,14},{14,10},{10,6},{6,2},{2,0},{1,3},{5,1},... | collective-permute-start | bytes 1327112 | tf_op jit(solution)/shard_map/ppermute | solution.py:360
  13.6 1.1 %collective-permute-done.3 = bf16[432,256]{1,0:T(8,128)(2,1)S(1)} collective-permute-done((bf16[432,256]{1,0:T(8,128)(2,1)}, bf16[432,256]{1,0:T(8,128)(2,1)S(1)}, u32[]{:S(2)}, u32[]{:S(2)}) %collective-permute-start.3) | collective-permute-done | bytes 221216 | tf_op jit(solution)/shard_map/ppermute | solution.py:359
  14.7 0.4 collective-permute-done.4
  15.1 0.1 collective-permute-start.6
  15.2 1.9 %collective-permute-start.5 = (bf16[864,256]{1,0:T(8,128)(2,1)S(1)}, bf16[864,256]{1,0:T(8,128)(2,1)S(1)}, u32[]{:S(2)}, u32[]{:S(2)}) collective-permute-start(bf16[864,256]{1,0:T(8,128)(2,1)S(1)} %constant_dynamic-update-slice_fusion.2.rest_1_.rest_10_), channel_id=1, source_target_pairs={{0,4},{4,8},{8,12},{12,14},{14,10},{10,6},{6,2},{2,0},{1,3},{5,1},... | collective-permute-start | bytes 1327112 | tf_op jit(solution)/shard_map/ppermute | solution.py:361
  17.2 6.4 %collective-permute-done.1.low = bf16[3,8,16,256]{3,2,1,0:T(8,128)(2,1)S(1)} collective-permute-done((bf16[3,8,16,256]{3,2,1,0:T(8,128)(2,1)S(1)}, bf16[3,8,16,256]{3,2,1,0:T(8,128)(2,1)S(1)}, u32[]{:S(2)}, u32[]{:S(2)}) %collective-permute-start.1) | collective-permute-done | bytes 196640 | tf_op jit(solution)/shard_map/ppermute | solution.py:355
  23.5 3.2 %collective-permute-done.2.high = bf16[3,8,16,256]{3,2,1,0:T(8,128)(2,1)S(1)} collective-permute-done((bf16[3,8,16,256]{3,2,1,0:T(8,128)(2,1)S(1)}, bf16[3,8,16,256]{3,2,1,0:T(8,128)(2,1)S(1)}, u32[]{:S(2)}, u32[]{:S(2)}) %collective-permute-start.2) | collective-permute-done | bytes 196640 | tf_op jit(solution)/shard_map/ppermute | solution.py:356
  26.7 0.3 collective-permute-start.15
  27.0 1.5 %collective-permute-start.16 = (bf16[864,256]{1,0:T(8,128)(2,1)S(1)}, bf16[864,256]{1,0:T(8,128)(2,1)S(1)}, u32[]{:S(2)}, u32[]{:S(2)}) collective-permute-start(bf16[864,256]{1,0:T(8,128)(2,1)S(1)} %collective-permute-done.13.rest_2_), channel_id=1, source_target_pairs={{0,1},{1,0},{2,3},{3,2},{4,5},{5,4},{6,7},{7,6},{8,9},{9,8},{10,11... | collective-permute-start | bytes 1327112 | tf_op jit(solution)/shard_map/ppermute | solution.py:362
  28.5 1.7 %collective-permute-start.7 = (bf16[864,256]{1,0:T(8,128)(2,1)S(1)}, bf16[864,256]{1,0:T(8,128)(2,1)S(1)}, u32[]{:S(2)}, u32[]{:S(2)}) collective-permute-start(bf16[864,256]{1,0:T(8,128)(2,1)S(1)} %collective-permute-done.5.rest_2_.rest_11_), channel_id=1, source_target_pairs={{0,4},{4,8},{8,12},{12,14},{14,10},{10,6},{6,2},{2,0},{1,3},{5,1},... | collective-permute-start | bytes 1327112 | tf_op jit(solution)/shard_map/ppermute | solution.py:382
  30.2 0.2 collective-permute-start.8
  30.4 1.3 %prep.1 = (bf16[8,10,16,768]{3,2,1,0:T(8,128)(2,1)S(1)}, bf16[6,10,16,768]{3,2,1,0:T(8,128)(2,1)S(1)}, bf16[256,768]{1,0:T(8,128)(2,1)S(1)}, bf16[3,128,256]{2,1,0:T(8,128)(2,1)S(1)}) custom-call(s32[2,4,16]{2,1,0:T(4,128)S(1)} %bitcast.1, bf16[3,8,16,256]{3,2,1,0:T(8,128)(2,1)S(1)} %collective-permute-done.1.low, bf16[4,8,16,256]{3,2,1,0:T(8,128)(2,1)S(1)} %copy-done, ...), custom_call_target="tpu_custom_call" | custom-call | bytes 4194304 | tf_op jit(solution)/shard_map/prep/pallas_call | solution.py:338
  31.7 3.3 %collective-permute-done.15.rest_3_ = bf16[864,256]{1,0:T(8,128)(2,1)S(1)} collective-permute-done((bf16[864,256]{1,0:T(8,128)(2,1)S(1)}, bf16[864,256]{1,0:T(8,128)(2,1)S(1)}, u32[]{:S(2)}, u32[]{:S(2)}) %collective-permute-start.15) | collective-permute-done | bytes 442400 | tf_op jit(solution)/shard_map/ppermute | solution.py:362
  35.1 0.3 collective-permute-start.17
  35.4 0.7 collective-permute-start.18
  36.1 0.1 collective-permute-start.10
  36.1 3.7 %collective-permute-done.7.rest_3_.rest_12_ = bf16[864,256]{1,0:T(8,128)(2,1)S(1)} collective-permute-done((bf16[864,256]{1,0:T(8,128)(2,1)S(1)}, bf16[864,256]{1,0:T(8,128)(2,1)S(1)}, u32[]{:S(2)}, u32[]{:S(2)}) %collective-permute-start.7) | collective-permute-done | bytes 442400 | tf_op jit(solution)/shard_map/ppermute | solution.py:382
  39.8 0.3 collective-permute-start.9
  40.1 2.0 %collective-permute-done.17.rest_4_ = bf16[432,256]{1,0:T(8,128)(2,1)S(1)} collective-permute-done((bf16[432,256]{1,0:T(8,128)(2,1)S(1)}, bf16[432,256]{1,0:T(8,128)(2,1)S(1)}, u32[]{:S(2)}, u32[]{:S(2)}) %collective-permute-start.17) | collective-permute-done | bytes 221216 | tf_op jit(solution)/shard_map/ppermute | solution.py:383
  42.2 0.5 collective-permute-start.19
  42.7 0.1 collective-permute-start.21
  42.8 3.0 %collective-permute-done.9.rest_4_.rest_13_ = bf16[432,256]{1,0:T(8,128)(2,1)S(1)} collective-permute-done((bf16[432,256]{1,0:T(8,128)(2,1)S(1)}, bf16[432,256]{1,0:T(8,128)(2,1)S(1)}, u32[]{:S(2)}, u32[]{:S(2)}) %collective-permute-start.9) | collective-permute-done | bytes 221216 | tf_op jit(solution)/shard_map/ppermute | solution.py:384
  45.8 2.3 %first.1 = (f32[512,256]{1,0:T(8,128)S(1)}, bf16[512,256]{1,0:T(8,128)(2,1)S(1)}, bf16[256,512]{1,0:T(8,128)(2,1)S(1)}) custom-call(bf16[8,10,16,768]{3,2,1,0:T(8,128)(2,1)S(1)} %get-tuple-element.29.sx_ref, bf16[3,128,256]{2,1,0:T(8,128)(2,1)S(1)} %get-tuple-element.30.mask_ref, bf16[864,256]{1,0:T(8,128)(2,1)S(1)} %constant_dynamic-update-slice_fusion.4.rest_0_, ...), custom_call_target="tpu_custom_call" | custom-call | flops 1811939328 | bytes 4194304 | tf_op jit(solution)/shard_map/first/pallas_call | solution.py:338
  48.2 2.2 %grad_two.1 = (bf16[3456,256]{1,0:T(8,128)(2,1)S(1)}, bf16[3456,256]{1,0:T(8,128)(2,1)S(1)}) custom-call(bf16[6,10,16,768]{3,2,1,0:T(8,128)(2,1)S(1)} %get-tuple-element.34.sc_ref, bf16[256,512]{1,0:T(8,128)(2,1)S(1)} %get-tuple-element.35.act_t_ref), custom_call_target="tpu_custom_call" | custom-call | flops 1811939328 | bytes 4194304 | tf_op jit(solution)/shard_map/grad_two/pallas_call | solution.py:338
  50.4 0.6 collective-permute-start.20
  51.0 2.4 %back.1.sd_ref = bf16[4,10,16,768]{3,2,1,0:T(8,128)(2,1)S(1)} custom-call(bf16[6,10,16,768]{3,2,1,0:T(8,128)(2,1)S(1)} %get-tuple-element.34.sc_ref, f32[512,256]{1,0:T(8,128)S(1)} %get-tuple-element.38.pre_ref, bf16[3,128,256]{2,1,0:T(8,128)(2,1)S(1)} %get-tuple-element.30.mask_ref, bf16[864,256]{1,0:T(8,128)(2,1)S(1)} %constant_dynamic-update-slice_fusion.rest_0_.rest_9_, ...), custom_call_target="tpu_custom_call" | custom-call | flops 1811939328 | bytes 4194304 | tf_op jit(solution)/shard_map/back/pallas_call | solution.py:338
  53.4 2.3 %grad_one.1 = (bf16[3456,256]{1,0:T(8,128)(2,1)S(1)}, bf16[3456,256]{1,0:T(8,128)(2,1)S(1)}) custom-call(bf16[4,10,16,768]{3,2,1,0:T(8,128)(2,1)S(1)} %back.1.sd_ref, bf16[256,768]{1,0:T(8,128)(2,1)S(1)} %get-tuple-element.39.int_ref), custom_call_target="tpu_custom_call" | custom-call | flops 1811939328 | bytes 4194304 | tf_op jit(solution)/shard_map/grad_one/pallas_call | solution.py:338
  55.6 0.1 collective-permute-start.24
  55.8 0.3 collective-permute-start.23
  56.1 3.3 %collective-permute-done.24 = bf16[3456,256]{1,0:T(8,128)(2,1)S(1)} collective-permute-done((bf16[3456,256]{1,0:T(8,128)(2,1)S(1)}, bf16[3456,256]{1,0:T(8,128)(2,1)S(1)}, u32[]{:S(2)}, u32[]{:S(2)}) %collective-permute-start.24) | collective-permute-done | bytes 1769504 | tf_op jit(solution)/shard_map/ppermute | solution.py:440
  59.5 0.3 collective-permute-start.25
  59.8 2.0 %collective-permute-done.23 = bf16[432,256]{1,0:T(8,128)(2,1)S(1)} collective-permute-done((bf16[432,256]{1,0:T(8,128)(2,1)S(1)}, bf16[432,256]{1,0:T(8,128)(2,1)S(1)}, u32[]{:S(2)}, u32[]{:S(2)}) %collective-permute-start.23) | collective-permute-done | bytes 221216 | tf_op jit(solution)/shard_map/ppermute | solution.py:439
  61.8 0.1 add_convert_fusion.2
  61.9 0.3 collective-permute-start.30
  62.2 3.2 %collective-permute-done.25 = bf16[432,256]{1,0:T(8,128)(2,1)S(1)} collective-permute-done((bf16[432,256]{1,0:T(8,128)(2,1)S(1)}, bf16[432,256]{1,0:T(8,128)(2,1)S(1)}, u32[]{:S(2)}, u32[]{:S(2)}) %collective-permute-start.25) | collective-permute-done | bytes 221216 | tf_op jit(solution)/shard_map/ppermute | solution.py:441
  65.4 0.2 add_convert_fusion.5
  65.6 0.5 collective-permute-start.26
  66.1 4.2 %third.1 = bf16[4,8,16,256]{3,2,1,0:T(8,128)(2,1)} custom-call(bf16[8,10,16,768]{3,2,1,0:T(8,128)(2,1)S(1)} %get-tuple-element.29.sx_ref, bf16[512,256]{1,0:T(8,128)(2,1)S(1)} %get-tuple-element.42.act_ref, bf16[3,128,256]{2,1,0:T(8,128)(2,1)S(1)} %get-tuple-element.30.mask_ref, bf16[864,256]{1,0:T(8,128)(2,1)S(1)} %constant_dynamic-update-slice_fusion.4.rest_0_, ...), custom_call_target="tpu_custom_call" | custom-call | flops 1811939328 | bytes 4194304 | tf_op jit(solution)/shard_map/third/pallas_call | solution.py:338
  70.3 0.2 add_convert_fusion.1
  70.5 2.2 %collective-permute-start.31 = (bf16[864,256]{1,0:T(8,128)(2,1)S(1)}, bf16[864,256]{1,0:T(8,128)(2,1)S(1)}, u32[]{:S(2)}, u32[]{:S(2)}) collective-permute-start(bf16[864,256]{1,0:T(8,128)(2,1)S(1)} %add_convert_fusion.1), channel_id=1, source_target_pairs={{0,4},{4,8},{8,12},{12,14},{14,10},{10,6},{6,2},{2,0},{1,3},{5,1},... | collective-permute-start | bytes 1327112 | tf_op jit(solution)/shard_map/ppermute | solution.py:457
  72.7 2.3 %collective-permute-done.26 = bf16[864,256]{1,0:T(8,128)(2,1)S(1)} collective-permute-done((bf16[864,256]{1,0:T(8,128)(2,1)S(1)}, bf16[864,256]{1,0:T(8,128)(2,1)S(1)}, u32[]{:S(2)}, u32[]{:S(2)}) %collective-permute-start.26) | collective-permute-done | bytes 442400 | tf_op jit(solution)/shard_map/ppermute | solution.py:456
  75.0 0.2 add_convert_fusion.4
  75.2 0.3 collective-permute-start.27
  75.5 4.3 %collective-permute-done.31 = bf16[864,256]{1,0:T(8,128)(2,1)S(1)} collective-permute-done((bf16[864,256]{1,0:T(8,128)(2,1)S(1)}, bf16[864,256]{1,0:T(8,128)(2,1)S(1)}, u32[]{:S(2)}, u32[]{:S(2)}) %collective-permute-start.31) | collective-permute-done | bytes 442400 | tf_op jit(solution)/shard_map/ppermute | solution.py:457
  79.8 0.2 add_convert_fusion
  80.0 1.3 %collective-permute-start.32 = (bf16[432,256]{1,0:T(8,128)(2,1)S(1)}, bf16[432,256]{1,0:T(8,128)(2,1)S(1)}, u32[]{:S(2)}, u32[]{:S(2)}) collective-permute-start(bf16[432,256]{1,0:T(8,128)(2,1)S(1)} %get-tuple-element.45), channel_id=1, source_target_pairs={{0,4},{4,8},{8,12},{12,14},{14,10},{10,6},{6,2},{2,0},{1,3},{5,1},... | collective-permute-start | bytes 663560 | tf_op jit(solution)/shard_map/ppermute | solution.py:421
  81.3 3.2 %collective-permute-done.27 = bf16[864,256]{1,0:T(8,128)(2,1)S(1)} collective-permute-done((bf16[864,256]{1,0:T(8,128)(2,1)S(1)}, bf16[864,256]{1,0:T(8,128)(2,1)S(1)}, u32[]{:S(2)}, u32[]{:S(2)}) %collective-permute-start.27) | collective-permute-done | bytes 442400 | tf_op jit(solution)/shard_map/ppermute | solution.py:458
  84.5 0.2 add_convert_fusion.3
  84.7 1.3 %collective-permute-start.28 = (bf16[432,256]{1,0:T(8,128)(2,1)S(1)}, bf16[432,256]{1,0:T(8,128)(2,1)S(1)}, u32[]{:S(2)}, u32[]{:S(2)}) collective-permute-start(bf16[432,256]{1,0:T(8,128)(2,1)S(1)} %get-tuple-element.47), channel_id=1, source_target_pairs={{0,4},{4,8},{8,12},{12,14},{14,10},{10,6},{6,2},{2,0},{1,3},{5,1},... | collective-permute-start | bytes 663560 | tf_op jit(solution)/shard_map/ppermute | solution.py:421
  86.0 0.8 collective-permute-done.32
  86.9 1.4 %collective-permute-done.33 = bf16[432,256]{1,0:T(8,128)(2,1)S(1)} collective-permute-done((bf16[432,256]{1,0:T(8,128)(2,1)S(1)}, bf16[432,256]{1,0:T(8,128)(2,1)S(1)}, u32[]{:S(2)}, u32[]{:S(2)}) %collective-permute-start.33) | collective-permute-done | bytes 221216 | tf_op jit(solution)/shard_map/ppermute | solution.py:422
  88.3 0.9 add_multiply_fusion
  89.2 2.4 %collective-permute-done.28 = bf16[432,256]{1,0:T(8,128)(2,1)S(1)} collective-permute-done((bf16[432,256]{1,0:T(8,128)(2,1)S(1)}, bf16[432,256]{1,0:T(8,128)(2,1)S(1)}, u32[]{:S(2)}, u32[]{:S(2)}) %collective-permute-start.28) | collective-permute-done | bytes 221216 | tf_op jit(solution)/shard_map/ppermute | solution.py:421
  91.6 1.4 %collective-permute-done.29 = bf16[432,256]{1,0:T(8,128)(2,1)S(1)} collective-permute-done((bf16[432,256]{1,0:T(8,128)(2,1)S(1)}, bf16[432,256]{1,0:T(8,128)(2,1)S(1)}, u32[]{:S(2)}, u32[]{:S(2)}) %collective-permute-start.29) | collective-permute-done | bytes 221216 | tf_op jit(solution)/shard_map/ppermute | solution.py:422
  93.1 0.9 add_multiply_fusion.1
  (44 shorter events, 0.5 us)
Async XLA Ops:
  0.6 12.8 %copy-start.1 = (bf16[4,8,16,256]{3,2,1,0:T(8,128)(2,1)S(1)}, bf16[4,8,16,256]{3,2,1,0:T(8,128)(2,1)}, u32[]{:S(2)}) copy-start(bf16[4,8,16,256]{3,2,1,0:T(8,128)(2,1)} %c_own.1) | copy-start | bytes 786436
  0.6 12.8 %copy-start = (bf16[4,8,16,256]{3,2,1,0:T(8,128)(2,1)S(1)}, bf16[4,8,16,256]{3,2,1,0:T(8,128)(2,1)}, u32[]{:S(2)}) copy-start(bf16[4,8,16,256]{3,2,1,0:T(8,128)(2,1)} %f_own.1) | copy-start | bytes 786436
  0.7 8.2 %collective-permute-start.11 = (bf16[432,256]{1,0:T(8,128)(2,1)}, bf16[432,256]{1,0:T(8,128)(2,1)S(1)}, u32[]{:S(2)}, u32[]{:S(2)}) collective-permute-start(bf16[432,256]{1,0:T(8,128)(2,1)} %param.6), channel_id=1, source_target_pairs={{0,4},{4,8},{8,12},{12,14},{14,10},{10,6},{6,2},{2,0},{1,3},{5,1},... | collective-permute-start | bytes 663560 | tf_op jit(solution)/shard_map/ppermute | solution.py:358
  3.7 6.7 %collective-permute-start.12 = (bf16[432,256]{1,0:T(8,128)(2,1)}, bf16[432,256]{1,0:T(8,128)(2,1)S(1)}, u32[]{:S(2)}, u32[]{:S(2)}) collective-permute-start(bf16[432,256]{1,0:T(8,128)(2,1)} %param.6), channel_id=1, source_target_pairs={{1,4},{5,8},{9,12},{13,14},{15,10},{11,6},{7,2},{3,0},{0,3},{4,1},... | collective-permute-start | bytes 663560 | tf_op jit(solution)/shard_map/ppermute | solution.py:358
  4.4 9.0 %collective-permute-start = (bf16[432,256]{1,0:T(8,128)(2,1)}, bf16[432,256]{1,0:T(8,128)(2,1)S(1)}, u32[]{:S(2)}, u32[]{:S(2)}) collective-permute-start(bf16[432,256]{1,0:T(8,128)(2,1)} %param.7), channel_id=1, source_target_pairs={{0,1},{1,0},{2,3},{3,2},{4,5},{5,4},{6,7},{7,6},{8,9},{9,8},{10,11... | collective-permute-start | bytes 663560 | tf_op jit(solution)/shard_map/ppermute | solution.py:353
  5.4 9.7 %collective-permute-start.4 = (bf16[432,256]{1,0:T(8,128)(2,1)}, bf16[432,256]{1,0:T(8,128)(2,1)S(1)}, u32[]{:S(2)}, u32[]{:S(2)}) collective-permute-start(bf16[432,256]{1,0:T(8,128)(2,1)} %param.7), channel_id=1, source_target_pairs={{1,4},{5,8},{9,12},{13,14},{15,10},{11,6},{7,2},{3,0},{0,3},{4,1},... | collective-permute-start | bytes 663560 | tf_op jit(solution)/shard_map/ppermute | solution.py:359
  6.1 8.6 %collective-permute-start.3 = (bf16[432,256]{1,0:T(8,128)(2,1)}, bf16[432,256]{1,0:T(8,128)(2,1)S(1)}, u32[]{:S(2)}, u32[]{:S(2)}) collective-permute-start(bf16[432,256]{1,0:T(8,128)(2,1)} %param.7), channel_id=1, source_target_pairs={{0,4},{4,8},{8,12},{12,14},{14,10},{10,6},{6,2},{2,0},{1,3},{5,1},... | collective-permute-start | bytes 663560 | tf_op jit(solution)/shard_map/ppermute | solution.py:359
  8.9 21.5 %copy-start.2 = (s32[16,2,4]{0,2,1:T(4,128)S(1)}, s32[16,2,4]{0,2,1:T(4,128)}, u32[]{:S(2)}) copy-start(s32[16,2,4]{0,2,1:T(4,128)} %param.9) | copy-start | bytes 1540
  10.4 16.3 %collective-permute-start.14 = (bf16[864,256]{1,0:T(8,128)(2,1)S(1)}, bf16[864,256]{1,0:T(8,128)(2,1)S(1)}, u32[]{:S(2)}, u32[]{:S(2)}) collective-permute-start(bf16[864,256]{1,0:T(8,128)(2,1)S(1)} %constant_dynamic-update-slice_fusion.6.rest_1_), channel_id=1, source_target_pairs={{0,1},{1,0},{2,3},{3,2},{4,5},{5,4},{6,7},{7,6},{8,9},{9,8},{10,11... | collective-permute-start | bytes 1327112 | tf_op jit(solution)/shard_map/ppermute | solution.py:360
  11.1 15.7 %collective-permute-start.13 = (bf16[864,256]{1,0:T(8,128)(2,1)S(1)}, bf16[864,256]{1,0:T(8,128)(2,1)S(1)}, u32[]{:S(2)}, u32[]{:S(2)}) collective-permute-start(bf16[864,256]{1,0:T(8,128)(2,1)S(1)} %constant_dynamic-update-slice_fusion.6.rest_1_), channel_id=1, source_target_pairs={{0,4},{4,8},{8,12},{12,14},{14,10},{10,6},{6,2},{2,0},{1,3},{5,1},... | collective-permute-start | bytes 1327112 | tf_op jit(solution)/shard_map/ppermute | solution.py:360
  13.5 22.6 %copy-start.3 = (bf16[432,256]{1,0:T(8,128)(2,1)S(1)}, bf16[432,256]{1,0:T(8,128)(2,1)}, u32[]{:S(2)}) copy-start(bf16[432,256]{1,0:T(8,128)(2,1)} %param.6) | copy-start | bytes 663556
  13.5 10.0 %collective-permute-start.1 = (bf16[3,8,16,256]{3,2,1,0:T(8,128)(2,1)S(1)}, bf16[3,8,16,256]{3,2,1,0:T(8,128)(2,1)S(1)}, u32[]{:S(2)}, u32[]{:S(2)}) collective-permute-start(bf16[3,8,16,256]{3,2,1,0:T(8,128)(2,1)S(1)} %pad_maximum_fusion), channel_id=1, source_target_pairs={{0,1},{1,2},{2,3},{3,4},{4,5},{5,6},{6,7},{7,8},{8,9},{9,10},{10,1... | collective-permute-start | bytes 589832 | tf_op jit(solution)/shard_map/ppermute | solution.py:355
  15.1 13.4 %collective-permute-start.6 = (bf16[864,256]{1,0:T(8,128)(2,1)S(1)}, bf16[864,256]{1,0:T(8,128)(2,1)S(1)}, u32[]{:S(2)}, u32[]{:S(2)}) collective-permute-start(bf16[864,256]{1,0:T(8,128)(2,1)S(1)} %constant_dynamic-update-slice_fusion.2.rest_1_.rest_10_), channel_id=1, source_target_pairs={{0,1},{1,0},{2,3},{3,2},{4,5},{5,4},{6,7},{7,6},{8,9},{9,8},{10,11... | collective-permute-start | bytes 1327112 | tf_op jit(solution)/shard_map/ppermute | solution.py:361
  15.2 13.3 %collective-permute-start.5 = (bf16[864,256]{1,0:T(8,128)(2,1)S(1)}, bf16[864,256]{1,0:T(8,128)(2,1)S(1)}, u32[]{:S(2)}, u32[]{:S(2)}) collective-permute-start(bf16[864,256]{1,0:T(8,128)(2,1)S(1)} %constant_dynamic-update-slice_fusion.2.rest_1_.rest_10_), channel_id=1, source_target_pairs={{0,4},{4,8},{8,12},{12,14},{14,10},{10,6},{6,2},{2,0},{1,3},{5,1},... | collective-permute-start | bytes 1327112 | tf_op jit(solution)/shard_map/ppermute | solution.py:361
  23.5 3.2 %collective-permute-start.2 = (bf16[3,8,16,256]{3,2,1,0:T(8,128)(2,1)S(1)}, bf16[3,8,16,256]{3,2,1,0:T(8,128)(2,1)S(1)}, u32[]{:S(2)}, u32[]{:S(2)}) collective-permute-start(bf16[3,8,16,256]{3,2,1,0:T(8,128)(2,1)S(1)} %pad_maximum_fusion.1), channel_id=1, source_target_pairs={{0,15},{1,0},{2,1},{3,2},{4,3},{5,4},{6,5},{7,6},{8,7},{9,8},{10,9... | collective-permute-start | bytes 589832 | tf_op jit(solution)/shard_map/ppermute | solution.py:356
  26.7 8.3 %collective-permute-start.15 = (bf16[864,256]{1,0:T(8,128)(2,1)S(1)}, bf16[864,256]{1,0:T(8,128)(2,1)S(1)}, u32[]{:S(2)}, u32[]{:S(2)}) collective-permute-start(bf16[864,256]{1,0:T(8,128)(2,1)S(1)} %collective-permute-done.13.rest_2_), channel_id=1, source_target_pairs={{0,4},{4,8},{8,12},{12,14},{14,10},{10,6},{6,2},{2,0},{1,3},{5,1},... | collective-permute-start | bytes 1327112 | tf_op jit(solution)/shard_map/ppermute | solution.py:362
  27.0 8.1 %collective-permute-start.16 = (bf16[864,256]{1,0:T(8,128)(2,1)S(1)}, bf16[864,256]{1,0:T(8,128)(2,1)S(1)}, u32[]{:S(2)}, u32[]{:S(2)}) collective-permute-start(bf16[864,256]{1,0:T(8,128)(2,1)S(1)} %collective-permute-done.13.rest_2_), channel_id=1, source_target_pairs={{0,1},{1,0},{2,3},{3,2},{4,5},{5,4},{6,7},{7,6},{8,9},{9,8},{10,11... | collective-permute-start | bytes 1327112 | tf_op jit(solution)/shard_map/ppermute | solution.py:362
  28.5 11.3 %collective-permute-start.7 = (bf16[864,256]{1,0:T(8,128)(2,1)S(1)}, bf16[864,256]{1,0:T(8,128)(2,1)S(1)}, u32[]{:S(2)}, u32[]{:S(2)}) collective-permute-start(bf16[864,256]{1,0:T(8,128)(2,1)S(1)} %collective-permute-done.5.rest_2_.rest_11_), channel_id=1, source_target_pairs={{0,4},{4,8},{8,12},{12,14},{14,10},{10,6},{6,2},{2,0},{1,3},{5,1},... | collective-permute-start | bytes 1327112 | tf_op jit(solution)/shard_map/ppermute | solution.py:382
  30.2 9.6 %collective-permute-start.8 = (bf16[864,256]{1,0:T(8,128)(2,1)S(1)}, bf16[864,256]{1,0:T(8,128)(2,1)S(1)}, u32[]{:S(2)}, u32[]{:S(2)}) collective-permute-start(bf16[864,256]{1,0:T(8,128)(2,1)S(1)} %collective-permute-done.5.rest_2_.rest_11_), channel_id=1, source_target_pairs={{0,1},{1,0},{2,3},{3,2},{4,5},{5,4},{6,7},{7,6},{8,9},{9,8},{10,11... | collective-permute-start | bytes 1327112 | tf_op jit(solution)/shard_map/ppermute | solution.py:382
  35.1 7.1 %collective-permute-start.17 = (bf16[432,256]{1,0:T(8,128)(2,1)S(1)}, bf16[432,256]{1,0:T(8,128)(2,1)S(1)}, u32[]{:S(2)}, u32[]{:S(2)}) collective-permute-start(bf16[432,256]{1,0:T(8,128)(2,1)S(1)} %slice.121), channel_id=1, source_target_pairs={{0,4},{4,8},{8,12},{12,14},{14,10},{10,6},{6,2},{2,0},{1,3},{5,1},... | collective-permute-start | bytes 663560 | tf_op jit(solution)/shard_map/ppermute | solution.py:383
  35.4 10.4 %collective-permute-start.18 = (bf16[864,256]{1,0:T(8,128)(2,1)S(1)}, bf16[864,256]{1,0:T(8,128)(2,1)S(1)}, u32[]{:S(2)}, u32[]{:S(2)}) collective-permute-start(bf16[864,256]{1,0:T(8,128)(2,1)S(1)} %collective-permute-done.15.rest_3_), channel_id=1, source_target_pairs={{0,1},{1,0},{2,3},{3,2},{4,5},{5,4},{6,7},{7,6},{8,9},{9,8},{10,11... | collective-permute-start | bytes 1327112 | tf_op jit(solution)/shard_map/ppermute | solution.py:383
  36.1 6.7 %collective-permute-start.10 = (bf16[432,256]{1,0:T(8,128)(2,1)S(1)}, bf16[432,256]{1,0:T(8,128)(2,1)S(1)}, u32[]{:S(2)}, u32[]{:S(2)}) collective-permute-start(bf16[432,256]{1,0:T(8,128)(2,1)S(1)} %copy-done.3), channel_id=1, source_target_pairs={{0,1},{1,0},{2,3},{3,2},{4,5},{5,4},{6,7},{7,6},{8,9},{9,8},{10,11... | collective-permute-start | bytes 663560 | tf_op jit(solution)/shard_map/ppermute | solution.py:352
  39.8 6.0 %collective-permute-start.9 = (bf16[432,256]{1,0:T(8,128)(2,1)S(1)}, bf16[432,256]{1,0:T(8,128)(2,1)S(1)}, u32[]{:S(2)}, u32[]{:S(2)}) collective-permute-start(bf16[432,256]{1,0:T(8,128)(2,1)S(1)} %slice.120), channel_id=1, source_target_pairs={{0,4},{4,8},{8,12},{12,14},{14,10},{10,6},{6,2},{2,0},{1,3},{5,1},... | collective-permute-start | bytes 663560 | tf_op jit(solution)/shard_map/ppermute | solution.py:384
  42.2 3.7 %collective-permute-start.19 = (bf16[432,256]{1,0:T(8,128)(2,1)S(1)}, bf16[432,256]{1,0:T(8,128)(2,1)S(1)}, u32[]{:S(2)}, u32[]{:S(2)}) collective-permute-start(bf16[432,256]{1,0:T(8,128)(2,1)S(1)} %collective-permute-done.17.rest_4_), channel_id=1, source_target_pairs={{0,1},{1,0},{2,3},{3,2},{4,5},{5,4},{6,7},{7,6},{8,9},{9,8},{10,11... | collective-permute-start | bytes 663560 | tf_op jit(solution)/shard_map/ppermute | solution.py:385
  42.7 8.2 %collective-permute-start.21 = (bf16[864,256]{1,0:T(8,128)(2,1)S(1)}, bf16[864,256]{1,0:T(8,128)(2,1)S(1)}, u32[]{:S(2)}, u32[]{:S(2)}) collective-permute-start(bf16[864,256]{1,0:T(8,128)(2,1)S(1)} %collective-permute-done.7.rest_3_.rest_12_), channel_id=1, source_target_pairs={{0,1},{1,0},{2,3},{3,2},{4,5},{5,4},{6,7},{7,6},{8,9},{9,8},{10,11... | collective-permute-start | bytes 1327112 | tf_op jit(solution)/shard_map/ppermute | solution.py:384
  45.8 5.2 %collective-permute-start.22 = (bf16[432,256]{1,0:T(8,128)(2,1)S(1)}, bf16[432,256]{1,0:T(8,128)(2,1)S(1)}, u32[]{:S(2)}, u32[]{:S(2)}) collective-permute-start(bf16[432,256]{1,0:T(8,128)(2,1)S(1)} %collective-permute-done.9.rest_4_.rest_13_), channel_id=1, source_target_pairs={{0,1},{1,0},{2,3},{3,2},{4,5},{5,4},{6,7},{7,6},{8,9},{9,8},{10,11... | collective-permute-start | bytes 663560 | tf_op jit(solution)/shard_map/ppermute | solution.py:385
  50.4 5.4 %collective-permute-start.20 = (bf16[3456,256]{1,0:T(8,128)(2,1)S(1)}, bf16[3456,256]{1,0:T(8,128)(2,1)S(1)}, u32[]{:S(2)}, u32[]{:S(2)}) collective-permute-start(bf16[3456,256]{1,0:T(8,128)(2,1)S(1)} %get-tuple-element.37), channel_id=1, source_target_pairs={{0,1},{1,0},{2,3},{3,2},{4,5},{5,4},{6,7},{7,6},{8,9},{9,8},{10,11... | collective-permute-start | bytes 5308424 | tf_op jit(solution)/shard_map/ppermute | solution.py:408
  55.6 3.8 %collective-permute-start.24 = (bf16[3456,256]{1,0:T(8,128)(2,1)S(1)}, bf16[3456,256]{1,0:T(8,128)(2,1)S(1)}, u32[]{:S(2)}, u32[]{:S(2)}) collective-permute-start(bf16[3456,256]{1,0:T(8,128)(2,1)S(1)} %get-tuple-element.43), channel_id=1, source_target_pairs={{0,1},{1,0},{2,3},{3,2},{4,5},{5,4},{6,7},{7,6},{8,9},{9,8},{10,11... | collective-permute-start | bytes 5308424 | tf_op jit(solution)/shard_map/ppermute | solution.py:440
  55.8 6.0 %collective-permute-start.23 = (bf16[432,256]{1,0:T(8,128)(2,1)S(1)}, bf16[432,256]{1,0:T(8,128)(2,1)S(1)}, u32[]{:S(2)}, u32[]{:S(2)}) collective-permute-start(bf16[432,256]{1,0:T(8,128)(2,1)S(1)} %add_convert_fusion.7), channel_id=1, source_target_pairs={{0,4},{4,8},{8,12},{12,14},{14,10},{10,6},{6,2},{2,0},{1,3},{5,1},... | collective-permute-start | bytes 663560 | tf_op jit(solution)/shard_map/ppermute | solution.py:439
  59.5 6.0 %collective-permute-start.25 = (bf16[432,256]{1,0:T(8,128)(2,1)S(1)}, bf16[432,256]{1,0:T(8,128)(2,1)S(1)}, u32[]{:S(2)}, u32[]{:S(2)}) collective-permute-start(bf16[432,256]{1,0:T(8,128)(2,1)S(1)} %add_convert_fusion.6), channel_id=1, source_target_pairs={{0,4},{4,8},{8,12},{12,14},{14,10},{10,6},{6,2},{2,0},{1,3},{5,1},... | collective-permute-start | bytes 663560 | tf_op jit(solution)/shard_map/ppermute | solution.py:441
  61.9 8.4 %collective-permute-start.30 = (bf16[864,256]{1,0:T(8,128)(2,1)S(1)}, bf16[864,256]{1,0:T(8,128)(2,1)S(1)}, u32[]{:S(2)}, u32[]{:S(2)}) collective-permute-start(bf16[864,256]{1,0:T(8,128)(2,1)S(1)} %add_convert_fusion.2), channel_id=1, source_target_pairs={{0,4},{4,8},{8,12},{12,14},{14,10},{10,6},{6,2},{2,0},{1,3},{5,1},... | collective-permute-start | bytes 1327112 | tf_op jit(solution)/shard_map/ppermute | solution.py:455
  65.6 9.4 %collective-permute-start.26 = (bf16[864,256]{1,0:T(8,128)(2,1)S(1)}, bf16[864,256]{1,0:T(8,128)(2,1)S(1)}, u32[]{:S(2)}, u32[]{:S(2)}) collective-permute-start(bf16[864,256]{1,0:T(8,128)(2,1)S(1)} %add_convert_fusion.5), channel_id=1, source_target_pairs={{0,4},{4,8},{8,12},{12,14},{14,10},{10,6},{6,2},{2,0},{1,3},{5,1},... | collective-permute-start | bytes 1327112 | tf_op jit(solution)/shard_map/ppermute | solution.py:456
  70.5 9.2 %collective-permute-start.31 = (bf16[864,256]{1,0:T(8,128)(2,1)S(1)}, bf16[864,256]{1,0:T(8,128)(2,1)S(1)}, u32[]{:S(2)}, u32[]{:S(2)}) collective-permute-start(bf16[864,256]{1,0:T(8,128)(2,1)S(1)} %add_convert_fusion.1), channel_id=1, source_target_pairs={{0,4},{4,8},{8,12},{12,14},{14,10},{10,6},{6,2},{2,0},{1,3},{5,1},... | collective-permute-start | bytes 1327112 | tf_op jit(solution)/shard_map/ppermute | solution.py:457
  75.2 9.3 %collective-permute-start.27 = (bf16[864,256]{1,0:T(8,128)(2,1)S(1)}, bf16[864,256]{1,0:T(8,128)(2,1)S(1)}, u32[]{:S(2)}, u32[]{:S(2)}) collective-permute-start(bf16[864,256]{1,0:T(8,128)(2,1)S(1)} %add_convert_fusion.4), channel_id=1, source_target_pairs={{0,4},{4,8},{8,12},{12,14},{14,10},{10,6},{6,2},{2,0},{1,3},{5,1},... | collective-permute-start | bytes 1327112 | tf_op jit(solution)/shard_map/ppermute | solution.py:458
  80.0 6.9 %collective-permute-start.32 = (bf16[432,256]{1,0:T(8,128)(2,1)S(1)}, bf16[432,256]{1,0:T(8,128)(2,1)S(1)}, u32[]{:S(2)}, u32[]{:S(2)}) collective-permute-start(bf16[432,256]{1,0:T(8,128)(2,1)S(1)} %get-tuple-element.45), channel_id=1, source_target_pairs={{0,4},{4,8},{8,12},{12,14},{14,10},{10,6},{6,2},{2,0},{1,3},{5,1},... | collective-permute-start | bytes 663560 | tf_op jit(solution)/shard_map/ppermute | solution.py:421
  81.3 7.0 %collective-permute-start.33 = (bf16[432,256]{1,0:T(8,128)(2,1)S(1)}, bf16[432,256]{1,0:T(8,128)(2,1)S(1)}, u32[]{:S(2)}, u32[]{:S(2)}) collective-permute-start(bf16[432,256]{1,0:T(8,128)(2,1)S(1)} %get-tuple-element.46), channel_id=1, source_target_pairs={{0,5},{4,9},{8,13},{12,15},{14,11},{10,7},{6,3},{2,1},{1,2},{5,0},... | collective-permute-start | bytes 663560 | tf_op jit(solution)/shard_map/ppermute | solution.py:422
  84.7 6.9 %collective-permute-start.28 = (bf16[432,256]{1,0:T(8,128)(2,1)S(1)}, bf16[432,256]{1,0:T(8,128)(2,1)S(1)}, u32[]{:S(2)}, u32[]{:S(2)}) collective-permute-start(bf16[432,256]{1,0:T(8,128)(2,1)S(1)} %get-tuple-element.47), channel_id=1, source_target_pairs={{0,4},{4,8},{8,12},{12,14},{14,10},{10,6},{6,2},{2,0},{1,3},{5,1},... | collective-permute-start | bytes 663560 | tf_op jit(solution)/shard_map/ppermute | solution.py:421
  86.0 7.0 %collective-permute-start.29 = (bf16[432,256]{1,0:T(8,128)(2,1)S(1)}, bf16[432,256]{1,0:T(8,128)(2,1)S(1)}, u32[]{:S(2)}, u32[]{:S(2)}) collective-permute-start(bf16[432,256]{1,0:T(8,128)(2,1)S(1)} %get-tuple-element.48), channel_id=1, source_target_pairs={{0,5},{4,9},{8,13},{12,15},{14,11},{10,7},{6,3},{2,1},{1,2},{5,0},... | collective-permute-start | bytes 663560 | tf_op jit(solution)/shard_map/ppermute | solution.py:422

commit v10 on v9

--- a/solution.py
+++ b/solution.py
@@ -358,8 +358,8 @@
     a1 = jnp.concatenate([onward(weight_one), gather_across(weight_one)])
     b1 = jnp.concatenate([onward(weight_two), gather_across(weight_two)])
     a2, qa1 = onward(a1), sibling(a1)
-    b2, qb1 = onward(b1), sibling(b1)
-    a3, qa2 = onward(after(a2, b1, low, high, qa1)), sibling(a2)
+    b2, qb1 = onward(after(b1, low, high)), sibling(b1)
+    a3, qa2 = onward(after(a2, b1)), sibling(a2)
     sx, sc, in_t, near = kernel(
         prep_kernel,
         "prep",
@@ -379,12 +379,11 @@
         high,
         smem=1,
     )
-    b3, qb2 = onward(after(b2, qb1)), sibling(b2)
-    a4, qa3 = onward(after(a3[:rows], b2, sx, qa2)), sibling(a3)
-    b4, qb3 = onward(after(b3[:rows], qb2)), sibling(b3)
-    qa4, qb4 = sibling(a4), sibling(b4)
+    b3, qb2 = onward(b2), sibling(b2)
+    a4, qa3 = onward(after(a3[:rows], b2, sx, qa1)), sibling(a3)
+    b4, qb3 = onward(after(b3[:rows], qb1)), sibling(b3)
+    qa4 = sibling(a4)
     ones = [a0, a1, a2, a3, a4, qa1, qa2, qa3, qa4]
-    twos = [b0, b1, b2, b3, b4, qb1, qb2, qb3, qb4]
     n = len(ones)
 
     pre, act, act_t = kernel(
@@ -398,10 +397,12 @@
             shape((channels, depth * area), BF),
         ),
         [weights],
-        after(sx, b4),
+        after(sx, b3),
         near,
         *ones,
     )
+    qb4 = sibling(after(b4, act_t))
+    twos = [b0, b1, b2, b3, b4, qb1, qb2, qb3, qb4]
     keep_two, send_two = kernel(
         grad_two_kernel, "grad_two", 8, 1, shards, [weights], sc, act_t
     )
@@ -447,15 +448,15 @@
         shape(features.shape, BF),
         [weights, weights, scratch((depth + 2, ny + 2, nz, 3 * channels), BF)],
         sx,
-        after(act, two),
+        after(act, two, one),
         near,
         *ones,
         *twos,
     )
     two = onward(step(keep_two, got_two, two, 1))
     one = onward(step(keep_one, got_one, one, 1))
-    two = onward(step(keep_two, got_two, after(two, features_out), 2))
-    one = onward(step(keep_one, got_one, one, 2))
+    two = onward(step(keep_two, got_two, two, 2))
+    one = onward(step(keep_one, got_one, after(one, features_out), 2))
     grad_two = finish(keep_two, got_two, step(keep_two, got_two, two, 3))
     return (features_out, finish(keep_one, got_one, step(keep_one, got_one, one, 3)), grad_two)
 

time: 94.4 us -> 93.9 us (level)
  starting transfers between devices: 24.3 us -> 17 us
  waiting for transfers between devices: 49.8 us -> 54.7 us
  local copies, waits for them, and re-layouts: 1.24 us -> 3.13 us
    ppermute x2, waiting for transfers between devices: 0.01 us -> 4.58 us  [on_ring(): a2, qa1 = (onward(a1), sibling(a1))]
    ppermute x14, starting transfers between devices: 10 us -> 5.51 us  [the longest x1 1.74 us: on_ring(): one = onward(step(keep_one, got_one, after(one, features_out), 2))]
    ppermute x1, waiting for transfers between devices: 0.01 us -> 4.37 us  [on_ring(): two = onward(step(keep_two, got_two, two, 1))]
    ppermute x1, waiting for transfers between devices: 3.19 us -> 0.01 us  [on_ring(): high = down(jnp.concatenate([features_late[:2], cot_late[:1]]))]
    ppermute x14, waiting for transfers between devices: 19.5 us -> 22.1 us  [the longest x1 3.95 us: on_ring(): one = onward(step(keep_one, got_one, after(one, features_out), 2))]
    ppermute x2, starting transfers between devices: 2.98 us -> 0.66 us  [on_ring(): a2, qa1 = (onward(a1), sibling(a1))]
    ppermute x1, waiting for transfers between devices: 2.29 us -> 0.01 us  [on_ring(): one = onward(step(keep_one, got_one, one, 1))]
    ppermute x1, starting transfers between devices: 0.01 us -> 1.9 us  [on_ring(): high = down(jnp.concatenate([features_late[:2], cot_late[:1]]))]
  transfers between devices with their start and end apart: 34 -> 34, of which waited for: 20 -> 21; matrix products, arithmetic and copies ran while one was open for 3% -> 5% of each run, Pallas kernels for 16% -> 16%
where the time goes in v10:
time: 93.9 us; the launch traced here: 93.4 us
  waiting for transfers between devices  54.7 us (58%)
  starting transfers between devices  17 us (18%)
  Pallas kernels  14.8 us (16%)
  local copies, waits for them, and re-layouts  3.13 us (3%)
  other arithmetic  2.87 us (3%)
    pallas_call x6, Pallas kernels, kernel(): pl.pallas_call(body, name=name, out_shape=outs, in_specs=[pl.BlockSpec(me...  14.8 us
    ppermute x1, waiting for transfers between devices, on_ring(): low = up(jnp.concatenate([features_late[-2:], cot_late[-1:]]))  4.81 us
    ppermute x2, waiting for transfers between devices, on_ring(): a2, qa1 = (onward(a1), sibling(a1))  4.58 us
    ppermute x1, waiting for transfers between devices, on_ring(): two = onward(step(keep_two, got_two, two, 1))  4.37 us
    ppermute x1, waiting for transfers between devices, on_ring(): one = onward(step(keep_one, got_one, after(one, features_out), 2))  3.95 us
    ppermute x2, waiting for transfers between devices, on_ring(): b2, qb1 = (onward(after(b1, low, high)), sibling(b1))  3.86 us
    ppermute x2, waiting for transfers between devices, on_ring(): b3, qb2 = (onward(b2), sibling(b2))  3.78 us
    ppermute x2, waiting for transfers between devices, finish(): total = both(keep, got, 7, 8) + onward(message[:rows]).astype(F32)  3.62 us
  transfers between devices with their start and end apart: 34, of which 21 were waited for; matrix products, arithmetic and copies ran while one was open for 5% of the time, Pallas kernels for 16%

profile of v10, /device:TPU:0, one launch (start us, length us, event | category | flops | bytes accessed | tf_op | source)
XLA Modules:
  0.0 93.4 jit_solution(1760039575700256334)
XLA Ops:
  0.6 0.5 collective-permute-start
  1.1 2.6 %collective-permute-start.9 = (bf16[432,256]{1,0:T(8,128)(2,1)}, bf16[432,256]{1,0:T(8,128)(2,1)S(1)}, u32[]{:S(2)}, u32[]{:S(2)}) collective-permute-start(bf16[432,256]{1,0:T(8,128)(2,1)} %param.6), channel_id=1, source_target_pairs={{1,4},{5,8},{9,12},{13,14},{15,10},{11,6},{7,2},{3,0},{0,3},{4,1},... | collective-permute-start | bytes 663560 | tf_op jit(solution)/shard_map/ppermute | solution.py:358
  3.9 1.3 %collective-permute-start.4 = (bf16[432,256]{1,0:T(8,128)(2,1)}, bf16[432,256]{1,0:T(8,128)(2,1)S(1)}, u32[]{:S(2)}, u32[]{:S(2)}) collective-permute-start(bf16[432,256]{1,0:T(8,128)(2,1)} %param.7), channel_id=1, source_target_pairs={{1,4},{5,8},{9,12},{13,14},{15,10},{11,6},{7,2},{3,0},{0,3},{4,1},... | collective-permute-start | bytes 663560 | tf_op jit(solution)/shard_map/ppermute | solution.py:359
  5.2 0.7 collective-permute-start.3
  5.9 1.0 %constant_dynamic-update-slice_fusion.1 = bf16[864,256]{1,0:T(8,128)(2,1)S(1)} fusion(bf16[432,256]{1,0:T(8,128)(2,1)} %param.7), kind=kLoop, calls=%fused_computation.13 | loop fusion | bytes 442368
  7.0 0.9 fusion.3
  7.9 1.0 %fusion.2 = (bf16[2,8,16,256]{3,2,1,0:T(8,128)(2,1)S(1)}, bf16[2,8,16,256]{3,2,1,0:T(8,128)(2,1)S(1)}) fusion(bf16[4,8,16,256]{3,2,1,0:T(8,128)(2,1)} %f_own.1), kind=kLoop, calls=%fused_computation.22 | loop fusion | bytes 524288 | tf_op jit(solution)/shard_map/slice | solution.py:356
  8.9 0.2 collective-permute-start.1
  9.1 3.2 %collective-permute-done.8 = bf16[432,256]{1,0:T(8,128)(2,1)S(1)} collective-permute-done((bf16[432,256]{1,0:T(8,128)(2,1)}, bf16[432,256]{1,0:T(8,128)(2,1)S(1)}, u32[]{:S(2)}, u32[]{:S(2)}) %collective-permute-start.8) | collective-permute-done | bytes 221216 | tf_op jit(solution)/shard_map/ppermute | solution.py:358
  12.3 1.9 %collective-permute-start.2 = (bf16[3,8,16,256]{3,2,1,0:T(8,128)(2,1)S(1)}, bf16[3,8,16,256]{3,2,1,0:T(8,128)(2,1)S(1)}, u32[]{:S(2)}, u32[]{:S(2)}) collective-permute-start(bf16[3,8,16,256]{3,2,1,0:T(8,128)(2,1)S(1)} %pad_maximum_fusion.1), channel_id=1, source_target_pairs={{0,15},{1,0},{2,1},{3,2},{4,3},{5,4},{6,5},{7,6},{8,7},{9,8},{10,9... | collective-permute-start | bytes 589832 | tf_op jit(solution)/shard_map/ppermute | solution.py:356
  14.4 0.3 collective-permute-done.3
  14.7 0.3 collective-permute-done.4
  15.0 4.8 %collective-permute-done.1.low = bf16[3,8,16,256]{3,2,1,0:T(8,128)(2,1)S(1)} collective-permute-done((bf16[3,8,16,256]{3,2,1,0:T(8,128)(2,1)S(1)}, bf16[3,8,16,256]{3,2,1,0:T(8,128)(2,1)S(1)}, u32[]{:S(2)}, u32[]{:S(2)}) %collective-permute-start.1) | collective-permute-done | bytes 196640 | tf_op jit(solution)/shard_map/ppermute | solution.py:355
  19.8 4.6 %collective-permute-done.10.rest_2_ = bf16[864,256]{1,0:T(8,128)(2,1)S(1)} collective-permute-done((bf16[864,256]{1,0:T(8,128)(2,1)S(1)}, bf16[864,256]{1,0:T(8,128)(2,1)S(1)}, u32[]{:S(2)}, u32[]{:S(2)}) %collective-permute-start.10) | collective-permute-done | bytes 442400 | tf_op jit(solution)/shard_map/ppermute | solution.py:360
  24.4 0.3 collective-permute-start.11
  24.7 0.6 collective-permute-start.12
  25.3 3.9 %collective-permute-done.5.rest_2_.rest_11_ = bf16[864,256]{1,0:T(8,128)(2,1)S(1)} collective-permute-done((bf16[864,256]{1,0:T(8,128)(2,1)S(1)}, bf16[864,256]{1,0:T(8,128)(2,1)S(1)}, u32[]{:S(2)}, u32[]{:S(2)}) %collective-permute-start.5) | collective-permute-done | bytes 442400 | tf_op jit(solution)/shard_map/ppermute | solution.py:361
  29.2 0.3 collective-permute-start.6
  29.4 0.6 collective-permute-start.18
  30.1 1.3 %prep.1 = (bf16[8,10,16,768]{3,2,1,0:T(8,128)(2,1)S(1)}, bf16[6,10,16,768]{3,2,1,0:T(8,128)(2,1)S(1)}, bf16[256,768]{1,0:T(8,128)(2,1)S(1)}, bf16[3,128,256]{2,1,0:T(8,128)(2,1)S(1)}) custom-call(s32[2,4,16]{2,1,0:T(4,128)S(1)} %bitcast.1, bf16[3,8,16,256]{3,2,1,0:T(8,128)(2,1)S(1)} %collective-permute-done.1.low, bf16[4,8,16,256]{3,2,1,0:T(8,128)(2,1)S(1)} %copy-done, ...), custom_call_target="tpu_custom_call" | custom-call | bytes 4194304 | tf_op jit(solution)/shard_map/prep/pallas_call | solution.py:338
  31.4 2.5 %collective-permute-done.11.rest_3_ = bf16[864,256]{1,0:T(8,128)(2,1)S(1)} collective-permute-done((bf16[864,256]{1,0:T(8,128)(2,1)S(1)}, bf16[864,256]{1,0:T(8,128)(2,1)S(1)}, u32[]{:S(2)}, u32[]{:S(2)}) %collective-permute-start.11) | collective-permute-done | bytes 442400 | tf_op jit(solution)/shard_map/ppermute | solution.py:362
  33.9 0.3 collective-permute-start.13
  34.3 0.6 collective-permute-start.15
  34.9 3.8 %collective-permute-done.6.rest_3_.rest_12_ = bf16[864,256]{1,0:T(8,128)(2,1)S(1)} collective-permute-done((bf16[864,256]{1,0:T(8,128)(2,1)S(1)}, bf16[864,256]{1,0:T(8,128)(2,1)S(1)}, u32[]{:S(2)}, u32[]{:S(2)}) %collective-permute-start.6) | collective-permute-done | bytes 442400 | tf_op jit(solution)/shard_map/ppermute | solution.py:382
  38.6 2.4 %collective-permute-done.13.rest_4_ = bf16[432,256]{1,0:T(8,128)(2,1)S(1)} collective-permute-done((bf16[432,256]{1,0:T(8,128)(2,1)S(1)}, bf16[432,256]{1,0:T(8,128)(2,1)S(1)}, u32[]{:S(2)}, u32[]{:S(2)}) %collective-permute-start.13) | collective-permute-done | bytes 221216 | tf_op jit(solution)/shard_map/ppermute | solution.py:383
  41.1 0.6 collective-permute-start.20
  41.6 0.3 collective-permute-start.19
  41.9 0.3 collective-permute-start.21
  42.3 0.2 collective-permute-done.16.rest_8_
  42.5 2.3 %first.1 = (f32[512,256]{1,0:T(8,128)S(1)}, bf16[512,256]{1,0:T(8,128)(2,1)S(1)}, bf16[256,512]{1,0:T(8,128)(2,1)S(1)}) custom-call(bf16[8,10,16,768]{3,2,1,0:T(8,128)(2,1)S(1)} %get-tuple-element.29.sx_ref, bf16[3,128,256]{2,1,0:T(8,128)(2,1)S(1)} %get-tuple-element.30.mask_ref, bf16[864,256]{1,0:T(8,128)(2,1)S(1)} %constant_dynamic-update-slice_fusion.4.rest_0_, ...), custom_call_target="tpu_custom_call" | custom-call | flops 1811939328 | bytes 4194304 | tf_op jit(solution)/shard_map/first/pallas_call | solution.py:338
  44.8 2.8 %collective-permute-done.19.rest_4_.rest_13_ = bf16[432,256]{1,0:T(8,128)(2,1)S(1)} collective-permute-done((bf16[432,256]{1,0:T(8,128)(2,1)S(1)}, bf16[432,256]{1,0:T(8,128)(2,1)S(1)}, u32[]{:S(2)}, u32[]{:S(2)}) %collective-permute-start.19) | collective-permute-done | bytes 221216 | tf_op jit(solution)/shard_map/ppermute | solution.py:384
  47.6 2.2 %grad_two.1 = (bf16[3456,256]{1,0:T(8,128)(2,1)S(1)}, bf16[3456,256]{1,0:T(8,128)(2,1)S(1)}) custom-call(bf16[6,10,16,768]{3,2,1,0:T(8,128)(2,1)S(1)} %get-tuple-element.34.sc_ref, bf16[256,512]{1,0:T(8,128)(2,1)S(1)} %get-tuple-element.35.act_t_ref), custom_call_target="tpu_custom_call" | custom-call | flops 1811939328 | bytes 4194304 | tf_op jit(solution)/shard_map/grad_two/pallas_call | solution.py:338
  49.8 0.6 collective-permute-start.17
  50.4 2.4 %back.1.sd_ref = bf16[4,10,16,768]{3,2,1,0:T(8,128)(2,1)S(1)} custom-call(bf16[6,10,16,768]{3,2,1,0:T(8,128)(2,1)S(1)} %get-tuple-element.34.sc_ref, f32[512,256]{1,0:T(8,128)S(1)} %get-tuple-element.38.pre_ref, bf16[3,128,256]{2,1,0:T(8,128)(2,1)S(1)} %get-tuple-element.30.mask_ref, bf16[864,256]{1,0:T(8,128)(2,1)S(1)} %constant_dynamic-update-slice_fusion.rest_0_.rest_9_, ...), custom_call_target="tpu_custom_call" | custom-call | flops 1811939328 | bytes 4194304 | tf_op jit(solution)/shard_map/back/pallas_call | solution.py:338
  52.8 2.3 %grad_one.1 = (bf16[3456,256]{1,0:T(8,128)(2,1)S(1)}, bf16[3456,256]{1,0:T(8,128)(2,1)S(1)}) custom-call(bf16[4,10,16,768]{3,2,1,0:T(8,128)(2,1)S(1)} %back.1.sd_ref, bf16[256,768]{1,0:T(8,128)(2,1)S(1)} %get-tuple-element.41.int_ref), custom_call_target="tpu_custom_call" | custom-call | flops 1811939328 | bytes 4194304 | tf_op jit(solution)/shard_map/grad_one/pallas_call | solution.py:338
  55.1 0.1 collective-permute-start.24
  55.3 0.3 collective-permute-start.23
  55.6 3.3 %collective-permute-done.24 = bf16[3456,256]{1,0:T(8,128)(2,1)S(1)} collective-permute-done((bf16[3456,256]{1,0:T(8,128)(2,1)S(1)}, bf16[3456,256]{1,0:T(8,128)(2,1)S(1)}, u32[]{:S(2)}, u32[]{:S(2)}) %collective-permute-start.24) | collective-permute-done | bytes 1769504 | tf_op jit(solution)/shard_map/ppermute | solution.py:441
  58.9 0.3 collective-permute-start.25
  59.2 2.0 %collective-permute-done.23 = bf16[432,256]{1,0:T(8,128)(2,1)S(1)} collective-permute-done((bf16[432,256]{1,0:T(8,128)(2,1)S(1)}, bf16[432,256]{1,0:T(8,128)(2,1)S(1)}, u32[]{:S(2)}, u32[]{:S(2)}) %collective-permute-start.23) | collective-permute-done | bytes 221216 | tf_op jit(solution)/shard_map/ppermute | solution.py:440
  61.2 0.1 add_convert_fusion.2
  61.4 0.3 collective-permute-start.30
  61.7 3.2 %collective-permute-done.25 = bf16[432,256]{1,0:T(8,128)(2,1)S(1)} collective-permute-done((bf16[432,256]{1,0:T(8,128)(2,1)S(1)}, bf16[432,256]{1,0:T(8,128)(2,1)S(1)}, u32[]{:S(2)}, u32[]{:S(2)}) %collective-permute-start.25) | collective-permute-done | bytes 221216 | tf_op jit(solution)/shard_map/ppermute | solution.py:442
  64.9 0.1 add_convert_fusion.5
  65.0 0.3 collective-permute-start.26
  65.4 4.4 %collective-permute-done.30 = bf16[864,256]{1,0:T(8,128)(2,1)S(1)} collective-permute-done((bf16[864,256]{1,0:T(8,128)(2,1)S(1)}, bf16[864,256]{1,0:T(8,128)(2,1)S(1)}, u32[]{:S(2)}, u32[]{:S(2)}) %collective-permute-start.30) | collective-permute-done | bytes 442400 | tf_op jit(solution)/shard_map/ppermute | solution.py:456
  69.7 0.2 add_convert_fusion.1
  69.9 0.5 collective-permute-start.31
  70.4 4.2 %third.1 = bf16[4,8,16,256]{3,2,1,0:T(8,128)(2,1)} custom-call(bf16[8,10,16,768]{3,2,1,0:T(8,128)(2,1)S(1)} %get-tuple-element.29.sx_ref, bf16[512,256]{1,0:T(8,128)(2,1)S(1)} %get-tuple-element.45.act_ref, bf16[3,128,256]{2,1,0:T(8,128)(2,1)S(1)} %get-tuple-element.30.mask_ref, bf16[864,256]{1,0:T(8,128)(2,1)S(1)} %constant_dynamic-update-slice_fusion.4.rest_0_, ...), custom_call_target="tpu_custom_call" | custom-call | flops 1811939328 | bytes 4194304 | tf_op jit(solution)/shard_map/third/pallas_call | solution.py:338
  74.6 0.2 add_convert_fusion.4
  74.8 1.7 %collective-permute-start.27 = (bf16[864,256]{1,0:T(8,128)(2,1)S(1)}, bf16[864,256]{1,0:T(8,128)(2,1)S(1)}, u32[]{:S(2)}, u32[]{:S(2)}) collective-permute-start(bf16[864,256]{1,0:T(8,128)(2,1)S(1)} %add_convert_fusion.4), channel_id=1, source_target_pairs={{0,4},{4,8},{8,12},{12,14},{14,10},{10,6},{6,2},{2,0},{1,3},{5,1},... | collective-permute-start | bytes 1327112 | tf_op jit(solution)/shard_map/ppermute | solution.py:459
  76.6 2.7 %collective-permute-done.31 = bf16[864,256]{1,0:T(8,128)(2,1)S(1)} collective-permute-done((bf16[864,256]{1,0:T(8,128)(2,1)S(1)}, bf16[864,256]{1,0:T(8,128)(2,1)S(1)}, u32[]{:S(2)}, u32[]{:S(2)}) %collective-permute-start.31) | collective-permute-done | bytes 442400 | tf_op jit(solution)/shard_map/ppermute | solution.py:458
  79.2 0.2 add_convert_fusion
  79.4 0.3 collective-permute-start.32
  79.8 0.2 collective-permute-start.33
  80.0 4.0 %collective-permute-done.27 = bf16[864,256]{1,0:T(8,128)(2,1)S(1)} collective-permute-done((bf16[864,256]{1,0:T(8,128)(2,1)S(1)}, bf16[864,256]{1,0:T(8,128)(2,1)S(1)}, u32[]{:S(2)}, u32[]{:S(2)}) %collective-permute-start.27) | collective-permute-done | bytes 442400 | tf_op jit(solution)/shard_map/ppermute | solution.py:459
  84.0 0.2 add_convert_fusion.3
  84.2 1.0 %collective-permute-start.28 = (bf16[432,256]{1,0:T(8,128)(2,1)S(1)}, bf16[432,256]{1,0:T(8,128)(2,1)S(1)}, u32[]{:S(2)}, u32[]{:S(2)}) collective-permute-start(bf16[432,256]{1,0:T(8,128)(2,1)S(1)} %get-tuple-element.49), channel_id=1, source_target_pairs={{0,4},{4,8},{8,12},{12,14},{14,10},{10,6},{6,2},{2,0},{1,3},{5,1},... | collective-permute-start | bytes 663560 | tf_op jit(solution)/shard_map/ppermute | solution.py:422
  85.1 1.2 %collective-permute-done.32 = bf16[432,256]{1,0:T(8,128)(2,1)S(1)} collective-permute-done((bf16[432,256]{1,0:T(8,128)(2,1)S(1)}, bf16[432,256]{1,0:T(8,128)(2,1)S(1)}, u32[]{:S(2)}, u32[]{:S(2)}) %collective-permute-start.32) | collective-permute-done | bytes 221216 | tf_op jit(solution)/shard_map/ppermute | solution.py:422
  86.3 1.4 %collective-permute-done.33 = bf16[432,256]{1,0:T(8,128)(2,1)S(1)} collective-permute-done((bf16[432,256]{1,0:T(8,128)(2,1)S(1)}, bf16[432,256]{1,0:T(8,128)(2,1)S(1)}, u32[]{:S(2)}, u32[]{:S(2)}) %collective-permute-start.33) | collective-permute-done | bytes 221216 | tf_op jit(solution)/shard_map/ppermute | solution.py:423
  87.8 0.9 add_multiply_fusion
  88.6 2.4 %collective-permute-done.28 = bf16[432,256]{1,0:T(8,128)(2,1)S(1)} collective-permute-done((bf16[432,256]{1,0:T(8,128)(2,1)S(1)}, bf16[432,256]{1,0:T(8,128)(2,1)S(1)}, u32[]{:S(2)}, u32[]{:S(2)}) %collective-permute-start.28) | collective-permute-done | bytes 221216 | tf_op jit(solution)/shard_map/ppermute | solution.py:422
  91.1 1.4 %collective-permute-done.29 = bf16[432,256]{1,0:T(8,128)(2,1)S(1)} collective-permute-done((bf16[432,256]{1,0:T(8,128)(2,1)S(1)}, bf16[432,256]{1,0:T(8,128)(2,1)S(1)}, u32[]{:S(2)}, u32[]{:S(2)}) %collective-permute-start.29) | collective-permute-done | bytes 221216 | tf_op jit(solution)/shard_map/ppermute | solution.py:423
  92.5 0.9 add_multiply_fusion.1
  (44 shorter events, 0.6 us)
Async XLA Ops:
  0.6 6.3 %collective-permute-start = (bf16[432,256]{1,0:T(8,128)(2,1)}, bf16[432,256]{1,0:T(8,128)(2,1)S(1)}, u32[]{:S(2)}, u32[]{:S(2)}) collective-permute-start(bf16[432,256]{1,0:T(8,128)(2,1)} %param.7), channel_id=1, source_target_pairs={{0,1},{1,0},{2,3},{3,2},{4,5},{5,4},{6,7},{7,6},{8,9},{9,8},{10,11... | collective-permute-start | bytes 663560 | tf_op jit(solution)/shard_map/ppermute | solution.py:353
  1.1 13.1 %collective-permute-start.9 = (bf16[432,256]{1,0:T(8,128)(2,1)}, bf16[432,256]{1,0:T(8,128)(2,1)S(1)}, u32[]{:S(2)}, u32[]{:S(2)}) collective-permute-start(bf16[432,256]{1,0:T(8,128)(2,1)} %param.6), channel_id=1, source_target_pairs={{1,4},{5,8},{9,12},{13,14},{15,10},{11,6},{7,2},{3,0},{0,3},{4,1},... | collective-permute-start | bytes 663560 | tf_op jit(solution)/shard_map/ppermute | solution.py:358
  3.8 8.6 %collective-permute-start.8 = (bf16[432,256]{1,0:T(8,128)(2,1)}, bf16[432,256]{1,0:T(8,128)(2,1)S(1)}, u32[]{:S(2)}, u32[]{:S(2)}) collective-permute-start(bf16[432,256]{1,0:T(8,128)(2,1)} %param.6), channel_id=1, source_target_pairs={{0,4},{4,8},{8,12},{12,14},{14,10},{10,6},{6,2},{2,0},{1,3},{5,1},... | collective-permute-start | bytes 663560 | tf_op jit(solution)/shard_map/ppermute | solution.py:358
  3.9 11.1 %collective-permute-start.4 = (bf16[432,256]{1,0:T(8,128)(2,1)}, bf16[432,256]{1,0:T(8,128)(2,1)S(1)}, u32[]{:S(2)}, u32[]{:S(2)}) collective-permute-start(bf16[432,256]{1,0:T(8,128)(2,1)} %param.7), channel_id=1, source_target_pairs={{1,4},{5,8},{9,12},{13,14},{15,10},{11,6},{7,2},{3,0},{0,3},{4,1},... | collective-permute-start | bytes 663560 | tf_op jit(solution)/shard_map/ppermute | solution.py:359
  5.2 9.5 %collective-permute-start.3 = (bf16[432,256]{1,0:T(8,128)(2,1)}, bf16[432,256]{1,0:T(8,128)(2,1)S(1)}, u32[]{:S(2)}, u32[]{:S(2)}) collective-permute-start(bf16[432,256]{1,0:T(8,128)(2,1)} %param.7), channel_id=1, source_target_pairs={{0,4},{4,8},{8,12},{12,14},{14,10},{10,6},{6,2},{2,0},{1,3},{5,1},... | collective-permute-start | bytes 663560 | tf_op jit(solution)/shard_map/ppermute | solution.py:359
  6.9 23.1 %copy-start = (bf16[4,8,16,256]{3,2,1,0:T(8,128)(2,1)S(1)}, bf16[4,8,16,256]{3,2,1,0:T(8,128)(2,1)}, u32[]{:S(2)}) copy-start(bf16[4,8,16,256]{3,2,1,0:T(8,128)(2,1)} %f_own.1) | copy-start | bytes 786436
  6.9 23.1 %copy-start.1 = (bf16[4,8,16,256]{3,2,1,0:T(8,128)(2,1)S(1)}, bf16[4,8,16,256]{3,2,1,0:T(8,128)(2,1)}, u32[]{:S(2)}) copy-start(bf16[4,8,16,256]{3,2,1,0:T(8,128)(2,1)} %c_own.1) | copy-start | bytes 786436
  6.9 23.1 %copy-start.2 = (s32[16,2,4]{0,2,1:T(4,128)S(1)}, s32[16,2,4]{0,2,1:T(4,128)}, u32[]{:S(2)}) copy-start(s32[16,2,4]{0,2,1:T(4,128)} %param.9) | copy-start | bytes 1540
  8.9 29.7 %copy-start.3 = (bf16[432,256]{1,0:T(8,128)(2,1)S(1)}, bf16[432,256]{1,0:T(8,128)(2,1)}, u32[]{:S(2)}) copy-start(bf16[432,256]{1,0:T(8,128)(2,1)} %param.6) | copy-start | bytes 663556
  8.9 10.9 %collective-permute-start.1 = (bf16[3,8,16,256]{3,2,1,0:T(8,128)(2,1)S(1)}, bf16[3,8,16,256]{3,2,1,0:T(8,128)(2,1)S(1)}, u32[]{:S(2)}, u32[]{:S(2)}) collective-permute-start(bf16[3,8,16,256]{3,2,1,0:T(8,128)(2,1)S(1)} %pad_maximum_fusion), channel_id=1, source_target_pairs={{0,1},{1,2},{2,3},{3,4},{4,5},{5,6},{6,7},{7,8},{8,9},{9,10},{10,1... | collective-permute-start | bytes 589832 | tf_op jit(solution)/shard_map/ppermute | solution.py:355
  12.3 7.5 %collective-permute-start.2 = (bf16[3,8,16,256]{3,2,1,0:T(8,128)(2,1)S(1)}, bf16[3,8,16,256]{3,2,1,0:T(8,128)(2,1)S(1)}, u32[]{:S(2)}, u32[]{:S(2)}) collective-permute-start(bf16[3,8,16,256]{3,2,1,0:T(8,128)(2,1)S(1)} %pad_maximum_fusion.1), channel_id=1, source_target_pairs={{0,15},{1,0},{2,1},{3,2},{4,3},{5,4},{6,5},{7,6},{8,7},{9,8},{10,9... | collective-permute-start | bytes 589832 | tf_op jit(solution)/shard_map/ppermute | solution.py:356
  14.3 10.1 %collective-permute-start.10 = (bf16[864,256]{1,0:T(8,128)(2,1)S(1)}, bf16[864,256]{1,0:T(8,128)(2,1)S(1)}, u32[]{:S(2)}, u32[]{:S(2)}) collective-permute-start(bf16[864,256]{1,0:T(8,128)(2,1)S(1)} %constant_dynamic-update-slice_fusion.6.rest_1_), channel_id=1, source_target_pairs={{0,4},{4,8},{8,12},{12,14},{14,10},{10,6},{6,2},{2,0},{1,3},{5,1},... | collective-permute-start | bytes 1327112 | tf_op jit(solution)/shard_map/ppermute | solution.py:360
  19.8 9.3 %collective-permute-start.5 = (bf16[864,256]{1,0:T(8,128)(2,1)S(1)}, bf16[864,256]{1,0:T(8,128)(2,1)S(1)}, u32[]{:S(2)}, u32[]{:S(2)}) collective-permute-start(bf16[864,256]{1,0:T(8,128)(2,1)S(1)} %constant_dynamic-update-slice_fusion.2.rest_1_.rest_10_), channel_id=1, source_target_pairs={{0,4},{4,8},{8,12},{12,14},{14,10},{10,6},{6,2},{2,0},{1,3},{5,1},... | collective-permute-start | bytes 1327112 | tf_op jit(solution)/shard_map/ppermute | solution.py:361
  24.4 9.5 %collective-permute-start.11 = (bf16[864,256]{1,0:T(8,128)(2,1)S(1)}, bf16[864,256]{1,0:T(8,128)(2,1)S(1)}, u32[]{:S(2)}, u32[]{:S(2)}) collective-permute-start(bf16[864,256]{1,0:T(8,128)(2,1)S(1)} %collective-permute-done.10.rest_2_), channel_id=1, source_target_pairs={{0,4},{4,8},{8,12},{12,14},{14,10},{10,6},{6,2},{2,0},{1,3},{5,1},... | collective-permute-start | bytes 1327112 | tf_op jit(solution)/shard_map/ppermute | solution.py:362
  24.7 9.2 %collective-permute-start.12 = (bf16[864,256]{1,0:T(8,128)(2,1)S(1)}, bf16[864,256]{1,0:T(8,128)(2,1)S(1)}, u32[]{:S(2)}, u32[]{:S(2)}) collective-permute-start(bf16[864,256]{1,0:T(8,128)(2,1)S(1)} %constant_dynamic-update-slice_fusion.6.rest_1_), channel_id=1, source_target_pairs={{0,1},{1,0},{2,3},{3,2},{4,5},{5,4},{6,7},{7,6},{8,9},{9,8},{10,11... | collective-permute-start | bytes 1327112 | tf_op jit(solution)/shard_map/ppermute | solution.py:360
  29.2 9.5 %collective-permute-start.6 = (bf16[864,256]{1,0:T(8,128)(2,1)S(1)}, bf16[864,256]{1,0:T(8,128)(2,1)S(1)}, u32[]{:S(2)}, u32[]{:S(2)}) collective-permute-start(bf16[864,256]{1,0:T(8,128)(2,1)S(1)} %collective-permute-done.5.rest_2_.rest_11_), channel_id=1, source_target_pairs={{0,4},{4,8},{8,12},{12,14},{14,10},{10,6},{6,2},{2,0},{1,3},{5,1},... | collective-permute-start | bytes 1327112 | tf_op jit(solution)/shard_map/ppermute | solution.py:382
  29.4 11.6 %collective-permute-start.18 = (bf16[864,256]{1,0:T(8,128)(2,1)S(1)}, bf16[864,256]{1,0:T(8,128)(2,1)S(1)}, u32[]{:S(2)}, u32[]{:S(2)}) collective-permute-start(bf16[864,256]{1,0:T(8,128)(2,1)S(1)} %constant_dynamic-update-slice_fusion.2.rest_1_.rest_10_), channel_id=1, source_target_pairs={{0,1},{1,0},{2,3},{3,2},{4,5},{5,4},{6,7},{7,6},{8,9},{9,8},{10,11... | collective-permute-start | bytes 1327112 | tf_op jit(solution)/shard_map/ppermute | solution.py:361
  30.0 11.9 %collective-permute-start.14 = (bf16[864,256]{1,0:T(8,128)(2,1)S(1)}, bf16[864,256]{1,0:T(8,128)(2,1)S(1)}, u32[]{:S(2)}, u32[]{:S(2)}) collective-permute-start(bf16[864,256]{1,0:T(8,128)(2,1)S(1)} %collective-permute-done.10.rest_2_), channel_id=1, source_target_pairs={{0,1},{1,0},{2,3},{3,2},{4,5},{5,4},{6,7},{7,6},{8,9},{9,8},{10,11... | collective-permute-start | bytes 1327112 | tf_op jit(solution)/shard_map/ppermute | solution.py:362
  33.9 7.1 %collective-permute-start.13 = (bf16[432,256]{1,0:T(8,128)(2,1)S(1)}, bf16[432,256]{1,0:T(8,128)(2,1)S(1)}, u32[]{:S(2)}, u32[]{:S(2)}) collective-permute-start(bf16[432,256]{1,0:T(8,128)(2,1)S(1)} %slice.120), channel_id=1, source_target_pairs={{0,4},{4,8},{8,12},{12,14},{14,10},{10,6},{6,2},{2,0},{1,3},{5,1},... | collective-permute-start | bytes 663560 | tf_op jit(solution)/shard_map/ppermute | solution.py:383
  34.3 8.0 %collective-permute-start.15 = (bf16[864,256]{1,0:T(8,128)(2,1)S(1)}, bf16[864,256]{1,0:T(8,128)(2,1)S(1)}, u32[]{:S(2)}, u32[]{:S(2)}) collective-permute-start(bf16[864,256]{1,0:T(8,128)(2,1)S(1)} %collective-permute-done.11.rest_3_), channel_id=1, source_target_pairs={{0,1},{1,0},{2,3},{3,2},{4,5},{5,4},{6,7},{7,6},{8,9},{9,8},{10,11... | collective-permute-start | bytes 1327112 | tf_op jit(solution)/shard_map/ppermute | solution.py:383
  38.6 3.0 %collective-permute-start.7 = (bf16[432,256]{1,0:T(8,128)(2,1)S(1)}, bf16[432,256]{1,0:T(8,128)(2,1)S(1)}, u32[]{:S(2)}, u32[]{:S(2)}) collective-permute-start(bf16[432,256]{1,0:T(8,128)(2,1)S(1)} %copy-done.3), channel_id=1, source_target_pairs={{0,1},{1,0},{2,3},{3,2},{4,5},{5,4},{6,7},{7,6},{8,9},{9,8},{10,11... | collective-permute-start | bytes 663560 | tf_op jit(solution)/shard_map/ppermute | solution.py:352
  41.0 1.5 %collective-permute-start.16 = (bf16[432,256]{1,0:T(8,128)(2,1)S(1)}, bf16[432,256]{1,0:T(8,128)(2,1)S(1)}, u32[]{:S(2)}, u32[]{:S(2)}) collective-permute-start(bf16[432,256]{1,0:T(8,128)(2,1)S(1)} %collective-permute-done.13.rest_4_), channel_id=1, source_target_pairs={{0,1},{1,0},{2,3},{3,2},{4,5},{5,4},{6,7},{7,6},{8,9},{9,8},{10,11... | collective-permute-start | bytes 663560 | tf_op jit(solution)/shard_map/ppermute | solution.py:385
  41.1 9.3 %collective-permute-start.20 = (bf16[864,256]{1,0:T(8,128)(2,1)S(1)}, bf16[864,256]{1,0:T(8,128)(2,1)S(1)}, u32[]{:S(2)}, u32[]{:S(2)}) collective-permute-start(bf16[864,256]{1,0:T(8,128)(2,1)S(1)} %collective-permute-done.5.rest_2_.rest_11_), channel_id=1, source_target_pairs={{0,1},{1,0},{2,3},{3,2},{4,5},{5,4},{6,7},{7,6},{8,9},{9,8},{10,11... | collective-permute-start | bytes 1327112 | tf_op jit(solution)/shard_map/ppermute | solution.py:382
  41.6 5.9 %collective-permute-start.19 = (bf16[432,256]{1,0:T(8,128)(2,1)S(1)}, bf16[432,256]{1,0:T(8,128)(2,1)S(1)}, u32[]{:S(2)}, u32[]{:S(2)}) collective-permute-start(bf16[432,256]{1,0:T(8,128)(2,1)S(1)} %slice.121), channel_id=1, source_target_pairs={{0,4},{4,8},{8,12},{12,14},{14,10},{10,6},{6,2},{2,0},{1,3},{5,1},... | collective-permute-start | bytes 663560 | tf_op jit(solution)/shard_map/ppermute | solution.py:384
  41.9 8.5 %collective-permute-start.21 = (bf16[864,256]{1,0:T(8,128)(2,1)S(1)}, bf16[864,256]{1,0:T(8,128)(2,1)S(1)}, u32[]{:S(2)}, u32[]{:S(2)}) collective-permute-start(bf16[864,256]{1,0:T(8,128)(2,1)S(1)} %collective-permute-done.6.rest_3_.rest_12_), channel_id=1, source_target_pairs={{0,1},{1,0},{2,3},{3,2},{4,5},{5,4},{6,7},{7,6},{8,9},{9,8},{10,11... | collective-permute-start | bytes 1327112 | tf_op jit(solution)/shard_map/ppermute | solution.py:384
  47.6 2.8 %collective-permute-start.22 = (bf16[432,256]{1,0:T(8,128)(2,1)S(1)}, bf16[432,256]{1,0:T(8,128)(2,1)S(1)}, u32[]{:S(2)}, u32[]{:S(2)}) collective-permute-start(bf16[432,256]{1,0:T(8,128)(2,1)S(1)} %collective-permute-done.19.rest_4_.rest_13_), channel_id=1, source_target_pairs={{0,1},{1,0},{2,3},{3,2},{4,5},{5,4},{6,7},{7,6},{8,9},{9,8},{10,11... | collective-permute-start | bytes 663560 | tf_op jit(solution)/shard_map/ppermute | solution.py:404
  49.8 5.4 %collective-permute-start.17 = (bf16[3456,256]{1,0:T(8,128)(2,1)S(1)}, bf16[3456,256]{1,0:T(8,128)(2,1)S(1)}, u32[]{:S(2)}, u32[]{:S(2)}) collective-permute-start(bf16[3456,256]{1,0:T(8,128)(2,1)S(1)} %get-tuple-element.37), channel_id=1, source_target_pairs={{0,1},{1,0},{2,3},{3,2},{4,5},{5,4},{6,7},{7,6},{8,9},{9,8},{10,11... | collective-permute-start | bytes 5308424 | tf_op jit(solution)/shard_map/ppermute | solution.py:409
  55.1 3.8 %collective-permute-start.24 = (bf16[3456,256]{1,0:T(8,128)(2,1)S(1)}, bf16[3456,256]{1,0:T(8,128)(2,1)S(1)}, u32[]{:S(2)}, u32[]{:S(2)}) collective-permute-start(bf16[3456,256]{1,0:T(8,128)(2,1)S(1)} %get-tuple-element.44), channel_id=1, source_target_pairs={{0,1},{1,0},{2,3},{3,2},{4,5},{5,4},{6,7},{7,6},{8,9},{9,8},{10,11... | collective-permute-start | bytes 5308424 | tf_op jit(solution)/shard_map/ppermute | solution.py:441
  55.3 6.0 %collective-permute-start.23 = (bf16[432,256]{1,0:T(8,128)(2,1)S(1)}, bf16[432,256]{1,0:T(8,128)(2,1)S(1)}, u32[]{:S(2)}, u32[]{:S(2)}) collective-permute-start(bf16[432,256]{1,0:T(8,128)(2,1)S(1)} %add_convert_fusion.7), channel_id=1, source_target_pairs={{0,4},{4,8},{8,12},{12,14},{14,10},{10,6},{6,2},{2,0},{1,3},{5,1},... | collective-permute-start | bytes 663560 | tf_op jit(solution)/shard_map/ppermute | solution.py:440
  58.9 6.0 %collective-permute-start.25 = (bf16[432,256]{1,0:T(8,128)(2,1)S(1)}, bf16[432,256]{1,0:T(8,128)(2,1)S(1)}, u32[]{:S(2)}, u32[]{:S(2)}) collective-permute-start(bf16[432,256]{1,0:T(8,128)(2,1)S(1)} %add_convert_fusion.6), channel_id=1, source_target_pairs={{0,4},{4,8},{8,12},{12,14},{14,10},{10,6},{6,2},{2,0},{1,3},{5,1},... | collective-permute-start | bytes 663560 | tf_op jit(solution)/shard_map/ppermute | solution.py:442
  61.4 8.4 %collective-permute-start.30 = (bf16[864,256]{1,0:T(8,128)(2,1)S(1)}, bf16[864,256]{1,0:T(8,128)(2,1)S(1)}, u32[]{:S(2)}, u32[]{:S(2)}) collective-permute-start(bf16[864,256]{1,0:T(8,128)(2,1)S(1)} %add_convert_fusion.2), channel_id=1, source_target_pairs={{0,4},{4,8},{8,12},{12,14},{14,10},{10,6},{6,2},{2,0},{1,3},{5,1},... | collective-permute-start | bytes 1327112 | tf_op jit(solution)/shard_map/ppermute | solution.py:456
  65.0 9.6 %collective-permute-start.26 = (bf16[864,256]{1,0:T(8,128)(2,1)S(1)}, bf16[864,256]{1,0:T(8,128)(2,1)S(1)}, u32[]{:S(2)}, u32[]{:S(2)}) collective-permute-start(bf16[864,256]{1,0:T(8,128)(2,1)S(1)} %add_convert_fusion.5), channel_id=1, source_target_pairs={{0,4},{4,8},{8,12},{12,14},{14,10},{10,6},{6,2},{2,0},{1,3},{5,1},... | collective-permute-start | bytes 1327112 | tf_op jit(solution)/shard_map/ppermute | solution.py:457
  69.9 9.3 %collective-permute-start.31 = (bf16[864,256]{1,0:T(8,128)(2,1)S(1)}, bf16[864,256]{1,0:T(8,128)(2,1)S(1)}, u32[]{:S(2)}, u32[]{:S(2)}) collective-permute-start(bf16[864,256]{1,0:T(8,128)(2,1)S(1)} %add_convert_fusion.1), channel_id=1, source_target_pairs={{0,4},{4,8},{8,12},{12,14},{14,10},{10,6},{6,2},{2,0},{1,3},{5,1},... | collective-permute-start | bytes 1327112 | tf_op jit(solution)/shard_map/ppermute | solution.py:458
  74.8 9.1 %collective-permute-start.27 = (bf16[864,256]{1,0:T(8,128)(2,1)S(1)}, bf16[864,256]{1,0:T(8,128)(2,1)S(1)}, u32[]{:S(2)}, u32[]{:S(2)}) collective-permute-start(bf16[864,256]{1,0:T(8,128)(2,1)S(1)} %add_convert_fusion.4), channel_id=1, source_target_pairs={{0,4},{4,8},{8,12},{12,14},{14,10},{10,6},{6,2},{2,0},{1,3},{5,1},... | collective-permute-start | bytes 1327112 | tf_op jit(solution)/shard_map/ppermute | solution.py:459
  79.4 6.9 %collective-permute-start.32 = (bf16[432,256]{1,0:T(8,128)(2,1)S(1)}, bf16[432,256]{1,0:T(8,128)(2,1)S(1)}, u32[]{:S(2)}, u32[]{:S(2)}) collective-permute-start(bf16[432,256]{1,0:T(8,128)(2,1)S(1)} %get-tuple-element.47), channel_id=1, source_target_pairs={{0,4},{4,8},{8,12},{12,14},{14,10},{10,6},{6,2},{2,0},{1,3},{5,1},... | collective-permute-start | bytes 663560 | tf_op jit(solution)/shard_map/ppermute | solution.py:422
  79.8 8.0 %collective-permute-start.33 = (bf16[432,256]{1,0:T(8,128)(2,1)S(1)}, bf16[432,256]{1,0:T(8,128)(2,1)S(1)}, u32[]{:S(2)}, u32[]{:S(2)}) collective-permute-start(bf16[432,256]{1,0:T(8,128)(2,1)S(1)} %get-tuple-element.48), channel_id=1, source_target_pairs={{0,5},{4,9},{8,13},{12,15},{14,11},{10,7},{6,3},{2,1},{1,2},{5,0},... | collective-permute-start | bytes 663560 | tf_op jit(solution)/shard_map/ppermute | solution.py:423
  84.2 6.9 %collective-permute-start.28 = (bf16[432,256]{1,0:T(8,128)(2,1)S(1)}, bf16[432,256]{1,0:T(8,128)(2,1)S(1)}, u32[]{:S(2)}, u32[]{:S(2)}) collective-permute-start(bf16[432,256]{1,0:T(8,128)(2,1)S(1)} %get-tuple-element.49), channel_id=1, source_target_pairs={{0,4},{4,8},{8,12},{12,14},{14,10},{10,6},{6,2},{2,0},{1,3},{5,1},... | collective-permute-start | bytes 663560 | tf_op jit(solution)/shard_map/ppermute | solution.py:422
  85.1 7.4 %collective-permute-start.29 = (bf16[432,256]{1,0:T(8,128)(2,1)S(1)}, bf16[432,256]{1,0:T(8,128)(2,1)S(1)}, u32[]{:S(2)}, u32[]{:S(2)}) collective-permute-start(bf16[432,256]{1,0:T(8,128)(2,1)S(1)} %get-tuple-element.50), channel_id=1, source_target_pairs={{0,5},{4,9},{8,13},{12,15},{14,11},{10,7},{6,3},{2,1},{1,2},{5,0},... | collective-permute-start | bytes 663560 | tf_op jit(solution)/shard_map/ppermute | solution.py:423

commit v11 on v10

--- a/solution.py
+++ b/solution.py
@@ -380,7 +380,7 @@
         smem=1,
     )
     b3, qb2 = onward(b2), sibling(b2)
-    a4, qa3 = onward(after(a3[:rows], b2, sx, qa1)), sibling(a3)
+    a4, qa3 = onward(after(a3[:rows], b2, qa1)), sibling(a3)
     b4, qb3 = onward(after(b3[:rows], qb1)), sibling(b3)
     qa4 = sibling(a4)
     ones = [a0, a1, a2, a3, a4, qa1, qa2, qa3, qa4]

time: 93.9 us -> 93.9 us (level)
  waiting for transfers between devices: 54.7 us -> 53.5 us
  starting transfers between devices: 17 us -> 18.1 us
    ppermute x2, waiting for transfers between devices: 2.52 us -> 3.86 us  [on_ring(): a3, qa2 = (onward(after(a2, b1)), sibling(a2))]
    ppermute x2, waiting for transfers between devices: 2.76 us -> 1.61 us  [on_ring(): b4, qb3 = (onward(after(b3[:rows], qb1)), sibling(b3))]
  transfers between devices with their start and end apart: 34 -> 34, of which waited for: 21 -> 20; matrix products, arithmetic and copies ran while one was open for 5% -> 5% of each run, Pallas kernels for 16% -> 16%
where the time goes in v11:
time: 93.9 us; the launch traced here: 93.4 us
  waiting for transfers between devices  53.5 us (57%)
  starting transfers between devices  18.1 us (19%)
  Pallas kernels  14.8 us (16%)
  local copies, waits for them, and re-layouts  3.12 us (3%)
  other arithmetic  2.91 us (3%)
    pallas_call x6, Pallas kernels, kernel(): pl.pallas_call(body, name=name, out_shape=outs, in_specs=[pl.BlockSpec(me...  14.8 us
    ppermute x1, waiting for transfers between devices, on_ring(): low = up(jnp.concatenate([features_late[-2:], cot_late[-1:]]))  4.81 us
    ppermute x2, waiting for transfers between devices, on_ring(): a2, qa1 = (onward(a1), sibling(a1))  4.58 us
    ppermute x1, waiting for transfers between devices, on_ring(): two = onward(step(keep_two, got_two, two, 1))  4.37 us
    ppermute x1, waiting for transfers between devices, on_ring(): one = onward(step(keep_one, got_one, after(one, features_out), 2))  3.97 us
    ppermute x2, waiting for transfers between devices, on_ring(): b2, qb1 = (onward(after(b1, low, high)), sibling(b1))  3.86 us
    ppermute x2, waiting for transfers between devices, on_ring(): a3, qa2 = (onward(after(a2, b1)), sibling(a2))  3.86 us
    ppermute x2, waiting for transfers between devices, on_ring(): b3, qb2 = (onward(b2), sibling(b2))  3.78 us
  transfers between devices with their start and end apart: 34, of which 20 were waited for; matrix products, arithmetic and copies ran while one was open for 5% of the time, Pallas kernels for 16%

profile of v11, /device:TPU:0, one launch (start us, length us, event | category | flops | bytes accessed | tf_op | source)
XLA Modules:
  0.0 93.4 jit_solution(3194666335680070339)
XLA Ops:
  0.6 0.5 collective-permute-start
  1.1 2.6 %collective-permute-start.9 = (bf16[432,256]{1,0:T(8,128)(2,1)}, bf16[432,256]{1,0:T(8,128)(2,1)S(1)}, u32[]{:S(2)}, u32[]{:S(2)}) collective-permute-start(bf16[432,256]{1,0:T(8,128)(2,1)} %param.6), channel_id=1, source_target_pairs={{1,4},{5,8},{9,12},{13,14},{15,10},{11,6},{7,2},{3,0},{0,3},{4,1},... | collective-permute-start | bytes 663560 | tf_op jit(solution)/shard_map/ppermute | solution.py:358
  3.8 0.1 collective-permute-start.8
  3.9 1.3 %collective-permute-start.4 = (bf16[432,256]{1,0:T(8,128)(2,1)}, bf16[432,256]{1,0:T(8,128)(2,1)S(1)}, u32[]{:S(2)}, u32[]{:S(2)}) collective-permute-start(bf16[432,256]{1,0:T(8,128)(2,1)} %param.7), channel_id=1, source_target_pairs={{1,4},{5,8},{9,12},{13,14},{15,10},{11,6},{7,2},{3,0},{0,3},{4,1},... | collective-permute-start | bytes 663560 | tf_op jit(solution)/shard_map/ppermute | solution.py:359
  5.2 0.7 collective-permute-start.3
  5.9 1.0 %constant_dynamic-update-slice_fusion.1 = bf16[864,256]{1,0:T(8,128)(2,1)S(1)} fusion(bf16[432,256]{1,0:T(8,128)(2,1)} %param.7), kind=kLoop, calls=%fused_computation.13 | loop fusion | bytes 442368
  6.9 0.9 fusion.3
  7.8 1.0 %fusion.2 = (bf16[2,8,16,256]{3,2,1,0:T(8,128)(2,1)S(1)}, bf16[2,8,16,256]{3,2,1,0:T(8,128)(2,1)S(1)}) fusion(bf16[4,8,16,256]{3,2,1,0:T(8,128)(2,1)} %f_own.1), kind=kLoop, calls=%fused_computation.22 | loop fusion | bytes 524288 | tf_op jit(solution)/shard_map/slice | solution.py:356
  8.9 0.2 collective-permute-start.1
  9.1 3.2 %collective-permute-done.8 = bf16[432,256]{1,0:T(8,128)(2,1)S(1)} collective-permute-done((bf16[432,256]{1,0:T(8,128)(2,1)}, bf16[432,256]{1,0:T(8,128)(2,1)S(1)}, u32[]{:S(2)}, u32[]{:S(2)}) %collective-permute-start.8) | collective-permute-done | bytes 221216 | tf_op jit(solution)/shard_map/ppermute | solution.py:358
  12.3 1.9 %collective-permute-start.2 = (bf16[3,8,16,256]{3,2,1,0:T(8,128)(2,1)S(1)}, bf16[3,8,16,256]{3,2,1,0:T(8,128)(2,1)S(1)}, u32[]{:S(2)}, u32[]{:S(2)}) collective-permute-start(bf16[3,8,16,256]{3,2,1,0:T(8,128)(2,1)S(1)} %pad_maximum_fusion.1), channel_id=1, source_target_pairs={{0,15},{1,0},{2,1},{3,2},{4,3},{5,4},{6,5},{7,6},{8,7},{9,8},{10,9... | collective-permute-start | bytes 589832 | tf_op jit(solution)/shard_map/ppermute | solution.py:356
  14.4 0.3 collective-permute-done.3
  14.7 0.3 collective-permute-done.4
  15.0 4.8 %collective-permute-done.1.low = bf16[3,8,16,256]{3,2,1,0:T(8,128)(2,1)S(1)} collective-permute-done((bf16[3,8,16,256]{3,2,1,0:T(8,128)(2,1)S(1)}, bf16[3,8,16,256]{3,2,1,0:T(8,128)(2,1)S(1)}, u32[]{:S(2)}, u32[]{:S(2)}) %collective-permute-start.1) | collective-permute-done | bytes 196640 | tf_op jit(solution)/shard_map/ppermute | solution.py:355
  19.8 4.6 %collective-permute-done.10.rest_2_ = bf16[864,256]{1,0:T(8,128)(2,1)S(1)} collective-permute-done((bf16[864,256]{1,0:T(8,128)(2,1)S(1)}, bf16[864,256]{1,0:T(8,128)(2,1)S(1)}, u32[]{:S(2)}, u32[]{:S(2)}) %collective-permute-start.10) | collective-permute-done | bytes 442400 | tf_op jit(solution)/shard_map/ppermute | solution.py:360
  24.4 0.3 collective-permute-start.11
  24.7 0.6 collective-permute-start.12
  25.3 3.9 %collective-permute-done.5.rest_2_.rest_11_ = bf16[864,256]{1,0:T(8,128)(2,1)S(1)} collective-permute-done((bf16[864,256]{1,0:T(8,128)(2,1)S(1)}, bf16[864,256]{1,0:T(8,128)(2,1)S(1)}, u32[]{:S(2)}, u32[]{:S(2)}) %collective-permute-start.5) | collective-permute-done | bytes 442400 | tf_op jit(solution)/shard_map/ppermute | solution.py:361
  29.2 0.3 collective-permute-start.6
  29.4 0.6 collective-permute-start.18
  30.0 3.9 %collective-permute-done.11.rest_3_ = bf16[864,256]{1,0:T(8,128)(2,1)S(1)} collective-permute-done((bf16[864,256]{1,0:T(8,128)(2,1)S(1)}, bf16[864,256]{1,0:T(8,128)(2,1)S(1)}, u32[]{:S(2)}, u32[]{:S(2)}) %collective-permute-start.11) | collective-permute-done | bytes 442400 | tf_op jit(solution)/shard_map/ppermute | solution.py:362
  33.9 0.3 collective-permute-start.13
  34.3 0.6 collective-permute-start.15
  34.9 3.8 %collective-permute-done.6.rest_3_.rest_12_ = bf16[864,256]{1,0:T(8,128)(2,1)S(1)} collective-permute-done((bf16[864,256]{1,0:T(8,128)(2,1)S(1)}, bf16[864,256]{1,0:T(8,128)(2,1)S(1)}, u32[]{:S(2)}, u32[]{:S(2)}) %collective-permute-start.6) | collective-permute-done | bytes 442400 | tf_op jit(solution)/shard_map/ppermute | solution.py:382
  38.6 2.4 %collective-permute-done.13.rest_4_ = bf16[432,256]{1,0:T(8,128)(2,1)S(1)} collective-permute-done((bf16[432,256]{1,0:T(8,128)(2,1)S(1)}, bf16[432,256]{1,0:T(8,128)(2,1)S(1)}, u32[]{:S(2)}, u32[]{:S(2)}) %collective-permute-start.13) | collective-permute-done | bytes 221216 | tf_op jit(solution)/shard_map/ppermute | solution.py:383
  41.1 0.6 collective-permute-start.20
  41.6 0.3 collective-permute-start.19
  41.9 0.3 collective-permute-start.21
  42.3 1.3 %prep.1 = (bf16[8,10,16,768]{3,2,1,0:T(8,128)(2,1)S(1)}, bf16[6,10,16,768]{3,2,1,0:T(8,128)(2,1)S(1)}, bf16[256,768]{1,0:T(8,128)(2,1)S(1)}, bf16[3,128,256]{2,1,0:T(8,128)(2,1)S(1)}) custom-call(s32[2,4,16]{2,1,0:T(4,128)S(1)} %bitcast.1, bf16[3,8,16,256]{3,2,1,0:T(8,128)(2,1)S(1)} %collective-permute-done.1.low, bf16[4,8,16,256]{3,2,1,0:T(8,128)(2,1)S(1)} %copy-done, ...), custom_call_target="tpu_custom_call" | custom-call | bytes 4194304 | tf_op jit(solution)/shard_map/prep/pallas_call | solution.py:338
  43.6 2.3 %first.1 = (f32[512,256]{1,0:T(8,128)S(1)}, bf16[512,256]{1,0:T(8,128)(2,1)S(1)}, bf16[256,512]{1,0:T(8,128)(2,1)S(1)}) custom-call(bf16[8,10,16,768]{3,2,1,0:T(8,128)(2,1)S(1)} %get-tuple-element.29.sx_ref, bf16[3,128,256]{2,1,0:T(8,128)(2,1)S(1)} %get-tuple-element.30.mask_ref, bf16[864,256]{1,0:T(8,128)(2,1)S(1)} %constant_dynamic-update-slice_fusion.4.rest_0_, ...), custom_call_target="tpu_custom_call" | custom-call | flops 1811939328 | bytes 4194304 | tf_op jit(solution)/shard_map/first/pallas_call | solution.py:338
  46.0 1.6 %collective-permute-done.19.rest_4_.rest_13_ = bf16[432,256]{1,0:T(8,128)(2,1)S(1)} collective-permute-done((bf16[432,256]{1,0:T(8,128)(2,1)S(1)}, bf16[432,256]{1,0:T(8,128)(2,1)S(1)}, u32[]{:S(2)}, u32[]{:S(2)}) %collective-permute-start.19) | collective-permute-done | bytes 221216 | tf_op jit(solution)/shard_map/ppermute | solution.py:384
  47.6 2.2 %grad_two.1 = (bf16[3456,256]{1,0:T(8,128)(2,1)S(1)}, bf16[3456,256]{1,0:T(8,128)(2,1)S(1)}) custom-call(bf16[6,10,16,768]{3,2,1,0:T(8,128)(2,1)S(1)} %get-tuple-element.34.sc_ref, bf16[256,512]{1,0:T(8,128)(2,1)S(1)} %get-tuple-element.35.act_t_ref), custom_call_target="tpu_custom_call" | custom-call | flops 1811939328 | bytes 4194304 | tf_op jit(solution)/shard_map/grad_two/pallas_call | solution.py:338
  49.8 0.6 collective-permute-start.17
  50.4 2.4 %back.1.sd_ref = bf16[4,10,16,768]{3,2,1,0:T(8,128)(2,1)S(1)} custom-call(bf16[6,10,16,768]{3,2,1,0:T(8,128)(2,1)S(1)} %get-tuple-element.34.sc_ref, f32[512,256]{1,0:T(8,128)S(1)} %get-tuple-element.38.pre_ref, bf16[3,128,256]{2,1,0:T(8,128)(2,1)S(1)} %get-tuple-element.30.mask_ref, bf16[864,256]{1,0:T(8,128)(2,1)S(1)} %constant_dynamic-update-slice_fusion.rest_0_.rest_9_, ...), custom_call_target="tpu_custom_call" | custom-call | flops 1811939328 | bytes 4194304 | tf_op jit(solution)/shard_map/back/pallas_call | solution.py:338
  52.8 2.2 %grad_one.1 = (bf16[3456,256]{1,0:T(8,128)(2,1)S(1)}, bf16[3456,256]{1,0:T(8,128)(2,1)S(1)}) custom-call(bf16[4,10,16,768]{3,2,1,0:T(8,128)(2,1)S(1)} %back.1.sd_ref, bf16[256,768]{1,0:T(8,128)(2,1)S(1)} %get-tuple-element.41.int_ref), custom_call_target="tpu_custom_call" | custom-call | flops 1811939328 | bytes 4194304 | tf_op jit(solution)/shard_map/grad_one/pallas_call | solution.py:338
  55.1 0.1 collective-permute-start.24
  55.2 0.3 collective-permute-start.23
  55.6 3.3 %collective-permute-done.24 = bf16[3456,256]{1,0:T(8,128)(2,1)S(1)} collective-permute-done((bf16[3456,256]{1,0:T(8,128)(2,1)S(1)}, bf16[3456,256]{1,0:T(8,128)(2,1)S(1)}, u32[]{:S(2)}, u32[]{:S(2)}) %collective-permute-start.24) | collective-permute-done | bytes 1769504 | tf_op jit(solution)/shard_map/ppermute | solution.py:441
  58.9 0.3 collective-permute-start.25
  59.2 2.0 %collective-permute-done.23 = bf16[432,256]{1,0:T(8,128)(2,1)S(1)} collective-permute-done((bf16[432,256]{1,0:T(8,128)(2,1)S(1)}, bf16[432,256]{1,0:T(8,128)(2,1)S(1)}, u32[]{:S(2)}, u32[]{:S(2)}) %collective-permute-start.23) | collective-permute-done | bytes 221216 | tf_op jit(solution)/shard_map/ppermute | solution.py:440
  61.2 0.2 add_convert_fusion.2
  61.4 0.3 collective-permute-start.30
  61.7 3.2 %collective-permute-done.25 = bf16[432,256]{1,0:T(8,128)(2,1)S(1)} collective-permute-done((bf16[432,256]{1,0:T(8,128)(2,1)S(1)}, bf16[432,256]{1,0:T(8,128)(2,1)S(1)}, u32[]{:S(2)}, u32[]{:S(2)}) %collective-permute-start.25) | collective-permute-done | bytes 221216 | tf_op jit(solution)/shard_map/ppermute | solution.py:442
  64.9 0.2 add_convert_fusion.5
  65.0 0.3 collective-permute-start.26
  65.4 4.4 %collective-permute-done.30 = bf16[864,256]{1,0:T(8,128)(2,1)S(1)} collective-permute-done((bf16[864,256]{1,0:T(8,128)(2,1)S(1)}, bf16[864,256]{1,0:T(8,128)(2,1)S(1)}, u32[]{:S(2)}, u32[]{:S(2)}) %collective-permute-start.30) | collective-permute-done | bytes 442400 | tf_op jit(solution)/shard_map/ppermute | solution.py:456
  69.7 0.2 add_convert_fusion.1
  69.9 0.5 collective-permute-start.31
  70.4 4.2 %third.1 = bf16[4,8,16,256]{3,2,1,0:T(8,128)(2,1)} custom-call(bf16[8,10,16,768]{3,2,1,0:T(8,128)(2,1)S(1)} %get-tuple-element.29.sx_ref, bf16[512,256]{1,0:T(8,128)(2,1)S(1)} %get-tuple-element.45.act_ref, bf16[3,128,256]{2,1,0:T(8,128)(2,1)S(1)} %get-tuple-element.30.mask_ref, bf16[864,256]{1,0:T(8,128)(2,1)S(1)} %constant_dynamic-update-slice_fusion.4.rest_0_, ...), custom_call_target="tpu_custom_call" | custom-call | flops 1811939328 | bytes 4194304 | tf_op jit(solution)/shard_map/third/pallas_call | solution.py:338
  74.6 0.2 add_convert_fusion.4
  74.8 2.3 %collective-permute-start.27 = (bf16[864,256]{1,0:T(8,128)(2,1)S(1)}, bf16[864,256]{1,0:T(8,128)(2,1)S(1)}, u32[]{:S(2)}, u32[]{:S(2)}) collective-permute-start(bf16[864,256]{1,0:T(8,128)(2,1)S(1)} %add_convert_fusion.4), channel_id=1, source_target_pairs={{0,4},{4,8},{8,12},{12,14},{14,10},{10,6},{6,2},{2,0},{1,3},{5,1},... | collective-permute-start | bytes 1327112 | tf_op jit(solution)/shard_map/ppermute | solution.py:459
  77.1 2.1 %collective-permute-done.31 = bf16[864,256]{1,0:T(8,128)(2,1)S(1)} collective-permute-done((bf16[864,256]{1,0:T(8,128)(2,1)S(1)}, bf16[864,256]{1,0:T(8,128)(2,1)S(1)}, u32[]{:S(2)}, u32[]{:S(2)}) %collective-permute-start.31) | collective-permute-done | bytes 442400 | tf_op jit(solution)/shard_map/ppermute | solution.py:458
  79.2 0.2 add_convert_fusion
  79.4 0.3 collective-permute-start.32
  79.8 0.2 collective-permute-start.33
  80.0 4.0 %collective-permute-done.27 = bf16[864,256]{1,0:T(8,128)(2,1)S(1)} collective-permute-done((bf16[864,256]{1,0:T(8,128)(2,1)S(1)}, bf16[864,256]{1,0:T(8,128)(2,1)S(1)}, u32[]{:S(2)}, u32[]{:S(2)}) %collective-permute-start.27) | collective-permute-done | bytes 442400 | tf_op jit(solution)/shard_map/ppermute | solution.py:459
  84.0 0.2 add_convert_fusion.3
  84.2 1.5 %collective-permute-start.28 = (bf16[432,256]{1,0:T(8,128)(2,1)S(1)}, bf16[432,256]{1,0:T(8,128)(2,1)S(1)}, u32[]{:S(2)}, u32[]{:S(2)}) collective-permute-start(bf16[432,256]{1,0:T(8,128)(2,1)S(1)} %get-tuple-element.49), channel_id=1, source_target_pairs={{0,4},{4,8},{8,12},{12,14},{14,10},{10,6},{6,2},{2,0},{1,3},{5,1},... | collective-permute-start | bytes 663560 | tf_op jit(solution)/shard_map/ppermute | solution.py:422
  85.7 0.6 collective-permute-done.32
  86.3 1.4 %collective-permute-done.33 = bf16[432,256]{1,0:T(8,128)(2,1)S(1)} collective-permute-done((bf16[432,256]{1,0:T(8,128)(2,1)S(1)}, bf16[432,256]{1,0:T(8,128)(2,1)S(1)}, u32[]{:S(2)}, u32[]{:S(2)}) %collective-permute-start.33) | collective-permute-done | bytes 221216 | tf_op jit(solution)/shard_map/ppermute | solution.py:423
  87.7 0.9 add_multiply_fusion
  88.6 2.4 %collective-permute-done.28 = bf16[432,256]{1,0:T(8,128)(2,1)S(1)} collective-permute-done((bf16[432,256]{1,0:T(8,128)(2,1)S(1)}, bf16[432,256]{1,0:T(8,128)(2,1)S(1)}, u32[]{:S(2)}, u32[]{:S(2)}) %collective-permute-start.28) | collective-permute-done | bytes 221216 | tf_op jit(solution)/shard_map/ppermute | solution.py:422
  91.1 1.4 %collective-permute-done.29 = bf16[432,256]{1,0:T(8,128)(2,1)S(1)} collective-permute-done((bf16[432,256]{1,0:T(8,128)(2,1)S(1)}, bf16[432,256]{1,0:T(8,128)(2,1)S(1)}, u32[]{:S(2)}, u32[]{:S(2)}) %collective-permute-start.29) | collective-permute-done | bytes 221216 | tf_op jit(solution)/shard_map/ppermute | solution.py:423
  92.5 0.9 add_multiply_fusion.1
  (44 shorter events, 0.5 us)
Async XLA Ops:
  0.6 6.3 %collective-permute-start = (bf16[432,256]{1,0:T(8,128)(2,1)}, bf16[432,256]{1,0:T(8,128)(2,1)S(1)}, u32[]{:S(2)}, u32[]{:S(2)}) collective-permute-start(bf16[432,256]{1,0:T(8,128)(2,1)} %param.7), channel_id=1, source_target_pairs={{0,1},{1,0},{2,3},{3,2},{4,5},{5,4},{6,7},{7,6},{8,9},{9,8},{10,11... | collective-permute-start | bytes 663560 | tf_op jit(solution)/shard_map/ppermute | solution.py:353
  1.1 13.1 %collective-permute-start.9 = (bf16[432,256]{1,0:T(8,128)(2,1)}, bf16[432,256]{1,0:T(8,128)(2,1)S(1)}, u32[]{:S(2)}, u32[]{:S(2)}) collective-permute-start(bf16[432,256]{1,0:T(8,128)(2,1)} %param.6), channel_id=1, source_target_pairs={{1,4},{5,8},{9,12},{13,14},{15,10},{11,6},{7,2},{3,0},{0,3},{4,1},... | collective-permute-start | bytes 663560 | tf_op jit(solution)/shard_map/ppermute | solution.py:358
  3.8 8.6 %collective-permute-start.8 = (bf16[432,256]{1,0:T(8,128)(2,1)}, bf16[432,256]{1,0:T(8,128)(2,1)S(1)}, u32[]{:S(2)}, u32[]{:S(2)}) collective-permute-start(bf16[432,256]{1,0:T(8,128)(2,1)} %param.6), channel_id=1, source_target_pairs={{0,4},{4,8},{8,12},{12,14},{14,10},{10,6},{6,2},{2,0},{1,3},{5,1},... | collective-permute-start | bytes 663560 | tf_op jit(solution)/shard_map/ppermute | solution.py:358
  3.9 11.1 %collective-permute-start.4 = (bf16[432,256]{1,0:T(8,128)(2,1)}, bf16[432,256]{1,0:T(8,128)(2,1)S(1)}, u32[]{:S(2)}, u32[]{:S(2)}) collective-permute-start(bf16[432,256]{1,0:T(8,128)(2,1)} %param.7), channel_id=1, source_target_pairs={{1,4},{5,8},{9,12},{13,14},{15,10},{11,6},{7,2},{3,0},{0,3},{4,1},... | collective-permute-start | bytes 663560 | tf_op jit(solution)/shard_map/ppermute | solution.py:359
  5.2 9.5 %collective-permute-start.3 = (bf16[432,256]{1,0:T(8,128)(2,1)}, bf16[432,256]{1,0:T(8,128)(2,1)S(1)}, u32[]{:S(2)}, u32[]{:S(2)}) collective-permute-start(bf16[432,256]{1,0:T(8,128)(2,1)} %param.7), channel_id=1, source_target_pairs={{0,4},{4,8},{8,12},{12,14},{14,10},{10,6},{6,2},{2,0},{1,3},{5,1},... | collective-permute-start | bytes 663560 | tf_op jit(solution)/shard_map/ppermute | solution.py:359
  7.8 30.8 %copy-start.3 = (bf16[432,256]{1,0:T(8,128)(2,1)S(1)}, bf16[432,256]{1,0:T(8,128)(2,1)}, u32[]{:S(2)}) copy-start(bf16[432,256]{1,0:T(8,128)(2,1)} %param.6) | copy-start | bytes 663556
  8.9 11.0 %collective-permute-start.1 = (bf16[3,8,16,256]{3,2,1,0:T(8,128)(2,1)S(1)}, bf16[3,8,16,256]{3,2,1,0:T(8,128)(2,1)S(1)}, u32[]{:S(2)}, u32[]{:S(2)}) collective-permute-start(bf16[3,8,16,256]{3,2,1,0:T(8,128)(2,1)S(1)} %pad_maximum_fusion), channel_id=1, source_target_pairs={{0,1},{1,2},{2,3},{3,4},{4,5},{5,6},{6,7},{7,8},{8,9},{9,10},{10,1... | collective-permute-start | bytes 589832 | tf_op jit(solution)/shard_map/ppermute | solution.py:355
  9.1 33.2 %copy-start = (bf16[4,8,16,256]{3,2,1,0:T(8,128)(2,1)S(1)}, bf16[4,8,16,256]{3,2,1,0:T(8,128)(2,1)}, u32[]{:S(2)}) copy-start(bf16[4,8,16,256]{3,2,1,0:T(8,128)(2,1)} %f_own.1) | copy-start | bytes 786436
  9.1 33.2 %copy-start.1 = (bf16[4,8,16,256]{3,2,1,0:T(8,128)(2,1)S(1)}, bf16[4,8,16,256]{3,2,1,0:T(8,128)(2,1)}, u32[]{:S(2)}) copy-start(bf16[4,8,16,256]{3,2,1,0:T(8,128)(2,1)} %c_own.1) | copy-start | bytes 786436
  9.1 33.2 %copy-start.2 = (s32[16,2,4]{0,2,1:T(4,128)S(1)}, s32[16,2,4]{0,2,1:T(4,128)}, u32[]{:S(2)}) copy-start(s32[16,2,4]{0,2,1:T(4,128)} %param.9) | copy-start | bytes 1540
  12.3 7.5 %collective-permute-start.2 = (bf16[3,8,16,256]{3,2,1,0:T(8,128)(2,1)S(1)}, bf16[3,8,16,256]{3,2,1,0:T(8,128)(2,1)S(1)}, u32[]{:S(2)}, u32[]{:S(2)}) collective-permute-start(bf16[3,8,16,256]{3,2,1,0:T(8,128)(2,1)S(1)} %pad_maximum_fusion.1), channel_id=1, source_target_pairs={{0,15},{1,0},{2,1},{3,2},{4,3},{5,4},{6,5},{7,6},{8,7},{9,8},{10,9... | collective-permute-start | bytes 589832 | tf_op jit(solution)/shard_map/ppermute | solution.py:356
  14.3 10.1 %collective-permute-start.10 = (bf16[864,256]{1,0:T(8,128)(2,1)S(1)}, bf16[864,256]{1,0:T(8,128)(2,1)S(1)}, u32[]{:S(2)}, u32[]{:S(2)}) collective-permute-start(bf16[864,256]{1,0:T(8,128)(2,1)S(1)} %constant_dynamic-update-slice_fusion.6.rest_1_), channel_id=1, source_target_pairs={{0,4},{4,8},{8,12},{12,14},{14,10},{10,6},{6,2},{2,0},{1,3},{5,1},... | collective-permute-start | bytes 1327112 | tf_op jit(solution)/shard_map/ppermute | solution.py:360
  19.8 9.3 %collective-permute-start.5 = (bf16[864,256]{1,0:T(8,128)(2,1)S(1)}, bf16[864,256]{1,0:T(8,128)(2,1)S(1)}, u32[]{:S(2)}, u32[]{:S(2)}) collective-permute-start(bf16[864,256]{1,0:T(8,128)(2,1)S(1)} %constant_dynamic-update-slice_fusion.2.rest_1_.rest_10_), channel_id=1, source_target_pairs={{0,4},{4,8},{8,12},{12,14},{14,10},{10,6},{6,2},{2,0},{1,3},{5,1},... | collective-permute-start | bytes 1327112 | tf_op jit(solution)/shard_map/ppermute | solution.py:361
  24.4 9.5 %collective-permute-start.11 = (bf16[864,256]{1,0:T(8,128)(2,1)S(1)}, bf16[864,256]{1,0:T(8,128)(2,1)S(1)}, u32[]{:S(2)}, u32[]{:S(2)}) collective-permute-start(bf16[864,256]{1,0:T(8,128)(2,1)S(1)} %collective-permute-done.10.rest_2_), channel_id=1, source_target_pairs={{0,4},{4,8},{8,12},{12,14},{14,10},{10,6},{6,2},{2,0},{1,3},{5,1},... | collective-permute-start | bytes 1327112 | tf_op jit(solution)/shard_map/ppermute | solution.py:362
  24.7 9.2 %collective-permute-start.12 = (bf16[864,256]{1,0:T(8,128)(2,1)S(1)}, bf16[864,256]{1,0:T(8,128)(2,1)S(1)}, u32[]{:S(2)}, u32[]{:S(2)}) collective-permute-start(bf16[864,256]{1,0:T(8,128)(2,1)S(1)} %constant_dynamic-update-slice_fusion.6.rest_1_), channel_id=1, source_target_pairs={{0,1},{1,0},{2,3},{3,2},{4,5},{5,4},{6,7},{7,6},{8,9},{9,8},{10,11... | collective-permute-start | bytes 1327112 | tf_op jit(solution)/shard_map/ppermute | solution.py:360
  29.2 9.5 %collective-permute-start.6 = (bf16[864,256]{1,0:T(8,128)(2,1)S(1)}, bf16[864,256]{1,0:T(8,128)(2,1)S(1)}, u32[]{:S(2)}, u32[]{:S(2)}) collective-permute-start(bf16[864,256]{1,0:T(8,128)(2,1)S(1)} %collective-permute-done.5.rest_2_.rest_11_), channel_id=1, source_target_pairs={{0,4},{4,8},{8,12},{12,14},{14,10},{10,6},{6,2},{2,0},{1,3},{5,1},... | collective-permute-start | bytes 1327112 | tf_op jit(solution)/shard_map/ppermute | solution.py:382
  29.4 11.6 %collective-permute-start.18 = (bf16[864,256]{1,0:T(8,128)(2,1)S(1)}, bf16[864,256]{1,0:T(8,128)(2,1)S(1)}, u32[]{:S(2)}, u32[]{:S(2)}) collective-permute-start(bf16[864,256]{1,0:T(8,128)(2,1)S(1)} %constant_dynamic-update-slice_fusion.2.rest_1_.rest_10_), channel_id=1, source_target_pairs={{0,1},{1,0},{2,3},{3,2},{4,5},{5,4},{6,7},{7,6},{8,9},{9,8},{10,11... | collective-permute-start | bytes 1327112 | tf_op jit(solution)/shard_map/ppermute | solution.py:361
  30.0 11.9 %collective-permute-start.14 = (bf16[864,256]{1,0:T(8,128)(2,1)S(1)}, bf16[864,256]{1,0:T(8,128)(2,1)S(1)}, u32[]{:S(2)}, u32[]{:S(2)}) collective-permute-start(bf16[864,256]{1,0:T(8,128)(2,1)S(1)} %collective-permute-done.10.rest_2_), channel_id=1, source_target_pairs={{0,1},{1,0},{2,3},{3,2},{4,5},{5,4},{6,7},{7,6},{8,9},{9,8},{10,11... | collective-permute-start | bytes 1327112 | tf_op jit(solution)/shard_map/ppermute | solution.py:362
  33.9 7.1 %collective-permute-start.13 = (bf16[432,256]{1,0:T(8,128)(2,1)S(1)}, bf16[432,256]{1,0:T(8,128)(2,1)S(1)}, u32[]{:S(2)}, u32[]{:S(2)}) collective-permute-start(bf16[432,256]{1,0:T(8,128)(2,1)S(1)} %slice.120), channel_id=1, source_target_pairs={{0,4},{4,8},{8,12},{12,14},{14,10},{10,6},{6,2},{2,0},{1,3},{5,1},... | collective-permute-start | bytes 663560 | tf_op jit(solution)/shard_map/ppermute | solution.py:383
  34.3 9.4 %collective-permute-start.15 = (bf16[864,256]{1,0:T(8,128)(2,1)S(1)}, bf16[864,256]{1,0:T(8,128)(2,1)S(1)}, u32[]{:S(2)}, u32[]{:S(2)}) collective-permute-start(bf16[864,256]{1,0:T(8,128)(2,1)S(1)} %collective-permute-done.11.rest_3_), channel_id=1, source_target_pairs={{0,1},{1,0},{2,3},{3,2},{4,5},{5,4},{6,7},{7,6},{8,9},{9,8},{10,11... | collective-permute-start | bytes 1327112 | tf_op jit(solution)/shard_map/ppermute | solution.py:383
  38.6 3.0 %collective-permute-start.7 = (bf16[432,256]{1,0:T(8,128)(2,1)S(1)}, bf16[432,256]{1,0:T(8,128)(2,1)S(1)}, u32[]{:S(2)}, u32[]{:S(2)}) collective-permute-start(bf16[432,256]{1,0:T(8,128)(2,1)S(1)} %copy-done.3), channel_id=1, source_target_pairs={{0,1},{1,0},{2,3},{3,2},{4,5},{5,4},{6,7},{7,6},{8,9},{9,8},{10,11... | collective-permute-start | bytes 663560 | tf_op jit(solution)/shard_map/ppermute | solution.py:352
  41.0 2.6 %collective-permute-start.16 = (bf16[432,256]{1,0:T(8,128)(2,1)S(1)}, bf16[432,256]{1,0:T(8,128)(2,1)S(1)}, u32[]{:S(2)}, u32[]{:S(2)}) collective-permute-start(bf16[432,256]{1,0:T(8,128)(2,1)S(1)} %collective-permute-done.13.rest_4_), channel_id=1, source_target_pairs={{0,1},{1,0},{2,3},{3,2},{4,5},{5,4},{6,7},{7,6},{8,9},{9,8},{10,11... | collective-permute-start | bytes 663560 | tf_op jit(solution)/shard_map/ppermute | solution.py:385
  41.1 9.3 %collective-permute-start.20 = (bf16[864,256]{1,0:T(8,128)(2,1)S(1)}, bf16[864,256]{1,0:T(8,128)(2,1)S(1)}, u32[]{:S(2)}, u32[]{:S(2)}) collective-permute-start(bf16[864,256]{1,0:T(8,128)(2,1)S(1)} %collective-permute-done.5.rest_2_.rest_11_), channel_id=1, source_target_pairs={{0,1},{1,0},{2,3},{3,2},{4,5},{5,4},{6,7},{7,6},{8,9},{9,8},{10,11... | collective-permute-start | bytes 1327112 | tf_op jit(solution)/shard_map/ppermute | solution.py:382
  41.6 5.9 %collective-permute-start.19 = (bf16[432,256]{1,0:T(8,128)(2,1)S(1)}, bf16[432,256]{1,0:T(8,128)(2,1)S(1)}, u32[]{:S(2)}, u32[]{:S(2)}) collective-permute-start(bf16[432,256]{1,0:T(8,128)(2,1)S(1)} %slice.121), channel_id=1, source_target_pairs={{0,4},{4,8},{8,12},{12,14},{14,10},{10,6},{6,2},{2,0},{1,3},{5,1},... | collective-permute-start | bytes 663560 | tf_op jit(solution)/shard_map/ppermute | solution.py:384
  41.9 8.5 %collective-permute-start.21 = (bf16[864,256]{1,0:T(8,128)(2,1)S(1)}, bf16[864,256]{1,0:T(8,128)(2,1)S(1)}, u32[]{:S(2)}, u32[]{:S(2)}) collective-permute-start(bf16[864,256]{1,0:T(8,128)(2,1)S(1)} %collective-permute-done.6.rest_3_.rest_12_), channel_id=1, source_target_pairs={{0,1},{1,0},{2,3},{3,2},{4,5},{5,4},{6,7},{7,6},{8,9},{9,8},{10,11... | collective-permute-start | bytes 1327112 | tf_op jit(solution)/shard_map/ppermute | solution.py:384
  47.6 2.8 %collective-permute-start.22 = (bf16[432,256]{1,0:T(8,128)(2,1)S(1)}, bf16[432,256]{1,0:T(8,128)(2,1)S(1)}, u32[]{:S(2)}, u32[]{:S(2)}) collective-permute-start(bf16[432,256]{1,0:T(8,128)(2,1)S(1)} %collective-permute-done.19.rest_4_.rest_13_), channel_id=1, source_target_pairs={{0,1},{1,0},{2,3},{3,2},{4,5},{5,4},{6,7},{7,6},{8,9},{9,8},{10,11... | collective-permute-start | bytes 663560 | tf_op jit(solution)/shard_map/ppermute | solution.py:404
  49.8 5.4 %collective-permute-start.17 = (bf16[3456,256]{1,0:T(8,128)(2,1)S(1)}, bf16[3456,256]{1,0:T(8,128)(2,1)S(1)}, u32[]{:S(2)}, u32[]{:S(2)}) collective-permute-start(bf16[3456,256]{1,0:T(8,128)(2,1)S(1)} %get-tuple-element.37), channel_id=1, source_target_pairs={{0,1},{1,0},{2,3},{3,2},{4,5},{5,4},{6,7},{7,6},{8,9},{9,8},{10,11... | collective-permute-start | bytes 5308424 | tf_op jit(solution)/shard_map/ppermute | solution.py:409
  55.1 3.8 %collective-permute-start.24 = (bf16[3456,256]{1,0:T(8,128)(2,1)S(1)}, bf16[3456,256]{1,0:T(8,128)(2,1)S(1)}, u32[]{:S(2)}, u32[]{:S(2)}) collective-permute-start(bf16[3456,256]{1,0:T(8,128)(2,1)S(1)} %get-tuple-element.44), channel_id=1, source_target_pairs={{0,1},{1,0},{2,3},{3,2},{4,5},{5,4},{6,7},{7,6},{8,9},{9,8},{10,11... | collective-permute-start | bytes 5308424 | tf_op jit(solution)/shard_map/ppermute | solution.py:441
  55.2 6.0 %collective-permute-start.23 = (bf16[432,256]{1,0:T(8,128)(2,1)S(1)}, bf16[432,256]{1,0:T(8,128)(2,1)S(1)}, u32[]{:S(2)}, u32[]{:S(2)}) collective-permute-start(bf16[432,256]{1,0:T(8,128)(2,1)S(1)} %add_convert_fusion.7), channel_id=1, source_target_pairs={{0,4},{4,8},{8,12},{12,14},{14,10},{10,6},{6,2},{2,0},{1,3},{5,1},... | collective-permute-start | bytes 663560 | tf_op jit(solution)/shard_map/ppermute | solution.py:440
  58.9 6.0 %collective-permute-start.25 = (bf16[432,256]{1,0:T(8,128)(2,1)S(1)}, bf16[432,256]{1,0:T(8,128)(2,1)S(1)}, u32[]{:S(2)}, u32[]{:S(2)}) collective-permute-start(bf16[432,256]{1,0:T(8,128)(2,1)S(1)} %add_convert_fusion.6), channel_id=1, source_target_pairs={{0,4},{4,8},{8,12},{12,14},{14,10},{10,6},{6,2},{2,0},{1,3},{5,1},... | collective-permute-start | bytes 663560 | tf_op jit(solution)/shard_map/ppermute | solution.py:442
  61.4 8.4 %collective-permute-start.30 = (bf16[864,256]{1,0:T(8,128)(2,1)S(1)}, bf16[864,256]{1,0:T(8,128)(2,1)S(1)}, u32[]{:S(2)}, u32[]{:S(2)}) collective-permute-start(bf16[864,256]{1,0:T(8,128)(2,1)S(1)} %add_convert_fusion.2), channel_id=1, source_target_pairs={{0,4},{4,8},{8,12},{12,14},{14,10},{10,6},{6,2},{2,0},{1,3},{5,1},... | collective-permute-start | bytes 1327112 | tf_op jit(solution)/shard_map/ppermute | solution.py:456
  65.0 9.6 %collective-permute-start.26 = (bf16[864,256]{1,0:T(8,128)(2,1)S(1)}, bf16[864,256]{1,0:T(8,128)(2,1)S(1)}, u32[]{:S(2)}, u32[]{:S(2)}) collective-permute-start(bf16[864,256]{1,0:T(8,128)(2,1)S(1)} %add_convert_fusion.5), channel_id=1, source_target_pairs={{0,4},{4,8},{8,12},{12,14},{14,10},{10,6},{6,2},{2,0},{1,3},{5,1},... | collective-permute-start | bytes 1327112 | tf_op jit(solution)/shard_map/ppermute | solution.py:457
  69.9 9.3 %collective-permute-start.31 = (bf16[864,256]{1,0:T(8,128)(2,1)S(1)}, bf16[864,256]{1,0:T(8,128)(2,1)S(1)}, u32[]{:S(2)}, u32[]{:S(2)}) collective-permute-start(bf16[864,256]{1,0:T(8,128)(2,1)S(1)} %add_convert_fusion.1), channel_id=1, source_target_pairs={{0,4},{4,8},{8,12},{12,14},{14,10},{10,6},{6,2},{2,0},{1,3},{5,1},... | collective-permute-start | bytes 1327112 | tf_op jit(solution)/shard_map/ppermute | solution.py:458
  74.8 9.1 %collective-permute-start.27 = (bf16[864,256]{1,0:T(8,128)(2,1)S(1)}, bf16[864,256]{1,0:T(8,128)(2,1)S(1)}, u32[]{:S(2)}, u32[]{:S(2)}) collective-permute-start(bf16[864,256]{1,0:T(8,128)(2,1)S(1)} %add_convert_fusion.4), channel_id=1, source_target_pairs={{0,4},{4,8},{8,12},{12,14},{14,10},{10,6},{6,2},{2,0},{1,3},{5,1},... | collective-permute-start | bytes 1327112 | tf_op jit(solution)/shard_map/ppermute | solution.py:459
  79.4 6.9 %collective-permute-start.32 = (bf16[432,256]{1,0:T(8,128)(2,1)S(1)}, bf16[432,256]{1,0:T(8,128)(2,1)S(1)}, u32[]{:S(2)}, u32[]{:S(2)}) collective-permute-start(bf16[432,256]{1,0:T(8,128)(2,1)S(1)} %get-tuple-element.47), channel_id=1, source_target_pairs={{0,4},{4,8},{8,12},{12,14},{14,10},{10,6},{6,2},{2,0},{1,3},{5,1},... | collective-permute-start | bytes 663560 | tf_op jit(solution)/shard_map/ppermute | solution.py:422
  79.8 8.0 %collective-permute-start.33 = (bf16[432,256]{1,0:T(8,128)(2,1)S(1)}, bf16[432,256]{1,0:T(8,128)(2,1)S(1)}, u32[]{:S(2)}, u32[]{:S(2)}) collective-permute-start(bf16[432,256]{1,0:T(8,128)(2,1)S(1)} %get-tuple-element.48), channel_id=1, source_target_pairs={{0,5},{4,9},{8,13},{12,15},{14,11},{10,7},{6,3},{2,1},{1,2},{5,0},... | collective-permute-start | bytes 663560 | tf_op jit(solution)/shard_map/ppermute | solution.py:423
  84.2 6.9 %collective-permute-start.28 = (bf16[432,256]{1,0:T(8,128)(2,1)S(1)}, bf16[432,256]{1,0:T(8,128)(2,1)S(1)}, u32[]{:S(2)}, u32[]{:S(2)}) collective-permute-start(bf16[432,256]{1,0:T(8,128)(2,1)S(1)} %get-tuple-element.49), channel_id=1, source_target_pairs={{0,4},{4,8},{8,12},{12,14},{14,10},{10,6},{6,2},{2,0},{1,3},{5,1},... | collective-permute-start | bytes 663560 | tf_op jit(solution)/shard_map/ppermute | solution.py:422
  85.7 6.8 %collective-permute-start.29 = (bf16[432,256]{1,0:T(8,128)(2,1)S(1)}, bf16[432,256]{1,0:T(8,128)(2,1)S(1)}, u32[]{:S(2)}, u32[]{:S(2)}) collective-permute-start(bf16[432,256]{1,0:T(8,128)(2,1)S(1)} %get-tuple-element.50), channel_id=1, source_target_pairs={{0,5},{4,9},{8,13},{12,15},{14,11},{10,7},{6,3},{2,1},{1,2},{5,0},... | collective-permute-start | bytes 663560 | tf_op jit(solution)/shard_map/ppermute | solution.py:423
